TPU v7x, 32 devices: a whole 2x2x4 slice. The times are simulated.
32 devices in a mesh: shard: 8 (over z, x), ctx: 2 (over y), tp: 2 (over core).
Axes of the slice: x: 2, y: 2, z: 4, core: 2. Of those that a mesh axis runs over, the one named last changes fastest.
Arguments:
- video_clips: bfloat16 [16, 8, 196, 768], P('shard', 'ctx', 'tp'), may hold values from -6 to 6
- cotangent: float32 [16, 8, 196, 768], P('shard', 'ctx', 'tp'), may hold values from -6 to 6
- slot_clip: int32 [16], P('shard'), may hold values from -1 to 9, as said below
- valid_places: int32 [10], replicated, may hold values from 49 to 196, as said below
- norm_gain: float32 [2, 3, 768], replicated, may hold values from 0.5 to 1.5
- norm_bias: float32 [2, 3, 768], replicated, may hold values from -1 to 1
- triple_weight: bfloat16 [2, 2, 768, 3, 768], P(None, None, ('shard', 'ctx'), None, 'tp'), may hold values from -0.21875 to 0.21875
- entry_bias: float32 [2, 2, 2, 768], P(None, None, None, 'tp'), may hold values from -1.5 to 1.5
- merge_weight: bfloat16 [2, 2, 768, 768], P(None, None, 'tp', ('shard', 'ctx')), may hold values from -0.625 to 0.625
- branch_bias: float32 [2, 4, 768], replicated, may hold values from -1.5 to 1.5
- mixing_weight: bfloat16 [2, 768, 768], P(None, ('shard', 'ctx', 'tp')), may hold values from -0.21875 to 0.21875
- up_weight: bfloat16 [2, 768, 3072], P(None, ('shard', 'ctx'), 'tp'), may hold values from -0.21875 to 0.21875
- up_bias: float32 [2, 3072], P(None, 'tp'), may hold values from -1.5 to 1.5
- down_weight: bfloat16 [2, 3072, 768], P(None, 'tp', ('shard', 'ctx')), may hold values from -0.109375 to 0.109375
Outputs:
- block_output: bfloat16 [16, 8, 196, 768], P('shard', 'ctx', 'tp')
- input_grad: float32 [16, 8, 196, 768], P('shard', 'ctx', 'tp')
- gain_grad: float32 [2, 3, 768], replicated
- shift_grad: float32 [2, 3, 768], replicated
- triple_grad: float32 [2, 2, 768, 3, 768], P(None, None, ('shard', 'ctx'), None, 'tp')
- entry_grad: float32 [2, 2, 2, 768], P(None, None, None, 'tp')
- merge_grad: float32 [2, 2, 768, 768], P(None, None, 'tp', ('shard', 'ctx'))
- branch_grad: float32 [2, 4, 768], replicated
- mixing_grad: float32 [2, 768, 768], P(None, ('shard', 'ctx', 'tp'))
- up_grad: float32 [2, 768, 3072], P(None, ('shard', 'ctx'), 'tp')
- up_bias_grad: float32 [2, 3072], P(None, 'tp')
- down_grad: float32 [2, 3072, 768], P(None, 'tp', ('shard', 'ctx'))
- root_squares: float32 [2, 4], replicated
Inputs may be any that keep to these rules, and one draw needn't show every extreme that they name: `slot_clip`: each of the 10 clips stands in exactly one slot. Slots 2 s and 2 s + 1 belong to index s of shard; the first always holds a clip, the second for 2 indices drawn from the seed; -1 marks an empty slot. `valid_places`: the first that many places of every frame of a clip are valid; at least one clip has all 196 valid.
All inputs are finite; a program needn't handle non-finite values.
Results may differ from a plain program's by a relative error of at most 0.03.
Values may be sent and summed in bfloat16 or wider, within the bound.
A program may use at most 384 MiB of HBM per device.

v0:
```python
import jax
import jax.numpy as jnp
from jax import lax
from jax.sharding import PartitionSpec as P

HEAD_DIM = 64
FRAMES = 8
LAYERS = 2


far_below = -1000000000.0
epsilon = 1e-06
root_half = 0.7071067811865476
gauss_scale = 0.3989422804014327
temporal_forms = ("cfphd,cgphd->cphfg", "cphfg,cgphd->cfphd", "cphfg,cfphd->cgphd")
spatial_forms = ("cfphd,cfqhd->cfhpq", "cfhpq,cfqhd->cfphd", "cfhpq,cfphd->cfqhd")


def dense(left, right):
    flat = left.reshape(-1, left.shape[-1])
    result = jnp.dot(flat, right, preferred_element_type=jnp.float32)
    return result.reshape(left.shape[:-1] + (right.shape[-1],))


def dense_back(incoming, right):
    flat = incoming.reshape(-1, incoming.shape[-1])
    result = lax.dot_general(
        flat, right, (((1,), (1,)), ((), ())), preferred_element_type=jnp.float32
    )
    return result.reshape(incoming.shape[:-1] + (right.shape[0],))


def outer_rows(left, right):
    first = left.reshape(-1, left.shape[-1])
    second = right.reshape(-1, right.shape[-1])
    return lax.dot_general(
        first, second, (((0,), (0,)), ((), ())), preferred_element_type=jnp.float32
    )


def row_total(value):
    return jnp.sum(value.astype(jnp.float32).reshape(-1, value.shape[-1]), axis=0)


def split_heads(value):
    return value.reshape(value.shape[:-1] + (value.shape[-1] // HEAD_DIM, HEAD_DIM))


def merge_heads(value):
    return value.reshape(value.shape[:-2] + (value.shape[-2] * value.shape[-1],))


def norm_forward(state, gain, shift):
    center = state - jnp.mean(state, axis=-1, keepdims=True)
    scale = lax.rsqrt(jnp.mean(center * center, axis=-1, keepdims=True) + epsilon)
    unit = center * scale
    return ((unit * gain + shift).astype(jnp.bfloat16), unit, scale)


def norm_backward(incoming, unit, scale, gain):
    along = incoming * gain
    back = scale * (
        along
        - jnp.mean(along, axis=-1, keepdims=True)
        - unit * jnp.mean(along * unit, axis=-1, keepdims=True)
    )
    return (back, row_total(incoming * unit), row_total(incoming))


def gelu_slope(hidden):
    below_share = 0.5 * (1.0 + lax.erf(hidden * root_half))
    return below_share + hidden * gauss_scale * jnp.exp(-0.5 * hidden * hidden)


def score_rows(query, keys, forms, allowed, scale):
    scores = jnp.einsum(forms[0], query, keys, preferred_element_type=jnp.float32) * scale
    if allowed is not None:
        scores = jnp.where(allowed, scores, far_below)
    return scores


def attend(query, keys, values, forms, allowed, scale):
    scores = score_rows(query, keys, forms, allowed, scale)
    top = jnp.max(scores, axis=-1, keepdims=True)
    raised = jnp.exp(scores - top)
    total = jnp.sum(raised, axis=-1, keepdims=True)
    shares = raised / total
    mixed = jnp.einsum(
        forms[1], shares.astype(jnp.bfloat16), values, preferred_element_type=jnp.float32
    )
    return (merge_heads(mixed.astype(jnp.bfloat16)), top, total)


def attend_back(back_mixed, query, keys, values, top, total, forms, allowed, scale):
    scores = score_rows(query, keys, forms, allowed, scale)
    shares = jnp.exp(scores - top) / total
    back_shares = jnp.einsum(forms[0], back_mixed, values, preferred_element_type=jnp.float32)
    values_grad = jnp.einsum(
        forms[2], shares.astype(jnp.bfloat16), back_mixed, preferred_element_type=jnp.float32
    )
    inner = jnp.sum(back_shares * shares, axis=-1, keepdims=True)
    back_scores = (shares * (back_shares - inner)).astype(jnp.bfloat16)
    query_grad = jnp.einsum(forms[1], back_scores, keys, preferred_element_type=jnp.float32) * scale
    keys_grad = jnp.einsum(forms[2], back_scores, query, preferred_element_type=jnp.float32) * scale
    return (
        merge_heads(query_grad.astype(jnp.bfloat16)),
        merge_heads(keys_grad.astype(jnp.bfloat16)),
        merge_heads(values_grad.astype(jnp.bfloat16)),
    )


def project_triple(normed, triple, entry):
    width = normed.shape[-1]
    split_width = triple.shape[-1]
    joined = dense(normed, triple.reshape(width, 3 * split_width))
    joined = joined.reshape(joined.shape[:-1] + (3, split_width))
    query = (joined[..., 0, :] + entry[0]).astype(jnp.bfloat16)
    keys = joined[..., 1, :].astype(jnp.bfloat16)
    values = (joined[..., 2, :] + entry[1]).astype(jnp.bfloat16)
    return (query, keys, values)


def triple_backward(normed, back_query, back_keys, back_values, triple):
    width = normed.shape[-1]
    split_width = triple.shape[-1]
    stacked = jnp.stack([back_query, back_keys, back_values], axis=-2)
    stacked = stacked.reshape(stacked.shape[:-2] + (3 * split_width,))
    triple_part = outer_rows(normed, stacked).reshape(width, 3, split_width)
    entry_part = jnp.stack([row_total(back_query), row_total(back_values)])
    back_normed = dense_back(stacked, triple.reshape(width, 3 * split_width))
    return (triple_part, entry_part, back_normed)


def temporal_weights(triple, merge, entry):
    return (triple[0], merge[0], entry[0])


def gather_layer(triple, merge, upward, downward, mixing, entry):
    gathered = (
        lax.all_gather(triple, ("shard", "ctx"), axis=1, tiled=True),
        lax.all_gather(merge, ("shard", "ctx"), axis=2, tiled=True),
        lax.all_gather(upward, ("shard", "ctx"), axis=0, tiled=True),
        lax.all_gather(downward, ("shard", "ctx"), axis=1, tiled=True),
    )
    mixing_full = lax.all_gather(mixing, ("shard", "ctx", "tp"), axis=0, tiled=True)
    own = tuple(gathered) + (mixing_full,)
    return own + temporal_weights(own[0], own[1], entry)


def token_rows(normed):
    return lax.all_gather(normed, "tp", axis=2, tiled=True)


def branch_sums(partial_value):
    return lax.psum_scatter(
        partial_value.astype(jnp.bfloat16), "tp", scatter_dimension=2, tiled=True
    ).astype(jnp.float32)


def grad_rows(rounded):
    return lax.all_gather(rounded, "tp", axis=2, tiled=True)


def input_sums(partial_value):
    return lax.psum_scatter(
        partial_value.astype(jnp.bfloat16), "tp", scatter_dimension=2, tiled=True
    ).astype(jnp.float32)


def per_device(
    video_clips,
    cotangent,
    slot_clip,
    valid_places,
    norm_gain,
    norm_bias,
    triple_weight,
    entry_bias,
    merge_weight,
    branch_bias,
    mixing_weight,
    up_weight,
    up_bias,
    down_weight,
):
    slots, frames_here, places_here, width = video_clips.shape
    all_places = places_here * lax.axis_size("tp")
    scale = HEAD_DIM ** (-0.5)
    clip_ids = jnp.arange(valid_places.shape[0], dtype=jnp.int32)
    counts = jnp.sum(
        jnp.where(slot_clip[:, None] == clip_ids[None, :], valid_places[None, :], 0), axis=1
    )
    place_ids = jnp.arange(all_places, dtype=jnp.int32)
    allowed_all = place_ids[None, :] < counts[:, None]
    spatial_mask = allowed_all[:, None, None, None, :]
    own_places = lax.axis_index("tp") * places_here + jnp.arange(places_here, dtype=jnp.int32)
    valid_here = (own_places[None, :] < counts[:, None]).astype(jnp.float32)[:, None, :, None]
    state = video_clips.astype(jnp.float32)
    stored = []
    squares = []
    for layer in range(LAYERS):
        weights = gather_layer(
            triple_weight[layer],
            merge_weight[layer],
            up_weight[layer],
            down_weight[layer],
            mixing_weight[layer],
            entry_bias[layer],
        )
        triple, merge, upward, downward, mixing, time_triple, time_merge, time_entry = weights
        gain = norm_gain[layer]
        shift = norm_bias[layer]
        entry = entry_bias[layer]
        bias = branch_bias[layer]
        normed, unit_t, scale_t = norm_forward(state, gain[0], shift[0])
        normed_t = token_rows(normed)
        query, keys, values = project_triple(normed_t, time_triple, time_entry)
        query_p, keys_p, values_p = (
            lax.all_to_all(query, "ctx", split_axis=2, concat_axis=1, tiled=True),
            lax.all_to_all(keys, "ctx", split_axis=2, concat_axis=1, tiled=True),
            lax.all_to_all(values, "ctx", split_axis=2, concat_axis=1, tiled=True),
        )
        mixed_p, top_t, total_t = attend(
            split_heads(query_p),
            split_heads(keys_p),
            split_heads(values_p),
            temporal_forms,
            None,
            scale,
        )
        mixed_t = lax.all_to_all(mixed_p, "ctx", split_axis=1, concat_axis=2, tiled=True)
        joined = (branch_sums(dense(mixed_t, time_merge)) + bias[0]).astype(jnp.bfloat16)
        temporal = dense(joined, mixing) + bias[1]
        state = state + temporal
        normed, unit_s, scale_s = norm_forward(state, gain[1], shift[1])
        normed_s = token_rows(normed)
        query_s, keys_s, values_s = project_triple(normed_s, triple[1], entry[1])
        mixed_s, top_s, total_s = attend(
            split_heads(query_s),
            split_heads(keys_s),
            split_heads(values_s),
            spatial_forms,
            spatial_mask,
            scale,
        )
        spatial = branch_sums(dense(mixed_s, merge[1])) + bias[2]
        state = state + spatial
        normed, unit_m, scale_m = norm_forward(state, gain[2], shift[2])
        normed_m = token_rows(normed)
        hidden = dense(normed_m, upward) + up_bias[layer]
        active = jax.nn.gelu(hidden, approximate=False).astype(jnp.bfloat16)
        dense_out = branch_sums(dense(active, downward)) + bias[3]
        state = state + dense_out
        squares.append(
            jnp.stack(
                [
                    jnp.sum(jnp.square(item) * valid_here)
                    for item in (temporal, spatial, dense_out, state)
                ]
            )
        )
        stored.append(
            (
                weights,
                unit_t,
                scale_t,
                normed_t,
                query_p,
                keys_p,
                values_p,
                top_t,
                total_t,
                mixed_t,
                joined,
                unit_s,
                scale_s,
                normed_s,
                query_s,
                keys_s,
                values_s,
                top_s,
                total_s,
                mixed_s,
                unit_m,
                scale_m,
                normed_m,
                hidden,
            )
        )
    block_output = state.astype(jnp.bfloat16)
    upstream = cotangent * valid_here
    gain_store = [None] * LAYERS
    shift_store = [None] * LAYERS
    bias_store = [None] * LAYERS
    entry_store = [None] * LAYERS
    hidden_store = [None] * LAYERS
    triple_store = [None] * LAYERS
    merge_store = [None] * LAYERS
    up_store = [None] * LAYERS
    down_store = [None] * LAYERS
    mixing_store = [None] * LAYERS
    for layer in range(LAYERS - 1, -1, -1):
        (
            weights,
            unit_t,
            scale_t,
            normed_t,
            query_p,
            keys_p,
            values_p,
            top_t,
            total_t,
            mixed_t,
            joined,
            unit_s,
            scale_s,
            normed_s,
            query_s,
            keys_s,
            values_s,
            top_s,
            total_s,
            mixed_s,
            unit_m,
            scale_m,
            normed_m,
            hidden,
        ) = stored[layer]
        weights = gather_layer(
            triple_weight[layer],
            merge_weight[layer],
            up_weight[layer],
            down_weight[layer],
            mixing_weight[layer],
            entry_bias[layer],
        )
        triple, merge, upward, downward, mixing, time_triple, time_merge, time_entry = weights
        gain = norm_gain[layer]
        rounded = upstream.astype(jnp.bfloat16)
        down_bias_part = row_total(rounded)
        full = grad_rows(rounded)
        active = jax.nn.gelu(hidden, approximate=False).astype(jnp.bfloat16)
        down_part = outer_rows(active, full)
        back_hidden = (dense_back(full, downward) * gelu_slope(hidden)).astype(jnp.bfloat16)
        hidden_part = row_total(back_hidden)
        up_part = outer_rows(normed_m, back_hidden)
        back_normed = input_sums(dense_back(back_hidden, upward))
        back_state, gain_m, shift_m = norm_backward(back_normed, unit_m, scale_m, gain[2])
        upstream = upstream + back_state
        rounded = upstream.astype(jnp.bfloat16)
        spatial_bias_part = row_total(rounded)
        full = grad_rows(rounded)
        merge_s_part = outer_rows(mixed_s, full)
        back_mixed = dense_back(full, merge[1]).astype(jnp.bfloat16)
        back_query, back_keys, back_values = attend_back(
            split_heads(back_mixed),
            split_heads(query_s),
            split_heads(keys_s),
            split_heads(values_s),
            top_s,
            total_s,
            spatial_forms,
            spatial_mask,
            scale,
        )
        triple_s_part, entry_s_part, back_normed = triple_backward(
            normed_s, back_query, back_keys, back_values, triple[1]
        )
        back_state, gain_s, shift_s = norm_backward(
            input_sums(back_normed), unit_s, scale_s, gain[1]
        )
        upstream = upstream + back_state
        rounded = upstream.astype(jnp.bfloat16)
        mixing_bias_part = row_total(rounded)
        mixing_part = outer_rows(joined, rounded)
        back_joined = dense_back(rounded, mixing).astype(jnp.bfloat16)
        merge_bias_part = row_total(back_joined)
        full = grad_rows(back_joined)
        merge_t_part = outer_rows(mixed_t, full)
        back_mixed = dense_back(full, time_merge).astype(jnp.bfloat16)
        back_places = lax.all_to_all(back_mixed, "ctx", split_axis=2, concat_axis=1, tiled=True)
        place_query, place_keys, place_values = attend_back(
            split_heads(back_places),
            split_heads(query_p),
            split_heads(keys_p),
            split_heads(values_p),
            top_t,
            total_t,
            temporal_forms,
            None,
            scale,
        )
        back_query, back_keys, back_values = (
            lax.all_to_all(place_query, "ctx", split_axis=1, concat_axis=2, tiled=True),
            lax.all_to_all(place_keys, "ctx", split_axis=1, concat_axis=2, tiled=True),
            lax.all_to_all(place_values, "ctx", split_axis=1, concat_axis=2, tiled=True),
        )
        triple_t_part, entry_t_part, back_normed = triple_backward(
            normed_t, back_query, back_keys, back_values, time_triple
        )
        back_normed = input_sums(back_normed)
        back_state, gain_t, shift_t = norm_backward(back_normed, unit_t, scale_t, gain[0])
        upstream = upstream + back_state
        triple_sum, merge_sum, up_sum, down_sum = (
            lax.psum_scatter(
                jnp.stack([triple_t_part, triple_s_part]),
                ("shard", "ctx"),
                scatter_dimension=1,
                tiled=True,
            ),
            lax.psum_scatter(
                jnp.stack([merge_t_part, merge_s_part]),
                ("shard", "ctx"),
                scatter_dimension=2,
                tiled=True,
            ),
            lax.psum_scatter(up_part, ("shard", "ctx"), scatter_dimension=0, tiled=True),
            lax.psum_scatter(down_part, ("shard", "ctx"), scatter_dimension=1, tiled=True),
        )
        mixing_sum = lax.psum_scatter(
            mixing_part, ("shard", "ctx", "tp"), scatter_dimension=0, tiled=True
        )
        triple_store[layer] = triple_sum
        merge_store[layer] = merge_sum
        up_store[layer] = up_sum
        down_store[layer] = down_sum
        mixing_store[layer] = mixing_sum
        gain_store[layer] = jnp.stack([gain_t, gain_s, gain_m])
        shift_store[layer] = jnp.stack([shift_t, shift_s, shift_m])
        bias_store[layer] = jnp.stack(
            [merge_bias_part, mixing_bias_part, spatial_bias_part, down_bias_part]
        )
        entry_store[layer] = jnp.stack([entry_t_part, entry_s_part])
        hidden_store[layer] = hidden_part
    entry_sum, hidden_sum = lax.psum(
        (jnp.stack(entry_store), jnp.stack(hidden_store)), ("shard", "ctx")
    )
    gain_sum, shift_sum, bias_sum, square_sum = lax.psum(
        (jnp.stack(gain_store), jnp.stack(shift_store), jnp.stack(bias_store), jnp.stack(squares)),
        ("shard", "ctx", "tp"),
    )
    total = FRAMES * width * jnp.sum(valid_places).astype(jnp.float32)
    root_squares = jnp.sqrt(square_sum / total)
    return (
        block_output,
        upstream,
        gain_sum,
        shift_sum,
        jnp.stack(triple_store),
        entry_sum,
        jnp.stack(merge_store),
        bias_sum,
        jnp.stack(mixing_store),
        jnp.stack(up_store),
        hidden_sum,
        jnp.stack(down_store),
        root_squares,
    )


def solution(mesh):
    return jax.shard_map(
        per_device,
        mesh=mesh,
        in_specs=(
            P("shard", "ctx", "tp", None),
            P("shard", "ctx", "tp", None),
            P("shard"),
            P(),
            P(),
            P(),
            P(None, None, ("shard", "ctx"), None, "tp"),
            P(None, None, None, "tp"),
            P(None, None, "tp", ("shard", "ctx")),
            P(),
            P(None, ("shard", "ctx", "tp"), None),
            P(None, ("shard", "ctx"), "tp"),
            P(None, "tp"),
            P(None, "tp", ("shard", "ctx")),
        ),
        out_specs=(
            P("shard", "ctx", "tp", None),
            P("shard", "ctx", "tp", None),
            P(),
            P(),
            P(None, None, ("shard", "ctx"), None, "tp"),
            P(None, None, None, "tp"),
            P(None, None, "tp", ("shard", "ctx")),
            P(),
            P(None, ("shard", "ctx", "tp"), None),
            P(None, ("shard", "ctx"), "tp"),
            P(None, "tp"),
            P(None, "tp", ("shard", "ctx")),
            P(),
        ),
        check_vma=False,
    )
```

profile of v0, /device:TPU:0, one launch (start us, length us, event | category | flops | bytes accessed | tf_op | source)
XLA Modules:
  0.0 2987.6 jit_solution(3998462361173975141)
XLA Ops:
  17.3 68.8 %all-gather.57.cloned.1.call-done = bf16[1,2,768,3,384]{4,1,3,0,2:T(2,128)(2,1)} async-done(((bf16[1,2,48,3,384]{4,1,3,0,2:T(2,128)(2,1)}), bf16[1,2,768,3,384]{4,1,3,0,2:T(2,128)(2,1)}) %all-gather.57.cloned.1.call-update) | async-done | bytes 3538960 | tf_op jit(solution)/shard_map/all_gather | solution.py:140
  86.0 8.7 fusion.255
  94.8 9.9 copy.658
  123.0 11.2 all-to-all-done.1
  141.6 10.7 all-to-all-done.2
  220.9 20.8 all-reduce.31.cloned.1.call-done
  243.4 34.6 %all-gather.61.cloned.1.call-done = bf16[1,768,768]{2,1,0:T(8,128)(2,1)} async-done(((bf16[1,24,768]{2,1,0:T(8,128)(2,1)}), bf16[1,768,768]{2,1,0:T(8,128)(2,1)}) %all-gather.61.cloned.1.call-update) | async-done | bytes 1179664 | tf_op jit(solution)/shard_map/all_gather | solution.py:145
  294.3 8.4 copy.661
  319.8 9.6 fusion.264
  341.4 19.8 all-reduce.33.cloned.1.call-done
  370.7 57.4 %all-gather.63.cloned.1.call-done = bf16[1,768,1536]{2,1,0:T(8,128)(2,1)} async-done(((bf16[1,48,1536]{2,1,0:T(8,128)(2,1)}), bf16[1,768,1536]{2,1,0:T(8,128)(2,1)}) %all-gather.63.cloned.1.call-update) | async-done | bytes 2359312 | tf_op jit(solution)/shard_map/all_gather | solution.py:142
  428.2 11.4 all-gather.37.cloned.1.call-done
  439.6 9.4 fusion.131
  452.7 23.9 fusion.6
  476.6 29.9 %all-gather.65.cloned.1.call-done = bf16[1,1536,768]{1,2,0:T(8,128)(2,1)} async-done(((bf16[1,1536,48]{1,2,0:T(8,128)(2,1)}), bf16[1,1536,768]{1,2,0:T(8,128)(2,1)}) %all-gather.65.cloned.1.call-update) | async-done | bytes 2359312 | tf_op jit(solution)/shard_map/all_gather | solution.py:143
  517.2 19.7 all-reduce.35.cloned.1.call-done
  543.1 69.8 %all-gather.67.cloned.1.call-done = bf16[1,2,768,3,384]{4,1,3,0,2:T(2,128)(2,1)} async-done(((bf16[1,2,48,3,384]{4,1,3,0,2:T(2,128)(2,1)}), bf16[1,2,768,3,384]{4,1,3,0,2:T(2,128)(2,1)}) %all-gather.67.cloned.1.call-update) | async-done | bytes 3538960 | tf_op jit(solution)/shard_map/all_gather | solution.py:140
  612.9 8.8 fusion.254
  621.7 8.5 copy.664
  647.7 10.9 all-to-all-done.5
  665.3 11.2 all-to-all-done.6
  744.5 23.1 all-reduce.37.cloned.1.call-done
  770.4 33.4 %all-gather.71.cloned.1.call-done = bf16[1,768,768]{2,1,0:T(8,128)(2,1)} async-done(((bf16[1,24,768]{2,1,0:T(8,128)(2,1)}), bf16[1,768,768]{2,1,0:T(8,128)(2,1)}) %all-gather.71.cloned.1.call-update) | async-done | bytes 1179664 | tf_op jit(solution)/shard_map/all_gather | solution.py:145
  815.7 11.7 copy.667
  846.9 10.5 fusion.266
  869.1 20.2 all-reduce.39.cloned.1.call-done
  900.5 56.0 %all-gather.73.cloned.1.call-done = bf16[1,768,1536]{2,1,0:T(8,128)(2,1)} async-done(((bf16[1,48,1536]{2,1,0:T(8,128)(2,1)}), bf16[1,768,1536]{2,1,0:T(8,128)(2,1)}) %all-gather.73.cloned.1.call-update) | async-done | bytes 2359312 | tf_op jit(solution)/shard_map/all_gather | solution.py:142
  956.5 11.4 all-gather.43.cloned.1.call-done
  967.8 14.4 fusion.132
  982.2 66.0 %all-gather.75.cloned.1.call-done = bf16[1,1536,768]{1,2,0:T(8,128)(2,1)} async-done(((bf16[1,1536,48]{1,2,0:T(8,128)(2,1)}), bf16[1,1536,768]{1,2,0:T(8,128)(2,1)}) %all-gather.75.cloned.1.call-update) | async-done | bytes 2359312 | tf_op jit(solution)/shard_map/all_gather | solution.py:143
  1048.3 12.1 convert_reduce_fusion
  1067.1 22.9 fusion.9
  1096.8 28.2 all-reduce.53.cloned.1.call-done
  1141.4 12.3 all-gather.47.cloned.1.call-done
  1175.6 11.2 multiply_convert_fusion.1
  1214.8 10.9 pad_maximum_fusion.2
  1242.1 23.0 all-reduce.41.cloned.1.call-done
  1273.8 12.4 all-gather.49.cloned.1.call-done
  1289.8 19.5 all_to_all.240
  1394.2 9.2 all-to-all-done.10
  1429.7 22.1 all-reduce.43.cloned.1.call-done
  1463.7 12.3 all-gather.51.cloned.1.call-done
  1476.0 12.0 convert_reduce_fusion.1
  1494.7 23.0 all-reduce.45.cloned.1.call-done
  1524.6 12.3 all-gather.53.cloned.1.call-done
  1558.9 11.1 multiply_convert_fusion
  1598.1 10.9 pad_maximum_fusion.3
  1609.0 8.2 dot_general.316
  1625.6 23.0 all-reduce.47.cloned.1.call-done
  1662.6 8.6 convolution_bitcast_fusion
  1673.2 8.7 convolution_bitcast_fusion.1
  1683.6 8.6 convolution_bitcast_fusion.2
  1693.9 8.6 convolution_bitcast_fusion.3
  1720.7 15.0 all-to-all-done.12
  1811.4 11.6 all-to-all-done.14
  2009.5 94.7 %reduce-scatter.19.cloned.1.call-done = f32[48,1536]{1,0:T(8,128)} async-done(((f32[768,1536]{1,0:T(8,128)}), f32[48,1536]{1,0:T(8,128)}) %reduce-scatter.19.cloned.1.call-update) | async-done | bytes 294928 | tf_op jit(solution)/shard_map/reduce_scatter | solution.py:417
  2104.2 142.6 %reduce-scatter.17.cloned.1.call-done = f32[48,1536]{1,0:T(8,128)} async-done(((f32[768,1536]{1,0:T(8,128)}), f32[48,1536]{1,0:T(8,128)}) %reduce-scatter.17.cloned.1.call-update) | async-done | bytes 294928 | tf_op jit(solution)/shard_map/reduce_scatter | solution.py:417
  2248.8 101.4 %reduce-scatter.15.cloned.1.call-done = f32[24,768]{1,0:T(8,128)} async-done(((f32[768,768]{1,0:T(8,128)}), f32[24,768]{1,0:T(8,128)}) %reduce-scatter.15.cloned.1.call-update) | async-done | bytes 73744 | tf_op jit(solution)/shard_map/reduce_scatter | solution.py:420
  2350.1 104.1 %reduce-scatter.13.cloned.1.call-done = f32[24,768]{1,0:T(8,128)} async-done(((f32[768,768]{1,0:T(8,128)}), f32[24,768]{1,0:T(8,128)}) %reduce-scatter.13.cloned.1.call-update) | async-done | bytes 73744 | tf_op jit(solution)/shard_map/reduce_scatter | solution.py:420
  2460.8 76.9 %all-reduce.15 = (f32[2,2,2,384]{3,2,1,0:T(2,128)}, f32[2,1536]{1,0:T(2,128)}) all-reduce(f32[2,2,2,384]{3,2,1,0:T(2,128)S(1)} %pad_maximum_fusion.16, f32[2,1536]{1,0:T(2,128)S(1)} %pad_maximum_fusion.17), channel_id=1, replica_groups=mesh['shard'=8,'ctx'=2,'tp'=2] {'shard','ctx'}, use_global_device_ids=true, to_apply=%region_73.74 | all-reduce | flops 6144 | bytes 49152 | tf_op jit(solution)/shard_map/psum | solution.py:435
  2540.9 39.0 %all-reduce.14 = (f32[2,3,768]{2,1,0:T(4,128)S(1)}, f32[2,3,768]{2,1,0:T(4,128)S(1)}, f32[2,4,768]{2,1,0:T(4,128)}, f32[2,4]{1,0:T(2,128)S(1)}) all-reduce(f32[2,3,768]{2,1,0:T(4,128)S(1)} %pad_maximum_fusion.13, f32[2,3,768]{2,1,0:T(4,128)S(1)} %pad_maximum_fusion.14, ...), channel_id=1, replica_groups=mesh['shard'=8,'ctx'=2,'tp'=2] {'shard','ctx','tp'}, use_global_device_ids=true, to_apply=%region_55.56 | all-reduce | flops 15368 | bytes 122944 | tf_op jit(solution)/shard_map/psum | solution.py:438
  2586.5 80.4 %all-reduce.51.cloned.1.call-done = (f32[2,384,768]{1,0,2:T(2,128)}, f32[2,384,768]{1,0,2:T(2,128)}) async-done(((f32[2,384,768]{1,0,2:T(2,128)}, f32[2,384,768]{1,0,2:T(2,128)}), (f32[2,384,768]{1,0,2:T(2,128)}, f32[2,384,768]{1,0,2:T(2,128)})) %all-reduce.51.cloned.1.call-update) | async-done | bytes 4718608
  2669.6 153.0 %reduce-scatter.11.cloned.1.call-done = f32[2,48,3,384]{3,1,2,0:T(8,128)} async-done(((f32[2,768,3,384]{3,1,2,0:T(8,128)}), f32[2,48,3,384]{3,1,2,0:T(8,128)}) %reduce-scatter.11.cloned.1.call-update) | async-done | bytes 442384 | tf_op jit(solution)/shard_map/reduce_scatter | solution.py:405
  2822.5 155.3 %reduce-scatter.9.cloned.1.call-done = f32[2,48,3,384]{3,1,2,0:T(8,128)} async-done(((f32[2,768,3,384]{3,1,2,0:T(8,128)}), f32[2,48,3,384]{3,1,2,0:T(8,128)}) %reduce-scatter.9.cloned.1.call-update) | async-done | bytes 442384 | tf_op jit(solution)/shard_map/reduce_scatter | solution.py:405
  (880 shorter events, 951.1 us)
Async XLA Ops:
  8.0 78.0 %all-gather.57.cloned.1.call-start = ((), (), s32[]{:S(2)}) async-start(), calls=%async_computation.44 | async-start | bytes 3760128 | tf_op jit(solution)/shard_map/all_gather | solution.py:140
  10.8 93.9 %all-gather.33.cloned.1.call-start = ((), (), s32[]{:S(2)}) async-start(), calls=%async_computation.24 | async-start | bytes 3612672 | tf_op jit(solution)/shard_map/all_gather | solution.py:151
  12.4 270.0 %copy-start.111 = (f32[768]{0:T(1024)}, f32[768]{0:T(1024)S(1)}, u32[]{:S(2)}) copy-start(f32[768]{0:T(1024)S(1)} %get-tuple-element.236) | copy-start | bytes 9220
  12.4 353.6 %copy-start.98 = (f32[768]{0:T(1024)}, f32[768]{0:T(1024)S(1)}, u32[]{:S(2)}) copy-start(f32[768]{0:T(1024)S(1)} %get-tuple-element.237) | copy-start | bytes 9220
  12.4 527.7 %copy-start.121 = (f32[768]{0:T(1024)}, f32[768]{0:T(1024)S(1)}, u32[]{:S(2)}) copy-start(f32[768]{0:T(1024)S(1)} %get-tuple-element.238) | copy-start | bytes 9220
  115.2 19.1 all-to-all-start.1
  134.2 18.1 all-to-all-start.2
  138.7 62.9 %all-gather.59.cloned.1.call-start = ((), (), s32[]{:S(2)}) async-start(), calls=%async_computation.45 | async-start | bytes 1253376 | tf_op jit(solution)/shard_map/all_gather | solution.py:141
  152.4 18.8 all-to-all-start
  197.6 16.3 all-to-all-start.3
  201.2 40.4 %all-reduce.31.cloned.1.call-start = ((), (), s32[]{:S(2)}) async-start(), calls=%async_computation.54 | async-start | bytes 4816896
  218.2 59.8 %all-gather.61.cloned.1.call-start = ((), (), s32[]{:S(2)}) async-start(), calls=%async_computation.46 | async-start | bytes 1216512 | tf_op jit(solution)/shard_map/all_gather | solution.py:145
  218.9 83.8 %all-gather.35.cloned.1.call-start = ((), (), s32[]{:S(2)}) async-start(), calls=%async_computation.25 | async-start | bytes 3612672 | tf_op jit(solution)/shard_map/all_gather | solution.py:151
  285.5 75.8 %all-reduce.33.cloned.1.call-start = ((), (), s32[]{:S(2)}) async-start(), calls=%async_computation.55 | async-start | bytes 4816896
  340.6 87.6 %all-gather.63.cloned.1.call-start = ((), (), s32[]{:S(2)}) async-start(), calls=%async_computation.47 | async-start | bytes 2506752 | tf_op jit(solution)/shard_map/all_gather | solution.py:142
  341.4 98.2 %all-gather.37.cloned.1.call-start = ((), (), s32[]{:S(2)}) async-start(), calls=%async_computation.26 | async-start | bytes 3612672 | tf_op jit(solution)/shard_map/all_gather | solution.py:151
  365.6 173.0 %copy-start = (f32[2,4,98,768]{3,2,1,0:T(8,128)}, f32[2,4,98,768]{3,2,1,0:T(8,128)S(1)}, u32[]{:S(2)}) copy-start(f32[2,4,98,768]{3,2,1,0:T(8,128)S(1)} %get-tuple-element.162) | copy-start | bytes 7225348
  369.0 137.5 %all-gather.65.cloned.1.call-start = ((), (), s32[]{:S(2)}) async-start(), calls=%async_computation.48 | async-start | bytes 2506752 | tf_op jit(solution)/shard_map/all_gather | solution.py:143
  369.8 167.0 %all-reduce.35.cloned.1.call-start = ((), (), s32[]{:S(2)}) async-start(), calls=%async_computation.56 | async-start | bytes 4816896
  516.2 96.7 %all-gather.67.cloned.1.call-start = ((), (), s32[]{:S(2)}) async-start(), calls=%async_computation.49 | async-start | bytes 3760128 | tf_op jit(solution)/shard_map/all_gather | solution.py:140
  517.1 113.1 %all-gather.39.cloned.1.call-start = ((), (), s32[]{:S(2)}) async-start(), calls=%async_computation.27 | async-start | bytes 3612672 | tf_op jit(solution)/shard_map/all_gather | solution.py:151
  640.6 17.9 all-to-all-start.5
  658.6 18.0 all-to-all-start.6
  663.1 63.9 %all-gather.69.cloned.1.call-start = ((), (), s32[]{:S(2)}) async-start(), calls=%async_computation.50 | async-start | bytes 1253376 | tf_op jit(solution)/shard_map/all_gather | solution.py:141
  676.6 19.2 all-to-all-start.4
  723.3 16.3 all-to-all-start.7
  726.9 40.7 %all-reduce.37.cloned.1.call-start = ((), (), s32[]{:S(2)}) async-start(), calls=%async_computation.57 | async-start | bytes 4816896
  743.9 59.9 %all-gather.71.cloned.1.call-start = ((), (), s32[]{:S(2)}) async-start(), calls=%async_computation.51 | async-start | bytes 1216512 | tf_op jit(solution)/shard_map/all_gather | solution.py:145
  744.5 82.9 %all-gather.41.cloned.1.call-start = ((), (), s32[]{:S(2)}) async-start(), calls=%async_computation.28 | async-start | bytes 3612672 | tf_op jit(solution)/shard_map/all_gather | solution.py:151
  812.0 77.3 %all-reduce.39.cloned.1.call-start = ((), (), s32[]{:S(2)}) async-start(), calls=%async_computation.58 | async-start | bytes 4816896
  868.5 88.0 %all-gather.73.cloned.1.call-start = ((), (), s32[]{:S(2)}) async-start(), calls=%async_computation.52 | async-start | bytes 2506752 | tf_op jit(solution)/shard_map/all_gather | solution.py:142
  869.1 98.8 %all-gather.43.cloned.1.call-start = ((), (), s32[]{:S(2)}) async-start(), calls=%async_computation.29 | async-start | bytes 3612672 | tf_op jit(solution)/shard_map/all_gather | solution.py:151
  895.1 87.2 %all-gather.45.cloned.1.call-start = ((), (), s32[]{:S(2)}) async-start(), calls=%async_computation.30 | async-start | bytes 3612672 | tf_op jit(solution)/shard_map/all_gather | solution.py:161
  899.7 148.6 %all-gather.75.cloned.1.call-start = ((), (), s32[]{:S(2)}) async-start(), calls=%async_computation.53 | async-start | bytes 2506752 | tf_op jit(solution)/shard_map/all_gather | solution.py:143
  900.3 224.8 %all-reduce.53.cloned.1.call-start = ((), (), s32[]{:S(2)}) async-start(), calls=%async_computation.65 | async-start | bytes 9633792
  1096.8 57.0 %all-gather.47.cloned.1.call-start = ((), (), s32[]{:S(2)}) async-start(), calls=%async_computation.31 | async-start | bytes 3612672 | tf_op jit(solution)/shard_map/all_gather | solution.py:161
  1141.4 123.7 %all-reduce.41.cloned.1.call-start = ((), (), s32[]{:S(2)}) async-start(), calls=%async_computation.59 | async-start | bytes 4816896
  1242.1 44.1 %all-gather.49.cloned.1.call-start = ((), (), s32[]{:S(2)}) async-start(), calls=%async_computation.32 | async-start | bytes 3612672 | tf_op jit(solution)/shard_map/all_gather | solution.py:161
  1341.2 23.2 all-to-all-start.11
  1364.4 19.8 all-to-all-start.9
  1384.1 19.3 all-to-all-start.10
  1388.6 63.2 %all-reduce.43.cloned.1.call-start = ((), (), s32[]{:S(2)}) async-start(), calls=%async_computation.60 | async-start | bytes 4816896
  1429.7 46.3 %all-gather.51.cloned.1.call-start = ((), (), s32[]{:S(2)}) async-start(), calls=%async_computation.33 | async-start | bytes 3612672 | tf_op jit(solution)/shard_map/all_gather | solution.py:161
  1463.6 54.0 %all-reduce.45.cloned.1.call-start = ((), (), s32[]{:S(2)}) async-start(), calls=%async_computation.61 | async-start | bytes 4816896
  1494.6 42.3 %all-gather.53.cloned.1.call-start = ((), (), s32[]{:S(2)}) async-start(), calls=%async_computation.34 | async-start | bytes 3612672 | tf_op jit(solution)/shard_map/all_gather | solution.py:161
  1524.6 124.0 %all-reduce.47.cloned.1.call-start = ((), (), s32[]{:S(2)}) async-start(), calls=%async_computation.62 | async-start | bytes 4816896
  1625.6 81.7 %all-gather.55.cloned.1.call-start = ((), (), s32[]{:S(2)}) async-start(), calls=%async_computation.35 | async-start | bytes 3612672 | tf_op jit(solution)/shard_map/all_gather | solution.py:161
  1662.0 345.6 %reduce-scatter.23.cloned.1.call-start = ((), (), s32[]{:S(2)}) async-start(), calls=%async_computation.43 | async-start | bytes 5013504 | tf_op jit(solution)/shard_map/reduce_scatter | solution.py:418
  1671.2 336.4 %reduce-scatter.21.cloned.1.call-start = ((), (), s32[]{:S(2)}) async-start(), calls=%async_computation.42 | async-start | bytes 5013504 | tf_op jit(solution)/shard_map/reduce_scatter | solution.py:418
  1682.0 422.3 %reduce-scatter.19.cloned.1.call-start = ((), (), s32[]{:S(2)}) async-start(), calls=%async_computation.41 | async-start | bytes 5013504 | tf_op jit(solution)/shard_map/reduce_scatter | solution.py:417
  1692.3 554.6 %reduce-scatter.17.cloned.1.call-start = ((), (), s32[]{:S(2)}) async-start(), calls=%async_computation.40 | async-start | bytes 5013504 | tf_op jit(solution)/shard_map/reduce_scatter | solution.py:417
  1702.6 647.5 %reduce-scatter.15.cloned.1.call-start = ((), (), s32[]{:S(2)}) async-start(), calls=%async_computation.39 | async-start | bytes 2433024 | tf_op jit(solution)/shard_map/reduce_scatter | solution.py:420
  1712.0 23.7 all-to-all-start.12
  1716.5 737.8 %reduce-scatter.13.cloned.1.call-start = ((), (), s32[]{:S(2)}) async-start(), calls=%async_computation.38 | async-start | bytes 2433024 | tf_op jit(solution)/shard_map/reduce_scatter | solution.py:420
  1760.6 21.9 all-to-all-start.15
  1782.5 20.8 all-to-all-start.13
  1803.3 19.7 all-to-all-start.14
  1807.9 729.8 %all-reduce.49.cloned.1.call-start = ((), (), s32[]{:S(2)}) async-start(), calls=%async_computation.63 | async-start | bytes 4816896
  1848.8 818.1 %all-reduce.51.cloned.1.call-start = ((), (), s32[]{:S(2)}) async-start(), calls=%async_computation.64 | async-start | bytes 9437184
  1899.0 923.5 %reduce-scatter.11.cloned.1.call-start = ((), (), s32[]{:S(2)}) async-start(), calls=%async_computation.37 | async-start | bytes 7520256 | tf_op jit(solution)/shard_map/reduce_scatter | solution.py:405
  1945.6 1032.3 %reduce-scatter.9.cloned.1.call-start = ((), (), s32[]{:S(2)}) async-start(), calls=%async_computation.36 | async-start | bytes 7520256 | tf_op jit(solution)/shard_map/reduce_scatter | solution.py:405
  2454.3 85.1 %copy-start.101 = (f32[2,4,98]{2,1,0:T(4,128)S(1)}, f32[2,4,98]{2,1,0:T(4,128)}, u32[]{:S(2)}) copy-start(f32[2,4,98]{2,1,0:T(4,128)} %copy-done.100) | copy-start | bytes 9412
  2454.3 85.1 %copy-start.116 = (f32[2,4,98]{2,1,0:T(4,128)S(1)}, f32[2,4,98]{2,1,0:T(4,128)}, u32[]{:S(2)}) copy-start(f32[2,4,98]{2,1,0:T(4,128)} %copy-done.115) | copy-start | bytes 9412
  2454.3 85.1 %copy-start.118 = (f32[768]{0:T(1024)S(1)}, f32[768]{0:T(1024)}, u32[]{:S(2)}) copy-start(f32[768]{0:T(1024)} %copy-done.117) | copy-start | bytes 9220
  (192 other events, 1854.4 us)
Sparse Core Ops, SparseCore 0:
  12.2 73.7 all-gather.56
  88.1 9.5 all-gather.32
  142.9 57.0 all-gather.58
  218.3 23.2 all-reduce.30
  285.6 9.9 all-gather.34
  340.7 20.5 all-reduce.32
  364.6 63.5 all-gather.62
  429.7 9.8 all-gather.36
  443.0 63.5 all-gather.64
  516.3 20.5 all-reduce.34
  540.6 72.2 all-gather.66
  614.4 9.5 all-gather.38
  667.7 57.1 all-gather.68
  744.0 23.5 all-reduce.36
  812.2 9.9 all-gather.40
  868.6 20.6 all-reduce.38
  892.9 63.5 all-gather.72
  957.9 9.8 all-gather.42
  969.4 12.1 all-gather.44
  984.7 63.5 all-gather.74
  1096.9 28.1 all-reduce.52
  1141.5 12.2 all-gather.46
  1242.2 22.8 all-reduce.40
  1273.9 12.2 all-gather.48
  1429.8 21.9 all-reduce.42
  1463.7 12.2 all-gather.50
  1494.7 22.8 all-reduce.44
  1524.7 12.2 all-gather.52
  1625.7 22.8 all-reduce.46
  1662.1 12.2 all-gather.54
  1679.5 140.4 reduce-scatter.22
  1826.0 136.4 reduce-scatter.20
  1967.6 136.6 reduce-scatter.18
  2110.2 136.5 reduce-scatter.16
  2252.1 97.9 reduce-scatter.14
  2356.1 98.0 reduce-scatter.12
  2457.0 20.6 all-reduce.48
  2484.5 182.3 all-reduce.50
  2672.1 150.4 reduce-scatter.10
  2827.9 149.9 reduce-scatter.8
Sparse Core Ops, SparseCore 1:
  222.1 55.7 all-gather.60
  747.7 56.1 all-gather.70
where the time goes:
time: 3000 us; the launch traced here: 2990 us
  waiting for transfers between devices  1640 us (55%)
  local copies, waits for them, and re-layouts  544 us (18%)
  matrix products  382 us (13%)
  other arithmetic  198 us (7%)
  blocking collectives  135 us (4%)
  starting transfers between devices  67.8 us (2%)
    reduce_scatter x2, waiting for transfers between devices, per_device(): lax.psum_scatter(jnp.stack([triple_t_part, triple_s_part]), ('shard', 'ct...  308 us
    unnamed x54, waiting for transfers between devices  305 us
    reduce_scatter x2, waiting for transfers between devices, per_device(): lax.psum_scatter(up_part, ('shard', 'ctx'), scatter_dimension=0, tiled=True)  237 us
    reduce_scatter x2, waiting for transfers between devices, per_device(): lax.psum_scatter(mixing_part, ('shard', 'ctx', 'tp'), scatter_dimension=0...  205 us
    all_gather x2, waiting for transfers between devices, gather_layer(): lax.all_gather(triple, ('shard', 'ctx'), axis=1, tiled=True)  139 us
    unnamed x430, local copies, waits for them, and re-layouts  122 us
    all_gather x2, waiting for transfers between devices, gather_layer(): lax.all_gather(upward, ('shard', 'ctx'), axis=0, tiled=True)  113 us
    all_gather x2, waiting for transfers between devices, gather_layer(): lax.all_gather(downward, ('shard', 'ctx'), axis=1, tiled=True)  96 us
  transfers between devices with their start and end apart: 57, of which 42 were waited for; matrix products, arithmetic and copies ran while one was open for 20% of the time, Pallas kernels for 0%

commit v1 on v0

v1 whole, which is shorter than its diff:
```python
import functools

import jax
import jax.numpy as jnp
from jax import lax
from jax.experimental import pallas as pl
from jax.experimental.pallas import tpu as pltpu
from jax.sharding import PartitionSpec as P

HEAD_DIM = 64
FRAMES = 8
LAYERS = 2
AXES = ("shard", "ctx", "tp")
BF = jnp.bfloat16
F32 = jnp.float32

far_below = -1000000000.0
epsilon = 1e-06
root_half = 0.7071067811865476
gauss_scale = 0.3989422804014327


def dot_nn(left, right):
    return lax.dot_general(left, right, (((1,), (0,)), ((), ())), preferred_element_type=F32)


def dot_nt(left, right):
    return lax.dot_general(left, right, (((1,), (1,)), ((), ())), preferred_element_type=F32)


def dot_tn(left, right):
    return lax.dot_general(left, right, (((0,), (0,)), ((), ())), preferred_element_type=F32)


def rows(value):
    return value.reshape(-1, value.shape[-1])


def row_total(value):
    return jnp.sum(rows(value).astype(F32), axis=0)


def lane_masks(shape):
    lane = lax.broadcasted_iota(jnp.int32, shape, 1)
    return lane < HEAD_DIM


def softmax_rows(scores):
    top = jnp.max(scores, axis=-1, keepdims=True)
    raised = jnp.exp(scores - top)
    total = jnp.sum(raised, axis=-1, keepdims=True)
    return raised * (1.0 / total)


def sides(value, first):
    zero = jnp.zeros_like(value)
    return [jnp.where(first, value, zero), jnp.where(first, zero, value)]


def heads_forward(qkv, fix, scale, put):
    first = lane_masks(qkv(0, 0).shape)
    scores = []
    for pair in range(3):
        k = qkv(1, pair)
        scores.append([dot_nt(q, k) for q in sides(qkv(0, pair), first)])
    shares = [[softmax_rows(fix(item * scale)).astype(BF) for item in both] for both in scores]
    for pair in range(3):
        v = qkv(2, pair)
        outs = [dot_nn(item, v) for item in shares[pair]]
        put(pair, jnp.where(first, outs[0], outs[1]).astype(BF))


def heads_backward(qkv, back, fix, scale, put):
    first = lane_masks(qkv(0, 0).shape)
    scores, backs = [], []
    for pair in range(3):
        k, v = qkv(1, pair), qkv(2, pair)
        scores.append([dot_nt(q, k) for q in sides(qkv(0, pair), first)])
        backs.append([dot_nt(b, v) for b in sides(back(pair), first)])
    low_shares, low_scores = [], []
    for pair in range(3):
        low_shares.append([])
        low_scores.append([])
        for side in range(2):
            shares = softmax_rows(fix(scores[pair][side] * scale))
            back_shares = backs[pair][side]
            inner = jnp.sum(back_shares * shares, axis=-1, keepdims=True)
            low_scores[pair].append((shares * (back_shares - inner)).astype(BF))
            low_shares[pair].append(shares.astype(BF))
    for pair in range(3):
        q, k, bm = qkv(0, pair), qkv(1, pair), back(pair)
        gq = [dot_nn(item, k) for item in low_scores[pair]]
        gk = [dot_tn(item, q) for item in low_scores[pair]]
        gv = [dot_tn(item, bm) for item in low_shares[pair]]
        put(0, pair, (jnp.where(first, gq[0], gq[1]) * scale).astype(BF))
        put(1, pair, (jnp.where(first, gk[0], gk[1]) * scale).astype(BF))
        put(2, pair, jnp.where(first, gv[0], gv[1]).astype(BF))


def column(part, pair):
    start = part * 384 + pair * 128
    return slice(start, start + 128)


def spatial_fix(count_ref, padded, places):
    col = lax.broadcasted_iota(jnp.int32, (padded, padded), 1)
    floor = jnp.where(col < places, far_below, 3.0 * far_below)
    allowed = col < jnp.minimum(count_ref[0], places)
    return lambda scores: jnp.where(allowed, scores, floor)


def spatial_fwd_body(places, scale, count_ref, own_ref, oth_ref, own_out, oth_out):
    fix = spatial_fix(count_ref, own_ref.shape[1], places)
    for src, dst in ((own_ref, own_out), (oth_ref, oth_out)):

        def put(pair, value, dst=dst):
            dst[0, :, pair * 128 : pair * 128 + 128] = value

        heads_forward(lambda part, pair, src=src: src[0, :, column(part, pair)], fix, scale, put)


def spatial_bwd_body(
    places, scale, count_ref, own_ref, oth_ref, bown_ref, both_ref, own_out, oth_out
):
    fix = spatial_fix(count_ref, own_ref.shape[1], places)
    for src, back, dst in ((own_ref, bown_ref, own_out), (oth_ref, both_ref, oth_out)):

        def put(part, pair, value, dst=dst):
            dst[0, :, column(part, pair)] = value

        heads_backward(
            lambda part, pair, src=src: src[0, :, column(part, pair)],
            lambda pair, back=back: back[0, :, pair * 128 : pair * 128 + 128],
            fix,
            scale,
            put,
        )


def temporal_fix(tile):
    size = FRAMES * tile
    row = lax.broadcasted_iota(jnp.int32, (size, size), 0)
    col = lax.broadcasted_iota(jnp.int32, (size, size), 1)
    same = (row & (tile - 1)) == (col & (tile - 1))
    return lambda scores: jnp.where(same, scores, 3.0 * far_below)


def temporal_fwd_body(scale, src, dst):
    tile = src.shape[1]
    fix = temporal_fix(tile)

    def put(pair, value):
        dst[:, :, pair * 128 : pair * 128 + 128] = value.reshape(FRAMES, tile, 128)

    heads_forward(
        lambda part, pair: src[:, :, column(part, pair)].reshape(FRAMES * tile, 128),
        fix,
        scale,
        put,
    )


def temporal_bwd_body(scale, src, back, dst):
    tile = src.shape[1]
    fix = temporal_fix(tile)

    def put(part, pair, value):
        dst[:, :, column(part, pair)] = value.reshape(FRAMES, tile, 128)

    heads_backward(
        lambda part, pair: src[:, :, column(part, pair)].reshape(FRAMES * tile, 128),
        lambda pair: back[:, :, pair * 128 : pair * 128 + 128].reshape(FRAMES * tile, 128),
        fix,
        scale,
        put,
    )


def spatial_call(count, ins, widths, places, scale, backward):
    frames, padded, _ = ins[0].shape
    spec = lambda width: pl.BlockSpec((1, padded, width), lambda f: (f, 0, 0))
    body = spatial_bwd_body if backward else spatial_fwd_body
    work = frames * 12 * padded * 256 * 128 * 2 * (5 if backward else 2)
    return pl.pallas_call(
        functools.partial(body, places, scale),
        grid=(frames,),
        in_specs=[pl.BlockSpec(memory_space=pltpu.SMEM)] + [spec(x.shape[-1]) for x in ins],
        out_specs=[spec(width) for width in widths],
        out_shape=[jax.ShapeDtypeStruct((frames, padded, width), BF) for width in widths],
        cost_estimate=pl.CostEstimate(
            flops=work * 4, bytes_accessed=8 * frames * padded * 2304, transcendentals=0
        ),
        name="spatial_back" if backward else "spatial_mix",
    )(count, *ins)


def temporal_call(ins, width, scale, backward):
    frames, padded, _ = ins[0].shape
    tile = 16
    spec = lambda lanes: pl.BlockSpec((frames, tile, lanes), lambda i: (0, i, 0))
    body = temporal_bwd_body if backward else temporal_fwd_body
    work = padded // tile * 6 * 128 * 128 * 128 * 2 * (5 if backward else 2)
    return pl.pallas_call(
        functools.partial(body, scale),
        grid=(padded // tile,),
        in_specs=[spec(x.shape[-1]) for x in ins],
        out_specs=spec(width),
        out_shape=jax.ShapeDtypeStruct((frames, padded, width), BF),
        cost_estimate=pl.CostEstimate(
            flops=work * 8, bytes_accessed=4 * frames * padded * 1152, transcendentals=0
        ),
        name="temporal_back" if backward else "temporal_mix",
    )(*ins)


class Grid:
    def __init__(self):
        self.shards = lax.axis_size("shard")
        self.depth = self.shards // 2
        shard = lax.axis_index("shard")
        self.z = shard // 2
        self.x = shard % 2
        self.y = lax.axis_index("ctx")
        self.t = lax.axis_index("tp")
        self.direct = self.depth == 4

    def perm(self, move):
        pairs = []
        for z in range(self.depth):
            for x in range(2):
                for y in range(2):
                    for t in range(2):
                        tz, tx, ty, tt = move(z, x, y, t)
                        pairs.append(
                            (((z * 2 + x) * 2 + y) * 2 + t, ((tz * 2 + tx) * 2 + ty) * 2 + tt)
                        )
        return pairs

    def over_x(self, value):
        return lax.ppermute(value, AXES, self.perm(lambda z, x, y, t: (z, 1 - x, y, t)))

    def over_y(self, value):
        return lax.ppermute(value, AXES, self.perm(lambda z, x, y, t: (z, x, 1 - y, t)))

    def over_t(self, value):
        return lax.ppermute(value, AXES, self.perm(lambda z, x, y, t: (z, x, y, 1 - t)))

    def over_z(self, value, step):
        depth = self.depth
        return lax.ppermute(
            value, AXES, self.perm(lambda z, x, y, t: ((z + step) % depth, x, y, t))
        )

    def over_bit(self, value, bit):
        pairs = []
        for s in range(self.shards):
            for y in range(2):
                for t in range(2):
                    pairs.append(((s * 2 + y) * 2 + t, ((s ^ bit) * 2 + y) * 2 + t))
        return lax.ppermute(value, AXES, pairs)

    def total(self, value, across):
        if across:
            value = value + self.over_t(value)
        value = value + self.over_y(value)
        bit = 1
        while bit < self.shards:
            value = value + self.over_bit(value, bit)
            bit *= 2
        return value


def place_body(widths, step_rows, half, at_ref, own, xn, yn, da, db, *outs):
    back = pl.program_id(0)
    x, y = at_ref[1], at_ref[2]

    def put(dx, dy, piece):
        bx = x if dx == 0 else 1 - x
        by = y if dy == 0 else 1 - y
        row = pl.multiple_of((bx * 2 + by) * step_rows, 16)
        start = 0
        for number, width in enumerate(widths):
            outs[number][pl.ds(row, step_rows), :] = piece[0, :, start : start + width]
            start += width

    put(0, 0, own)
    put(1, 0, xn)
    put(0, 1, yn)

    @pl.when(back < half)
    def _():
        put(1, 1, da)

    @pl.when(back >= half)
    def _():
        put(1, 1, db)


def gather_rows(grid, block, widths):
    step_rows, lanes = block.shape
    if not grid.direct:
        full = lax.all_gather(block, ("shard", "ctx"), axis=0, tiled=True)
        outs, start = [], 0
        for width in widths:
            outs.append(full[:, start : start + width])
            start += width
        return outs
    depth = grid.depth
    half = depth // 2
    own = jnp.stack([block] + [grid.over_z(block, k) for k in range(1, depth)])
    xn = grid.over_x(own)
    yn = grid.over_y(own)
    da = grid.over_y(xn[:half])
    db = grid.over_x(yn[half:])
    at = jnp.stack([grid.z, grid.x, grid.y]).astype(jnp.int32)
    piece = lambda index: pl.BlockSpec((1, step_rows, lanes), index)
    straight = piece(lambda k, at_ref: (k, 0, 0))
    return pl.pallas_call(
        functools.partial(place_body, tuple(widths), step_rows, half),
        grid_spec=pltpu.PrefetchScalarGridSpec(
            num_scalar_prefetch=1,
            grid=(depth,),
            in_specs=[
                straight,
                straight,
                straight,
                piece(lambda k, at_ref: (jnp.minimum(k, half - 1), 0, 0)),
                piece(lambda k, at_ref: (jnp.maximum(k - half, 0), 0, 0)),
            ],
            out_specs=[
                pl.BlockSpec(
                    (4 * step_rows, width),
                    lambda k, at_ref: (lax.rem(at_ref[0] - k + depth, depth), 0),
                )
                for width in widths
            ],
        ),
        out_shape=[
            jax.ShapeDtypeStruct((depth * 4 * step_rows, width), block.dtype) for width in widths
        ],
        cost_estimate=pl.CostEstimate(
            flops=0, bytes_accessed=depth * 4 * step_rows * lanes * 4, transcendentals=0
        ),
        name="place_rows",
    )(at, own, xn, yn, da, db)


def scatter_rows(grid, parts):
    if not grid.direct:
        whole = jnp.concatenate(parts, axis=1).astype(F32)
        return lax.psum_scatter(whole, ("shard", "ctx"), scatter_dimension=0, tiled=True)
    depth = grid.depth
    half = depth // 2

    def pick(dx, dy):
        out = []
        for part in parts:
            step_rows = part.shape[0] // (depth * 4)
            cube = part.reshape(depth, 2, 2, step_rows, part.shape[1])
            bx = grid.x if dx == 0 else 1 - grid.x
            by = grid.y if dy == 0 else 1 - grid.y
            out.append(
                lax.dynamic_slice(
                    cube, (0, bx, by, 0, 0), (depth, 1, 1, step_rows, part.shape[1])
                ).reshape(depth, step_rows, part.shape[1])
            )
        return jnp.concatenate(out, axis=-1)

    far = pick(1, 1)
    ra = grid.over_y(far[:half])
    rb = grid.over_x(far[half:])
    sx = pick(1, 0)
    sy = pick(0, 1)
    sx = jnp.concatenate([(sx[:half].astype(F32) + ra.astype(F32)).astype(BF), sx[half:]])
    sy = jnp.concatenate([sy[:half], (sy[half:].astype(F32) + rb.astype(F32)).astype(BF)])
    rx = grid.over_x(sx)
    ry = grid.over_y(sy)
    kept = pick(0, 0).astype(F32) + rx.astype(F32) + ry.astype(F32)
    own = lax.dynamic_index_in_dim(kept, grid.z, 0, keepdims=False)
    low = kept.astype(BF)
    for k in range(1, depth):
        block = lax.dynamic_index_in_dim(low, (grid.z + k) % depth, 0, keepdims=False)
        own = own + grid.over_z(block, k).astype(F32)
    return own


def split_columns(value, widths):
    outs, start = [], 0
    for width in widths:
        outs.append(value[..., start : start + width])
        start += width
    return outs


def norm_forward(state, gain, shift):
    center = state - jnp.mean(state, axis=-1, keepdims=True)
    scale = lax.rsqrt(jnp.mean(center * center, axis=-1, keepdims=True) + epsilon)
    unit = center * scale
    return ((unit * gain + shift).astype(BF), unit, scale)


def norm_backward(incoming, unit, scale, gain):
    along = incoming * gain
    back = scale * (
        along
        - jnp.mean(along, axis=-1, keepdims=True)
        - unit * jnp.mean(along * unit, axis=-1, keepdims=True)
    )
    return (back, row_total(incoming * unit), row_total(incoming))


def per_device(
    video_clips,
    cotangent,
    slot_clip,
    valid_places,
    norm_gain,
    norm_bias,
    triple_weight,
    entry_bias,
    merge_weight,
    branch_bias,
    mixing_weight,
    up_weight,
    up_bias,
    down_weight,
):
    grid = Grid()
    slots, frames_here, places_here, width = video_clips.shape
    places = places_here * 2
    padded = -(-places // 16) * 16
    scale = HEAD_DIM ** (-0.5)
    step_rows = triple_weight.shape[2]
    half_rows = step_rows // 2
    own_first = grid.t == 0
    straight = grid.t == grid.y

    clip_ids = jnp.arange(valid_places.shape[0], dtype=jnp.int32)
    my_clip = lax.dynamic_index_in_dim(slot_clip, grid.y, 0, keepdims=False)
    count = jnp.sum(jnp.where(my_clip == clip_ids, valid_places, 0)).astype(jnp.int32)
    valid_here = (jnp.arange(padded, dtype=jnp.int32) < count).astype(F32)[None, :, None]
    count_ref = count.reshape(1)

    def spread_in(value):
        mine = lax.dynamic_index_in_dim(value, grid.y, 0, keepdims=False)
        theirs = lax.dynamic_index_in_dim(value, 1 - grid.y, 0, keepdims=False)
        got = grid.over_y(theirs)
        keep = jnp.where(straight, mine, got)
        send = jnp.where(straight, got, mine)
        swap = grid.over_t(send)
        low = jnp.where(own_first, keep, swap)
        high = jnp.where(own_first, swap, keep)
        gap = jnp.zeros((frames_here, padded - places, width), value.dtype)
        return jnp.concatenate([low, high, gap], axis=1)

    def spread_out(value):
        low = value[:, :places_here]
        high = value[:, places_here:places]
        keep = jnp.where(own_first, low, high)
        send = jnp.where(own_first, high, low)
        swap = grid.over_t(send)
        mine = jnp.where(straight, keep, swap)
        away = jnp.where(straight, swap, keep)
        got = grid.over_y(away)
        first = jnp.where(grid.y == 0, mine, got)
        second = jnp.where(grid.y == 0, got, mine)
        return jnp.stack([first, second])

    def pack_mix(item):
        return jnp.concatenate([item[..., : width // 2], item[..., width // 2 :]], axis=-2)

    def block_t(layer):
        return jnp.concatenate(
            [triple_weight[layer, 0, :, i] for i in range(3)]
            + [merge_weight[layer, 0].T, pack_mix(mixing_weight[layer])],
            axis=1,
        )

    def block_s(layer):
        return jnp.concatenate(
            [triple_weight[layer, 1, :, i] for i in range(3)] + [merge_weight[layer, 1].T], axis=1
        )

    def block_m(layer):
        return jnp.concatenate([up_weight[layer], down_weight[layer].T], axis=1)

    split = triple_weight.shape[-1]
    hid = up_weight.shape[-1]
    wide_t = (3 * split, split, width // 2)
    wide_s = (3 * split, split)
    wide_m = (hid, hid)

    start_clips = spread_in(video_clips)
    gathered = [None] * LAYERS
    for layer in range(LAYERS):
        if layer == 0:
            got = gather_rows(grid, block_t(layer), wide_t)
            got += gather_rows(
                grid, jnp.concatenate([block_s(layer), block_m(layer)], axis=1), wide_s + wide_m
            )
        else:
            got = gather_rows(
                grid,
                jnp.concatenate([block_t(layer), block_s(layer), block_m(layer)], axis=1),
                wide_t + wide_s + wide_m,
            )
        triple_t, merge_t, mix, triple_s, merge_s, upward, downward = got
        other = [grid.over_t(item) for item in (merge_t, mix, triple_s, merge_s, upward, downward)]

        def unpack_mix(item):
            cube = item.reshape(-1, 2, half_rows, width // 2)
            return jnp.concatenate([cube[:, 0], cube[:, 1]], axis=-1)

        mix_own, mix_oth = unpack_mix(mix), unpack_mix(other[1])
        mixing = jnp.stack(
            [jnp.where(own_first, mix_own, mix_oth), jnp.where(own_first, mix_oth, mix_own)],
            axis=1,
        ).reshape(width, width)
        gathered[layer] = dict(
            triple_t=triple_t,
            mixing=mixing,
            merge_t=(merge_t, other[0]),
            triple_s=(triple_s, other[2]),
            merge_s=(merge_s, other[3]),
            up=(upward, other[4]),
            down=(downward, other[5]),
        )

    small = jnp.concatenate([entry_bias[:, 1].reshape(-1), up_bias.reshape(-1)])
    small_oth = grid.over_t(small)
    entry_count = LAYERS * 2 * split
    entry_s = (
        small[:entry_count].reshape(LAYERS, 2, split),
        small_oth[:entry_count].reshape(LAYERS, 2, split),
    )
    up_bias2 = (
        small[entry_count:].reshape(LAYERS, hid),
        small_oth[entry_count:].reshape(LAYERS, hid),
    )

    def triple_bias(pair):
        return jnp.concatenate([pair[0], jnp.zeros((split,), F32), pair[1]])

    def cube(value):
        return value.reshape(-1, padded, value.shape[-1])

    state = start_clips.astype(F32)
    upstream = spread_in(cotangent.astype(BF)).astype(F32) * valid_here
    stored = []
    squares = []
    for layer in range(LAYERS):
        w = gathered[layer]
        gain, shift, bias = norm_gain[layer], norm_bias[layer], branch_bias[layer]
        normed, unit_t, scale_t = norm_forward(state, gain[0], shift[0])
        normed_t = jnp.concatenate([normed, grid.over_t(normed)], axis=0)
        qkv_t = cube(
            (dot_nn(rows(normed_t), w["triple_t"]) + triple_bias(entry_bias[layer, 0])).astype(BF)
        )
        mixed = temporal_call([qkv_t], split, scale, False)
        mine = mixed[:frames_here]
        swap = grid.over_t(mixed[frames_here:])
        joined = (
            dot_nt(rows(mine), w["merge_t"][0]) + dot_nt(rows(swap), w["merge_t"][1]) + bias[0]
        ).astype(BF)
        temporal = cube(dot_nn(joined, w["mixing"]) + bias[1])
        state = state + temporal
        normed_s, unit_s, scale_s = norm_forward(state, gain[1], shift[1])
        qkv_s = [
            cube(
                (
                    dot_nn(rows(normed_s), w["triple_s"][i]) + triple_bias(entry_s[i][layer])
                ).astype(BF)
            )
            for i in range(2)
        ]
        mixed_s = spatial_call(count_ref, qkv_s, (split, split), places, scale, False)
        spatial = cube(
            dot_nt(rows(mixed_s[0]), w["merge_s"][0])
            + dot_nt(rows(mixed_s[1]), w["merge_s"][1])
            + bias[2]
        )
        state = state + spatial
        normed_m, unit_m, scale_m = norm_forward(state, gain[2], shift[2])
        active, slope = [], []
        for i in range(2):
            hidden = dot_nn(rows(normed_m), w["up"][i]) + up_bias2[i][layer]
            below = 0.5 * (1.0 + lax.erf(hidden * root_half))
            active.append((hidden * below).astype(BF))
            slope.append(
                (below + hidden * gauss_scale * jnp.exp(-0.5 * hidden * hidden)).astype(BF)
            )
        dense = cube(
            dot_nt(active[0], w["down"][0]) + dot_nt(active[1], w["down"][1]) + bias[3]
        )
        state = state + dense
        squares.append(
            jnp.stack(
                [
                    jnp.sum(jnp.square(item) * valid_here)
                    for item in (temporal, spatial, dense, state)
                ]
            )
        )
        stored.append(
            dict(
                unit_t=unit_t,
                scale_t=scale_t,
                normed_t=normed_t,
                qkv_t=qkv_t,
                mixed_t=(mine, swap),
                joined=joined,
                unit_s=unit_s,
                scale_s=scale_s,
                normed_s=normed_s,
                qkv_s=qkv_s,
                mixed_s=mixed_s,
                unit_m=unit_m,
                scale_m=scale_m,
                normed_m=normed_m,
                active=active,
                slope=slope,
            )
        )
    block_output = spread_out(state.astype(BF))

    whole_sums = [None] * LAYERS
    half_sums = [None] * LAYERS
    shards = [None] * LAYERS

    def join_halves(mine, theirs):
        return (mine + grid.over_t(theirs.astype(BF)).astype(F32)).astype(BF)

    for layer in range(LAYERS - 1, -1, -1):
        w, kept = gathered[layer], stored[layer]
        gain = norm_gain[layer]
        r = rows(upstream).astype(BF)
        down_bias_part = row_total(r)
        back_hidden = [
            (dot_nn(r, w["down"][i]) * kept["slope"][i].astype(F32)).astype(BF) for i in range(2)
        ]
        down_part = join_halves(*[dot_tn(r, kept["active"][i]) for i in range(2)])
        up_part = join_halves(
            *[dot_tn(rows(kept["normed_m"]), back_hidden[i]) for i in range(2)]
        )
        hidden_part = [row_total(back_hidden[i]) for i in range(2)]
        back_normed = cube(
            dot_nt(back_hidden[0], w["up"][0]) + dot_nt(back_hidden[1], w["up"][1])
        )
        back_state, gain_m, shift_m = norm_backward(
            back_normed, kept["unit_m"], kept["scale_m"], gain[2]
        )
        upstream = upstream + back_state
        r = rows(upstream).astype(BF)
        spatial_bias_part = row_total(r)
        merge_s_part = join_halves(*[dot_tn(r, rows(kept["mixed_s"][i])) for i in range(2)])
        back_mixed = [cube(dot_nn(r, w["merge_s"][i]).astype(BF)) for i in range(2)]
        back_qkv = spatial_call(
            count_ref,
            list(kept["qkv_s"]) + back_mixed,
            (3 * split, 3 * split),
            places,
            scale,
            True,
        )
        triple_s_part = join_halves(
            *[dot_tn(rows(kept["normed_s"]), rows(back_qkv[i])) for i in range(2)]
        )
        qkv_sums = [row_total(back_qkv[i]) for i in range(2)]
        entry_s_part = [jnp.stack([q[:split], q[2 * split :]]) for q in qkv_sums]
        back_normed = cube(
            dot_nt(rows(back_qkv[0]), w["triple_s"][0])
            + dot_nt(rows(back_qkv[1]), w["triple_s"][1])
        )
        back_state, gain_s, shift_s = norm_backward(
            back_normed, kept["unit_s"], kept["scale_s"], gain[1]
        )
        upstream = upstream + back_state
        r = rows(upstream).astype(BF)
        mixing_bias_part = row_total(r)
        mixing_part = dot_tn(kept["joined"], r).reshape(-1, 2, half_rows, width)
        mix_mine = lax.dynamic_index_in_dim(mixing_part, grid.t, 1, keepdims=False)
        mix_theirs = lax.dynamic_index_in_dim(mixing_part, 1 - grid.t, 1, keepdims=False)
        mixing_part = pack_mix(join_halves(mix_mine, mix_theirs)).reshape(width, width // 2)
        back_joined = dot_nt(r, w["mixing"]).astype(BF)
        merge_bias_part = row_total(back_joined)
        merge_t_part = join_halves(
            *[dot_tn(back_joined, rows(kept["mixed_t"][i])) for i in range(2)]
        )
        back_mine, back_away = [
            cube(dot_nn(back_joined, w["merge_t"][i]).astype(BF)) for i in range(2)
        ]
        back_mixed = jnp.concatenate([back_mine, grid.over_t(back_away)], axis=0)
        back_qkv = temporal_call([kept["qkv_t"], back_mixed], 3 * split, scale, True)
        triple_t_part = dot_tn(rows(kept["normed_t"]), rows(back_qkv)).astype(BF)
        qkv_sum = row_total(back_qkv)
        entry_t_part = jnp.stack([qkv_sum[:split], qkv_sum[2 * split :]])
        back_own = dot_nt(rows(back_qkv[:frames_here]), w["triple_t"])
        back_oth = dot_nt(rows(back_qkv[frames_here:]), w["triple_t"]).astype(BF)
        back_normed = cube(back_own + grid.over_t(back_oth).astype(F32))
        back_state, gain_t, shift_t = norm_backward(
            back_normed, kept["unit_t"], kept["scale_t"], gain[0]
        )
        upstream = upstream + back_state

        parts_t = [triple_t_part, merge_t_part, mixing_part]
        parts_sm = [triple_s_part, merge_s_part, up_part, down_part]
        if layer == 0:
            late = scatter_rows(grid, parts_sm)
            early = scatter_rows(grid, parts_t)
            shards[layer] = split_columns(early, wide_t) + split_columns(late, wide_s + wide_m)
        else:
            shards[layer] = split_columns(
                scatter_rows(grid, parts_t + parts_sm), wide_t + wide_s + wide_m
            )
        whole_sums[layer] = jnp.concatenate(
            [
                gain_t,
                gain_s,
                gain_m,
                shift_t,
                shift_s,
                shift_m,
                merge_bias_part,
                mixing_bias_part,
                spatial_bias_part,
                down_bias_part,
                squares[layer],
            ]
        )
        theirs = jnp.concatenate([entry_s_part[1].reshape(-1), hidden_part[1]])
        mine = jnp.concatenate([entry_s_part[0].reshape(-1), hidden_part[0]])
        half_sums[layer] = jnp.concatenate(
            [entry_t_part.reshape(-1), mine + grid.over_t(theirs)]
        )

    input_grad = spread_out(upstream.astype(BF)).astype(F32)
    whole = jnp.stack(whole_sums)
    halves = jnp.stack(half_sums)
    whole = whole + grid.over_t(whole)
    both = grid.total(jnp.concatenate([whole, halves], axis=1), False)
    whole, halves = both[:, : whole.shape[1]], both[:, whole.shape[1] :]
    gain_sum = whole[:, : 3 * width].reshape(LAYERS, 3, width)
    shift_sum = whole[:, 3 * width : 6 * width].reshape(LAYERS, 3, width)
    bias_sum = whole[:, 6 * width : 10 * width].reshape(LAYERS, 4, width)
    square_sum = whole[:, 10 * width :]
    entry_sum = halves[:, : 4 * split].reshape(LAYERS, 2, 2, split)
    hidden_sum = halves[:, 4 * split :]
    tokens = FRAMES * width * jnp.sum(valid_places).astype(F32)
    root_squares = jnp.sqrt(square_sum / tokens)

    def unpack_rows(item):
        return jnp.concatenate([item[:half_rows], item[half_rows:]], axis=-1)

    def triple_shape(item):
        return item.reshape(step_rows, 3, split)

    return (
        block_output,
        input_grad,
        gain_sum,
        shift_sum,
        jnp.stack([jnp.stack([triple_shape(s[0]), triple_shape(s[3])]) for s in shards]),
        entry_sum,
        jnp.stack([jnp.stack([s[1].T, s[4].T]) for s in shards]),
        bias_sum,
        jnp.stack([unpack_rows(s[2]) for s in shards]),
        jnp.stack([s[5] for s in shards]),
        hidden_sum,
        jnp.stack([s[6].T for s in shards]),
        root_squares,
    )


def solution(mesh):
    return jax.shard_map(
        per_device,
        mesh=mesh,
        in_specs=(
            P("shard", "ctx", "tp", None),
            P("shard", "ctx", "tp", None),
            P("shard"),
            P(),
            P(),
            P(),
            P(None, None, ("shard", "ctx"), None, "tp"),
            P(None, None, None, "tp"),
            P(None, None, "tp", ("shard", "ctx")),
            P(),
            P(None, ("shard", "ctx", "tp"), None),
            P(None, ("shard", "ctx"), "tp"),
            P(None, "tp"),
            P(None, "tp", ("shard", "ctx")),
        ),
        out_specs=(
            P("shard", "ctx", "tp", None),
            P("shard", "ctx", "tp", None),
            P(),
            P(),
            P(None, None, ("shard", "ctx"), None, "tp"),
            P(None, None, None, "tp"),
            P(None, None, "tp", ("shard", "ctx")),
            P(),
            P(None, ("shard", "ctx", "tp"), None),
            P(None, ("shard", "ctx"), "tp"),
            P(None, "tp"),
            P(None, "tp", ("shard", "ctx")),
            P(),
        ),
        check_vma=False,
    )
```

time: 3000 us -> 1010 us (0.34)
  waiting for transfers between devices: 1640 us -> 262 us
  local copies, waits for them, and re-layouts: 544 us -> 121 us
  blocking collectives: 135 us -> 0 us
  Pallas kernels: 0 us -> 123 us
  matrix products: 382 us -> 273 us
  other arithmetic: 198 us -> 110 us
  starting transfers between devices: 67.8 us -> 99.9 us
    reduce_scatter x8 -> x0, waiting for transfers between devices: 751 us -> none  [the longest x2 308 us: per_device(): lax.psum_scatter(jnp.stack([triple_t_part, triple_s_part]), ('shard', 'ct...]
    all_gather x22 -> x0, waiting for transfers between devices: 488 us -> none  [the longest x2 139 us: gather_layer(): lax.all_gather(triple, ('shard', 'ctx'), axis=1, tiled=True)]
    unnamed x54 -> x0, waiting for transfers between devices: 305 us -> none
    ppermute x0 -> x90, waiting for transfers between devices: none -> 262 us  [the longest x17 122 us: over_y(): lax.ppermute(value, AXES, self.perm(lambda z, x, y, t: (z, x, 1 - y, t)))]
    pallas_call x0 -> x11, Pallas kernels: none -> 123 us  [the longest x4 54.7 us: temporal_call(): pl.pallas_call(functools.partial(body, scale), grid=(padded // tile,), in...]
    psum x2 -> x0, blocking collectives: 116 us -> none  [the longest x1 76.9 us: per_device(): lax.psum((jnp.stack(entry_store), jnp.stack(hidden_store)), ('shard', 'ct...]
    convert_element_type x46 -> x4, local copies, waits for them, and re-layouts: 105 us -> 4.17 us  [the longest x2 2.4 us: per_device(): joined = (dot_nt(rows(mine), w['merge_t'][0]) + dot_nt(rows(swap), w['mer...]
    ppermute x0 -> x90, starting transfers between devices: none -> 99.9 us  [the longest x18 37.8 us: over_z(): lax.ppermute(value, AXES, self.perm(lambda z, x, y, t: ((z + step) % dept...]
  transfers between devices with their start and end apart: 57 -> 90, of which waited for: 42 -> 29; matrix products, arithmetic and copies ran while one was open for 20% -> 39% of each run, Pallas kernels for 0% -> 11%
where the time goes in v1:
time: 1010 us; the launch traced here: 993 us
  matrix products  273 us (27%)
  waiting for transfers between devices  262 us (26%)
  Pallas kernels  123 us (12%)
  local copies, waits for them, and re-layouts  121 us (12%)
  other arithmetic  110 us (11%)
  starting transfers between devices  99.9 us (10%)
    ppermute x17, waiting for transfers between devices, over_y(): lax.ppermute(value, AXES, self.perm(lambda z, x, y, t: (z, x, 1 - y, t)))  122 us
    ppermute x18, waiting for transfers between devices, over_z(): lax.ppermute(value, AXES, self.perm(lambda z, x, y, t: ((z + step) % dept...  101 us
    dot_general x24, matrix products, dot_nn(): lax.dot_general(left, right, (((1,), (0,)), ((), ())), preferred_element_...  95.9 us
    dot_general x26, matrix products, dot_nt(): lax.dot_general(left, right, (((1,), (1,)), ((), ())), preferred_element_...  93.3 us
    dot_general x24, matrix products, dot_tn(): lax.dot_general(left, right, (((0,), (0,)), ((), ())), preferred_element_...  84.1 us
    pallas_call x4, Pallas kernels, temporal_call(): pl.pallas_call(functools.partial(body, scale), grid=(padded // tile,), in...  54.7 us
    pallas_call x4, Pallas kernels, spatial_call(): pl.pallas_call(functools.partial(body, places, scale), grid=(frames,), in...  47.6 us
    unnamed x566, local copies, waits for them, and re-layouts  41.7 us
  transfers between devices with their start and end apart: 90, of which 29 were waited for; matrix products, arithmetic and copies ran while one was open for 39% of the time, Pallas kernels for 11%

profile of v1, /device:TPU:0, one launch (start us, length us, event | category | flops | bytes accessed | tf_op | source)
XLA Modules:
  0.0 993.4 jit_solution(17486832156843512338)
XLA Ops:
  44.9 6.6 collective-permute-done.13
  51.5 19.0 %collective-permute-done.14 = bf16[48,4608]{1,0:T(8,128)(2,1)S(1)} collective-permute-done((bf16[48,4608]{1,0:T(8,128)(2,1)S(1)}, bf16[48,4608]{1,0:T(8,128)(2,1)S(1)}, u32[]{:S(2)}, u32[]{:S(2)}) %collective-permute-start.14) | collective-permute-done | bytes 442400 | tf_op jit(solution)/shard_map/ppermute | solution.py:250
  71.3 14.8 %collective-permute-done.42 = bf16[4,98,768]{2,0,1:T(4,128)(2,1)S(1)} collective-permute-done((bf16[4,98,768]{2,0,1:T(4,128)(2,1)}, bf16[4,98,768]{2,0,1:T(4,128)(2,1)S(1)}, u32[]{:S(2)}, u32[]{:S(2)}) %collective-permute-start.42) | collective-permute-done | bytes 602144 | tf_op jit(solution)/shard_map/ppermute | solution.py:243
  93.3 12.2 %collective-permute-done.6.xn = bf16[4,48,1920]{2,1,0:T(8,128)(2,1)S(1)} collective-permute-done((bf16[4,48,1920]{2,1,0:T(8,128)(2,1)S(1)}, bf16[4,48,1920]{2,1,0:T(8,128)(2,1)S(1)}, u32[]{:S(2)}, u32[]{:S(2)}) %collective-permute-start.6) | collective-permute-done | bytes 737312 | tf_op jit(solution)/shard_map/ppermute | solution.py:240
  110.4 9.5 collective-permute-done.27
  126.7 27.8 %collective-permute-done.8.da = bf16[2,48,1920]{2,1,0:T(8,128)(2,1)S(1)} collective-permute-done((bf16[2,48,1920]{2,1,0:T(8,128)(2,1)S(1)}, bf16[2,48,1920]{2,1,0:T(8,128)(2,1)S(1)}, u32[]{:S(2)}, u32[]{:S(2)}) %collective-permute-start.8) | collective-permute-done | bytes 368672 | tf_op jit(solution)/shard_map/ppermute | solution.py:243
  155.2 5.4 place_rows.3
  168.4 4.9 fusion
  173.3 11.8 %temporal_mix.2 = bf16[8,208,384]{2,1,0:T(8,128)(2,1)} custom-call(bf16[8,208,1152]{2,1,0:T(8,128)(2,1)} %bitcast.637), custom_call_target="tpu_custom_call" | custom-call | flops 5234491392 | bytes 7667712 | tf_op jit(solution)/shard_map/temporal_mix/pallas_call | solution.py:203
  194.1 6.9 place_rows.4
  209.5 5.0 fusion.18
  214.9 4.7 fusion.19
  219.7 8.3 spatial_mix.2
  235.8 4.3 multiply_convert_fusion.7
  240.1 6.5 multiply_convert_fusion.6
  246.7 4.8 fusion.97
  251.5 6.3 fusion.64
  260.3 5.8 add_convert_fusion.14
  278.1 20.8 %collective-permute-done.31.da = bf16[2,48,6528]{2,1,0:T(8,128)(2,1)} collective-permute-done((bf16[2,48,6528]{2,1,0:T(8,128)(2,1)}, bf16[2,48,6528]{2,1,0:T(8,128)(2,1)}, u32[]{:S(2)}, u32[]{:S(2)}) %collective-permute-start.31) | collective-permute-done | bytes 1253408 | tf_op jit(solution)/shard_map/ppermute | solution.py:243
  302.0 8.5 place_rows.5
  313.0 4.9 fusion.1
  317.9 12.2 %temporal_mix.3 = bf16[8,208,384]{2,1,0:T(8,128)(2,1)} custom-call(bf16[8,208,1152]{2,1,0:T(8,128)(2,1)} %bitcast.639), custom_call_target="tpu_custom_call" | custom-call | flops 5234491392 | bytes 7667712 | tf_op jit(solution)/shard_map/temporal_mix/pallas_call | solution.py:203
  343.0 4.8 fusion.20
  347.8 4.7 fusion.21
  352.6 8.1 spatial_mix.3
  366.3 4.7 multiply_convert_fusion.4
  377.9 7.3 convert_reduce_fusion.3
  385.2 4.8 convert_reduce_fusion.2
  397.9 5.3 add_add_fusion
  403.2 5.5 fusion.101
  408.7 9.3 multiply_reduce_fusion.8
  429.6 15.4 %spatial_back.2 = (bf16[4,208,1152]{2,1,0:T(8,128)(2,1)}, bf16[4,208,1152]{2,1,0:T(8,128)(2,1)}) custom-call(s32[1]{0:T(128)} %bitcast.24.count_ref, bf16[4,208,1152]{2,1,0:T(8,128)(2,1)} %bitcast.646, bf16[4,208,1152]{2,1,0:T(8,128)(2,1)} %bitcast.648, bf16[4,208,384]{2,1,0:T(8,128)(2,1)} %bitcast.650, bf16[4,208,384]{2,1,0:T(8,128)(2,1)} %bitcast.652), custom_call_target="tpu_custom_call" | custom-call | flops 13086228480 | bytes 15335424 | tf_op jit(solution)/shard_map/spatial_back/pallas_call | solution.py:184
  471.6 4.4 add_convert_fusion.6
  499.6 15.3 %temporal_back.2 = bf16[8,208,1152]{2,1,0:T(8,128)(2,1)} custom-call(bf16[8,208,1152]{2,1,0:T(8,128)(2,1)} %bitcast.640, bf16[8,208,384]{2,1,0:T(8,128)(2,1)} %pad_maximum_fusion.12.back), custom_call_target="tpu_custom_call" | custom-call | flops 13086228480 | bytes 7667712 | tf_op jit(solution)/shard_map/temporal_back/pallas_call | solution.py:203
  523.2 6.6 fusion.23
  542.3 4.8 multiply_reduce_fusion.6
  548.7 5.3 convert_reduce_fusion.5
  554.0 5.7 convert_reduce_fusion.4
  559.8 4.8 fusion.103
  579.2 15.7 %spatial_back.3 = (bf16[4,208,1152]{2,1,0:T(8,128)(2,1)}, bf16[4,208,1152]{2,1,0:T(8,128)(2,1)}) custom-call(s32[1]{0:T(128)} %bitcast.24.count_ref, bf16[4,208,1152]{2,1,0:T(8,128)(2,1)} %bitcast.642, bf16[4,208,1152]{2,1,0:T(8,128)(2,1)} %bitcast.644, bf16[4,208,384]{2,1,0:T(8,128)(2,1)} %bitcast.649, bf16[4,208,384]{2,1,0:T(8,128)(2,1)} %bitcast.651), custom_call_target="tpu_custom_call" | custom-call | flops 13086228480 | bytes 15335424 | tf_op jit(solution)/shard_map/spatial_back/pallas_call | solution.py:184
  594.9 5.1 fusion.24
  604.7 4.4 multiply_reduce_fusion.12
  640.9 5.2 add_convert_fusion.1
  648.5 4.2 add_convert_fusion
  664.1 15.4 %temporal_back.3 = bf16[8,208,1152]{2,1,0:T(8,128)(2,1)} custom-call(bf16[8,208,1152]{2,1,0:T(8,128)(2,1)} %bitcast.638, bf16[8,208,384]{2,1,0:T(8,128)(2,1)} %pad_maximum_fusion.13.back), custom_call_target="tpu_custom_call" | custom-call | flops 13086228480 | bytes 7667712 | tf_op jit(solution)/shard_map/temporal_back/pallas_call | solution.py:203
  679.4 4.4 fusion.67
  688.6 5.6 fusion.22
  712.6 4.4 multiply_reduce_fusion.13
  720.7 11.2 %add_convert_fusion.8 = bf16[4,208,768]{2,1,0:T(8,128)(2,1)S(1)} fusion(f32[4,208,768]{2,1,0:T(8,128)} %bitcast.574, f32[4,208,768]{2,1,0:T(8,128)} %bitcast.573, f32[4,208,768]{2,1,0:T(8,128)} %bitcast.572, f32[4,208,768]{2,1,0:T(8,128)} %bitcast.571, f32[4,208,768]{2,1,0:T(8,128)} %bitcast.570, f32[4,208,768]{2,1,0:T(8,128)} %bitcast.569, ...), kind=kLoop, calls=%fused_computation.103 | loop fusion | flops 41533440 | bytes 31900896 | tf_op jit(solution)/shard_map/convert_element_type | solution.py:736
  734.6 26.4 %collective-permute-done.53 = f32[2,10756]{1,0:T(2,128)S(1)} collective-permute-done((f32[2,10756]{1,0:T(2,128)S(1)}, f32[2,10756]{1,0:T(2,128)S(1)}, u32[]{:S(2)}, u32[]{:S(2)}) %collective-permute-start.53) | collective-permute-done | bytes 86080 | tf_op jit(solution)/shard_map/ppermute | solution.py:243
  762.3 8.6 collective-permute-done.59
  772.5 7.5 collective-permute-done.61
  784.5 22.1 %collective-permute-start.55 = (f32[2,10756]{1,0:T(2,128)S(1)}, f32[2,10756]{1,0:T(2,128)S(1)}, u32[]{:S(2)}, u32[]{:S(2)}) collective-permute-start(f32[2,10756]{1,0:T(2,128)S(1)} %add.983), channel_id=1, source_target_pairs={{0,8},{1,9},{2,10},{3,11},{4,12},{5,13},{6,14},{7,15},{8,0},{9,1},... | collective-permute-start | bytes 258152 | tf_op jit(solution)/shard_map/ppermute | solution.py:260
  811.2 5.3 collective-permute-done.56
  820.1 5.1 add_convert_fusion.3
  826.5 4.2 add_convert_fusion.2
  838.8 5.2 collective-permute-done.62
  855.1 5.2 collective-permute-done.64
  869.3 16.2 %collective-permute-done.49 = bf16[4,98,768]{2,0,1:T(4,128)(2,1)} collective-permute-done((bf16[4,98,768]{2,0,1:T(4,128)(2,1)}, bf16[4,98,768]{2,0,1:T(4,128)(2,1)}, u32[]{:S(2)}, u32[]{:S(2)}) %collective-permute-start.49) | collective-permute-done | bytes 602144 | tf_op jit(solution)/shard_map/ppermute | solution.py:243
  906.0 10.8 %collective-permute-done.87 = bf16[48,6528]{1,0:T(8,128)(2,1)S(1)} collective-permute-done((bf16[48,6528]{1,0:T(8,128)(2,1)S(1)}, bf16[48,6528]{1,0:T(8,128)(2,1)S(1)}, u32[]{:S(2)}, u32[]{:S(2)}) %collective-permute-start.87) | collective-permute-done | bytes 626720 | tf_op jit(solution)/shard_map/ppermute | solution.py:250
  916.8 21.4 %collective-permute-done.88 = bf16[48,6528]{1,0:T(8,128)(2,1)S(1)} collective-permute-done((bf16[48,6528]{1,0:T(8,128)(2,1)S(1)}, bf16[48,6528]{1,0:T(8,128)(2,1)S(1)}, u32[]{:S(2)}, u32[]{:S(2)}) %collective-permute-start.88) | collective-permute-done | bytes 626720 | tf_op jit(solution)/shard_map/ppermute | solution.py:250
  945.8 14.0 %collective-permute-start.74 = (bf16[48,4608]{1,0:T(8,128)(2,1)S(1)}, bf16[48,4608]{1,0:T(8,128)(2,1)S(1)}, u32[]{:S(2)}, u32[]{:S(2)}) collective-permute-start(bf16[48,4608]{1,0:T(8,128)(2,1)S(1)} %get-tuple-element.246), channel_id=1, source_target_pairs={{0,8},{1,9},{2,10},{3,11},{4,12},{5,13},{6,14},{7,15},{8,16},{9,17... | collective-permute-start | bytes 1327112 | tf_op jit(solution)/shard_map/ppermute | solution.py:250
  962.3 10.4 %collective-permute-done.74 = bf16[48,4608]{1,0:T(8,128)(2,1)S(1)} collective-permute-done((bf16[48,4608]{1,0:T(8,128)(2,1)S(1)}, bf16[48,4608]{1,0:T(8,128)(2,1)S(1)}, u32[]{:S(2)}, u32[]{:S(2)}) %collective-permute-start.74) | collective-permute-done | bytes 442400 | tf_op jit(solution)/shard_map/ppermute | solution.py:250
  972.6 14.5 %collective-permute-done.75 = bf16[48,4608]{1,0:T(8,128)(2,1)S(1)} collective-permute-done((bf16[48,4608]{1,0:T(8,128)(2,1)S(1)}, bf16[48,4608]{1,0:T(8,128)(2,1)S(1)}, u32[]{:S(2)}, u32[]{:S(2)}) %collective-permute-start.75) | collective-permute-done | bytes 442400 | tf_op jit(solution)/shard_map/ppermute | solution.py:250
  (1046 shorter events, 407.6 us)
Async XLA Ops:
  14.1 23.8 %collective-permute-start.3 = (bf16[48,1920]{1,0:T(8,128)(2,1)}, bf16[48,1920]{1,0:T(8,128)(2,1)}, u32[]{:S(2)}, u32[]{:S(2)}) collective-permute-start(bf16[48,1920]{1,0:T(8,128)(2,1)} %constant_dynamic-update-slice_fusion), channel_id=1, source_target_pairs={{0,8},{1,9},{2,10},{3,11},{4,12},{5,13},{6,14},{7,15},{8,16},{9,17... | collective-permute-start | bytes 552968 | tf_op jit(solution)/shard_map/ppermute | solution.py:250
  17.1 21.2 %collective-permute-start.4 = (bf16[48,1920]{1,0:T(8,128)(2,1)}, bf16[48,1920]{1,0:T(8,128)(2,1)}, u32[]{:S(2)}, u32[]{:S(2)}) collective-permute-start(bf16[48,1920]{1,0:T(8,128)(2,1)} %constant_dynamic-update-slice_fusion), channel_id=1, source_target_pairs={{0,16},{1,17},{2,18},{3,19},{4,20},{5,21},{6,22},{7,23},{8,24},{9,... | collective-permute-start | bytes 552968 | tf_op jit(solution)/shard_map/ppermute | solution.py:250
  19.7 21.4 %collective-permute-start.5 = (bf16[48,1920]{1,0:T(8,128)(2,1)}, bf16[48,1920]{1,0:T(8,128)(2,1)}, u32[]{:S(2)}, u32[]{:S(2)}) collective-permute-start(bf16[48,1920]{1,0:T(8,128)(2,1)} %constant_dynamic-update-slice_fusion), channel_id=1, source_target_pairs={{0,24},{1,25},{2,26},{3,27},{4,28},{5,29},{6,30},{7,31},{8,0},{9,1... | collective-permute-start | bytes 552968 | tf_op jit(solution)/shard_map/ppermute | solution.py:250
  23.5 19.5 %collective-permute-start = (bf16[4,98,768]{2,0,1:T(4,128)(2,1)}, bf16[4,98,768]{2,0,1:T(4,128)(2,1)S(1)}, u32[]{:S(2)}, u32[]{:S(2)}) collective-permute-start(bf16[4,98,768]{2,0,1:T(4,128)(2,1)} %get-tuple-element.278), channel_id=1, source_target_pairs={{0,2},{1,3},{2,0},{3,1},{4,6},{5,7},{6,4},{7,5},{8,10},{9,11},{10,... | collective-permute-start | bytes 1806344 | tf_op jit(solution)/shard_map/ppermute | solution.py:243
  37.9 32.6 %collective-permute-start.14 = (bf16[48,4608]{1,0:T(8,128)(2,1)S(1)}, bf16[48,4608]{1,0:T(8,128)(2,1)S(1)}, u32[]{:S(2)}, u32[]{:S(2)}) collective-permute-start(bf16[48,4608]{1,0:T(8,128)(2,1)S(1)} %get-tuple-element.338), channel_id=1, source_target_pairs={{0,16},{1,17},{2,18},{3,19},{4,20},{5,21},{6,22},{7,23},{8,24},{9,... | collective-permute-start | bytes 1327112 | tf_op jit(solution)/shard_map/ppermute | solution.py:250
  38.2 32.8 %collective-permute-start.15 = (bf16[48,4608]{1,0:T(8,128)(2,1)S(1)}, bf16[48,4608]{1,0:T(8,128)(2,1)S(1)}, u32[]{:S(2)}, u32[]{:S(2)}) collective-permute-start(bf16[48,4608]{1,0:T(8,128)(2,1)S(1)} %get-tuple-element.338), channel_id=1, source_target_pairs={{0,24},{1,25},{2,26},{3,27},{4,28},{5,29},{6,30},{7,31},{8,0},{9,1... | collective-permute-start | bytes 1327112 | tf_op jit(solution)/shard_map/ppermute | solution.py:250
  41.1 51.7 %collective-permute-start.26 = (bf16[48,6528]{1,0:T(8,128)(2,1)}, bf16[48,6528]{1,0:T(8,128)(2,1)S(1)}, u32[]{:S(2)}, u32[]{:S(2)}) collective-permute-start(bf16[48,6528]{1,0:T(8,128)(2,1)} %get-tuple-element.337), channel_id=1, source_target_pairs={{0,8},{1,9},{2,10},{3,11},{4,12},{5,13},{6,14},{7,15},{8,16},{9,17... | collective-permute-start | bytes 1880072 | tf_op jit(solution)/shard_map/ppermute | solution.py:250
  43.0 76.9 %collective-permute-start.27 = (bf16[48,6528]{1,0:T(8,128)(2,1)}, bf16[48,6528]{1,0:T(8,128)(2,1)S(1)}, u32[]{:S(2)}, u32[]{:S(2)}) collective-permute-start(bf16[48,6528]{1,0:T(8,128)(2,1)} %get-tuple-element.337), channel_id=1, source_target_pairs={{0,16},{1,17},{2,18},{3,19},{4,20},{5,21},{6,22},{7,23},{8,24},{9,... | collective-permute-start | bytes 1880072 | tf_op jit(solution)/shard_map/ppermute | solution.py:250
  51.5 68.9 %collective-permute-start.28 = (bf16[48,6528]{1,0:T(8,128)(2,1)}, bf16[48,6528]{1,0:T(8,128)(2,1)S(1)}, u32[]{:S(2)}, u32[]{:S(2)}) collective-permute-start(bf16[48,6528]{1,0:T(8,128)(2,1)} %get-tuple-element.337), channel_id=1, source_target_pairs={{0,24},{1,25},{2,26},{3,27},{4,28},{5,29},{6,30},{7,31},{8,0},{9,1... | collective-permute-start | bytes 1880072 | tf_op jit(solution)/shard_map/ppermute | solution.py:250
  86.1 19.4 %collective-permute-start.6 = (bf16[4,48,1920]{2,1,0:T(8,128)(2,1)S(1)}, bf16[4,48,1920]{2,1,0:T(8,128)(2,1)S(1)}, u32[]{:S(2)}, u32[]{:S(2)}) collective-permute-start(bf16[4,48,1920]{2,1,0:T(8,128)(2,1)S(1)} %pad_maximum_fusion.17.own), channel_id=1, source_target_pairs={{0,4},{1,5},{2,6},{3,7},{4,0},{5,1},{6,2},{7,3},{8,12},{9,13},{10,... | collective-permute-start | bytes 2211848 | tf_op jit(solution)/shard_map/ppermute | solution.py:240
  90.1 19.3 %collective-permute-start.7 = (bf16[4,48,1920]{2,1,0:T(8,128)(2,1)S(1)}, bf16[4,48,1920]{2,1,0:T(8,128)(2,1)S(1)}, u32[]{:S(2)}, u32[]{:S(2)}) collective-permute-start(bf16[4,48,1920]{2,1,0:T(8,128)(2,1)S(1)} %pad_maximum_fusion.17.own), channel_id=1, source_target_pairs={{0,2},{1,3},{2,0},{3,1},{4,6},{5,7},{6,4},{7,5},{8,10},{9,11},{10,... | collective-permute-start | bytes 2211848 | tf_op jit(solution)/shard_map/ppermute | solution.py:243
  92.8 68.3 %collective-permute-start.16 = (bf16[4,48,4608]{2,1,0:T(8,128)(2,1)S(1)}, bf16[4,48,4608]{2,1,0:T(8,128)(2,1)}, u32[]{:S(2)}, u32[]{:S(2)}) collective-permute-start(bf16[4,48,4608]{2,1,0:T(8,128)(2,1)S(1)} %pad_maximum_fusion.5.own), channel_id=1, source_target_pairs={{0,4},{1,5},{2,6},{3,7},{4,0},{5,1},{6,2},{7,3},{8,12},{9,13},{10,... | collective-permute-start | bytes 5308424 | tf_op jit(solution)/shard_map/ppermute | solution.py:240
  105.5 58.2 %collective-permute-start.17 = (bf16[4,48,4608]{2,1,0:T(8,128)(2,1)S(1)}, bf16[4,48,4608]{2,1,0:T(8,128)(2,1)}, u32[]{:S(2)}, u32[]{:S(2)}) collective-permute-start(bf16[4,48,4608]{2,1,0:T(8,128)(2,1)S(1)} %pad_maximum_fusion.5.own), channel_id=1, source_target_pairs={{0,2},{1,3},{2,0},{3,1},{4,6},{5,7},{6,4},{7,5},{8,10},{9,11},{10,... | collective-permute-start | bytes 5308424 | tf_op jit(solution)/shard_map/ppermute | solution.py:243
  109.4 57.0 %collective-permute-start.2 = (bf16[4,208,768]{2,1,0:T(8,128)(2,1)}, bf16[4,208,768]{2,1,0:T(8,128)(2,1)}, u32[]{:S(2)}, u32[]{:S(2)}) collective-permute-start(bf16[4,208,768]{2,1,0:T(8,128)(2,1)} %add_convert_fusion.18), channel_id=1, source_target_pairs={{0,1},{1,0},{2,3},{3,2},{4,5},{5,4},{6,7},{7,6},{8,9},{9,8},{10,11... | collective-permute-start | bytes 3833864 | tf_op jit(solution)/shard_map/ppermute | solution.py:246
  119.9 34.6 %collective-permute-start.8 = (bf16[2,48,1920]{2,1,0:T(8,128)(2,1)S(1)}, bf16[2,48,1920]{2,1,0:T(8,128)(2,1)S(1)}, u32[]{:S(2)}, u32[]{:S(2)}) collective-permute-start(bf16[2,48,1920]{2,1,0:T(8,128)(2,1)S(1)} %slice.694), channel_id=1, source_target_pairs={{0,2},{1,3},{2,0},{3,1},{4,6},{5,7},{6,4},{7,5},{8,10},{9,11},{10,... | collective-permute-start | bytes 1105928 | tf_op jit(solution)/shard_map/ppermute | solution.py:243
  120.4 34.1 %collective-permute-start.9 = (bf16[2,48,1920]{2,1,0:T(8,128)(2,1)S(1)}, bf16[2,48,1920]{2,1,0:T(8,128)(2,1)}, u32[]{:S(2)}, u32[]{:S(2)}) collective-permute-start(bf16[2,48,1920]{2,1,0:T(8,128)(2,1)S(1)} %slice.695), channel_id=1, source_target_pairs={{0,4},{1,5},{2,6},{3,7},{4,0},{5,1},{6,2},{7,3},{8,12},{9,13},{10,... | collective-permute-start | bytes 1105928 | tf_op jit(solution)/shard_map/ppermute | solution.py:240
  160.6 27.0 %collective-permute-start.12 = (bf16[768,384]{1,0:T(8,128)(2,1)}, bf16[768,384]{1,0:T(8,128)(2,1)}, u32[]{:S(2)}, u32[]{:S(2)}) collective-permute-start(bf16[768,384]{1,0:T(8,128)(2,1)} %get-tuple-element.37), channel_id=1, source_target_pairs={{0,1},{1,0},{2,3},{3,2},{4,5},{5,4},{6,7},{7,6},{8,9},{9,8},{10,11... | collective-permute-start | bytes 1769480 | tf_op jit(solution)/shard_map/ppermute | solution.py:246
  160.6 40.4 %collective-permute-start.11 = (bf16[768,384]{1,0:T(8,128)(2,1)}, bf16[768,384]{1,0:T(8,128)(2,1)}, u32[]{:S(2)}, u32[]{:S(2)}) collective-permute-start(bf16[768,384]{1,0:T(8,128)(2,1)} %get-tuple-element.36), channel_id=1, source_target_pairs={{0,1},{1,0},{2,3},{3,2},{4,5},{5,4},{6,7},{7,6},{8,9},{9,8},{10,11... | collective-permute-start | bytes 1769480 | tf_op jit(solution)/shard_map/ppermute | solution.py:246
  163.3 28.4 %collective-permute-start.18 = (bf16[2,48,4608]{2,1,0:T(8,128)(2,1)}, bf16[2,48,4608]{2,1,0:T(8,128)(2,1)S(1)}, u32[]{:S(2)}, u32[]{:S(2)}) collective-permute-start(bf16[2,48,4608]{2,1,0:T(8,128)(2,1)} %slice.702), channel_id=1, source_target_pairs={{0,2},{1,3},{2,0},{3,1},{4,6},{5,7},{6,4},{7,5},{8,10},{9,11},{10,... | collective-permute-start | bytes 2654216 | tf_op jit(solution)/shard_map/ppermute | solution.py:243
  165.9 27.2 %collective-permute-start.19 = (bf16[2,48,4608]{2,1,0:T(8,128)(2,1)}, bf16[2,48,4608]{2,1,0:T(8,128)(2,1)S(1)}, u32[]{:S(2)}, u32[]{:S(2)}) collective-permute-start(bf16[2,48,4608]{2,1,0:T(8,128)(2,1)} %slice.703), channel_id=1, source_target_pairs={{0,4},{1,5},{2,6},{3,7},{4,0},{5,1},{6,2},{7,3},{8,12},{9,13},{10,... | collective-permute-start | bytes 2654216 | tf_op jit(solution)/shard_map/ppermute | solution.py:240
  187.6 78.7 %collective-permute-start.29 = (bf16[4,48,6528]{2,1,0:T(8,128)(2,1)}, bf16[4,48,6528]{2,1,0:T(8,128)(2,1)}, u32[]{:S(2)}, u32[]{:S(2)}) collective-permute-start(bf16[4,48,6528]{2,1,0:T(8,128)(2,1)} %pad_maximum_fusion.2.own), channel_id=1, source_target_pairs={{0,4},{1,5},{2,6},{3,7},{4,0},{5,1},{6,2},{7,3},{8,12},{9,13},{10,... | collective-permute-start | bytes 7520264 | tf_op jit(solution)/shard_map/ppermute | solution.py:240
  191.6 78.2 %collective-permute-start.30 = (bf16[4,48,6528]{2,1,0:T(8,128)(2,1)}, bf16[4,48,6528]{2,1,0:T(8,128)(2,1)}, u32[]{:S(2)}, u32[]{:S(2)}) collective-permute-start(bf16[4,48,6528]{2,1,0:T(8,128)(2,1)} %pad_maximum_fusion.2.own), channel_id=1, source_target_pairs={{0,2},{1,3},{2,0},{3,1},{4,6},{5,7},{6,4},{7,5},{8,10},{9,11},{10,... | collective-permute-start | bytes 7520264 | tf_op jit(solution)/shard_map/ppermute | solution.py:243
  201.0 27.0 %collective-permute-start.22 = (bf16[768,384]{1,0:T(8,128)(2,1)}, bf16[768,384]{1,0:T(8,128)(2,1)}, u32[]{:S(2)}, u32[]{:S(2)}) collective-permute-start(bf16[768,384]{1,0:T(8,128)(2,1)} %get-tuple-element.40), channel_id=1, source_target_pairs={{0,1},{1,0},{2,3},{3,2},{4,5},{5,4},{6,7},{7,6},{8,9},{9,8},{10,11... | collective-permute-start | bytes 1769480 | tf_op jit(solution)/shard_map/ppermute | solution.py:246
  201.5 38.6 %collective-permute-start.23 = (bf16[768,1536]{1,0:T(8,128)(2,1)}, bf16[768,1536]{1,0:T(8,128)(2,1)}, u32[]{:S(2)}, u32[]{:S(2)}) collective-permute-start(bf16[768,1536]{1,0:T(8,128)(2,1)} %get-tuple-element.42), channel_id=1, source_target_pairs={{0,1},{1,0},{2,3},{3,2},{4,5},{5,4},{6,7},{7,6},{8,9},{9,8},{10,11... | collective-permute-start | bytes 7077896 | tf_op jit(solution)/shard_map/ppermute | solution.py:246
  214.5 32.1 %collective-permute-start.24 = (bf16[768,1536]{1,0:T(8,128)(2,1)}, bf16[768,1536]{1,0:T(8,128)(2,1)}, u32[]{:S(2)}, u32[]{:S(2)}) collective-permute-start(bf16[768,1536]{1,0:T(8,128)(2,1)} %get-tuple-element.43), channel_id=1, source_target_pairs={{0,1},{1,0},{2,3},{3,2},{4,5},{5,4},{6,7},{7,6},{8,9},{9,8},{10,11... | collective-permute-start | bytes 7077896 | tf_op jit(solution)/shard_map/ppermute | solution.py:246
  266.1 44.8 %collective-permute-start.25 = (bf16[4,208,768]{2,1,0:T(8,128)(2,1)}, bf16[4,208,768]{2,1,0:T(8,128)(2,1)}, u32[]{:S(2)}, u32[]{:S(2)}) collective-permute-start(bf16[4,208,768]{2,1,0:T(8,128)(2,1)} %get-tuple-element.198), channel_id=1, source_target_pairs={{0,1},{1,0},{2,3},{3,2},{4,5},{5,4},{6,7},{7,6},{8,9},{9,8},{10,11... | collective-permute-start | bytes 3833864 | tf_op jit(solution)/shard_map/ppermute | solution.py:246
  268.8 30.1 %collective-permute-start.31 = (bf16[2,48,6528]{2,1,0:T(8,128)(2,1)}, bf16[2,48,6528]{2,1,0:T(8,128)(2,1)}, u32[]{:S(2)}, u32[]{:S(2)}) collective-permute-start(bf16[2,48,6528]{2,1,0:T(8,128)(2,1)} %slice.709), channel_id=1, source_target_pairs={{0,2},{1,3},{2,0},{3,1},{4,6},{5,7},{6,4},{7,5},{8,10},{9,11},{10,... | collective-permute-start | bytes 3760136 | tf_op jit(solution)/shard_map/ppermute | solution.py:243
  272.3 29.7 %collective-permute-start.32 = (bf16[2,48,6528]{2,1,0:T(8,128)(2,1)}, bf16[2,48,6528]{2,1,0:T(8,128)(2,1)}, u32[]{:S(2)}, u32[]{:S(2)}) collective-permute-start(bf16[2,48,6528]{2,1,0:T(8,128)(2,1)} %slice.710), channel_id=1, source_target_pairs={{0,4},{1,5},{2,6},{3,7},{4,0},{5,1},{6,2},{7,3},{8,12},{9,13},{10,... | collective-permute-start | bytes 3760136 | tf_op jit(solution)/shard_map/ppermute | solution.py:240
  310.5 24.3 %collective-permute-start.35 = (bf16[768,384]{1,0:T(8,128)(2,1)}, bf16[768,384]{1,0:T(8,128)(2,1)S(1)}, u32[]{:S(2)}, u32[]{:S(2)}) collective-permute-start(bf16[768,384]{1,0:T(8,128)(2,1)} %get-tuple-element.46), channel_id=1, source_target_pairs={{0,1},{1,0},{2,3},{3,2},{4,5},{5,4},{6,7},{7,6},{8,9},{9,8},{10,11... | collective-permute-start | bytes 1769480 | tf_op jit(solution)/shard_map/ppermute | solution.py:246
  310.5 24.9 %collective-permute-start.34 = (bf16[768,384]{1,0:T(8,128)(2,1)}, bf16[768,384]{1,0:T(8,128)(2,1)}, u32[]{:S(2)}, u32[]{:S(2)}) collective-permute-start(bf16[768,384]{1,0:T(8,128)(2,1)} %get-tuple-element.45), channel_id=1, source_target_pairs={{0,1},{1,0},{2,3},{3,2},{4,5},{5,4},{6,7},{7,6},{8,9},{9,8},{10,11... | collective-permute-start | bytes 1769480 | tf_op jit(solution)/shard_map/ppermute | solution.py:246
  333.1 27.6 %collective-permute-start.37 = (bf16[768,384]{1,0:T(8,128)(2,1)}, bf16[768,384]{1,0:T(8,128)(2,1)}, u32[]{:S(2)}, u32[]{:S(2)}) collective-permute-start(bf16[768,384]{1,0:T(8,128)(2,1)} %get-tuple-element.49), channel_id=1, source_target_pairs={{0,1},{1,0},{2,3},{3,2},{4,5},{5,4},{6,7},{7,6},{8,9},{9,8},{10,11... | collective-permute-start | bytes 1769480 | tf_op jit(solution)/shard_map/ppermute | solution.py:246
  334.8 31.5 %collective-permute-start.38 = (bf16[768,1536]{1,0:T(8,128)(2,1)}, bf16[768,1536]{1,0:T(8,128)(2,1)}, u32[]{:S(2)}, u32[]{:S(2)}) collective-permute-start(bf16[768,1536]{1,0:T(8,128)(2,1)} %get-tuple-element.51), channel_id=1, source_target_pairs={{0,1},{1,0},{2,3},{3,2},{4,5},{5,4},{6,7},{7,6},{8,9},{9,8},{10,11... | collective-permute-start | bytes 7077896 | tf_op jit(solution)/shard_map/ppermute | solution.py:246
  335.4 49.7 %collective-permute-start.39 = (bf16[768,1536]{1,0:T(8,128)(2,1)}, bf16[768,1536]{1,0:T(8,128)(2,1)}, u32[]{:S(2)}, u32[]{:S(2)}) collective-permute-start(bf16[768,1536]{1,0:T(8,128)(2,1)} %get-tuple-element.52), channel_id=1, source_target_pairs={{0,1},{1,0},{2,3},{3,2},{4,5},{5,4},{6,7},{7,6},{8,9},{9,8},{10,11... | collective-permute-start | bytes 7077896 | tf_op jit(solution)/shard_map/ppermute | solution.py:246
  471.1 26.3 %collective-permute-start.44 = (bf16[4,208,384]{2,1,0:T(8,128)(2,1)}, bf16[4,208,384]{2,1,0:T(8,128)(2,1)}, u32[]{:S(2)}, u32[]{:S(2)}) collective-permute-start(bf16[4,208,384]{2,1,0:T(8,128)(2,1)} %bitcast.88), channel_id=1, source_target_pairs={{0,1},{1,0},{2,3},{3,2},{4,5},{5,4},{6,7},{7,6},{8,9},{9,8},{10,11... | collective-permute-start | bytes 1916936 | tf_op jit(solution)/shard_map/ppermute | solution.py:246
  471.3 175.8 %collective-permute-start.82 = (bf16[768,1536]{1,0:T(8,128)(2,1)}, bf16[768,1536]{1,0:T(8,128)(2,1)}, u32[]{:S(2)}, u32[]{:S(2)}) collective-permute-start(bf16[768,1536]{1,0:T(8,128)(2,1)} %convolution_convert_fusion), channel_id=1, source_target_pairs={{0,1},{1,0},{2,3},{3,2},{4,5},{5,4},{6,7},{7,6},{8,9},{9,8},{10,11... | collective-permute-start | bytes 7077896 | tf_op jit(solution)/shard_map/ppermute | solution.py:246
  487.9 152.5 %collective-permute-start.81 = (bf16[768,1536]{1,0:T(8,128)(2,1)}, bf16[768,1536]{1,0:T(8,128)(2,1)}, u32[]{:S(2)}, u32[]{:S(2)}) collective-permute-start(bf16[768,1536]{1,0:T(8,128)(2,1)} %convolution_convert_fusion.1), channel_id=1, source_target_pairs={{0,1},{1,0},{2,3},{3,2},{4,5},{5,4},{6,7},{7,6},{8,9},{9,8},{10,11... | collective-permute-start | bytes 7077896 | tf_op jit(solution)/shard_map/ppermute | solution.py:246
  493.5 39.5 %collective-permute-start.79 = (bf16[768,1152]{1,0:T(8,128)(2,1)}, bf16[768,1152]{1,0:T(8,128)(2,1)}, u32[]{:S(2)}, u32[]{:S(2)}) collective-permute-start(bf16[768,1152]{1,0:T(8,128)(2,1)} %fusion.25), channel_id=1, source_target_pairs={{0,1},{1,0},{2,3},{3,2},{4,5},{5,4},{6,7},{7,6},{8,9},{9,8},{10,11... | collective-permute-start | bytes 5308424 | tf_op jit(solution)/shard_map/ppermute | solution.py:246
  496.2 35.0 %collective-permute-start.41 = (bf16[4,98,768]{2,0,1:T(4,128)(2,1)S(1)}, bf16[4,98,768]{2,0,1:T(4,128)(2,1)S(1)}, u32[]{:S(2)}, u32[]{:S(2)}) collective-permute-start(bf16[4,98,768]{2,0,1:T(4,128)(2,1)S(1)} %copy.57), channel_id=1, source_target_pairs={{0,2},{1,3},{2,0},{3,1},{4,6},{5,7},{6,4},{7,5},{8,10},{9,11},{10,... | collective-permute-start | bytes 1806344 | tf_op jit(solution)/shard_map/ppermute | solution.py:243
  600.0 102.4 %collective-permute-start.66 = (bf16[768,1152]{1,0:T(8,128)(2,1)}, bf16[768,1152]{1,0:T(8,128)(2,1)}, u32[]{:S(2)}, u32[]{:S(2)}) collective-permute-start(bf16[768,1152]{1,0:T(8,128)(2,1)} %fusion.24), channel_id=1, source_target_pairs={{0,1},{1,0},{2,3},{3,2},{4,5},{5,4},{6,7},{7,6},{8,9},{9,8},{10,11... | collective-permute-start | bytes 5308424 | tf_op jit(solution)/shard_map/ppermute | solution.py:246
  618.3 44.0 %collective-permute-start.46 = (bf16[4,208,384]{2,1,0:T(8,128)(2,1)}, bf16[4,208,384]{2,1,0:T(8,128)(2,1)S(1)}, u32[]{:S(2)}, u32[]{:S(2)}) collective-permute-start(bf16[4,208,384]{2,1,0:T(8,128)(2,1)} %bitcast.99), channel_id=1, source_target_pairs={{0,1},{1,0},{2,3},{3,2},{4,5},{5,4},{6,7},{7,6},{8,9},{9,8},{10,11... | collective-permute-start | bytes 1916936 | tf_op jit(solution)/shard_map/ppermute | solution.py:246
  622.2 18.0 %collective-permute-start.51 = (f32[2304]{0:T(1024)S(1)}, f32[2304]{0:T(1024)S(1)}, u32[]{:S(2)}, u32[]{:S(2)}) collective-permute-start(f32[2304]{0:T(1024)S(1)} %pad_maximum_fusion.41), channel_id=1, source_target_pairs={{0,1},{1,0},{2,3},{3,2},{4,5},{5,4},{6,7},{7,6},{8,9},{9,8},{10,11... | collective-permute-start | bytes 27656 | tf_op jit(solution)/shard_map/ppermute | solution.py:246
  640.4 18.9 %collective-permute-start.67 = (bf16[768,384]{1,0:T(8,128)(2,1)}, bf16[768,384]{1,0:T(8,128)(2,1)S(1)}, u32[]{:S(2)}, u32[]{:S(2)}) collective-permute-start(bf16[768,384]{1,0:T(8,128)(2,1)} %convolution_convert_fusion.18), channel_id=1, source_target_pairs={{0,1},{1,0},{2,3},{3,2},{4,5},{5,4},{6,7},{7,6},{8,9},{9,8},{10,11... | collective-permute-start | bytes 1769480 | tf_op jit(solution)/shard_map/ppermute | solution.py:246
  655.7 164.0 %collective-permute-start.68 = (bf16[768,1536]{1,0:T(8,128)(2,1)}, bf16[768,1536]{1,0:T(8,128)(2,1)}, u32[]{:S(2)}, u32[]{:S(2)}) collective-permute-start(bf16[768,1536]{1,0:T(8,128)(2,1)} %convolution_convert_fusion.3), channel_id=1, source_target_pairs={{0,1},{1,0},{2,3},{3,2},{4,5},{5,4},{6,7},{7,6},{8,9},{9,8},{10,11... | collective-permute-start | bytes 7077896 | tf_op jit(solution)/shard_map/ppermute | solution.py:246
  658.2 167.1 %collective-permute-start.69 = (bf16[768,1536]{1,0:T(8,128)(2,1)}, bf16[768,1536]{1,0:T(8,128)(2,1)}, u32[]{:S(2)}, u32[]{:S(2)}) collective-permute-start(bf16[768,1536]{1,0:T(8,128)(2,1)} %convolution_convert_fusion.2), channel_id=1, source_target_pairs={{0,1},{1,0},{2,3},{3,2},{4,5},{5,4},{6,7},{7,6},{8,9},{9,8},{10,11... | collective-permute-start | bytes 7077896 | tf_op jit(solution)/shard_map/ppermute | solution.py:246
  659.3 34.9 %collective-permute-start.83 = (bf16[2,48,6528]{2,1,0:T(8,128)(2,1)}, bf16[2,48,6528]{2,1,0:T(8,128)(2,1)}, u32[]{:S(2)}, u32[]{:S(2)}) collective-permute-start(bf16[2,48,6528]{2,1,0:T(8,128)(2,1)} %get-tuple-element.216), channel_id=1, source_target_pairs={{0,2},{1,3},{2,0},{3,1},{4,6},{5,7},{6,4},{7,5},{8,10},{9,11},{10,... | collective-permute-start | bytes 3760136 | tf_op jit(solution)/shard_map/ppermute | solution.py:243
  662.3 35.3 %collective-permute-start.85 = (bf16[2,48,6528]{2,1,0:T(8,128)(2,1)}, bf16[2,48,6528]{2,1,0:T(8,128)(2,1)}, u32[]{:S(2)}, u32[]{:S(2)}) collective-permute-start(bf16[2,48,6528]{2,1,0:T(8,128)(2,1)} %get-tuple-element.217), channel_id=1, source_target_pairs={{0,4},{1,5},{2,6},{3,7},{4,0},{5,1},{6,2},{7,3},{8,12},{9,13},{10,... | collective-permute-start | bytes 3760136 | tf_op jit(solution)/shard_map/ppermute | solution.py:240
  697.6 196.6 %collective-permute-start.84 = (bf16[4,48,6528]{2,1,0:T(8,128)(2,1)}, bf16[4,48,6528]{2,1,0:T(8,128)(2,1)}, u32[]{:S(2)}, u32[]{:S(2)}) collective-permute-start(bf16[4,48,6528]{2,1,0:T(8,128)(2,1)} %pad_maximum_fusion.3), channel_id=1, source_target_pairs={{0,4},{1,5},{2,6},{3,7},{4,0},{5,1},{6,2},{7,3},{8,12},{9,13},{10,... | collective-permute-start | bytes 7520264 | tf_op jit(solution)/shard_map/ppermute | solution.py:240
  702.4 191.8 %collective-permute-start.86 = (bf16[4,48,6528]{2,1,0:T(8,128)(2,1)}, bf16[4,48,6528]{2,1,0:T(8,128)(2,1)}, u32[]{:S(2)}, u32[]{:S(2)}) collective-permute-start(bf16[4,48,6528]{2,1,0:T(8,128)(2,1)} %pad_maximum_fusion.4), channel_id=1, source_target_pairs={{0,2},{1,3},{2,0},{3,1},{4,6},{5,7},{6,4},{7,5},{8,10},{9,11},{10,... | collective-permute-start | bytes 7520264 | tf_op jit(solution)/shard_map/ppermute | solution.py:243
  732.2 28.9 %collective-permute-start.53 = (f32[2,10756]{1,0:T(2,128)S(1)}, f32[2,10756]{1,0:T(2,128)S(1)}, u32[]{:S(2)}, u32[]{:S(2)}) collective-permute-start(f32[2,10756]{1,0:T(2,128)S(1)} %maximum_maximum_fusion.2), channel_id=1, source_target_pairs={{0,2},{1,3},{2,0},{3,1},{4,6},{5,7},{6,4},{7,5},{8,10},{9,11},{10,... | collective-permute-start | bytes 258152 | tf_op jit(solution)/shard_map/ppermute | solution.py:243
  784.5 25.5 %collective-permute-start.55 = (f32[2,10756]{1,0:T(2,128)S(1)}, f32[2,10756]{1,0:T(2,128)S(1)}, u32[]{:S(2)}, u32[]{:S(2)}) collective-permute-start(f32[2,10756]{1,0:T(2,128)S(1)} %add.983), channel_id=1, source_target_pairs={{0,8},{1,9},{2,10},{3,11},{4,12},{5,13},{6,14},{7,15},{8,0},{9,1},... | collective-permute-start | bytes 258152 | tf_op jit(solution)/shard_map/ppermute | solution.py:260
  816.5 29.1 %collective-permute-start.48 = (bf16[4,98,768]{2,0,1:T(4,128)(2,1)}, bf16[4,98,768]{2,0,1:T(4,128)(2,1)}, u32[]{:S(2)}, u32[]{:S(2)}) collective-permute-start(bf16[4,98,768]{2,0,1:T(4,128)(2,1)} %copy.66), channel_id=1, source_target_pairs={{0,1},{1,0},{2,3},{3,2},{4,5},{5,4},{6,7},{7,6},{8,9},{9,8},{10,11... | collective-permute-start | bytes 1806344 | tf_op jit(solution)/shard_map/ppermute | solution.py:246
  819.7 19.2 %collective-permute-start.60 = (bf16[4,48,1920]{2,1,0:T(8,128)(2,1)}, bf16[4,48,1920]{2,1,0:T(8,128)(2,1)S(1)}, u32[]{:S(2)}, u32[]{:S(2)}) collective-permute-start(bf16[4,48,1920]{2,1,0:T(8,128)(2,1)} %pad_maximum_fusion.20), channel_id=1, source_target_pairs={{0,4},{1,5},{2,6},{3,7},{4,0},{5,1},{6,2},{7,3},{8,12},{9,13},{10,... | collective-permute-start | bytes 2211848 | tf_op jit(solution)/shard_map/ppermute | solution.py:240
  825.2 18.8 %collective-permute-start.62 = (bf16[4,48,1920]{2,1,0:T(8,128)(2,1)}, bf16[4,48,1920]{2,1,0:T(8,128)(2,1)S(1)}, u32[]{:S(2)}, u32[]{:S(2)}) collective-permute-start(bf16[4,48,1920]{2,1,0:T(8,128)(2,1)} %pad_maximum_fusion.22), channel_id=1, source_target_pairs={{0,2},{1,3},{2,0},{3,1},{4,6},{5,7},{6,4},{7,5},{8,10},{9,11},{10,... | collective-permute-start | bytes 2211848 | tf_op jit(solution)/shard_map/ppermute | solution.py:243
  854.0 35.7 %collective-permute-start.70 = (bf16[2,48,4608]{2,1,0:T(8,128)(2,1)}, bf16[2,48,4608]{2,1,0:T(8,128)(2,1)}, u32[]{:S(2)}, u32[]{:S(2)}) collective-permute-start(bf16[2,48,4608]{2,1,0:T(8,128)(2,1)} %get-tuple-element.253), channel_id=1, source_target_pairs={{0,2},{1,3},{2,0},{3,1},{4,6},{5,7},{6,4},{7,5},{8,10},{9,11},{10,... | collective-permute-start | bytes 2654216 | tf_op jit(solution)/shard_map/ppermute | solution.py:243
  860.3 42.0 %collective-permute-start.72 = (bf16[2,48,4608]{2,1,0:T(8,128)(2,1)}, bf16[2,48,4608]{2,1,0:T(8,128)(2,1)}, u32[]{:S(2)}, u32[]{:S(2)}) collective-permute-start(bf16[2,48,4608]{2,1,0:T(8,128)(2,1)} %get-tuple-element.254), channel_id=1, source_target_pairs={{0,4},{1,5},{2,6},{3,7},{4,0},{5,1},{6,2},{7,3},{8,12},{9,13},{10,... | collective-permute-start | bytes 2654216 | tf_op jit(solution)/shard_map/ppermute | solution.py:240
  861.9 23.6 %collective-permute-start.49 = (bf16[4,98,768]{2,0,1:T(4,128)(2,1)}, bf16[4,98,768]{2,0,1:T(4,128)(2,1)}, u32[]{:S(2)}, u32[]{:S(2)}) collective-permute-start(bf16[4,98,768]{2,0,1:T(4,128)(2,1)} %copy.69), channel_id=1, source_target_pairs={{0,2},{1,3},{2,0},{3,1},{4,6},{5,7},{6,4},{7,5},{8,10},{9,11},{10,... | collective-permute-start | bytes 1806344 | tf_op jit(solution)/shard_map/ppermute | solution.py:243
  892.6 50.2 %collective-permute-start.71 = (bf16[4,48,4608]{2,1,0:T(8,128)(2,1)}, bf16[4,48,4608]{2,1,0:T(8,128)(2,1)}, u32[]{:S(2)}, u32[]{:S(2)}) collective-permute-start(bf16[4,48,4608]{2,1,0:T(8,128)(2,1)} %pad_maximum_fusion.8), channel_id=1, source_target_pairs={{0,4},{1,5},{2,6},{3,7},{4,0},{5,1},{6,2},{7,3},{8,12},{9,13},{10,... | collective-permute-start | bytes 5308424 | tf_op jit(solution)/shard_map/ppermute | solution.py:240
  897.8 19.0 %collective-permute-start.87 = (bf16[48,6528]{1,0:T(8,128)(2,1)S(1)}, bf16[48,6528]{1,0:T(8,128)(2,1)S(1)}, u32[]{:S(2)}, u32[]{:S(2)}) collective-permute-start(bf16[48,6528]{1,0:T(8,128)(2,1)S(1)} %get-tuple-element.213), channel_id=1, source_target_pairs={{0,8},{1,9},{2,10},{3,11},{4,12},{5,13},{6,14},{7,15},{8,16},{9,17... | collective-permute-start | bytes 1880072 | tf_op jit(solution)/shard_map/ppermute | solution.py:250
  898.2 40.0 %collective-permute-start.88 = (bf16[48,6528]{1,0:T(8,128)(2,1)S(1)}, bf16[48,6528]{1,0:T(8,128)(2,1)S(1)}, u32[]{:S(2)}, u32[]{:S(2)}) collective-permute-start(bf16[48,6528]{1,0:T(8,128)(2,1)S(1)} %get-tuple-element.215), channel_id=1, source_target_pairs={{0,16},{1,17},{2,18},{3,19},{4,20},{5,21},{6,22},{7,23},{8,24},{9,... | collective-permute-start | bytes 1880072 | tf_op jit(solution)/shard_map/ppermute | solution.py:250
  899.5 38.7 %collective-permute-start.89 = (bf16[48,6528]{1,0:T(8,128)(2,1)S(1)}, bf16[48,6528]{1,0:T(8,128)(2,1)S(1)}, u32[]{:S(2)}, u32[]{:S(2)}) collective-permute-start(bf16[48,6528]{1,0:T(8,128)(2,1)S(1)} %get-tuple-element.214), channel_id=1, source_target_pairs={{0,24},{1,25},{2,26},{3,27},{4,28},{5,29},{6,30},{7,31},{8,0},{9,1... | collective-permute-start | bytes 1880072 | tf_op jit(solution)/shard_map/ppermute | solution.py:250
  905.1 37.6 %collective-permute-start.73 = (bf16[4,48,4608]{2,1,0:T(8,128)(2,1)}, bf16[4,48,4608]{2,1,0:T(8,128)(2,1)}, u32[]{:S(2)}, u32[]{:S(2)}) collective-permute-start(bf16[4,48,4608]{2,1,0:T(8,128)(2,1)} %pad_maximum_fusion.10), channel_id=1, source_target_pairs={{0,2},{1,3},{2,0},{3,1},{4,6},{5,7},{6,4},{7,5},{8,10},{9,11},{10,... | collective-permute-start | bytes 5308424 | tf_op jit(solution)/shard_map/ppermute | solution.py:243
  945.8 26.8 %collective-permute-start.74 = (bf16[48,4608]{1,0:T(8,128)(2,1)S(1)}, bf16[48,4608]{1,0:T(8,128)(2,1)S(1)}, u32[]{:S(2)}, u32[]{:S(2)}) collective-permute-start(bf16[48,4608]{1,0:T(8,128)(2,1)S(1)} %get-tuple-element.246), channel_id=1, source_target_pairs={{0,8},{1,9},{2,10},{3,11},{4,12},{5,13},{6,14},{7,15},{8,16},{9,17... | collective-permute-start | bytes 1327112 | tf_op jit(solution)/shard_map/ppermute | solution.py:250
  959.8 27.3 %collective-permute-start.75 = (bf16[48,4608]{1,0:T(8,128)(2,1)S(1)}, bf16[48,4608]{1,0:T(8,128)(2,1)S(1)}, u32[]{:S(2)}, u32[]{:S(2)}) collective-permute-start(bf16[48,4608]{1,0:T(8,128)(2,1)S(1)} %get-tuple-element.248), channel_id=1, source_target_pairs={{0,16},{1,17},{2,18},{3,19},{4,20},{5,21},{6,22},{7,23},{8,24},{9,... | collective-permute-start | bytes 1327112 | tf_op jit(solution)/shard_map/ppermute | solution.py:250
  962.0 26.4 %collective-permute-start.76 = (bf16[48,4608]{1,0:T(8,128)(2,1)S(1)}, bf16[48,4608]{1,0:T(8,128)(2,1)S(1)}, u32[]{:S(2)}, u32[]{:S(2)}) collective-permute-start(bf16[48,4608]{1,0:T(8,128)(2,1)S(1)} %get-tuple-element.247), channel_id=1, source_target_pairs={{0,24},{1,25},{2,26},{3,27},{4,28},{5,29},{6,30},{7,31},{8,0},{9,1... | collective-permute-start | bytes 1327112 | tf_op jit(solution)/shard_map/ppermute | solution.py:250
  (302 other events, 5129.0 us)

commit v2 on v1

--- a/solution.py
+++ b/solution.py
@@ -236,20 +236,21 @@
                         )
         return pairs
 
+    def send(self, value, pairs):
+        return lax.ppermute(value, AXES, pairs)
+
     def over_x(self, value):
-        return lax.ppermute(value, AXES, self.perm(lambda z, x, y, t: (z, 1 - x, y, t)))
+        return self.send(value, self.perm(lambda z, x, y, t: (z, 1 - x, y, t)))
 
     def over_y(self, value):
-        return lax.ppermute(value, AXES, self.perm(lambda z, x, y, t: (z, x, 1 - y, t)))
+        return self.send(value, self.perm(lambda z, x, y, t: (z, x, 1 - y, t)))
 
     def over_t(self, value):
-        return lax.ppermute(value, AXES, self.perm(lambda z, x, y, t: (z, x, y, 1 - t)))
+        return self.send(value, self.perm(lambda z, x, y, t: (z, x, y, 1 - t)))
 
     def over_z(self, value, step):
         depth = self.depth
-        return lax.ppermute(
-            value, AXES, self.perm(lambda z, x, y, t: ((z + step) % depth, x, y, t))
-        )
+        return self.send(value, self.perm(lambda z, x, y, t: ((z + step) % depth, x, y, t)))
 
     def over_bit(self, value, bit):
         pairs = []
@@ -257,7 +258,7 @@
             for y in range(2):
                 for t in range(2):
                     pairs.append(((s * 2 + y) * 2 + t, ((s ^ bit) * 2 + y) * 2 + t))
-        return lax.ppermute(value, AXES, pairs)
+        return self.send(value, pairs)
 
     def total(self, value, across):
         if across:
@@ -296,23 +297,53 @@
         put(1, 1, db)
 
 
-def gather_rows(grid, block, widths):
-    step_rows, lanes = block.shape
-    if not grid.direct:
-        full = lax.all_gather(block, ("shard", "ctx"), axis=0, tiled=True)
-        outs, start = [], 0
-        for width in widths:
-            outs.append(full[:, start : start + width])
-            start += width
-        return outs
-    depth = grid.depth
+def tie(value, *others):
+    return lax.optimization_barrier((value, *others))[0]
+
+
+class Feed:
+    def __init__(self, grid, items, widths, *behind):
+        self.grid, self.widths = grid, widths
+        block = tie(jnp.concatenate(items, axis=1), *behind)
+        if grid.direct:
+            self.blocks = [block] + [grid.over_z(block, k) for k in range(1, grid.depth)]
+        else:
+            self.blocks = [block]
+
+    def near(self, *behind):
+        grid = self.grid
+        if grid.direct:
+            self.own = tie(jnp.stack(self.blocks), *behind)
+            self.xn = grid.over_x(self.own)
+            self.yn = grid.over_y(self.own)
+        return self
+
+    def far(self, *behind):
+        grid = self.grid
+        if grid.direct:
+            half = grid.depth // 2
+            xn, yn = tie(self.xn[:half], *behind), tie(self.yn[half:], *behind)
+            self.last = (grid.over_y(xn), grid.over_x(yn))
+        return self
+
+    def done(self):
+        grid = self.grid
+        if not grid.direct:
+            full = lax.all_gather(self.blocks[0], ("shard", "ctx"), axis=0, tiled=True)
+            return split_columns(full, self.widths)
+        at = jnp.stack([grid.z, grid.x, grid.y]).astype(jnp.int32)
+        return place_rows(grid, at, self.own, self.xn, self.yn, *self.last, self.widths)
+
+    def near_parts(self):
+        return (self.xn, self.yn) if self.grid.direct else ()
+
+    def far_parts(self):
+        return self.last if self.grid.direct else ()
+
+
+def place_rows(grid, at, own, xn, yn, da, db, widths):
+    depth, step_rows, lanes = own.shape
     half = depth // 2
-    own = jnp.stack([block] + [grid.over_z(block, k) for k in range(1, depth)])
-    xn = grid.over_x(own)
-    yn = grid.over_y(own)
-    da = grid.over_y(xn[:half])
-    db = grid.over_x(yn[half:])
-    at = jnp.stack([grid.z, grid.x, grid.y]).astype(jnp.int32)
     piece = lambda index: pl.BlockSpec((1, step_rows, lanes), index)
     straight = piece(lambda k, at_ref: (k, 0, 0))
     return pl.pallas_call(
@@ -336,52 +367,231 @@
             ],
         ),
         out_shape=[
-            jax.ShapeDtypeStruct((depth * 4 * step_rows, width), block.dtype) for width in widths
+            jax.ShapeDtypeStruct((depth * 4 * step_rows, width), own.dtype) for width in widths
         ],
         cost_estimate=pl.CostEstimate(
             flops=0, bytes_accessed=depth * 4 * step_rows * lanes * 4, transcendentals=0
         ),
+        compiler_params=pltpu.CompilerParams(vmem_limit_bytes=48 << 20),
         name="place_rows",
     )(at, own, xn, yn, da, db)
 
 
-def scatter_rows(grid, parts):
-    if not grid.direct:
-        whole = jnp.concatenate(parts, axis=1).astype(F32)
-        return lax.psum_scatter(whole, ("shard", "ctx"), scatter_dimension=0, tiled=True)
+class Sums:
+    def __init__(self, place, part, own, ra, rb, sx, sy, rx, ry, low, gz, send, recv):
+        self.place, self.part, self.own = place, part, own
+        self.ra, self.rb, self.sx, self.sy = ra, rb, sx, sy
+        self.rx, self.ry, self.low, self.gz = rx, ry, low, gz
+        self.send, self.recv = send, recv
+        self.half = part.shape[0] // 2
+
+    def copy(self, number, src, dst, target):
+        return pltpu.make_async_remote_copy(
+            src_ref=src,
+            dst_ref=dst,
+            send_sem=self.send.at[number],
+            recv_sem=self.recv.at[number],
+            device_id=target,
+            device_id_type=pl.DeviceIdType.MESH,
+        )
+
+    def first(self):
+        z, x, y = self.place.z, self.place.x, self.place.y
+        low, high = pl.ds(0, self.half), pl.ds(self.half, self.half)
+        self.far = [
+            self.copy(0, self.part.at[low, 1 - x, 1 - y], self.ra, self.place.over_y()),
+            self.copy(1, self.part.at[high, 1 - x, 1 - y], self.rb, self.place.over_x()),
+        ]
+        for item in self.far:
+            item.start()
+
+    def second(self):
+        x, y, half = self.place.x, self.place.y, self.half
+        for item in self.far:
+            item.wait()
+        for k in range(2 * half):
+            toward_x, toward_y = self.part[k, 1 - x, y], self.part[k, x, 1 - y]
+            if k < half:
+                toward_x = (toward_x.astype(F32) + self.ra[k].astype(F32)).astype(BF)
+            else:
+                toward_y = (toward_y.astype(F32) + self.rb[k - half].astype(F32)).astype(BF)
+            self.sx[k] = toward_x
+            self.sy[k] = toward_y
+        self.near = [
+            self.copy(2, self.sx, self.rx, self.place.over_x()),
+            self.copy(3, self.sy, self.ry, self.place.over_y()),
+        ]
+        for item in self.near:
+            item.start()
+
+    def kept(self, k):
+        mine = self.part[k, self.place.x, self.place.y].astype(F32)
+        return mine + self.rx[k].astype(F32) + self.ry[k].astype(F32)
+
+    def third(self):
+        depth = 2 * self.half
+        for item in self.near:
+            item.wait()
+        for k in range(depth):
+            self.low[k] = self.kept(k).astype(BF)
+        self.deep = [
+            self.copy(
+                3 + k,
+                self.low.at[lax.rem(self.place.z + k, depth)],
+                self.gz.at[k - 1],
+                self.place.over_z(k),
+            )
+            for k in range(1, depth)
+        ]
+        for item in self.deep:
+            item.start()
+
+    def last(self):
+        for item in self.deep:
+            item.wait()
+        total = self.kept(self.place.z)
+        for k in range(2 * self.half - 1):
+            total = total + self.gz[k].astype(F32)
+        self.own[...] = total
+
+
+class Place:
+    def __init__(self, depth):
+        self.depth = depth
+        shard = lax.axis_index("shard")
+        self.z = shard // 2
+        self.x = lax.rem(shard, 2)
+        self.y = lax.axis_index("ctx")
+
+    def over_x(self):
+        return {"shard": self.z * 2 + 1 - self.x}
+
+    def over_y(self):
+        return {"ctx": 1 - self.y}
+
+    def over_z(self, step):
+        return {"shard": lax.rem(self.z + step, self.depth) * 2 + self.x}
+
+    def meet(self):
+        barrier = pltpu.get_barrier_semaphore()
+        targets = [self.over_x(), self.over_y()]
+        targets += [self.over_z(k) for k in range(1, self.depth)]
+        for target in targets:
+            pl.semaphore_signal(
+                barrier, inc=1, device_id=target, device_id_type=pl.DeviceIdType.MESH
+            )
+        pl.semaphore_wait(barrier, len(targets))
+
+
+def sum_body(depth, ins, parts, outs, payload, *refs):
+    refs = list(refs)
+    take = lambda count: [refs.pop(0) for _ in range(count)]
+    in_refs, part_refs, out_refs, own_refs = take(ins), take(parts), take(outs), take(parts)
+    place = Place(depth)
+    sums = [
+        Sums(place, part, own, *take(10)) for part, own in zip(part_refs, own_refs)
+    ]
+    place.meet()
+    for item in sums:
+        item.first()
+    payload(0, in_refs, out_refs)
+    for item in sums:
+        item.second()
+    payload(1, in_refs, out_refs)
+    for item in sums:
+        item.third()
+    for item in sums:
+        item.last()
+
+
+def no_payload(stage, in_refs, out_refs):
+    return None
+
+
+def sum_rows(grid, number, parts, payload=no_payload, ins=(), outs=(), smem=0):
     depth = grid.depth
-    half = depth // 2
-
-    def pick(dx, dy):
-        out = []
-        for part in parts:
-            step_rows = part.shape[0] // (depth * 4)
-            cube = part.reshape(depth, 2, 2, step_rows, part.shape[1])
-            bx = grid.x if dx == 0 else 1 - grid.x
-            by = grid.y if dy == 0 else 1 - grid.y
-            out.append(
-                lax.dynamic_slice(
-                    cube, (0, bx, by, 0, 0), (depth, 1, 1, step_rows, part.shape[1])
-                ).reshape(depth, step_rows, part.shape[1])
-            )
-        return jnp.concatenate(out, axis=-1)
-
-    far = pick(1, 1)
-    ra = grid.over_y(far[:half])
-    rb = grid.over_x(far[half:])
-    sx = pick(1, 0)
-    sy = pick(0, 1)
-    sx = jnp.concatenate([(sx[:half].astype(F32) + ra.astype(F32)).astype(BF), sx[half:]])
-    sy = jnp.concatenate([sy[:half], (sy[half:].astype(F32) + rb.astype(F32)).astype(BF)])
-    rx = grid.over_x(sx)
-    ry = grid.over_y(sy)
-    kept = pick(0, 0).astype(F32) + rx.astype(F32) + ry.astype(F32)
-    own = lax.dynamic_index_in_dim(kept, grid.z, 0, keepdims=False)
-    low = kept.astype(BF)
-    for k in range(1, depth):
-        block = lax.dynamic_index_in_dim(low, (grid.z + k) % depth, 0, keepdims=False)
-        own = own + grid.over_z(block, k).astype(F32)
-    return own
+    step_rows = parts[0].shape[0] // (depth * 4)
+    cubes = [part.reshape(depth, 2, 2, step_rows, part.shape[1]) for part in parts]
+    scratch = []
+    for part in parts:
+        block = lambda count, lanes=part.shape[1]: pltpu.VMEM((count, step_rows, lanes), BF)
+        scratch += [block(depth // 2)] * 2 + [block(depth)] * 5 + [block(depth - 1)]
+        scratch += [pltpu.SemaphoreType.DMA((3 + depth,))] * 2
+    vmem = pl.BlockSpec(memory_space=pltpu.VMEM)
+    results = pl.pallas_call(
+        functools.partial(sum_body, depth, len(ins), len(parts), len(outs), payload),
+        in_specs=[pl.BlockSpec(memory_space=pltpu.SMEM)] * smem
+        + [vmem] * (len(ins) - smem + len(parts)),
+        out_specs=[vmem] * (len(outs) + len(parts)),
+        out_shape=list(outs)
+        + [jax.ShapeDtypeStruct((step_rows, part.shape[1]), F32) for part in parts],
+        scratch_shapes=scratch,
+        compiler_params=pltpu.CompilerParams(
+            collective_id=number, has_side_effects=True, vmem_limit_bytes=56 << 20
+        ),
+        cost_estimate=pl.CostEstimate(
+            flops=20000000000, bytes_accessed=50000000, transcendentals=0
+        ),
+        name="sum_rows",
+    )(*ins, *cubes)
+    return results[: len(outs)], results[len(outs) :]
+
+
+def plain_sums(parts):
+    return [
+        lax.psum_scatter(part.astype(F32), ("shard", "ctx"), scatter_dimension=0, tiled=True)
+        for part in parts
+    ]
+
+
+def spatial_back_payload(places, scale, stage, ins, outs):
+    count_ref, own_ref, oth_ref, bown_ref, both_ref = ins
+    frames = own_ref.shape[0]
+    fix = spatial_fix(count_ref, own_ref.shape[1], places)
+
+    def frame(f, carry):
+        for src, back, dst in ((own_ref, bown_ref, outs[0]), (oth_ref, both_ref, outs[1])):
+
+            def put(part, pair, value, dst=dst):
+                dst[f, :, column(part, pair)] = value
+
+            heads_backward(
+                lambda part, pair, src=src: src[f, :, column(part, pair)],
+                lambda pair, back=back: back[f, :, pair * 128 : pair * 128 + 128],
+                fix,
+                scale,
+                put,
+            )
+        return carry
+
+    half = frames // 2
+    lax.fori_loop(stage * half, half if stage == 0 else frames, frame, 0)
+
+
+def temporal_back_payload(scale, stage, ins, outs):
+    src, back = ins
+    dst = outs[0]
+    tile = 16
+    tiles = src.shape[1] // tile
+    fix = temporal_fix(tile)
+
+    def one(i, carry):
+        at = pl.ds(pl.multiple_of(i * tile, tile), tile)
+
+        def put(part, pair, value):
+            dst[:, at, column(part, pair)] = value.reshape(FRAMES, tile, 128)
+
+        heads_backward(
+            lambda part, pair: src[:, at, column(part, pair)].reshape(FRAMES * tile, 128),
+            lambda pair: back[:, at, pair * 128 : pair * 128 + 128].reshape(FRAMES * tile, 128),
+            fix,
+            scale,
+            put,
+        )
+        return carry
+
+    half = tiles // 2
+    lax.fori_loop(stage * half, half if stage == 0 else tiles, one, 0)
 
 
 def split_columns(value, widths):
@@ -469,20 +679,17 @@
     def pack_mix(item):
         return jnp.concatenate([item[..., : width // 2], item[..., width // 2 :]], axis=-2)
 
-    def block_t(layer):
-        return jnp.concatenate(
-            [triple_weight[layer, 0, :, i] for i in range(3)]
-            + [merge_weight[layer, 0].T, pack_mix(mixing_weight[layer])],
-            axis=1,
-        )
+    def block_triple(layer, part):
+        return [triple_weight[layer, part, :, i] for i in range(3)]
+
+    def block_out(layer):
+        return [merge_weight[layer, 0].T, pack_mix(mixing_weight[layer])]
 
     def block_s(layer):
-        return jnp.concatenate(
-            [triple_weight[layer, 1, :, i] for i in range(3)] + [merge_weight[layer, 1].T], axis=1
-        )
+        return block_triple(layer, 1) + [merge_weight[layer, 1].T]
 
     def block_m(layer):
-        return jnp.concatenate([up_weight[layer], down_weight[layer].T], axis=1)
+        return [up_weight[layer], down_weight[layer].T]
 
     split = triple_weight.shape[-1]
     hid = up_weight.shape[-1]
@@ -490,41 +697,20 @@
     wide_s = (3 * split, split)
     wide_m = (hid, hid)
 
-    start_clips = spread_in(video_clips)
-    gathered = [None] * LAYERS
-    for layer in range(LAYERS):
-        if layer == 0:
-            got = gather_rows(grid, block_t(layer), wide_t)
-            got += gather_rows(
-                grid, jnp.concatenate([block_s(layer), block_m(layer)], axis=1), wide_s + wide_m
-            )
-        else:
-            got = gather_rows(
-                grid,
-                jnp.concatenate([block_t(layer), block_s(layer), block_m(layer)], axis=1),
-                wide_t + wide_s + wide_m,
-            )
-        triple_t, merge_t, mix, triple_s, merge_s, upward, downward = got
-        other = [grid.over_t(item) for item in (merge_t, mix, triple_s, merge_s, upward, downward)]
-
-        def unpack_mix(item):
-            cube = item.reshape(-1, 2, half_rows, width // 2)
-            return jnp.concatenate([cube[:, 0], cube[:, 1]], axis=-1)
-
-        mix_own, mix_oth = unpack_mix(mix), unpack_mix(other[1])
+    def unpack_mix(item):
+        cube = item.reshape(-1, 2, half_rows, width // 2)
+        return jnp.concatenate([cube[:, 0], cube[:, 1]], axis=-1)
+
+    def with_other(item):
+        return (item, grid.over_t(item))
+
+    def out_weights(merge_t, mix):
+        mix_own, mix_oth = [unpack_mix(item) for item in with_other(mix)]
         mixing = jnp.stack(
             [jnp.where(own_first, mix_own, mix_oth), jnp.where(own_first, mix_oth, mix_own)],
             axis=1,
         ).reshape(width, width)
-        gathered[layer] = dict(
-            triple_t=triple_t,
-            mixing=mixing,
-            merge_t=(merge_t, other[0]),
-            triple_s=(triple_s, other[2]),
-            merge_s=(merge_s, other[3]),
-            up=(upward, other[4]),
-            down=(downward, other[5]),
-        )
+        return dict(merge_t=with_other(merge_t), mixing=mixing)
 
     small = jnp.concatenate([entry_bias[:, 1].reshape(-1), up_bias.reshape(-1)])
     small_oth = grid.over_t(small)
@@ -544,8 +730,14 @@
     def cube(value):
         return value.reshape(-1, padded, value.shape[-1])
 
-    state = start_clips.astype(F32)
-    upstream = spread_in(cotangent.astype(BF)).astype(F32) * valid_here
+    gathered = [dict() for _ in range(LAYERS)]
+    feed1 = Feed(grid, block_triple(0, 0), wide_t[:1]).near().far()
+    gathered[0]["triple_t"] = feed1.done()[0]
+    feed2 = Feed(grid, block_out(0) + block_s(0), wide_t[1:] + wide_s, *feed1.near_parts())
+    state = spread_in(video_clips).astype(F32)
+
+    def corner(value):
+        return value[(slice(0, 1),) * (value.ndim - 2) + (slice(0, 8), slice(0, 128))]
     stored = []
     squares = []
     for layer in range(LAYERS):
@@ -556,7 +748,20 @@
         qkv_t = cube(
             (dot_nn(rows(normed_t), w["triple_t"]) + triple_bias(entry_bias[layer, 0])).astype(BF)
         )
+        if layer == 0:
+            feed2.near(*feed1.far_parts(), corner(normed_t)).far(corner(qkv_t))
+            merge_t, mix, triple_s, merge_s = feed2.done()
+            w.update(out_weights(merge_t, mix))
+            w.update(triple_s=with_other(triple_s), merge_s=with_other(merge_s))
+            feed3 = Feed(grid, block_m(0), wide_m, corner(qkv_t))
         mixed = temporal_call([qkv_t], split, scale, False)
+        if layer == 0:
+            feed3.near(*feed2.far_parts(), corner(mixed))
+        elif layer == 1:
+            feed5.far(corner(mixed))
+            triple_s, merge_s, upward, downward = feed5.done()
+            w.update(triple_s=with_other(triple_s), merge_s=with_other(merge_s))
+            w.update(up=with_other(upward), down=with_other(downward))
         mine = mixed[:frames_here]
         swap = grid.over_t(mixed[frames_here:])
         joined = (
@@ -573,7 +778,16 @@
             )
             for i in range(2)
         ]
+        if layer == 0:
+            upward, downward = feed3.far(corner(qkv_s[0])).done()
+            w.update(up=with_other(upward), down=with_other(downward))
+            feed4 = Feed(grid, block_triple(1, 0) + block_out(1), wide_t, corner(joined))
         mixed_s = spatial_call(count_ref, qkv_s, (split, split), places, scale, False)
+        if layer == 0:
+            feed4.near(*feed3.far_parts(), corner(mixed_s[0]))
+            feed5 = Feed(grid, block_s(1) + block_m(1), wide_s + wide_m, corner(mixed_s[0]))
+            late_cotangent = tie(cotangent, corner(mixed_s[0]))
+            upstream = spread_in(late_cotangent.astype(BF)).astype(F32) * valid_here
         spatial = cube(
             dot_nt(rows(mixed_s[0]), w["merge_s"][0])
             + dot_nt(rows(mixed_s[1]), w["merge_s"][1])
@@ -589,6 +803,10 @@
             slope.append(
                 (below + hidden * gauss_scale * jnp.exp(-0.5 * hidden * hidden)).astype(BF)
             )
+        if layer == 0:
+            triple_t, merge_t, mix = feed4.far(corner(active[0])).done()
+            gathered[1].update(triple_t=triple_t, **out_weights(merge_t, mix))
+            feed5.near(*feed4.far_parts(), corner(active[1]))
         dense = cube(
             dot_nt(active[0], w["down"][0]) + dot_nt(active[1], w["down"][1]) + bias[3]
         )
@@ -623,75 +841,116 @@
         )
     block_output = spread_out(state.astype(BF))
 
-    whole_sums = [None] * LAYERS
-    half_sums = [None] * LAYERS
     shards = [None] * LAYERS
-
-    def join_halves(mine, theirs):
-        return (mine + grid.over_t(theirs.astype(BF)).astype(F32)).astype(BF)
+    whole_early, half_early = [], []
+    sums = {}
+
+    def add_up(wholes, halves):
+        whole = jnp.concatenate(wholes)
+        whole = whole + grid.over_t(whole)
+        return grid.total(jnp.concatenate([whole] + halves), False)
+
+    def join(make):
+        got = grid.over_t(make(1).astype(BF))
+        return (make(0) + got.astype(F32)).astype(BF)
 
     for layer in range(LAYERS - 1, -1, -1):
         w, kept = gathered[layer], stored[layer]
         gain = norm_gain[layer]
         r = rows(upstream).astype(BF)
         down_bias_part = row_total(r)
+        back_active = [dot_nn(r, w["down"][i]) for i in range(2)]
         back_hidden = [
-            (dot_nn(r, w["down"][i]) * kept["slope"][i].astype(F32)).astype(BF) for i in range(2)
+            (back_active[i] * kept["slope"][i].astype(F32)).astype(BF) for i in range(2)
         ]
-        down_part = join_halves(*[dot_tn(r, kept["active"][i]) for i in range(2)])
-        up_part = join_halves(
-            *[dot_tn(rows(kept["normed_m"]), back_hidden[i]) for i in range(2)]
-        )
         hidden_part = [row_total(back_hidden[i]) for i in range(2)]
-        back_normed = cube(
-            dot_nt(back_hidden[0], w["up"][0]) + dot_nt(back_hidden[1], w["up"][1])
-        )
+        back_sides = [dot_nt(back_hidden[i], w["up"][i]) for i in range(2)]
+        back_normed = cube(back_sides[0] + back_sides[1])
         back_state, gain_m, shift_m = norm_backward(
             back_normed, kept["unit_m"], kept["scale_m"], gain[2]
         )
         upstream = upstream + back_state
-        r = rows(upstream).astype(BF)
+        parts_m = [
+            join(lambda i: dot_tn(rows(kept["normed_m"]), back_hidden[i])),
+            join(lambda i: dot_tn(r, kept["active"][i])),
+        ]
+        rs = rows(upstream).astype(BF)
+        r = rs
         spatial_bias_part = row_total(r)
-        merge_s_part = join_halves(*[dot_tn(r, rows(kept["mixed_s"][i])) for i in range(2)])
         back_mixed = [cube(dot_nn(r, w["merge_s"][i]).astype(BF)) for i in range(2)]
-        back_qkv = spatial_call(
-            count_ref,
-            list(kept["qkv_s"]) + back_mixed,
-            (3 * split, 3 * split),
-            places,
-            scale,
-            True,
-        )
-        triple_s_part = join_halves(
-            *[dot_tn(rows(kept["normed_s"]), rows(back_qkv[i])) for i in range(2)]
-        )
+        spatial_ins = list(kept["qkv_s"]) + back_mixed
+        if grid.direct:
+            back_qkv, sums["m", layer] = sum_rows(
+                grid,
+                layer,
+                parts_m,
+                functools.partial(spatial_back_payload, places, scale),
+                [count_ref] + spatial_ins,
+                [jax.ShapeDtypeStruct(item.shape, BF) for item in kept["qkv_s"]],
+                1,
+            )
+        else:
+            back_qkv = spatial_call(
+                count_ref, spatial_ins, (3 * split, 3 * split), places, scale, True
+            )
+            sums["m", layer] = plain_sums(parts_m)
         qkv_sums = [row_total(back_qkv[i]) for i in range(2)]
         entry_s_part = [jnp.stack([q[:split], q[2 * split :]]) for q in qkv_sums]
-        back_normed = cube(
-            dot_nt(rows(back_qkv[0]), w["triple_s"][0])
-            + dot_nt(rows(back_qkv[1]), w["triple_s"][1])
-        )
+        back_sides = [dot_nt(rows(back_qkv[i]), w["triple_s"][i]) for i in range(2)]
+        back_normed = cube(back_sides[0] + back_sides[1])
         back_state, gain_s, shift_s = norm_backward(
             back_normed, kept["unit_s"], kept["scale_s"], gain[1]
         )
         upstream = upstream + back_state
+        parts_s = [
+            join(lambda i: dot_tn(rows(kept["normed_s"]), rows(back_qkv[i]))),
+            join(lambda i: dot_tn(rs, rows(kept["mixed_s"][i]))),
+        ]
+        theirs = jnp.concatenate([entry_s_part[1].reshape(-1), hidden_part[1]])
+        mine = jnp.concatenate([entry_s_part[0].reshape(-1), hidden_part[0]])
+        half_early.append(mine + grid.over_t(theirs))
+        whole_early.append(
+            jnp.concatenate(
+                [gain_s, gain_m, shift_s, shift_m, spatial_bias_part, down_bias_part]
+                + [squares[layer], jnp.zeros((124,), F32)]
+            )
+        )
         r = rows(upstream).astype(BF)
         mixing_bias_part = row_total(r)
-        mixing_part = dot_tn(kept["joined"], r).reshape(-1, 2, half_rows, width)
-        mix_mine = lax.dynamic_index_in_dim(mixing_part, grid.t, 1, keepdims=False)
-        mix_theirs = lax.dynamic_index_in_dim(mixing_part, 1 - grid.t, 1, keepdims=False)
-        mixing_part = pack_mix(join_halves(mix_mine, mix_theirs)).reshape(width, width // 2)
         back_joined = dot_nt(r, w["mixing"]).astype(BF)
         merge_bias_part = row_total(back_joined)
-        merge_t_part = join_halves(
-            *[dot_tn(back_joined, rows(kept["mixed_t"][i])) for i in range(2)]
-        )
         back_mine, back_away = [
             cube(dot_nn(back_joined, w["merge_t"][i]).astype(BF)) for i in range(2)
         ]
         back_mixed = jnp.concatenate([back_mine, grid.over_t(back_away)], axis=0)
-        back_qkv = temporal_call([kept["qkv_t"], back_mixed], 3 * split, scale, True)
-        triple_t_part = dot_tn(rows(kept["normed_t"]), rows(back_qkv)).astype(BF)
+        mix_part = dot_tn(kept["joined"], r).reshape(-1, 2, half_rows, width)
+
+        def mix_half(i, mix_part=mix_part):
+            chosen = grid.t if i == 0 else 1 - grid.t
+            half = lax.dynamic_index_in_dim(mix_part, chosen, 1, keepdims=False)
+            return pack_mix(half).reshape(width, width // 2)
+
+        parts_o = [
+            join(lambda i: dot_tn(back_joined, rows(kept["mixed_t"][i]))),
+            join(mix_half),
+        ]
+        if grid.direct:
+            (back_qkv,), sums["s", layer] = sum_rows(
+                grid,
+                2 + layer,
+                parts_s,
+                functools.partial(temporal_back_payload, scale),
+                [kept["qkv_t"], back_mixed],
+                [jax.ShapeDtypeStruct(kept["qkv_t"].shape, BF)],
+            )
+        else:
+            back_qkv = temporal_call([kept["qkv_t"], back_mixed], 3 * split, scale, True)
+            sums["s", layer] = plain_sums(parts_s)
+        parts_t = [dot_tn(rows(kept["normed_t"]), rows(back_qkv)).astype(BF)] + parts_o
+        if grid.direct:
+            sums["t", layer] = sum_rows(grid, 4 + layer, parts_t)[1]
+        else:
+            sums["t", layer] = plain_sums(parts_t)
         qkv_sum = row_total(back_qkv)
         entry_t_part = jnp.stack([qkv_sum[:split], qkv_sum[2 * split :]])
         back_own = dot_nt(rows(back_qkv[:frames_here]), w["triple_t"])
@@ -701,50 +960,66 @@
             back_normed, kept["unit_t"], kept["scale_t"], gain[0]
         )
         upstream = upstream + back_state
-
-        parts_t = [triple_t_part, merge_t_part, mixing_part]
-        parts_sm = [triple_s_part, merge_s_part, up_part, down_part]
-        if layer == 0:
-            late = scatter_rows(grid, parts_sm)
-            early = scatter_rows(grid, parts_t)
-            shards[layer] = split_columns(early, wide_t) + split_columns(late, wide_s + wide_m)
+        late_whole = jnp.concatenate([gain_t, shift_t, merge_bias_part, mixing_bias_part])
+        late_half = entry_t_part.reshape(-1)
+        if layer > 0:
+            whole_early.append(late_whole)
+            half_early.append(late_half)
         else:
-            shards[layer] = split_columns(
-                scatter_rows(grid, parts_t + parts_sm), wide_t + wide_s + wide_m
-            )
-        whole_sums[layer] = jnp.concatenate(
-            [
-                gain_t,
-                gain_s,
-                gain_m,
-                shift_t,
-                shift_s,
-                shift_m,
-                merge_bias_part,
-                mixing_bias_part,
-                spatial_bias_part,
-                down_bias_part,
-                squares[layer],
-            ]
-        )
-        theirs = jnp.concatenate([entry_s_part[1].reshape(-1), hidden_part[1]])
-        mine = jnp.concatenate([entry_s_part[0].reshape(-1), hidden_part[0]])
-        half_sums[layer] = jnp.concatenate(
-            [entry_t_part.reshape(-1), mine + grid.over_t(theirs)]
-        )
+            early = add_up(whole_early, half_early)
+            late = add_up([late_whole], [late_half])
 
     input_grad = spread_out(upstream.astype(BF)).astype(F32)
-    whole = jnp.stack(whole_sums)
-    halves = jnp.stack(half_sums)
-    whole = whole + grid.over_t(whole)
-    both = grid.total(jnp.concatenate([whole, halves], axis=1), False)
-    whole, halves = both[:, : whole.shape[1]], both[:, whole.shape[1] :]
-    gain_sum = whole[:, : 3 * width].reshape(LAYERS, 3, width)
-    shift_sum = whole[:, 3 * width : 6 * width].reshape(LAYERS, 3, width)
-    bias_sum = whole[:, 6 * width : 10 * width].reshape(LAYERS, 4, width)
-    square_sum = whole[:, 10 * width :]
-    entry_sum = halves[:, : 4 * split].reshape(LAYERS, 2, 2, split)
-    hidden_sum = halves[:, 4 * split :]
+    for layer in range(LAYERS):
+        shards[layer] = [
+            *sums["t", layer],
+            *sums["s", layer],
+            *sums["m", layer],
+        ]
+    size_s = 6 * width + 128
+    tail_t = 4 * width
+    size_h = 2 * split + hid
+    gains, shifts, biases, square_sums, entries, hiddens = [], [], [], [], [], []
+    start = 0
+    tails = []
+    wholes = []
+    for layer in range(LAYERS - 1, -1, -1):
+        wholes.insert(0, early[start : start + size_s])
+        start += size_s
+        if layer > 0:
+            tails.insert(0, early[start : start + tail_t])
+            start += tail_t
+    tails.insert(0, late[:tail_t])
+    half_parts, half_tails = [], []
+    for layer in range(LAYERS - 1, -1, -1):
+        half_parts.insert(0, early[start : start + size_h])
+        start += size_h
+        if layer > 0:
+            half_tails.insert(0, early[start : start + 2 * split])
+            start += 2 * split
+    half_tails.insert(0, late[tail_t:])
+    for layer in range(LAYERS):
+        six = wholes[layer][: 6 * width].reshape(6, width)
+        four = tails[layer].reshape(4, width)
+        gains.append(jnp.stack([four[0], six[0], six[1]]))
+        shifts.append(jnp.stack([four[1], six[2], six[3]]))
+        biases.append(jnp.stack([four[2], four[3], six[4], six[5]]))
+        square_sums.append(wholes[layer][6 * width : 6 * width + 4])
+        entries.append(
+            jnp.stack(
+                [
+                    half_tails[layer].reshape(2, split),
+                    half_parts[layer][: 2 * split].reshape(2, split),
+                ]
+            )
+        )
+        hiddens.append(half_parts[layer][2 * split :])
+    gain_sum, shift_sum, bias_sum = jnp.stack(gains), jnp.stack(shifts), jnp.stack(biases)
+    square_sum, entry_sum, hidden_sum = (
+        jnp.stack(square_sums),
+        jnp.stack(entries),
+        jnp.stack(hiddens),
+    )
     tokens = FRAMES * width * jnp.sum(valid_places).astype(F32)
     root_squares = jnp.sqrt(square_sum / tokens)
 

time: 1010 us -> 1030 us (1.020)
  Pallas kernels: 123 us -> 347 us
  waiting for transfers between devices: 262 us -> 113 us
  local copies, waits for them, and re-layouts: 121 us -> 95.2 us
  starting transfers between devices: 99.9 us -> 77.3 us
    pallas_call x3 -> x11, Pallas kernels: 20.7 us -> 307 us  [the longest x6 289 us: sum_rows(): pl.pallas_call(functools.partial(sum_body, depth, len(ins), len(parts), l...]
    ppermute x90 -> x88, waiting for transfers between devices: 262 us -> 113 us  [send(): return lax.ppermute(value, AXES, pairs)]
    pallas_call x4 -> x2, Pallas kernels: 47.6 us -> 16.2 us  [spatial_call(): pl.pallas_call(functools.partial(body, places, scale), grid=(frames,), in...]
    pallas_call x4 -> x2, Pallas kernels: 54.7 us -> 23.7 us  [temporal_call(): pl.pallas_call(functools.partial(body, scale), grid=(padded // tile,), in...]
    ppermute x90 -> x88, starting transfers between devices: 99.9 us -> 77.3 us  [send(): return lax.ppermute(value, AXES, pairs)]
    unnamed x566 -> x557, local copies, waits for them, and re-layouts: 41.7 us -> 31.5 us
  transfers between devices with their start and end apart: 90 -> 88, of which waited for: 29 -> 25; matrix products, arithmetic and copies ran while one was open for 39% -> 35% of each run, Pallas kernels for 11% -> 13%
where the time goes in v2:
time: 1030 us; the launch traced here: 1020 us
  Pallas kernels  347 us (34%)
  matrix products  273 us (27%)
  waiting for transfers between devices  113 us (11%)
  other arithmetic  104 us (10%)
  local copies, waits for them, and re-layouts  95.2 us (9%)
  starting transfers between devices  77.3 us (8%)
    pallas_call x6, Pallas kernels, sum_rows(): pl.pallas_call(functools.partial(sum_body, depth, len(ins), len(parts), l...  289 us
    ppermute x88, waiting for transfers between devices, send(): return lax.ppermute(value, AXES, pairs)  113 us
    dot_general x24, matrix products, dot_nn(): lax.dot_general(left, right, (((1,), (0,)), ((), ())), preferred_element_...  97.2 us
    dot_general x26, matrix products, dot_nt(): lax.dot_general(left, right, (((1,), (1,)), ((), ())), preferred_element_...  88.3 us
    dot_general x24, matrix products, dot_tn(): lax.dot_general(left, right, (((0,), (0,)), ((), ())), preferred_element_...  87.8 us
    ppermute x88, starting transfers between devices, send(): return lax.ppermute(value, AXES, pairs)  77.3 us
    unnamed x557, local copies, waits for them, and re-layouts  31.5 us
    pallas_call x2, Pallas kernels, temporal_call(): pl.pallas_call(functools.partial(body, scale), grid=(padded // tile,), in...  23.7 us
  transfers between devices with their start and end apart: 88, of which 25 were waited for; matrix products, arithmetic and copies ran while one was open for 35% of the time, Pallas kernels for 13%

profile of v2, /device:TPU:0, one launch (start us, length us, event | category | flops | bytes accessed | tf_op | source)
XLA Modules:
  0.0 1015.5 jit_solution(5910613270679324417)
XLA Ops:
  31.1 9.7 collective-permute-done.6.xn
  52.8 7.1 collective-permute-done.11
  60.6 5.1 collective-permute-start.34
  77.6 9.6 collective-permute-done.14.yn
  89.9 5.0 fusion
  100.4 11.8 %temporal_mix.2 = bf16[8,208,384]{2,1,0:T(8,128)(2,1)} custom-call(bf16[8,208,1152]{2,1,0:T(8,128)(2,1)} %bitcast.519), custom_call_target="tpu_custom_call" | custom-call | flops 5234491392 | bytes 7667712 | tf_op jit(solution)/shard_map/temporal_mix/pallas_call | solution.py:203
  113.8 4.3 place_rows.6
  133.6 5.7 fusion.20
  139.4 9.2 collective-permute-done.27.yn
  154.9 4.8 fusion.21
  159.7 8.1 spatial_mix.2
  182.7 5.3 place_rows.7
  188.9 10.3 %collective-permute-done.56 = bf16[4,98,768]{2,0,1:T(4,128)(2,1)S(1)} collective-permute-done((bf16[4,98,768]{2,0,1:T(4,128)(2,1)S(1)}, bf16[4,98,768]{2,0,1:T(4,128)(2,1)S(1)}, u32[]{:S(2)}, u32[]{:S(2)}) %collective-permute-start.56) | collective-permute-done | bytes 602144 | tf_op jit(solution)/shard_map/ppermute | solution.py:240
  204.0 4.8 multiply_convert_fusion.7
  209.8 11.0 %collective-permute-done.44 = bf16[48,4608]{1,0:T(8,128)(2,1)S(1)} collective-permute-done((bf16[48,4608]{1,0:T(8,128)(2,1)}, bf16[48,4608]{1,0:T(8,128)(2,1)S(1)}, u32[]{:S(2)}, u32[]{:S(2)}) %collective-permute-start.44) | collective-permute-done | bytes 442400 | tf_op jit(solution)/shard_map/ppermute | solution.py:240
  224.5 4.2 collective-permute-done.39.db
  236.4 4.3 multiply_convert_fusion.6
  243.0 4.7 fusion.58
  250.1 6.9 add_convert_fusion.12
  275.2 5.0 fusion.1
  280.2 11.8 %temporal_mix.3 = bf16[8,208,384]{2,1,0:T(8,128)(2,1)} custom-call(bf16[8,208,1152]{2,1,0:T(8,128)(2,1)} %bitcast.521), custom_call_target="tpu_custom_call" | custom-call | flops 5234491392 | bytes 7667712 | tf_op jit(solution)/shard_map/temporal_mix/pallas_call | solution.py:203
  300.5 13.8 %collective-permute-done.49.db = bf16[2,48,4608]{2,1,0:T(8,128)(2,1)S(1)} collective-permute-done((bf16[2,48,4608]{2,1,0:T(8,128)(2,1)}, bf16[2,48,4608]{2,1,0:T(8,128)(2,1)S(1)}, u32[]{:S(2)}, u32[]{:S(2)}) %collective-permute-start.49) | collective-permute-done | bytes 884768 | tf_op jit(solution)/shard_map/ppermute | solution.py:240
  314.4 6.0 place_rows.9
  329.4 4.8 fusion.22
  334.2 4.8 fusion.23
  339.1 8.1 spatial_mix.3
  354.4 4.6 multiply_convert_fusion.5
  360.4 7.3 convert_reduce_fusion.5
  367.7 4.4 multiply_convert_fusion.4
  372.0 4.0 convolution_convert_fusion.2
  376.3 4.8 convert_reduce_fusion.4
  381.1 4.4 convolution_convert_fusion.3
  385.5 4.0 fusion.93
  396.2 5.4 fusion.94
  401.7 9.4 multiply_reduce_fusion.1
  429.8 6.4 collective-permute-done.55
  440.1 5.5 add_convert_fusion.2
  445.7 5.2 add_convert_fusion.3
  450.9 68.6 %sum_rows.6 = (bf16[4,208,1152]{2,1,0:T(8,128)(2,1)}, bf16[4,208,1152]{2,1,0:T(8,128)(2,1)}, f32[48,1536]{1,0:T(8,128)}, f32[48,1536]{1,0:T(8,128)}) custom-call(s32[1]{0:T(128)} %bitcast.33.count_ref.refs_0_, bf16[4,208,1152]{2,1,0:T(8,128)(2,1)} %bitcast.532, bf16[4,208,1152]{2,1,0:T(8,128)(2,1)} %bitcast.534, bf16[4,208,384]{2,1,0:T(8,128)(2,1)} %bitcast.539, ...), custom_call_target="tpu_custom_call" | custom-call | flops 20000000000 | bytes 50000000 | tf_op jit(solution)/shard_map/sum_rows/pallas_call | solution.py:521
  521.4 5.1 fusion.28
  530.1 5.9 multiply_reduce_fusion.12
  537.4 4.1 convert_reduce_fusion.12
  564.2 4.9 fusion.24
  569.1 39.4 %sum_rows.7 = (bf16[8,208,1152]{2,1,0:T(8,128)(2,1)}, f32[48,1152]{1,0:T(8,128)}, f32[48,384]{1,0:T(8,128)}) custom-call(bf16[8,208,1152]{2,1,0:T(8,128)(2,1)} %bitcast.522, bf16[8,208,384]{2,1,0:T(8,128)(2,1)} %pad_maximum_fusion.4.refs_1_, bf16[4,2,2,48,1152]{4,3,2,1,0:T(8,128)(2,1)} %bitcast.535, bf16[4,2,2,48,384]{4,3,2,1,0:T(8,128)(2,1)} %bitcast.544), custom_call_target="tpu_custom_call" | custom-call | flops 20000000000 | bytes 50000000 | tf_op jit(solution)/shard_map/sum_rows/pallas_call | solution.py:521
  615.3 6.7 fusion.27
  622.0 41.2 %sum_rows.11 = (f32[48,1152]{1,0:T(8,128)}, f32[48,384]{1,0:T(8,128)}, f32[48,384]{1,0:T(8,128)}) custom-call(bf16[4,2,2,48,1152]{4,3,2,1,0:T(8,128)(2,1)} %bitcast.537, bf16[4,2,2,48,384]{4,3,2,1,0:T(8,128)(2,1)} %bitcast.498, bf16[4,2,2,48,384]{4,3,2,1,0:T(8,128)(2,1)} %bitcast.496), custom_call_target="tpu_custom_call" | custom-call | flops 20000000000 | bytes 50000000 | tf_op jit(solution)/shard_map/sum_rows/pallas_call | solution.py:521
  666.7 6.1 multiply_reduce_fusion.6
  675.5 4.0 convolution_convert_fusion
  679.5 5.5 convert_reduce_fusion.2
  685.0 3.9 convolution_convert_fusion.1
  689.5 5.3 convert_reduce_fusion.3
  717.6 5.5 add_convert_fusion
  723.1 5.6 add_convert_fusion.1
  728.7 62.1 %sum_rows.8 = (bf16[4,208,1152]{2,1,0:T(8,128)(2,1)}, bf16[4,208,1152]{2,1,0:T(8,128)(2,1)}, f32[48,1536]{1,0:T(8,128)}, f32[48,1536]{1,0:T(8,128)}) custom-call(s32[1]{0:T(128)} %bitcast.33.count_ref.refs_0_, bf16[4,208,1152]{2,1,0:T(8,128)(2,1)} %bitcast.528, bf16[4,208,1152]{2,1,0:T(8,128)(2,1)} %bitcast.530, bf16[4,208,384]{2,1,0:T(8,128)(2,1)} %bitcast.541, ...), custom_call_target="tpu_custom_call" | custom-call | flops 20000000000 | bytes 50000000 | tf_op jit(solution)/shard_map/sum_rows/pallas_call | solution.py:521
  797.9 4.6 multiply_reduce_fusion.5
  814.1 5.7 concatenate.198
  822.8 4.9 fusion.29
  863.7 4.9 fusion.25
  868.6 34.6 %sum_rows.9 = (bf16[8,208,1152]{2,1,0:T(8,128)(2,1)}, f32[48,1152]{1,0:T(8,128)}, f32[48,384]{1,0:T(8,128)}) custom-call(bf16[8,208,1152]{2,1,0:T(8,128)(2,1)} %bitcast.520, bf16[8,208,384]{2,1,0:T(8,128)(2,1)} %pad_maximum_fusion.5.refs_1_, bf16[4,2,2,48,1152]{4,3,2,1,0:T(8,128)(2,1)} %bitcast.536, bf16[4,2,2,48,384]{4,3,2,1,0:T(8,128)(2,1)} %bitcast.543), custom_call_target="tpu_custom_call" | custom-call | flops 20000000000 | bytes 50000000 | tf_op jit(solution)/shard_map/sum_rows/pallas_call | solution.py:521
  910.0 4.9 fusion.26
  914.8 42.6 %sum_rows.10 = (f32[48,1152]{1,0:T(8,128)}, f32[48,384]{1,0:T(8,128)}, f32[48,384]{1,0:T(8,128)}) custom-call(bf16[4,2,2,48,1152]{4,3,2,1,0:T(8,128)(2,1)} %bitcast.538, bf16[4,2,2,48,384]{4,3,2,1,0:T(8,128)(2,1)} %bitcast.499, bf16[4,2,2,48,384]{4,3,2,1,0:T(8,128)(2,1)} %bitcast.497), custom_call_target="tpu_custom_call" | custom-call | flops 20000000000 | bytes 50000000 | tf_op jit(solution)/shard_map/sum_rows/pallas_call | solution.py:521
  966.0 6.0 multiply_reduce_fusion.13
  973.6 13.4 %add_convert_fusion.4 = bf16[4,208,768]{2,1,0:T(8,128)(2,1)S(1)} fusion(f32[4,208,768]{2,1,0:T(8,128)} %bitcast.457, f32[4,208,768]{2,1,0:T(8,128)} %bitcast.456, f32[4,208,768]{2,1,0:T(8,128)} %bitcast.455, f32[4,208,768]{2,1,0:T(8,128)} %bitcast.454, f32[4,208,768]{2,1,0:T(8,128)} %bitcast.453, f32[4,208,768]{2,1,0:T(8,128)} %bitcast.452, ...), kind=kLoop, calls=%fused_computation.101 | loop fusion | flops 41533440 | bytes 31900896 | tf_op jit(solution)/shard_map/convert_element_type | solution.py:972
  1004.5 7.9 collective-permute-done.71
  (1046 shorter events, 355.0 us)
Async XLA Ops:
  1.7 25.3 %collective-permute-start.3 = (bf16[48,1152]{1,0:T(8,128)(2,1)S(1)}, bf16[48,1152]{1,0:T(8,128)(2,1)}, u32[]{:S(2)}, u32[]{:S(2)}) collective-permute-start(bf16[48,1152]{1,0:T(8,128)(2,1)S(1)} %pad_maximum_fusion.26), channel_id=1, source_target_pairs={{0,8},{1,9},{2,10},{3,11},{4,12},{5,13},{6,14},{7,15},{8,16},{9,17... | collective-permute-start | bytes 331784 | tf_op jit(solution)/shard_map/ppermute | solution.py:240
  4.8 22.5 %collective-permute-start.4 = (bf16[48,1152]{1,0:T(8,128)(2,1)S(1)}, bf16[48,1152]{1,0:T(8,128)(2,1)}, u32[]{:S(2)}, u32[]{:S(2)}) collective-permute-start(bf16[48,1152]{1,0:T(8,128)(2,1)S(1)} %pad_maximum_fusion.26), channel_id=1, source_target_pairs={{0,16},{1,17},{2,18},{3,19},{4,20},{5,21},{6,22},{7,23},{8,24},{9,... | collective-permute-start | bytes 331784 | tf_op jit(solution)/shard_map/ppermute | solution.py:240
  7.3 19.9 %collective-permute-start.5 = (bf16[48,1152]{1,0:T(8,128)(2,1)S(1)}, bf16[48,1152]{1,0:T(8,128)(2,1)}, u32[]{:S(2)}, u32[]{:S(2)}) collective-permute-start(bf16[48,1152]{1,0:T(8,128)(2,1)S(1)} %pad_maximum_fusion.26), channel_id=1, source_target_pairs={{0,24},{1,25},{2,26},{3,27},{4,28},{5,29},{6,30},{7,31},{8,0},{9,1... | collective-permute-start | bytes 331784 | tf_op jit(solution)/shard_map/ppermute | solution.py:240
  10.4 15.5 %collective-permute-start = (bf16[4,98,768]{2,0,1:T(4,128)(2,1)S(1)}, bf16[4,98,768]{2,0,1:T(4,128)(2,1)S(1)}, u32[]{:S(2)}, u32[]{:S(2)}) collective-permute-start(bf16[4,98,768]{2,0,1:T(4,128)(2,1)S(1)} %get-tuple-element.282), channel_id=1, source_target_pairs={{0,2},{1,3},{2,0},{3,1},{4,6},{5,7},{6,4},{7,5},{8,10},{9,11},{10,... | collective-permute-start | bytes 1806344 | tf_op jit(solution)/shard_map/ppermute | solution.py:240
  12.6 54.9 %collective-permute-start.21 = (f32[4608]{0:T(1024)}, f32[4608]{0:T(1024)S(1)}, u32[]{:S(2)}, u32[]{:S(2)}) collective-permute-start(f32[4608]{0:T(1024)} %pad_maximum_fusion.37), channel_id=1, source_target_pairs={{0,1},{1,0},{2,3},{3,2},{4,5},{5,4},{6,7},{7,6},{8,9},{9,8},{10,11... | collective-permute-start | bytes 55304 | tf_op jit(solution)/shard_map/ppermute | solution.py:240
  25.9 42.3 %collective-permute-start.33 = (bf16[48,1920]{1,0:T(8,128)(2,1)}, bf16[48,1920]{1,0:T(8,128)(2,1)S(1)}, u32[]{:S(2)}, u32[]{:S(2)}) collective-permute-start(bf16[48,1920]{1,0:T(8,128)(2,1)} %maximum_dynamic-update-slice_fusion.1), channel_id=1, source_target_pairs={{0,8},{1,9},{2,10},{3,11},{4,12},{5,13},{6,14},{7,15},{8,16},{9,17... | collective-permute-start | bytes 552968 | tf_op jit(solution)/shard_map/ppermute | solution.py:240
  27.0 18.8 %collective-permute-start.1 = (bf16[4,98,768]{2,0,1:T(4,128)(2,1)S(1)}, bf16[4,98,768]{2,0,1:T(4,128)(2,1)S(1)}, u32[]{:S(2)}, u32[]{:S(2)}) collective-permute-start(bf16[4,98,768]{2,0,1:T(4,128)(2,1)S(1)} %copy.53), channel_id=1, source_target_pairs={{0,1},{1,0},{2,3},{3,2},{4,5},{5,4},{6,7},{7,6},{8,9},{9,8},{10,11... | collective-permute-start | bytes 1806344 | tf_op jit(solution)/shard_map/ppermute | solution.py:240
  28.3 12.4 %collective-permute-start.6 = (bf16[4,48,1152]{2,1,0:T(8,128)(2,1)S(1)}, bf16[4,48,1152]{2,1,0:T(8,128)(2,1)S(1)}, u32[]{:S(2)}, u32[]{:S(2)}) collective-permute-start(bf16[4,48,1152]{2,1,0:T(8,128)(2,1)S(1)} %pad_maximum_fusion.22.own), channel_id=1, source_target_pairs={{0,4},{1,5},{2,6},{3,7},{4,0},{5,1},{6,2},{7,3},{8,12},{9,13},{10,... | collective-permute-start | bytes 1327112 | tf_op jit(solution)/shard_map/ppermute | solution.py:240
  29.9 12.1 %collective-permute-start.7 = (bf16[4,48,1152]{2,1,0:T(8,128)(2,1)S(1)}, bf16[4,48,1152]{2,1,0:T(8,128)(2,1)S(1)}, u32[]{:S(2)}, u32[]{:S(2)}) collective-permute-start(bf16[4,48,1152]{2,1,0:T(8,128)(2,1)S(1)} %pad_maximum_fusion.22.own), channel_id=1, source_target_pairs={{0,2},{1,3},{2,0},{3,1},{4,6},{5,7},{6,4},{7,5},{8,10},{9,11},{10,... | collective-permute-start | bytes 1327112 | tf_op jit(solution)/shard_map/ppermute | solution.py:240
  42.0 10.2 %collective-permute-start.10 = (bf16[48,2304]{1,0:T(8,128)(2,1)S(1)}, bf16[48,2304]{1,0:T(8,128)(2,1)S(1)}, u32[]{:S(2)}, u32[]{:S(2)}) collective-permute-start(bf16[48,2304]{1,0:T(8,128)(2,1)S(1)} %get-tuple-element.66), channel_id=1, source_target_pairs={{0,8},{1,9},{2,10},{3,11},{4,12},{5,13},{6,14},{7,15},{8,16},{9,17... | collective-permute-start | bytes 663560 | tf_op jit(solution)/shard_map/ppermute | solution.py:240
  42.2 17.6 %collective-permute-start.11 = (bf16[48,2304]{1,0:T(8,128)(2,1)S(1)}, bf16[48,2304]{1,0:T(8,128)(2,1)S(1)}, u32[]{:S(2)}, u32[]{:S(2)}) collective-permute-start(bf16[48,2304]{1,0:T(8,128)(2,1)S(1)} %get-tuple-element.66), channel_id=1, source_target_pairs={{0,16},{1,17},{2,18},{3,19},{4,20},{5,21},{6,22},{7,23},{8,24},{9,... | collective-permute-start | bytes 663560 | tf_op jit(solution)/shard_map/ppermute | solution.py:240
  45.8 14.7 %collective-permute-start.12 = (bf16[48,2304]{1,0:T(8,128)(2,1)S(1)}, bf16[48,2304]{1,0:T(8,128)(2,1)S(1)}, u32[]{:S(2)}, u32[]{:S(2)}) collective-permute-start(bf16[48,2304]{1,0:T(8,128)(2,1)S(1)} %get-tuple-element.66), channel_id=1, source_target_pairs={{0,24},{1,25},{2,26},{3,27},{4,28},{5,29},{6,30},{7,31},{8,0},{9,1... | collective-permute-start | bytes 663560 | tf_op jit(solution)/shard_map/ppermute | solution.py:240
  60.4 28.4 %collective-permute-start.2 = (bf16[4,208,768]{2,1,0:T(8,128)(2,1)S(1)}, bf16[4,208,768]{2,1,0:T(8,128)(2,1)S(1)}, u32[]{:S(2)}, u32[]{:S(2)}) collective-permute-start(bf16[4,208,768]{2,1,0:T(8,128)(2,1)S(1)} %add_convert_fusion.16), channel_id=1, source_target_pairs={{0,1},{1,0},{2,3},{3,2},{4,5},{5,4},{6,7},{7,6},{8,9},{9,8},{10,11... | collective-permute-start | bytes 3833864 | tf_op jit(solution)/shard_map/ppermute | solution.py:240
  60.6 13.5 %collective-permute-start.34 = (bf16[48,1920]{1,0:T(8,128)(2,1)S(1)}, bf16[48,1920]{1,0:T(8,128)(2,1)S(1)}, u32[]{:S(2)}, u32[]{:S(2)}) collective-permute-start(bf16[48,1920]{1,0:T(8,128)(2,1)S(1)} %copy-done.111), channel_id=1, source_target_pairs={{0,16},{1,17},{2,18},{3,19},{4,20},{5,21},{6,22},{7,23},{8,24},{9,... | collective-permute-start | bytes 552968 | tf_op jit(solution)/shard_map/ppermute | solution.py:240
  66.9 20.4 %collective-permute-start.14 = (bf16[4,48,2304]{2,1,0:T(8,128)(2,1)S(1)}, bf16[4,48,2304]{2,1,0:T(8,128)(2,1)S(1)}, u32[]{:S(2)}, u32[]{:S(2)}) collective-permute-start(bf16[4,48,2304]{2,1,0:T(8,128)(2,1)S(1)} %pad_maximum_fusion.12.own), channel_id=1, source_target_pairs={{0,2},{1,3},{2,0},{3,1},{4,6},{5,7},{6,4},{7,5},{8,10},{9,11},{10,... | collective-permute-start | bytes 2654216 | tf_op jit(solution)/shard_map/ppermute | solution.py:240
  67.5 20.5 %collective-permute-start.13 = (bf16[4,48,2304]{2,1,0:T(8,128)(2,1)S(1)}, bf16[4,48,2304]{2,1,0:T(8,128)(2,1)S(1)}, u32[]{:S(2)}, u32[]{:S(2)}) collective-permute-start(bf16[4,48,2304]{2,1,0:T(8,128)(2,1)S(1)} %pad_maximum_fusion.12.own), channel_id=1, source_target_pairs={{0,4},{1,5},{2,6},{3,7},{4,0},{5,1},{6,2},{7,3},{8,12},{9,13},{10,... | collective-permute-start | bytes 2654216 | tf_op jit(solution)/shard_map/ppermute | solution.py:240
  94.9 23.7 %collective-permute-start.23 = (bf16[48,3072]{1,0:T(8,128)(2,1)}, bf16[48,3072]{1,0:T(8,128)(2,1)}, u32[]{:S(2)}, u32[]{:S(2)}) collective-permute-start(bf16[48,3072]{1,0:T(8,128)(2,1)} %pad_maximum_fusion.23), channel_id=1, source_target_pairs={{0,8},{1,9},{2,10},{3,11},{4,12},{5,13},{6,14},{7,15},{8,16},{9,17... | collective-permute-start | bytes 884744 | tf_op jit(solution)/shard_map/ppermute | solution.py:240
  94.9 23.7 %collective-permute-start.24 = (bf16[48,3072]{1,0:T(8,128)(2,1)}, bf16[48,3072]{1,0:T(8,128)(2,1)}, u32[]{:S(2)}, u32[]{:S(2)}) collective-permute-start(bf16[48,3072]{1,0:T(8,128)(2,1)} %pad_maximum_fusion.23), channel_id=1, source_target_pairs={{0,16},{1,17},{2,18},{3,19},{4,20},{5,21},{6,22},{7,23},{8,24},{9,... | collective-permute-start | bytes 884744 | tf_op jit(solution)/shard_map/ppermute | solution.py:240
  97.5 21.2 %collective-permute-start.25 = (bf16[48,3072]{1,0:T(8,128)(2,1)}, bf16[48,3072]{1,0:T(8,128)(2,1)}, u32[]{:S(2)}, u32[]{:S(2)}) collective-permute-start(bf16[48,3072]{1,0:T(8,128)(2,1)} %pad_maximum_fusion.23), channel_id=1, source_target_pairs={{0,24},{1,25},{2,26},{3,27},{4,28},{5,29},{6,30},{7,31},{8,0},{9,1... | collective-permute-start | bytes 884744 | tf_op jit(solution)/shard_map/ppermute | solution.py:240
  98.9 14.8 %collective-permute-start.16 = (bf16[2,48,2304]{2,1,0:T(8,128)(2,1)}, bf16[2,48,2304]{2,1,0:T(8,128)(2,1)}, u32[]{:S(2)}, u32[]{:S(2)}) collective-permute-start(bf16[2,48,2304]{2,1,0:T(8,128)(2,1)} %slice.843), channel_id=1, source_target_pairs={{0,4},{1,5},{2,6},{3,7},{4,0},{5,1},{6,2},{7,3},{8,12},{9,13},{10,... | collective-permute-start | bytes 1327112 | tf_op jit(solution)/shard_map/ppermute | solution.py:240
  99.5 14.3 %collective-permute-start.15 = (bf16[2,48,2304]{2,1,0:T(8,128)(2,1)}, bf16[2,48,2304]{2,1,0:T(8,128)(2,1)}, u32[]{:S(2)}, u32[]{:S(2)}) collective-permute-start(bf16[2,48,2304]{2,1,0:T(8,128)(2,1)} %slice.841), channel_id=1, source_target_pairs={{0,2},{1,3},{2,0},{3,1},{4,6},{5,7},{6,4},{7,5},{8,10},{9,11},{10,... | collective-permute-start | bytes 1327112 | tf_op jit(solution)/shard_map/ppermute | solution.py:240
  120.0 28.5 %collective-permute-start.27 = (bf16[4,48,3072]{2,1,0:T(8,128)(2,1)S(1)}, bf16[4,48,3072]{2,1,0:T(8,128)(2,1)}, u32[]{:S(2)}, u32[]{:S(2)}) collective-permute-start(bf16[4,48,3072]{2,1,0:T(8,128)(2,1)S(1)} %pad_maximum_fusion.7.own), channel_id=1, source_target_pairs={{0,2},{1,3},{2,0},{3,1},{4,6},{5,7},{6,4},{7,5},{8,10},{9,11},{10,... | collective-permute-start | bytes 3538952 | tf_op jit(solution)/shard_map/ppermute | solution.py:240
  121.2 30.7 %collective-permute-start.26 = (bf16[4,48,3072]{2,1,0:T(8,128)(2,1)S(1)}, bf16[4,48,3072]{2,1,0:T(8,128)(2,1)}, u32[]{:S(2)}, u32[]{:S(2)}) collective-permute-start(bf16[4,48,3072]{2,1,0:T(8,128)(2,1)S(1)} %pad_maximum_fusion.7.own), channel_id=1, source_target_pairs={{0,4},{1,5},{2,6},{3,7},{4,0},{5,1},{6,2},{7,3},{8,12},{9,13},{10,... | collective-permute-start | bytes 3538952 | tf_op jit(solution)/shard_map/ppermute | solution.py:240
  122.7 32.2 %collective-permute-start.20 = (bf16[768,1152]{1,0:T(8,128)(2,1)}, bf16[768,1152]{1,0:T(8,128)(2,1)}, u32[]{:S(2)}, u32[]{:S(2)}) collective-permute-start(bf16[768,1152]{1,0:T(8,128)(2,1)} %get-tuple-element.72), channel_id=1, source_target_pairs={{0,1},{1,0},{2,3},{3,2},{4,5},{5,4},{6,7},{7,6},{8,9},{9,8},{10,11... | collective-permute-start | bytes 5308424 | tf_op jit(solution)/shard_map/ppermute | solution.py:240
  122.8 54.3 %collective-permute-start.22 = (bf16[768,384]{1,0:T(8,128)(2,1)}, bf16[768,384]{1,0:T(8,128)(2,1)}, u32[]{:S(2)}, u32[]{:S(2)}) collective-permute-start(bf16[768,384]{1,0:T(8,128)(2,1)} %get-tuple-element.74), channel_id=1, source_target_pairs={{0,1},{1,0},{2,3},{3,2},{4,5},{5,4},{6,7},{7,6},{8,9},{9,8},{10,11... | collective-permute-start | bytes 1769480 | tf_op jit(solution)/shard_map/ppermute | solution.py:240
  150.5 17.4 %collective-permute-start.29 = (bf16[2,48,3072]{2,1,0:T(8,128)(2,1)}, bf16[2,48,3072]{2,1,0:T(8,128)(2,1)S(1)}, u32[]{:S(2)}, u32[]{:S(2)}) collective-permute-start(bf16[2,48,3072]{2,1,0:T(8,128)(2,1)} %slice.853), channel_id=1, source_target_pairs={{0,4},{1,5},{2,6},{3,7},{4,0},{5,1},{6,2},{7,3},{8,12},{9,13},{10,... | collective-permute-start | bytes 1769480 | tf_op jit(solution)/shard_map/ppermute | solution.py:240
  153.8 14.8 %collective-permute-start.28 = (bf16[2,48,3072]{2,1,0:T(8,128)(2,1)}, bf16[2,48,3072]{2,1,0:T(8,128)(2,1)S(1)}, u32[]{:S(2)}, u32[]{:S(2)}) collective-permute-start(bf16[2,48,3072]{2,1,0:T(8,128)(2,1)} %slice.851), channel_id=1, source_target_pairs={{0,2},{1,3},{2,0},{3,1},{4,6},{5,7},{6,4},{7,5},{8,10},{9,11},{10,... | collective-permute-start | bytes 1769480 | tf_op jit(solution)/shard_map/ppermute | solution.py:240
  169.4 31.2 %collective-permute-start.37 = (bf16[4,48,1920]{2,1,0:T(8,128)(2,1)S(1)}, bf16[4,48,1920]{2,1,0:T(8,128)(2,1)S(1)}, u32[]{:S(2)}, u32[]{:S(2)}) collective-permute-start(bf16[4,48,1920]{2,1,0:T(8,128)(2,1)S(1)} %pad_maximum_fusion.13.own), channel_id=1, source_target_pairs={{0,2},{1,3},{2,0},{3,1},{4,6},{5,7},{6,4},{7,5},{8,10},{9,11},{10,... | collective-permute-start | bytes 2211848 | tf_op jit(solution)/shard_map/ppermute | solution.py:240
  170.5 33.4 %collective-permute-start.36 = (bf16[4,48,1920]{2,1,0:T(8,128)(2,1)S(1)}, bf16[4,48,1920]{2,1,0:T(8,128)(2,1)S(1)}, u32[]{:S(2)}, u32[]{:S(2)}) collective-permute-start(bf16[4,48,1920]{2,1,0:T(8,128)(2,1)S(1)} %pad_maximum_fusion.13.own), channel_id=1, source_target_pairs={{0,4},{1,5},{2,6},{3,7},{4,0},{5,1},{6,2},{7,3},{8,12},{9,13},{10,... | collective-permute-start | bytes 2211848 | tf_op jit(solution)/shard_map/ppermute | solution.py:240
  173.7 25.5 %collective-permute-start.56 = (bf16[4,98,768]{2,0,1:T(4,128)(2,1)S(1)}, bf16[4,98,768]{2,0,1:T(4,128)(2,1)S(1)}, u32[]{:S(2)}, u32[]{:S(2)}) collective-permute-start(bf16[4,98,768]{2,0,1:T(4,128)(2,1)S(1)} %get-tuple-element.280), channel_id=1, source_target_pairs={{0,2},{1,3},{2,0},{3,1},{4,6},{5,7},{6,4},{7,5},{8,10},{9,11},{10,... | collective-permute-start | bytes 1806344 | tf_op jit(solution)/shard_map/ppermute | solution.py:240
  174.7 34.6 %collective-permute-start.43 = (bf16[48,4608]{1,0:T(8,128)(2,1)}, bf16[48,4608]{1,0:T(8,128)(2,1)}, u32[]{:S(2)}, u32[]{:S(2)}) collective-permute-start(bf16[48,4608]{1,0:T(8,128)(2,1)} %bitcast_dynamic-update-slice_fusion), channel_id=1, source_target_pairs={{0,8},{1,9},{2,10},{3,11},{4,12},{5,13},{6,14},{7,15},{8,16},{9,17... | collective-permute-start | bytes 1327112 | tf_op jit(solution)/shard_map/ppermute | solution.py:240
  187.9 48.4 %collective-permute-start.30 = (bf16[768,1536]{1,0:T(8,128)(2,1)}, bf16[768,1536]{1,0:T(8,128)(2,1)S(1)}, u32[]{:S(2)}, u32[]{:S(2)}) collective-permute-start(bf16[768,1536]{1,0:T(8,128)(2,1)} %get-tuple-element.80), channel_id=1, source_target_pairs={{0,1},{1,0},{2,3},{3,2},{4,5},{5,4},{6,7},{7,6},{8,9},{9,8},{10,11... | collective-permute-start | bytes 7077896 | tf_op jit(solution)/shard_map/ppermute | solution.py:240
  199.2 21.6 %collective-permute-start.44 = (bf16[48,4608]{1,0:T(8,128)(2,1)}, bf16[48,4608]{1,0:T(8,128)(2,1)S(1)}, u32[]{:S(2)}, u32[]{:S(2)}) collective-permute-start(bf16[48,4608]{1,0:T(8,128)(2,1)} %bitcast_dynamic-update-slice_fusion), channel_id=1, source_target_pairs={{0,16},{1,17},{2,18},{3,19},{4,20},{5,21},{6,22},{7,23},{8,24},{9,... | collective-permute-start | bytes 1327112 | tf_op jit(solution)/shard_map/ppermute | solution.py:240
  200.6 21.0 %collective-permute-start.45 = (bf16[48,4608]{1,0:T(8,128)(2,1)}, bf16[48,4608]{1,0:T(8,128)(2,1)S(1)}, u32[]{:S(2)}, u32[]{:S(2)}) collective-permute-start(bf16[48,4608]{1,0:T(8,128)(2,1)} %bitcast_dynamic-update-slice_fusion), channel_id=1, source_target_pairs={{0,24},{1,25},{2,26},{3,27},{4,28},{5,29},{6,30},{7,31},{8,0},{9,1... | collective-permute-start | bytes 1327112 | tf_op jit(solution)/shard_map/ppermute | solution.py:240
  203.9 36.9 %collective-permute-start.31 = (bf16[768,1536]{1,0:T(8,128)(2,1)S(1)}, bf16[768,1536]{1,0:T(8,128)(2,1)S(1)}, u32[]{:S(2)}, u32[]{:S(2)}) collective-permute-start(bf16[768,1536]{1,0:T(8,128)(2,1)S(1)} %copy-done.247), channel_id=1, source_target_pairs={{0,1},{1,0},{2,3},{3,2},{4,5},{5,4},{6,7},{7,6},{8,9},{9,8},{10,11... | collective-permute-start | bytes 7077896 | tf_op jit(solution)/shard_map/ppermute | solution.py:240
  209.3 25.8 %collective-permute-start.57 = (bf16[4,98,768]{2,0,1:T(4,128)(2,1)S(1)}, bf16[4,98,768]{2,0,1:T(4,128)(2,1)S(1)}, u32[]{:S(2)}, u32[]{:S(2)}) collective-permute-start(bf16[4,98,768]{2,0,1:T(4,128)(2,1)S(1)} %copy.65), channel_id=1, source_target_pairs={{0,1},{1,0},{2,3},{3,2},{4,5},{5,4},{6,7},{7,6},{8,9},{9,8},{10,11... | collective-permute-start | bytes 1806344 | tf_op jit(solution)/shard_map/ppermute | solution.py:240
  230.1 38.8 %collective-permute-start.47 = (bf16[4,48,4608]{2,1,0:T(8,128)(2,1)S(1)}, bf16[4,48,4608]{2,1,0:T(8,128)(2,1)}, u32[]{:S(2)}, u32[]{:S(2)}) collective-permute-start(bf16[4,48,4608]{2,1,0:T(8,128)(2,1)S(1)} %pad_maximum_fusion.2.own), channel_id=1, source_target_pairs={{0,2},{1,3},{2,0},{3,1},{4,6},{5,7},{6,4},{7,5},{8,10},{9,11},{10,... | collective-permute-start | bytes 5308424 | tf_op jit(solution)/shard_map/ppermute | solution.py:240
  232.5 38.6 %collective-permute-start.46 = (bf16[4,48,4608]{2,1,0:T(8,128)(2,1)S(1)}, bf16[4,48,4608]{2,1,0:T(8,128)(2,1)}, u32[]{:S(2)}, u32[]{:S(2)}) collective-permute-start(bf16[4,48,4608]{2,1,0:T(8,128)(2,1)S(1)} %pad_maximum_fusion.2.own), channel_id=1, source_target_pairs={{0,4},{1,5},{2,6},{3,7},{4,0},{5,1},{6,2},{7,3},{8,12},{9,13},{10,... | collective-permute-start | bytes 5308424 | tf_op jit(solution)/shard_map/ppermute | solution.py:240
  257.1 16.2 %collective-permute-start.32 = (bf16[4,208,768]{2,1,0:T(8,128)(2,1)}, bf16[4,208,768]{2,1,0:T(8,128)(2,1)}, u32[]{:S(2)}, u32[]{:S(2)}) collective-permute-start(bf16[4,208,768]{2,1,0:T(8,128)(2,1)} %get-tuple-element.252), channel_id=1, source_target_pairs={{0,1},{1,0},{2,3},{3,2},{4,5},{5,4},{6,7},{7,6},{8,9},{9,8},{10,11... | collective-permute-start | bytes 3833864 | tf_op jit(solution)/shard_map/ppermute | solution.py:240
  268.4 29.4 %collective-permute-start.42 = (bf16[768,384]{1,0:T(8,128)(2,1)}, bf16[768,384]{1,0:T(8,128)(2,1)S(1)}, u32[]{:S(2)}, u32[]{:S(2)}) collective-permute-start(bf16[768,384]{1,0:T(8,128)(2,1)} %get-tuple-element.87), channel_id=1, source_target_pairs={{0,1},{1,0},{2,3},{3,2},{4,5},{5,4},{6,7},{7,6},{8,9},{9,8},{10,11... | collective-permute-start | bytes 1769480 | tf_op jit(solution)/shard_map/ppermute | solution.py:240
  268.9 29.3 %collective-permute-start.41 = (bf16[768,384]{1,0:T(8,128)(2,1)}, bf16[768,384]{1,0:T(8,128)(2,1)}, u32[]{:S(2)}, u32[]{:S(2)}) collective-permute-start(bf16[768,384]{1,0:T(8,128)(2,1)} %get-tuple-element.86), channel_id=1, source_target_pairs={{0,1},{1,0},{2,3},{3,2},{4,5},{5,4},{6,7},{7,6},{8,9},{9,8},{10,11... | collective-permute-start | bytes 1769480 | tf_op jit(solution)/shard_map/ppermute | solution.py:240
  292.1 22.2 %collective-permute-start.49 = (bf16[2,48,4608]{2,1,0:T(8,128)(2,1)}, bf16[2,48,4608]{2,1,0:T(8,128)(2,1)S(1)}, u32[]{:S(2)}, u32[]{:S(2)}) collective-permute-start(bf16[2,48,4608]{2,1,0:T(8,128)(2,1)} %slice.868), channel_id=1, source_target_pairs={{0,4},{1,5},{2,6},{3,7},{4,0},{5,1},{6,2},{7,3},{8,12},{9,13},{10,... | collective-permute-start | bytes 2654216 | tf_op jit(solution)/shard_map/ppermute | solution.py:240
  292.1 22.3 %collective-permute-start.48 = (bf16[2,48,4608]{2,1,0:T(8,128)(2,1)}, bf16[2,48,4608]{2,1,0:T(8,128)(2,1)S(1)}, u32[]{:S(2)}, u32[]{:S(2)}) collective-permute-start(bf16[2,48,4608]{2,1,0:T(8,128)(2,1)} %slice.866), channel_id=1, source_target_pairs={{0,2},{1,3},{2,0},{3,1},{4,6},{5,7},{6,4},{7,5},{8,10},{9,11},{10,... | collective-permute-start | bytes 2654216 | tf_op jit(solution)/shard_map/ppermute | solution.py:240
  320.4 13.8 %collective-permute-start.50 = (bf16[768,1152]{1,0:T(8,128)(2,1)}, bf16[768,1152]{1,0:T(8,128)(2,1)}, u32[]{:S(2)}, u32[]{:S(2)}) collective-permute-start(bf16[768,1152]{1,0:T(8,128)(2,1)} %get-tuple-element.92), channel_id=1, source_target_pairs={{0,1},{1,0},{2,3},{3,2},{4,5},{5,4},{6,7},{7,6},{8,9},{9,8},{10,11... | collective-permute-start | bytes 5308424 | tf_op jit(solution)/shard_map/ppermute | solution.py:240
  328.6 18.6 %collective-permute-start.51 = (bf16[768,384]{1,0:T(8,128)(2,1)S(1)}, bf16[768,384]{1,0:T(8,128)(2,1)}, u32[]{:S(2)}, u32[]{:S(2)}) collective-permute-start(bf16[768,384]{1,0:T(8,128)(2,1)S(1)} %get-tuple-element.94), channel_id=1, source_target_pairs={{0,1},{1,0},{2,3},{3,2},{4,5},{5,4},{6,7},{7,6},{8,9},{9,8},{10,11... | collective-permute-start | bytes 1769480 | tf_op jit(solution)/shard_map/ppermute | solution.py:240
  328.9 38.8 %collective-permute-start.52 = (bf16[768,1536]{1,0:T(8,128)(2,1)}, bf16[768,1536]{1,0:T(8,128)(2,1)}, u32[]{:S(2)}, u32[]{:S(2)}) collective-permute-start(bf16[768,1536]{1,0:T(8,128)(2,1)} %get-tuple-element.96), channel_id=1, source_target_pairs={{0,1},{1,0},{2,3},{3,2},{4,5},{5,4},{6,7},{7,6},{8,9},{9,8},{10,11... | collective-permute-start | bytes 7077896 | tf_op jit(solution)/shard_map/ppermute | solution.py:240
  329.1 47.2 %collective-permute-start.53 = (bf16[768,1536]{1,0:T(8,128)(2,1)}, bf16[768,1536]{1,0:T(8,128)(2,1)}, u32[]{:S(2)}, u32[]{:S(2)}) collective-permute-start(bf16[768,1536]{1,0:T(8,128)(2,1)} %get-tuple-element.97), channel_id=1, source_target_pairs={{0,1},{1,0},{2,3},{3,2},{4,5},{5,4},{6,7},{7,6},{8,9},{9,8},{10,11... | collective-permute-start | bytes 7077896 | tf_op jit(solution)/shard_map/ppermute | solution.py:240
  376.0 63.2 %collective-permute-start.59 = (bf16[768,1536]{1,0:T(8,128)(2,1)}, bf16[768,1536]{1,0:T(8,128)(2,1)}, u32[]{:S(2)}, u32[]{:S(2)}) collective-permute-start(bf16[768,1536]{1,0:T(8,128)(2,1)} %convolution_convert_fusion.2), channel_id=1, source_target_pairs={{0,1},{1,0},{2,3},{3,2},{4,5},{5,4},{6,7},{7,6},{8,9},{9,8},{10,11... | collective-permute-start | bytes 7077896 | tf_op jit(solution)/shard_map/ppermute | solution.py:240
  395.9 20.9 %collective-permute-start.54 = (bf16[4,98,768]{2,0,1:T(4,128)(2,1)}, bf16[4,98,768]{2,0,1:T(4,128)(2,1)}, u32[]{:S(2)}, u32[]{:S(2)}) collective-permute-start(bf16[4,98,768]{2,0,1:T(4,128)(2,1)} %copy.56), channel_id=1, source_target_pairs={{0,1},{1,0},{2,3},{3,2},{4,5},{5,4},{6,7},{7,6},{8,9},{9,8},{10,11... | collective-permute-start | bytes 1806344 | tf_op jit(solution)/shard_map/ppermute | solution.py:240
  411.1 34.6 %collective-permute-start.58 = (bf16[768,1536]{1,0:T(8,128)(2,1)}, bf16[768,1536]{1,0:T(8,128)(2,1)}, u32[]{:S(2)}, u32[]{:S(2)}) collective-permute-start(bf16[768,1536]{1,0:T(8,128)(2,1)} %convolution_convert_fusion.3), channel_id=1, source_target_pairs={{0,1},{1,0},{2,3},{3,2},{4,5},{5,4},{6,7},{7,6},{8,9},{9,8},{10,11... | collective-permute-start | bytes 7077896 | tf_op jit(solution)/shard_map/ppermute | solution.py:240
  416.6 10.1 collective-permute-start.62
  420.0 16.1 %collective-permute-start.55 = (bf16[4,98,768]{2,0,1:T(4,128)(2,1)}, bf16[4,98,768]{2,0,1:T(4,128)(2,1)}, u32[]{:S(2)}, u32[]{:S(2)}) collective-permute-start(bf16[4,98,768]{2,0,1:T(4,128)(2,1)} %copy.59), channel_id=1, source_target_pairs={{0,2},{1,3},{2,0},{3,1},{4,6},{5,7},{6,4},{7,5},{8,10},{9,11},{10,... | collective-permute-start | bytes 1806344 | tf_op jit(solution)/shard_map/ppermute | solution.py:240
  526.5 37.7 %collective-permute-start.61 = (bf16[768,1152]{1,0:T(8,128)(2,1)}, bf16[768,1152]{1,0:T(8,128)(2,1)}, u32[]{:S(2)}, u32[]{:S(2)}) collective-permute-start(bf16[768,1152]{1,0:T(8,128)(2,1)} %fusion.28), channel_id=1, source_target_pairs={{0,1},{1,0},{2,3},{3,2},{4,5},{5,4},{6,7},{7,6},{8,9},{9,8},{10,11... | collective-permute-start | bytes 5308424 | tf_op jit(solution)/shard_map/ppermute | solution.py:240
  547.8 15.2 %collective-permute-start.60 = (bf16[4,208,384]{2,1,0:T(8,128)(2,1)}, bf16[4,208,384]{2,1,0:T(8,128)(2,1)S(1)}, u32[]{:S(2)}, u32[]{:S(2)}) collective-permute-start(bf16[4,208,384]{2,1,0:T(8,128)(2,1)} %bitcast.98), channel_id=1, source_target_pairs={{0,1},{1,0},{2,3},{3,2},{4,5},{5,4},{6,7},{7,6},{8,9},{9,8},{10,11... | collective-permute-start | bytes 1916936 | tf_op jit(solution)/shard_map/ppermute | solution.py:240
  615.3 51.3 %collective-permute-start.63 = (bf16[832,768]{1,0:T(8,128)(2,1)}, bf16[832,768]{1,0:T(8,128)(2,1)}, u32[]{:S(2)}, u32[]{:S(2)}) collective-permute-start(bf16[832,768]{1,0:T(8,128)(2,1)} %convolution_convert_fusion.6), channel_id=1, source_target_pairs={{0,1},{1,0},{2,3},{3,2},{4,5},{5,4},{6,7},{7,6},{8,9},{9,8},{10,11... | collective-permute-start | bytes 3833864 | tf_op jit(solution)/shard_map/ppermute | solution.py:240
  679.5 37.6 %collective-permute-start.65 = (bf16[768,1536]{1,0:T(8,128)(2,1)}, bf16[768,1536]{1,0:T(8,128)(2,1)}, u32[]{:S(2)}, u32[]{:S(2)}) collective-permute-start(bf16[768,1536]{1,0:T(8,128)(2,1)} %convolution_convert_fusion), channel_id=1, source_target_pairs={{0,1},{1,0},{2,3},{3,2},{4,5},{5,4},{6,7},{7,6},{8,9},{9,8},{10,11... | collective-permute-start | bytes 7077896 | tf_op jit(solution)/shard_map/ppermute | solution.py:240
  689.0 34.1 %collective-permute-start.64 = (bf16[768,1536]{1,0:T(8,128)(2,1)}, bf16[768,1536]{1,0:T(8,128)(2,1)}, u32[]{:S(2)}, u32[]{:S(2)}) collective-permute-start(bf16[768,1536]{1,0:T(8,128)(2,1)} %convolution_convert_fusion.1), channel_id=1, source_target_pairs={{0,1},{1,0},{2,3},{3,2},{4,5},{5,4},{6,7},{7,6},{8,9},{9,8},{10,11... | collective-permute-start | bytes 7077896 | tf_op jit(solution)/shard_map/ppermute | solution.py:240
  822.1 34.9 %collective-permute-start.85 = (bf16[768,384]{1,0:T(8,128)(2,1)}, bf16[768,384]{1,0:T(8,128)(2,1)}, u32[]{:S(2)}, u32[]{:S(2)}) collective-permute-start(bf16[768,384]{1,0:T(8,128)(2,1)} %bitcast.147), channel_id=1, source_target_pairs={{0,1},{1,0},{2,3},{3,2},{4,5},{5,4},{6,7},{7,6},{8,9},{9,8},{10,11... | collective-permute-start | bytes 1769480 | tf_op jit(solution)/shard_map/ppermute | solution.py:240
  822.2 36.9 %collective-permute-start.84 = (bf16[768,384]{1,0:T(8,128)(2,1)}, bf16[768,384]{1,0:T(8,128)(2,1)}, u32[]{:S(2)}, u32[]{:S(2)}) collective-permute-start(bf16[768,384]{1,0:T(8,128)(2,1)} %convolution_convert_fusion.17), channel_id=1, source_target_pairs={{0,1},{1,0},{2,3},{3,2},{4,5},{5,4},{6,7},{7,6},{8,9},{9,8},{10,11... | collective-permute-start | bytes 1769480 | tf_op jit(solution)/shard_map/ppermute | solution.py:240
  827.7 36.0 %collective-permute-start.67 = (bf16[768,1152]{1,0:T(8,128)(2,1)}, bf16[768,1152]{1,0:T(8,128)(2,1)}, u32[]{:S(2)}, u32[]{:S(2)}) collective-permute-start(bf16[768,1152]{1,0:T(8,128)(2,1)} %fusion.29), channel_id=1, source_target_pairs={{0,1},{1,0},{2,3},{3,2},{4,5},{5,4},{6,7},{7,6},{8,9},{9,8},{10,11... | collective-permute-start | bytes 5308424 | tf_op jit(solution)/shard_map/ppermute | solution.py:240
  831.4 29.9 %collective-permute-start.66 = (bf16[4,208,384]{2,1,0:T(8,128)(2,1)}, bf16[4,208,384]{2,1,0:T(8,128)(2,1)}, u32[]{:S(2)}, u32[]{:S(2)}) collective-permute-start(bf16[4,208,384]{2,1,0:T(8,128)(2,1)} %bitcast.115), channel_id=1, source_target_pairs={{0,1},{1,0},{2,3},{3,2},{4,5},{5,4},{6,7},{7,6},{8,9},{9,8},{10,11... | collective-permute-start | bytes 1916936 | tf_op jit(solution)/shard_map/ppermute | solution.py:240
  909.9 55.7 %collective-permute-start.69 = (bf16[832,768]{1,0:T(8,128)(2,1)}, bf16[832,768]{1,0:T(8,128)(2,1)}, u32[]{:S(2)}, u32[]{:S(2)}) collective-permute-start(bf16[832,768]{1,0:T(8,128)(2,1)} %convolution_convert_fusion.4), channel_id=1, source_target_pairs={{0,1},{1,0},{2,3},{3,2},{4,5},{5,4},{6,7},{7,6},{8,9},{9,8},{10,11... | collective-permute-start | bytes 3833864 | tf_op jit(solution)/shard_map/ppermute | solution.py:240
  973.3 13.7 %collective-permute-start.73 = (f32[3840]{0:T(1024)S(1)}, f32[3840]{0:T(1024)S(1)}, u32[]{:S(2)}, u32[]{:S(2)}) collective-permute-start(f32[3840]{0:T(1024)S(1)} %pad_maximum_fusion.38), channel_id=1, source_target_pairs={{0,2},{1,3},{2,0},{3,1},{4,6},{5,7},{6,4},{7,5},{8,10},{9,11},{10,... | collective-permute-start | bytes 46088 | tf_op jit(solution)/shard_map/ppermute | solution.py:240
  999.9 12.6 %collective-permute-start.71 = (bf16[4,98,768]{2,0,1:T(4,128)(2,1)S(1)}, bf16[4,98,768]{2,0,1:T(4,128)(2,1)S(1)}, u32[]{:S(2)}, u32[]{:S(2)}) collective-permute-start(bf16[4,98,768]{2,0,1:T(4,128)(2,1)S(1)} %copy.71), channel_id=1, source_target_pairs={{0,2},{1,3},{2,0},{3,1},{4,6},{5,7},{6,4},{7,5},{8,10},{9,11},{10,... | collective-permute-start | bytes 1806344 | tf_op jit(solution)/shard_map/ppermute | solution.py:240
  (298 other events, 5203.1 us)

commit v3 on v2

--- a/solution.py
+++ b/solution.py
@@ -383,31 +383,44 @@
         self.ra, self.rb, self.sx, self.sy = ra, rb, sx, sy
         self.rx, self.ry, self.low, self.gz = rx, ry, low, gz
         self.send, self.recv = send, recv
+        self.depth = part.shape[0]
         self.half = part.shape[0] // 2
 
     def copy(self, number, src, dst, target):
-        return pltpu.make_async_remote_copy(
-            src_ref=src,
-            dst_ref=dst,
-            send_sem=self.send.at[number],
-            recv_sem=self.recv.at[number],
-            device_id=target,
-            device_id_type=pl.DeviceIdType.MESH,
-        )
-
-    def first(self):
-        z, x, y = self.place.z, self.place.x, self.place.y
+        return remote(src, dst, self.send.at[number], self.recv.at[number], target)
+
+    def far(self):
+        x, y = self.place.x, self.place.y
         low, high = pl.ds(0, self.half), pl.ds(self.half, self.half)
-        self.far = [
+        return [
             self.copy(0, self.part.at[low, 1 - x, 1 - y], self.ra, self.place.over_y()),
             self.copy(1, self.part.at[high, 1 - x, 1 - y], self.rb, self.place.over_x()),
         ]
-        for item in self.far:
+
+    def near(self):
+        return [
+            self.copy(2, self.sx, self.rx, self.place.over_x()),
+            self.copy(3, self.sy, self.ry, self.place.over_y()),
+        ]
+
+    def deep(self):
+        return [
+            self.copy(
+                3 + k,
+                self.low.at[lax.rem(self.place.z + k, self.depth)],
+                self.gz.at[k - 1],
+                self.place.over_z(k),
+            )
+            for k in range(1, self.depth)
+        ]
+
+    def first(self):
+        for item in self.far():
             item.start()
 
     def second(self):
         x, y, half = self.place.x, self.place.y, self.half
-        for item in self.far:
+        for item in self.far():
             item.wait()
         for k in range(2 * half):
             toward_x, toward_y = self.part[k, 1 - x, y], self.part[k, x, 1 - y]
@@ -417,11 +430,7 @@
                 toward_y = (toward_y.astype(F32) + self.rb[k - half].astype(F32)).astype(BF)
             self.sx[k] = toward_x
             self.sy[k] = toward_y
-        self.near = [
-            self.copy(2, self.sx, self.rx, self.place.over_x()),
-            self.copy(3, self.sy, self.ry, self.place.over_y()),
-        ]
-        for item in self.near:
+        for item in self.near():
             item.start()
 
     def kept(self, k):
@@ -429,30 +438,31 @@
         return mine + self.rx[k].astype(F32) + self.ry[k].astype(F32)
 
     def third(self):
-        depth = 2 * self.half
-        for item in self.near:
+        for item in self.near():
             item.wait()
-        for k in range(depth):
+        for k in range(self.depth):
             self.low[k] = self.kept(k).astype(BF)
-        self.deep = [
-            self.copy(
-                3 + k,
-                self.low.at[lax.rem(self.place.z + k, depth)],
-                self.gz.at[k - 1],
-                self.place.over_z(k),
-            )
-            for k in range(1, depth)
-        ]
-        for item in self.deep:
+        for item in self.deep():
             item.start()
 
     def last(self):
-        for item in self.deep:
+        for item in self.deep():
             item.wait()
         total = self.kept(self.place.z)
-        for k in range(2 * self.half - 1):
+        for k in range(self.depth - 1):
             total = total + self.gz[k].astype(F32)
         self.own[...] = total
+
+
+def remote(src, dst, send, recv, target):
+    return pltpu.make_async_remote_copy(
+        src_ref=src,
+        dst_ref=dst,
+        send_sem=send,
+        recv_sem=recv,
+        device_id=target,
+        device_id_type=pl.DeviceIdType.MESH,
+    )
 
 
 class Place:
@@ -462,6 +472,7 @@
         self.z = shard // 2
         self.x = lax.rem(shard, 2)
         self.y = lax.axis_index("ctx")
+        self.t = lax.axis_index("tp")
 
     def over_x(self):
         return {"shard": self.z * 2 + 1 - self.x}
@@ -469,13 +480,18 @@
     def over_y(self):
         return {"ctx": 1 - self.y}
 
+    def over_t(self):
+        return {"tp": 1 - self.t}
+
     def over_z(self, step):
         return {"shard": lax.rem(self.z + step, self.depth) * 2 + self.x}
 
-    def meet(self):
+    def meet(self, chips, cores):
         barrier = pltpu.get_barrier_semaphore()
-        targets = [self.over_x(), self.over_y()]
-        targets += [self.over_z(k) for k in range(1, self.depth)]
+        targets = [self.over_t()] if cores else []
+        if chips:
+            targets += [self.over_x(), self.over_y()]
+            targets += [self.over_z(k) for k in range(1, self.depth)]
         for target in targets:
             pl.semaphore_signal(
                 barrier, inc=1, device_id=target, device_id_type=pl.DeviceIdType.MESH
@@ -483,58 +499,498 @@
         pl.semaphore_wait(barrier, len(targets))
 
 
-def sum_body(depth, ins, parts, outs, payload, *refs):
-    refs = list(refs)
-    take = lambda count: [refs.pop(0) for _ in range(count)]
-    in_refs, part_refs, out_refs, own_refs = take(ins), take(parts), take(outs), take(parts)
-    place = Place(depth)
-    sums = [
-        Sums(place, part, own, *take(10)) for part, own in zip(part_refs, own_refs)
-    ]
-    place.meet()
-    for item in sums:
-        item.first()
-    payload(0, in_refs, out_refs)
-    for item in sums:
-        item.second()
-    payload(1, in_refs, out_refs)
-    for item in sums:
-        item.third()
-    for item in sums:
-        item.last()
-
-
-def no_payload(stage, in_refs, out_refs):
-    return None
-
-
-def sum_rows(grid, number, parts, payload=no_payload, ins=(), outs=(), smem=0):
+class Carrier:
+    def __init__(self, place, cores, parts, owns, scratch):
+        self.place, self.cores = place, cores
+        self.sums = [
+            Sums(place, part, own, *scratch[10 * i : 10 * i + 10])
+            for i, (part, own) in enumerate(zip(parts, owns))
+        ]
+
+    def step(self, number):
+        lead, rest = self.sums[:1], self.sums[1:]
+        if number == 0:
+            self.place.meet(bool(self.sums), self.cores)
+            for item in lead + rest:
+                item.first()
+        elif number == 1:
+            for item in lead:
+                item.second()
+        elif number == 2:
+            for item in lead:
+                item.third()
+            for item in rest:
+                item.second()
+        elif number == 3:
+            for item in rest:
+                item.third()
+        else:
+            for item in lead + rest:
+                item.last()
+
+
+def carried(grid, parts):
     depth = grid.depth
-    step_rows = parts[0].shape[0] // (depth * 4)
-    cubes = [part.reshape(depth, 2, 2, step_rows, part.shape[1]) for part in parts]
-    scratch = []
+    cubes, shapes, scratch = [], [], []
     for part in parts:
-        block = lambda count, lanes=part.shape[1]: pltpu.VMEM((count, step_rows, lanes), BF)
+        step_rows, lanes = part.shape[0] // (depth * 4), part.shape[1]
+        block = lambda count: pltpu.VMEM((count, step_rows, lanes), BF)
+        cubes.append(part.reshape(depth, 2, 2, step_rows, lanes))
+        shapes.append(jax.ShapeDtypeStruct((step_rows, lanes), F32))
         scratch += [block(depth // 2)] * 2 + [block(depth)] * 5 + [block(depth - 1)]
         scratch += [pltpu.SemaphoreType.DMA((3 + depth,))] * 2
-    vmem = pl.BlockSpec(memory_space=pltpu.VMEM)
-    results = pl.pallas_call(
-        functools.partial(sum_body, depth, len(ins), len(parts), len(outs), payload),
-        in_specs=[pl.BlockSpec(memory_space=pltpu.SMEM)] * smem
-        + [vmem] * (len(ins) - smem + len(parts)),
-        out_specs=[vmem] * (len(outs) + len(parts)),
-        out_shape=list(outs)
-        + [jax.ShapeDtypeStruct((step_rows, part.shape[1]), F32) for part in parts],
+    return cubes, shapes, scratch
+
+
+def stage_params(number, vmem=58):
+    return pltpu.CompilerParams(
+        collective_id=number, has_side_effects=True, vmem_limit_bytes=vmem << 20
+    )
+
+
+def stage_cost(flops):
+    return pl.CostEstimate(flops=flops, bytes_accessed=30000000, transcendentals=0)
+
+
+VMEM_SPEC = pl.BlockSpec(memory_space=pltpu.VMEM)
+SMEM_SPEC = pl.BlockSpec(memory_space=pltpu.SMEM)
+
+
+def splitter(refs):
+    refs = list(refs)
+    return lambda count: [refs.pop(0) for _ in range(count)]
+
+
+def tail_body(depth, count, *refs):
+    take = splitter(refs)
+    parts, owns, scratch = take(count), take(count), take(10 * count)
+    carrier = Carrier(Place(depth), False, parts, owns, scratch)
+    for number in range(5):
+        carrier.step(number)
+
+
+def tail_sums(grid, number, parts):
+    cubes, shapes, scratch = carried(grid, parts)
+    return pl.pallas_call(
+        functools.partial(tail_body, grid.depth, len(parts)),
+        in_specs=[VMEM_SPEC] * len(parts),
+        out_specs=[VMEM_SPEC] * len(parts),
+        out_shape=shapes,
         scratch_shapes=scratch,
-        compiler_params=pltpu.CompilerParams(
-            collective_id=number, has_side_effects=True, vmem_limit_bytes=56 << 20
-        ),
-        cost_estimate=pl.CostEstimate(
-            flops=20000000000, bytes_accessed=50000000, transcendentals=0
-        ),
+        compiler_params=stage_params(number),
+        cost_estimate=stage_cost(20000000000),
         name="sum_rows",
-    )(*ins, *cubes)
-    return results[: len(outs)], results[len(outs) :]
+    )(*cubes)
+
+
+def norm_back_rows(e, unit, scale, gain):
+    along = e * gain
+    lanes = e.shape[-1]
+    mean_along = jnp.sum(along, axis=-1, keepdims=True) * (1.0 / lanes)
+    mean_unit = jnp.sum(along * unit, axis=-1, keepdims=True) * (1.0 / lanes)
+    return scale * (along - mean_along - unit * mean_unit)
+
+
+def column_sum(value):
+    return jnp.sum(value, axis=0, keepdims=True)
+
+
+def feed_back_body(depth, count, steps, *refs):
+    take = splitter(refs)
+    state, normed, unit, scale, gain = take(5)
+    oth, own = take(4), take(4)
+    parts = take(count)
+    out, sums, g_up, g_down, h_own, h_oth = take(6)
+    owns = take(count)
+    r, rt, nt, bh, s_up, s_down, r_up, r_down, send, recv = take(10)
+    place = Place(depth)
+    carrier = Carrier(place, True, parts, owns, take(10 * count))
+    frames, padded, width = state.shape
+    rows_all = frames * padded
+    i = pl.program_id(0)
+
+    @pl.when(i == 0)
+    def _():
+        carrier.step(0)
+        sums[...] = jnp.zeros_like(sums)
+
+        def begin(f, carry):
+            low = state[f].astype(BF)
+            r[f] = low
+            out[f] = jnp.zeros((padded, width), F32)
+            return carry + column_sum(low.astype(F32))
+
+        sums[0:1] = lax.fori_loop(0, frames, begin, jnp.zeros((1, width), F32))
+        rt[...] = r[...].reshape(rows_all, width).T
+        nt[...] = normed[...].reshape(rows_all, width).T
+
+    def work(down, up, active, slope, h_sum):
+        lanes = down.shape[1]
+
+        def one(f, carry):
+            value = (dot_nn(r[f], down[...]) * slope[f].astype(F32)).astype(BF)
+            bh[f] = value
+            out[f] += dot_nt(value, up[...])
+            return carry + column_sum(value.astype(F32))
+
+        h_sum[...] = lax.fori_loop(0, frames, one, jnp.zeros((1, lanes), F32))
+        return (
+            dot_nn(nt[...], bh[...].reshape(rows_all, lanes)),
+            dot_nn(rt[...], active[...].reshape(rows_all, lanes)),
+        )
+
+    def swaps(j):
+        return [
+            remote(s_up.at[j], r_up.at[j], send.at[0, j], recv.at[0, j], place.over_t()),
+            remote(s_down.at[j], r_down.at[j], send.at[1, j], recv.at[1, j], place.over_t()),
+        ]
+
+    @pl.when(i < steps)
+    def _():
+        up_part, down_part = work(*oth, h_oth)
+        s_up[i] = up_part.astype(BF)
+        s_down[i] = down_part.astype(BF)
+        for item in swaps(i):
+            item.start()
+
+    for number, at in ((1, 1), (2, 3), (3, 4)):
+        if count:
+
+            @pl.when(i == at)
+            def _(number=number):
+                carrier.step(number)
+
+    @pl.when(i >= steps)
+    def _():
+        j = i - steps
+        up_part, down_part = work(*own, h_own)
+        for item in swaps(j):
+            item.wait()
+        g_up[...] = (up_part + r_up[j].astype(F32)).astype(BF)
+        g_down[...] = (down_part + r_down[j].astype(F32)).astype(BF)
+
+    @pl.when(i == 2 * steps - 1)
+    def _():
+        def finish(f, carry):
+            e, u = out[f], unit[f]
+            out[f] = state[f] + norm_back_rows(e, u, scale[f], gain[...])
+            return (carry[0] + column_sum(e * u), carry[1] + column_sum(e))
+
+        zero = jnp.zeros((1, width), F32)
+        sums[1:2], sums[2:3] = lax.fori_loop(0, frames, finish, (zero, zero))
+        carrier.step(4)
+
+
+def feed_back(grid, number, state, kept, gain, w, parts):
+    frames, padded, width = state.shape
+    hid = w["up"][0].shape[1]
+    steps = 3
+    lanes = hid // steps
+    cubes, shapes, scratch = carried(grid, parts)
+    whole = lambda item: pl.BlockSpec(
+        item.shape, lambda i: (0,) * item.ndim, pipeline_mode=pl.Buffered(1)
+    )
+    first = lambda i: jnp.minimum(i, steps - 1)
+    later = lambda i: jnp.maximum(i - steps, 0)
+
+    def side(at):
+        weight = pl.BlockSpec((width, lanes), lambda i: (0, at(i)))
+        token = pl.BlockSpec((frames, padded, lanes), lambda i: (0, 0, at(i)))
+        return [weight, weight, token, token]
+
+    tokens = lambda item: item.reshape(frames, padded, hid)
+    sides = [
+        [w["down"][k], w["up"][k], tokens(kept["active"][k]), tokens(kept["slope"][k])]
+        for k in (1, 0)
+    ]
+    fixed = [state, kept["normed_m"], kept["unit_m"], kept["scale_m"], gain]
+    vec = lambda at: pl.BlockSpec((1, lanes), lambda i: (0, at(i)))
+    result = pl.pallas_call(
+        functools.partial(feed_back_body, grid.depth, len(parts), steps),
+        grid=(2 * steps,),
+        in_specs=[whole(item) for item in fixed]
+        + side(first)
+        + side(later)
+        + [whole(item) for item in cubes],
+        out_specs=[
+            pl.BlockSpec((frames, padded, width), lambda i: (0, 0, 0)),
+            pl.BlockSpec((8, width), lambda i: (0, 0)),
+            pl.BlockSpec((width, lanes), lambda i: (0, later(i))),
+            pl.BlockSpec((width, lanes), lambda i: (0, later(i))),
+            vec(later),
+            vec(first),
+        ]
+        + [pl.BlockSpec(item.shape, lambda i: (0, 0)) for item in shapes],
+        out_shape=[
+            jax.ShapeDtypeStruct((frames, padded, width), F32),
+            jax.ShapeDtypeStruct((8, width), F32),
+            jax.ShapeDtypeStruct((width, hid), BF),
+            jax.ShapeDtypeStruct((width, hid), BF),
+            jax.ShapeDtypeStruct((1, hid), F32),
+            jax.ShapeDtypeStruct((1, hid), F32),
+        ]
+        + shapes,
+        scratch_shapes=[
+            pltpu.VMEM((frames, padded, width), BF),
+            pltpu.VMEM((width, frames * padded), BF),
+            pltpu.VMEM((width, frames * padded), BF),
+            pltpu.VMEM((frames, padded, lanes), BF),
+        ]
+        + [pltpu.VMEM((steps, width, lanes), BF)] * 4
+        + [pltpu.SemaphoreType.DMA((2, steps))] * 2
+        + scratch,
+        compiler_params=stage_params(number),
+        cost_estimate=stage_cost(24000000000),
+        name="feed_back",
+    )(*fixed, *sides[0], *sides[1], *cubes)
+    return result[0], result[1], result[2:4], (result[4], result[5]), result[6:]
+
+
+def spatial_back_body(depth, count, places, att_scale, *refs):
+    take = splitter(refs)
+    (count_ref, state, merge0, merge1, mixed0, mixed1, qkv0, qkv1) = take(8)
+    tri0, tri1, normed, unit, scale, gain = take(6)
+    parts = take(count)
+    out, sums, q_sums, g_tri, g_merge = take(5)
+    owns = take(count)
+    r, bm0, bm1, b0, b1, rt, nt, s_tri, r_tri, s_merge, r_merge, send, recv = take(13)
+    place = Place(depth)
+    carrier = Carrier(place, True, parts, owns, take(10 * count))
+    frames, padded, width = state.shape
+    rows_all = frames * padded
+    split = merge0.shape[1]
+    fix = spatial_fix(count_ref, padded, places)
+    carrier.step(0)
+
+    def one(f, carry):
+        low = state[f].astype(BF)
+        r[f] = low
+        for merge, bm, src, dst in ((merge0, bm0, qkv0, b0), (merge1, bm1, qkv1, b1)):
+            bm[...] = dot_nn(low, merge[...]).astype(BF)
+
+            def put(part, pair, value, dst=dst):
+                dst[f, :, column(part, pair)] = value
+
+            heads_backward(
+                lambda part, pair, src=src: src[f, :, column(part, pair)],
+                lambda pair, bm=bm: bm[:, pair * 128 : pair * 128 + 128],
+                fix,
+                att_scale,
+                put,
+            )
+        return carry + column_sum(low.astype(F32))
+
+    sums[...] = jnp.zeros_like(sums)
+    q_sums[...] = jnp.zeros_like(q_sums)
+    half = frames // 2
+    total = lax.fori_loop(0, half, one, jnp.zeros((1, width), F32))
+    carrier.step(1)
+    sums[0:1] = lax.fori_loop(half, frames, one, total)
+    carrier.step(2)
+    rt[...] = r[...].reshape(rows_all, width).T
+    nt[...] = normed[...].reshape(rows_all, width).T
+    flat = lambda ref, part: ref[:, :, part * split : (part + 1) * split].reshape(rows_all, split)
+    swap_tri = remote(s_tri, r_tri, send.at[0], recv.at[0], place.over_t())
+    swap_merge = remote(s_merge, r_merge, send.at[1], recv.at[1], place.over_t())
+    s_merge[...] = dot_nn(rt[...], mixed1[...]).astype(BF)
+    swap_merge.start()
+    for part in range(3):
+        cols = slice(part * split, (part + 1) * split)
+        s_tri[:, cols] = dot_nn(nt[...], flat(b1, part)).astype(BF)
+    swap_tri.start()
+    carrier.step(3)
+
+    def finish(f, carry):
+        e = dot_nt(b0[f], tri0[...]) + dot_nt(b1[f], tri1[...])
+        u = unit[f]
+        out[f] = state[f] + norm_back_rows(e, u, scale[f], gain[...])
+        return (
+            carry[0] + column_sum(e * u),
+            carry[1] + column_sum(e),
+            carry[2] + column_sum(b0[f].astype(F32)),
+            carry[3] + column_sum(b1[f].astype(F32)),
+        )
+
+    zero, wide = jnp.zeros((1, width), F32), jnp.zeros((1, 3 * split), F32)
+    sums[1:2], sums[2:3], q_sums[0:1], q_sums[1:2] = lax.fori_loop(
+        0, frames, finish, (zero, zero, wide, wide)
+    )
+    swap_merge.wait()
+    g_merge[...] = (dot_nn(rt[...], mixed0[...]) + r_merge[...].astype(F32)).astype(BF)
+    swap_tri.wait()
+    for part in range(3):
+        cols = slice(part * split, (part + 1) * split)
+        mine = dot_nn(nt[...], flat(b0, part))
+        g_tri[:, cols] = (mine + r_tri[:, cols].astype(F32)).astype(BF)
+    carrier.step(4)
+
+
+def spatial_back(grid, number, count_ref, state, kept, gain, w, parts, places, att_scale):
+    frames, padded, width = state.shape
+    split = w["merge_s"][0].shape[1]
+    cubes, shapes, scratch = carried(grid, parts)
+    flat = [item.reshape(frames * padded, split) for item in kept["mixed_s"]]
+    fixed = [count_ref, state, *w["merge_s"], *flat, *kept["qkv_s"], *w["triple_s"]]
+    fixed += [kept["normed_s"], kept["unit_s"], kept["scale_s"], gain]
+    result = pl.pallas_call(
+        functools.partial(spatial_back_body, grid.depth, len(parts), places, att_scale),
+        in_specs=[SMEM_SPEC] + [VMEM_SPEC] * (len(fixed) - 1 + len(parts)),
+        out_specs=[VMEM_SPEC] * (5 + len(parts)),
+        out_shape=[
+            jax.ShapeDtypeStruct((frames, padded, width), F32),
+            jax.ShapeDtypeStruct((8, width), F32),
+            jax.ShapeDtypeStruct((8, 3 * split), F32),
+            jax.ShapeDtypeStruct((width, 3 * split), BF),
+            jax.ShapeDtypeStruct((width, split), BF),
+        ]
+        + shapes,
+        scratch_shapes=[pltpu.VMEM((frames, padded, width), BF)]
+        + [pltpu.VMEM((padded, split), BF)] * 2
+        + [pltpu.VMEM((frames, padded, 3 * split), BF)] * 2
+        + [pltpu.VMEM((width, frames * padded), BF)] * 2
+        + [pltpu.VMEM((width, 3 * split), BF)] * 2
+        + [pltpu.VMEM((width, split), BF)] * 2
+        + [pltpu.SemaphoreType.DMA((2,))] * 2
+        + scratch,
+        compiler_params=stage_params(number),
+        cost_estimate=stage_cost(24000000000),
+        name="spatial_stage",
+    )(*fixed, *cubes)
+    return result[0], result[1], result[2], result[3:5], result[5:]
+
+
+def temporal_back_body(depth, count, att_scale, *refs):
+    take = splitter(refs)
+    state, mixing, joined, merge0, merge1, mine, swap, qkv, tri = take(9)
+    normed, unit, scale, gain = take(4)
+    parts = take(count)
+    out, sums, q_sums, g_tri, g_merge, g_mix = take(6)
+    owns = take(count)
+    r, bj, away, bm, b, nt, rt, s_merge, r_merge, s_back, r_back, send, recv = take(13)
+    place = Place(depth)
+    carrier = Carrier(place, True, parts, owns, take(10 * count))
+    frames, padded, width = state.shape
+    rows_all = frames * padded
+    split = merge0.shape[1]
+    carrier.step(0)
+
+    def begin(f, carry):
+        low = state[f].astype(BF)
+        r[f] = low
+        value = dot_nt(low, mixing[...]).astype(BF)
+        bj[f] = value
+        bm[f] = dot_nn(value, merge0[...]).astype(BF)
+        away[f] = dot_nn(value, merge1[...]).astype(BF)
+        return (carry[0] + column_sum(low.astype(F32)), carry[1] + column_sum(value.astype(F32)))
+
+    sums[...] = jnp.zeros_like(sums)
+    q_sums[...] = jnp.zeros_like(q_sums)
+    zero = jnp.zeros((1, width), F32)
+    sums[0:1], sums[1:2] = lax.fori_loop(0, frames, begin, (zero, zero))
+    swap_bm = remote(
+        away, bm.at[pl.ds(frames, frames)], send.at[0], recv.at[0], place.over_t()
+    )
+    swap_bm.start()
+    rt[...] = bj[...].reshape(rows_all, width).T
+    s_merge[...] = dot_nn(rt[...], swap[...]).astype(BF)
+    swap_merge = remote(s_merge, r_merge, send.at[1], recv.at[1], place.over_t())
+    swap_merge.start()
+    carrier.step(1)
+    rt[...] = joined[...].T
+    for half in range(2):
+        cols = slice(half * split, (half + 1) * split)
+        g_mix[:, cols] = dot_nn(rt[...], r[:, :, cols].reshape(rows_all, split))
+    rt[...] = bj[...].reshape(rows_all, width).T
+    swap_merge.wait()
+    g_merge[...] = (dot_nn(rt[...], mine[...]) + r_merge[...].astype(F32)).astype(BF)
+    swap_bm.wait()
+    tile = 16
+    fix = temporal_fix(tile)
+
+    def one(i, carry):
+        at = pl.ds(pl.multiple_of(i * tile, tile), tile)
+
+        def put(part, pair, value):
+            b[:, at, column(part, pair)] = value.reshape(FRAMES, tile, 128)
+
+        heads_backward(
+            lambda part, pair: qkv[:, at, column(part, pair)].reshape(FRAMES * tile, 128),
+            lambda pair: bm[:, at, pair * 128 : pair * 128 + 128].reshape(FRAMES * tile, 128),
+            fix,
+            att_scale,
+            put,
+        )
+        return carry
+
+    tiles = padded // tile
+    lax.fori_loop(0, tiles // 2, one, 0)
+    carrier.step(2)
+    lax.fori_loop(tiles // 2, tiles, one, 0)
+    carrier.step(3)
+
+    def toward(f, carry):
+        s_back[f] = dot_nt(b[f + frames], tri[...]).astype(BF)
+        return carry
+
+    lax.fori_loop(0, frames, toward, 0)
+    swap_back = remote(s_back, r_back, send.at[2], recv.at[2], place.over_t())
+    swap_back.start()
+    nt[...] = normed[...].T
+    for part in range(3):
+        cols = slice(part * split, (part + 1) * split)
+        g_tri[:, cols] = dot_nn(
+            nt[...], b[:, :, cols].reshape(2 * rows_all, split)
+        ).astype(BF)
+    swap_back.wait()
+
+    def finish(f, carry):
+        e = dot_nt(b[f], tri[...]) + r_back[f].astype(F32)
+        u = unit[f]
+        out[f] = state[f] + norm_back_rows(e, u, scale[f], gain[...])
+        both = column_sum(b[f].astype(F32)) + column_sum(b[f + frames].astype(F32))
+        return (carry[0] + column_sum(e * u), carry[1] + column_sum(e), carry[2] + both)
+
+    sums[2:3], sums[3:4], q_sums[0:1] = lax.fori_loop(
+        0, frames, finish, (zero, zero, jnp.zeros((1, 3 * split), F32))
+    )
+    carrier.step(4)
+
+
+def temporal_back(grid, number, state, kept, gain, w, parts, att_scale):
+    frames, padded, width = state.shape
+    split = w["merge_t"][0].shape[1]
+    cubes, shapes, scratch = carried(grid, parts)
+    flat = [item.reshape(frames * padded, split) for item in kept["mixed_t"]]
+    fixed = [state, w["mixing"], kept["joined"], *w["merge_t"], *flat, kept["qkv_t"]]
+    fixed += [w["triple_t"], rows(kept["normed_t"]), kept["unit_t"], kept["scale_t"], gain]
+    result = pl.pallas_call(
+        functools.partial(temporal_back_body, grid.depth, len(parts), att_scale),
+        in_specs=[VMEM_SPEC] * (len(fixed) + len(parts)),
+        out_specs=[VMEM_SPEC] * (6 + len(parts)),
+        out_shape=[
+            jax.ShapeDtypeStruct((frames, padded, width), F32),
+            jax.ShapeDtypeStruct((8, width), F32),
+            jax.ShapeDtypeStruct((8, 3 * split), F32),
+            jax.ShapeDtypeStruct((width, 3 * split), BF),
+            jax.ShapeDtypeStruct((width, split), BF),
+            jax.ShapeDtypeStruct((width, width), F32),
+        ]
+        + shapes,
+        scratch_shapes=[pltpu.VMEM((frames, padded, width), BF)] * 2
+        + [pltpu.VMEM((frames, padded, split), BF)]
+        + [pltpu.VMEM((2 * frames, padded, split), BF)]
+        + [pltpu.VMEM((2 * frames, padded, 3 * split), BF)]
+        + [pltpu.VMEM((width, 2 * frames * padded), BF)]
+        + [pltpu.VMEM((width, frames * padded), BF)]
+        + [pltpu.VMEM((width, split), BF)] * 2
+        + [pltpu.VMEM((frames, padded, width), BF)] * 2
+        + [pltpu.SemaphoreType.DMA((3,))] * 2
+        + scratch,
+        compiler_params=stage_params(number),
+        cost_estimate=stage_cost(24000000000),
+        name="temporal_stage",
+    )(*fixed, *cubes)
+    return result[0], result[1], result[2], result[3:6], result[6:]
 
 
 def plain_sums(parts):
@@ -542,56 +998,6 @@
         lax.psum_scatter(part.astype(F32), ("shard", "ctx"), scatter_dimension=0, tiled=True)
         for part in parts
     ]
-
-
-def spatial_back_payload(places, scale, stage, ins, outs):
-    count_ref, own_ref, oth_ref, bown_ref, both_ref = ins
-    frames = own_ref.shape[0]
-    fix = spatial_fix(count_ref, own_ref.shape[1], places)
-
-    def frame(f, carry):
-        for src, back, dst in ((own_ref, bown_ref, outs[0]), (oth_ref, both_ref, outs[1])):
-
-            def put(part, pair, value, dst=dst):
-                dst[f, :, column(part, pair)] = value
-
-            heads_backward(
-                lambda part, pair, src=src: src[f, :, column(part, pair)],
-                lambda pair, back=back: back[f, :, pair * 128 : pair * 128 + 128],
-                fix,
-                scale,
-                put,
-            )
-        return carry
-
-    half = frames // 2
-    lax.fori_loop(stage * half, half if stage == 0 else frames, frame, 0)
-
-
-def temporal_back_payload(scale, stage, ins, outs):
-    src, back = ins
-    dst = outs[0]
-    tile = 16
-    tiles = src.shape[1] // tile
-    fix = temporal_fix(tile)
-
-    def one(i, carry):
-        at = pl.ds(pl.multiple_of(i * tile, tile), tile)
-
-        def put(part, pair, value):
-            dst[:, at, column(part, pair)] = value.reshape(FRAMES, tile, 128)
-
-        heads_backward(
-            lambda part, pair: src[:, at, column(part, pair)].reshape(FRAMES * tile, 128),
-            lambda pair: back[:, at, pair * 128 : pair * 128 + 128].reshape(FRAMES * tile, 128),
-            fix,
-            scale,
-            put,
-        )
-        return carry
-
-    half = tiles // 2
-    lax.fori_loop(stage * half, half if stage == 0 else tiles, one, 0)
 
 
 def split_columns(value, widths):
@@ -850,118 +1256,59 @@
         whole = whole + grid.over_t(whole)
         return grid.total(jnp.concatenate([whole] + halves), False)
 
-    def join(make):
-        got = grid.over_t(make(1).astype(BF))
-        return (make(0) + got.astype(F32)).astype(BF)
+    waiting = None
+
+    def carry_sums(name, parts):
+        nonlocal waiting
+        if not grid.direct:
+            sums[name] = plain_sums(parts)
+            return
+        waiting = (name, parts)
+
+    def carried_parts():
+        return waiting[1] if waiting else []
+
+    def arrived_sums(result):
+        nonlocal waiting
+        if waiting:
+            sums[waiting[0]] = list(result)
+        waiting = None
 
     for layer in range(LAYERS - 1, -1, -1):
         w, kept = gathered[layer], stored[layer]
-        gain = norm_gain[layer]
-        r = rows(upstream).astype(BF)
-        down_bias_part = row_total(r)
-        back_active = [dot_nn(r, w["down"][i]) for i in range(2)]
-        back_hidden = [
-            (back_active[i] * kept["slope"][i].astype(F32)).astype(BF) for i in range(2)
-        ]
-        hidden_part = [row_total(back_hidden[i]) for i in range(2)]
-        back_sides = [dot_nt(back_hidden[i], w["up"][i]) for i in range(2)]
-        back_normed = cube(back_sides[0] + back_sides[1])
-        back_state, gain_m, shift_m = norm_backward(
-            back_normed, kept["unit_m"], kept["scale_m"], gain[2]
+        gain = [norm_gain[layer, part : part + 1] for part in range(3)]
+        upstream, vec_m, parts_m, hidden_part, got = feed_back(
+            grid, layer, upstream, kept, gain[2], w, carried_parts()
         )
-        upstream = upstream + back_state
-        parts_m = [
-            join(lambda i: dot_tn(rows(kept["normed_m"]), back_hidden[i])),
-            join(lambda i: dot_tn(r, kept["active"][i])),
-        ]
-        rs = rows(upstream).astype(BF)
-        r = rs
-        spatial_bias_part = row_total(r)
-        back_mixed = [cube(dot_nn(r, w["merge_s"][i]).astype(BF)) for i in range(2)]
-        spatial_ins = list(kept["qkv_s"]) + back_mixed
-        if grid.direct:
-            back_qkv, sums["m", layer] = sum_rows(
-                grid,
-                layer,
-                parts_m,
-                functools.partial(spatial_back_payload, places, scale),
-                [count_ref] + spatial_ins,
-                [jax.ShapeDtypeStruct(item.shape, BF) for item in kept["qkv_s"]],
-                1,
-            )
-        else:
-            back_qkv = spatial_call(
-                count_ref, spatial_ins, (3 * split, 3 * split), places, scale, True
-            )
-            sums["m", layer] = plain_sums(parts_m)
-        qkv_sums = [row_total(back_qkv[i]) for i in range(2)]
-        entry_s_part = [jnp.stack([q[:split], q[2 * split :]]) for q in qkv_sums]
-        back_sides = [dot_nt(rows(back_qkv[i]), w["triple_s"][i]) for i in range(2)]
-        back_normed = cube(back_sides[0] + back_sides[1])
-        back_state, gain_s, shift_s = norm_backward(
-            back_normed, kept["unit_s"], kept["scale_s"], gain[1]
+        arrived_sums(got)
+        carry_sums(("m", layer), parts_m)
+        upstream, vec_s, q_sums, parts_s, got = spatial_back(
+            grid, 2 + layer, count_ref, upstream, kept, gain[1], w, carried_parts(), places, scale
         )
-        upstream = upstream + back_state
-        parts_s = [
-            join(lambda i: dot_tn(rows(kept["normed_s"]), rows(back_qkv[i]))),
-            join(lambda i: dot_tn(rs, rows(kept["mixed_s"][i]))),
-        ]
-        theirs = jnp.concatenate([entry_s_part[1].reshape(-1), hidden_part[1]])
-        mine = jnp.concatenate([entry_s_part[0].reshape(-1), hidden_part[0]])
+        arrived_sums(got)
+        carry_sums(("s", layer), parts_s)
+        entry_of = lambda row: jnp.stack([row[:split], row[2 * split :]]).reshape(-1)
+        theirs = jnp.concatenate([entry_of(q_sums[1]), hidden_part[1][0]])
+        mine = jnp.concatenate([entry_of(q_sums[0]), hidden_part[0][0]])
         half_early.append(mine + grid.over_t(theirs))
         whole_early.append(
             jnp.concatenate(
-                [gain_s, gain_m, shift_s, shift_m, spatial_bias_part, down_bias_part]
+                [vec_s[1], vec_m[1], vec_s[2], vec_m[2], vec_s[0], vec_m[0]]
                 + [squares[layer], jnp.zeros((124,), F32)]
             )
         )
-        r = rows(upstream).astype(BF)
-        mixing_bias_part = row_total(r)
-        back_joined = dot_nt(r, w["mixing"]).astype(BF)
-        merge_bias_part = row_total(back_joined)
-        back_mine, back_away = [
-            cube(dot_nn(back_joined, w["merge_t"][i]).astype(BF)) for i in range(2)
-        ]
-        back_mixed = jnp.concatenate([back_mine, grid.over_t(back_away)], axis=0)
-        mix_part = dot_tn(kept["joined"], r).reshape(-1, 2, half_rows, width)
-
-        def mix_half(i, mix_part=mix_part):
-            chosen = grid.t if i == 0 else 1 - grid.t
-            half = lax.dynamic_index_in_dim(mix_part, chosen, 1, keepdims=False)
-            return pack_mix(half).reshape(width, width // 2)
-
-        parts_o = [
-            join(lambda i: dot_tn(back_joined, rows(kept["mixed_t"][i]))),
-            join(mix_half),
-        ]
-        if grid.direct:
-            (back_qkv,), sums["s", layer] = sum_rows(
-                grid,
-                2 + layer,
-                parts_s,
-                functools.partial(temporal_back_payload, scale),
-                [kept["qkv_t"], back_mixed],
-                [jax.ShapeDtypeStruct(kept["qkv_t"].shape, BF)],
-            )
-        else:
-            back_qkv = temporal_call([kept["qkv_t"], back_mixed], 3 * split, scale, True)
-            sums["s", layer] = plain_sums(parts_s)
-        parts_t = [dot_tn(rows(kept["normed_t"]), rows(back_qkv)).astype(BF)] + parts_o
-        if grid.direct:
-            sums["t", layer] = sum_rows(grid, 4 + layer, parts_t)[1]
-        else:
-            sums["t", layer] = plain_sums(parts_t)
-        qkv_sum = row_total(back_qkv)
-        entry_t_part = jnp.stack([qkv_sum[:split], qkv_sum[2 * split :]])
-        back_own = dot_nt(rows(back_qkv[:frames_here]), w["triple_t"])
-        back_oth = dot_nt(rows(back_qkv[frames_here:]), w["triple_t"]).astype(BF)
-        back_normed = cube(back_own + grid.over_t(back_oth).astype(F32))
-        back_state, gain_t, shift_t = norm_backward(
-            back_normed, kept["unit_t"], kept["scale_t"], gain[0]
+        upstream, vec_t, q_sums, parts_t, got = temporal_back(
+            grid, 4 + layer, upstream, kept, gain[0], w, carried_parts(), scale
         )
-        upstream = upstream + back_state
-        late_whole = jnp.concatenate([gain_t, shift_t, merge_bias_part, mixing_bias_part])
-        late_half = entry_t_part.reshape(-1)
+        arrived_sums(got)
+        mix_part = parts_t[2].reshape(-1, 2, half_rows, width)
+        mix_mine = lax.dynamic_index_in_dim(mix_part, grid.t, 1, keepdims=False)
+        mix_theirs = lax.dynamic_index_in_dim(mix_part, 1 - grid.t, 1, keepdims=False)
+        mix_got = grid.over_t(mix_theirs.astype(BF)).astype(F32)
+        mix_sum = pack_mix((mix_mine + mix_got).astype(BF)).reshape(width, width // 2)
+        carry_sums(("t", layer), [parts_t[0], parts_t[1], mix_sum])
+        late_whole = jnp.concatenate([vec_t[2], vec_t[3], vec_t[1], vec_t[0]])
+        late_half = entry_of(q_sums[0])
         if layer > 0:
             whole_early.append(late_whole)
             half_early.append(late_half)
@@ -969,6 +1316,8 @@
             early = add_up(whole_early, half_early)
             late = add_up([late_whole], [late_half])
 
+    if waiting:
+        arrived_sums(tail_sums(grid, 6, carried_parts()))
     input_grad = spread_out(upstream.astype(BF)).astype(F32)
     for layer in range(LAYERS):
         shards[layer] = [

time: 1030 us -> 847 us (0.82)
  matrix products: 273 us -> 94 us
  Pallas kernels: 347 us -> 410 us
  other arithmetic: 104 us -> 82.7 us
  waiting for transfers between devices: 113 us -> 92 us
    dot_general x24 -> x0, matrix products: 87.8 us -> none  [dot_tn(): lax.dot_general(left, right, (((0,), (0,)), ((), ())), preferred_element_...]
    pallas_call x6 -> x7, Pallas kernels: 289 us -> 354 us  [the longest x2 130 us: spatial_back(): pl.pallas_call(functools.partial(spatial_back_body, grid.depth, len(parts...]
    dot_general x26 -> x12, matrix products: 88.3 us -> 36.7 us  [dot_nt(): lax.dot_general(left, right, (((1,), (1,)), ((), ())), preferred_element_...]
    dot_general x24 -> x12, matrix products: 97.2 us -> 57.3 us  [dot_nn(): lax.dot_general(left, right, (((1,), (0,)), ((), ())), preferred_element_...]
    ppermute x88 -> x74, waiting for transfers between devices: 113 us -> 92 us  [send(): return lax.ppermute(value, AXES, pairs)]
    reduce_sum x11 -> x1, other arithmetic: 18.9 us -> 6.38 us  [per_device(): jnp.sum(jnp.square(item) * valid_here)]
    convert_element_type x2, other arithmetic: 13.5 us -> 2.03 us  [per_device(): input_grad = spread_out(upstream.astype(BF)).astype(F32)]
    unnamed x557 -> x259, local copies, waits for them, and re-layouts: 31.5 us -> 20.8 us
  transfers between devices with their start and end apart: 88 -> 74, of which waited for: 25 -> 22; matrix products, arithmetic and copies ran while one was open for 35% -> 27% of each run, Pallas kernels for 13% -> 48%
where the time goes in v3:
time: 847 us; the launch traced here: 837 us
  Pallas kernels  410 us (48%)
  matrix products  94 us (11%)
  waiting for transfers between devices  92 us (11%)
  local copies, waits for them, and re-layouts  85.8 us (10%)
  other arithmetic  82.7 us (10%)
  starting transfers between devices  68.3 us (8%)
    pallas_call x2, Pallas kernels, spatial_back(): pl.pallas_call(functools.partial(spatial_back_body, grid.depth, len(parts...  130 us
    pallas_call x2, Pallas kernels, temporal_back(): pl.pallas_call(functools.partial(temporal_back_body, grid.depth, len(part...  96.9 us
    pallas_call x2, Pallas kernels, feed_back(): pl.pallas_call(functools.partial(feed_back_body, grid.depth, len(parts),...  92.2 us
    ppermute x74, waiting for transfers between devices, send(): return lax.ppermute(value, AXES, pairs)  92 us
    ppermute x74, starting transfers between devices, send(): return lax.ppermute(value, AXES, pairs)  68.3 us
    dot_general x12, matrix products, dot_nn(): lax.dot_general(left, right, (((1,), (0,)), ((), ())), preferred_element_...  57.3 us
    dot_general x12, matrix products, dot_nt(): lax.dot_general(left, right, (((1,), (1,)), ((), ())), preferred_element_...  36.7 us
    pallas_call x1, Pallas kernels, tail_sums(): pl.pallas_call(functools.partial(tail_body, grid.depth, len(parts)), in_s...  35.1 us
  transfers between devices with their start and end apart: 74, of which 22 were waited for; matrix products, arithmetic and copies ran while one was open for 27% of the time, Pallas kernels for 48%

profile of v3, /device:TPU:0, one launch (start us, length us, event | category | flops | bytes accessed | tf_op | source)
XLA Modules:
  0.0 837.1 jit_solution(13516009712189306143)
XLA Ops:
  1.7 5.1 collective-permute-start.5
  24.0 3.1 collective-permute-start.35
  32.7 8.6 %collective-permute-done.6.xn = bf16[4,48,1152]{2,1,0:T(8,128)(2,1)S(1)} collective-permute-done((bf16[4,48,1152]{2,1,0:T(8,128)(2,1)S(1)}, bf16[4,48,1152]{2,1,0:T(8,128)(2,1)S(1)}, u32[]{:S(2)}, u32[]{:S(2)}) %collective-permute-start.6) | collective-permute-done | bytes 442400 | tf_op jit(solution)/shard_map/ppermute | solution.py:240
  47.3 2.3 subtract_multiply_fusion.5
  51.8 10.7 %collective-permute-done.11 = bf16[48,2304]{1,0:T(8,128)(2,1)S(1)} collective-permute-done((bf16[48,2304]{1,0:T(8,128)(2,1)S(1)}, bf16[48,2304]{1,0:T(8,128)(2,1)S(1)}, u32[]{:S(2)}, u32[]{:S(2)}) %collective-permute-start.11) | collective-permute-done | bytes 221216 | tf_op jit(solution)/shard_map/ppermute | solution.py:240
  65.2 3.5 collective-permute-done.9.db
  73.8 2.8 collective-permute-done.34
  76.6 3.1 collective-permute-done.33
  82.7 5.3 collective-permute-done.13.xn
  89.8 5.0 fusion
  100.1 11.8 %temporal_mix.2 = bf16[8,208,384]{2,1,0:T(8,128)(2,1)} custom-call(bf16[8,208,1152]{2,1,0:T(8,128)(2,1)} %bitcast.351), custom_call_target="tpu_custom_call" | custom-call | flops 5234491392 | bytes 7667712 | tf_op jit(solution)/shard_map/temporal_mix/pallas_call | solution.py:203
  113.4 4.3 place_rows.6
  131.0 3.3 fusion.18
  134.3 13.6 %collective-permute-done.26.xn = bf16[4,48,3072]{2,1,0:T(8,128)(2,1)S(1)} collective-permute-done((bf16[4,48,3072]{2,1,0:T(8,128)(2,1)S(1)}, bf16[4,48,3072]{2,1,0:T(8,128)(2,1)S(1)}, u32[]{:S(2)}, u32[]{:S(2)}) %collective-permute-start.26) | collective-permute-done | bytes 1179680 | tf_op jit(solution)/shard_map/ppermute | solution.py:240
  151.5 3.3 fusion.19
  154.9 8.1 spatial_mix.2
  166.4 4.0 collective-permute-start.45
  175.8 3.2 place_rows.7
  181.3 3.6 fusion.48
  186.2 2.4 collective-permute-start.43
  189.5 5.5 fusion.17
  195.2 2.2 convert_element_type.169
  200.5 8.2 collective-permute-done.44
  212.5 10.5 %collective-permute-done.38.da = bf16[2,48,1920]{2,1,0:T(8,128)(2,1)S(1)} collective-permute-done((bf16[2,48,1920]{2,1,0:T(8,128)(2,1)S(1)}, bf16[2,48,1920]{2,1,0:T(8,128)(2,1)S(1)}, u32[]{:S(2)}, u32[]{:S(2)}) %collective-permute-start.38) | collective-permute-done | bytes 368672 | tf_op jit(solution)/shard_map/ppermute | solution.py:240
  226.3 6.9 fusion.13
  233.2 4.8 fusion.73
  238.0 6.3 fusion.47
  244.5 6.4 multiply_reduce_fusion
  251.0 7.0 add_convert_fusion.1
  268.9 2.3 place_rows.8
  271.2 2.4 fusion.54
  273.7 2.6 broadcast_select_fusion.3
  278.4 2.2 slice.940
  282.6 5.2 fusion.1
  287.7 11.8 %temporal_mix.3 = bf16[8,208,384]{2,1,0:T(8,128)(2,1)} custom-call(bf16[8,208,1152]{2,1,0:T(8,128)(2,1)} %bitcast.353), custom_call_target="tpu_custom_call" | custom-call | flops 5234491392 | bytes 7667712 | tf_op jit(solution)/shard_map/temporal_mix/pallas_call | solution.py:203
  299.6 2.6 fusion.50
  304.8 4.7 add_convert_fusion
  315.3 9.2 %collective-permute-done.48.da = bf16[2,48,4608]{2,1,0:T(8,128)(2,1)S(1)} collective-permute-done((bf16[2,48,4608]{2,1,0:T(8,128)(2,1)}, bf16[2,48,4608]{2,1,0:T(8,128)(2,1)S(1)}, u32[]{:S(2)}, u32[]{:S(2)}) %collective-permute-start.48) | collective-permute-done | bytes 884768 | tf_op jit(solution)/shard_map/ppermute | solution.py:240
  324.7 5.9 place_rows.9
  330.7 2.2 add_convert_fusion.7.refs_2_
  333.0 2.7 fusion.45
  338.1 4.8 fusion.20
  343.0 4.8 fusion.21
  347.7 8.3 spatial_mix.3
  358.2 3.4 fusion.44
  361.7 2.3 multiply_reduce_fusion.8
  365.2 6.9 fusion.9
  372.1 7.8 fusion.5
  379.9 4.8 fusion.76
  384.8 3.6 multiply_reduce_fusion.4
  388.4 3.8 add_convert_fusion.2
  395.0 39.2 %feed_back.2 = (f32[4,208,768]{2,1,0:T(8,128)}, f32[8,768]{1,0:T(8,128)}, bf16[768,1536]{1,0:T(8,128)(2,1)}, bf16[768,1536]{1,0:T(8,128)(2,1)}, f32[1,1536]{1,0:T(1,128)}, /*index=5*/f32[1,1536]{1,0:T(1,128)}) custom-call(f32[4,208,768]{2,1,0:T(8,128)} %get-tuple-element.438.refs_0_, bf16[4,208,768]{2,1,0:T(8,128)(2,1)} %get-tuple-element.313.refs_1_, ...), custom_call_target="tpu_custom_call" | custom-call | flops 24000000000 | bytes 30000000 | tf_op jit(solution)/shard_map/feed_back/pallas_call | solution.py:708
  434.1 67.4 %spatial_stage.2 = (f32[4,208,768]{2,1,0:T(8,128)}, f32[8,768]{1,0:T(8,128)}, f32[8,1152]{1,0:T(8,128)}, bf16[768,1152]{1,0:T(8,128)(2,1)}, bf16[768,384]{1,0:T(...) custom-call(s32[1]{0:T(128)} %bitcast.33.count_ref.refs_0_, f32[4,208,768]{2,1,0:T(8,128)} %get-tuple-element.127.refs_1_, ...), custom_call_target="tpu_custom_call" | custom-call | flops 24000000000 | bytes 30000000 | tf_op jit(solution)/shard_map/spatial_stage/pallas_call | solution.py:835
  501.5 47.6 %temporal_stage.2 = (f32[4,208,768]{2,1,0:T(8,128)}, f32[8,768]{1,0:T(8,128)}, f32[8,1152]{1,0:T(8,128)}, bf16[768,1152]{1,0:T(8,128)(2,1)}, bf16[768,384]{1,0:T...) custom-call(f32[4,208,768]{2,1,0:T(8,128)} %get-tuple-element.130.refs_0_, ...), custom_call_target="tpu_custom_call" | custom-call | flops 24000000000 | bytes 30000000 | tf_op jit(solution)/shard_map/temporal_stage/pallas_call | solution.py:966
  558.9 53.0 %feed_back.3 = (f32[4,208,768]{2,1,0:T(8,128)}, f32[8,768]{1,0:T(8,128)}, bf16[768,1536]{1,0:T(8,128)(2,1)}, bf16[768,1536]{1,0:T(8,128)(2,1)}, f32[1,1536]{1,0:...) custom-call(f32[4,208,768]{2,1,0:T(8,128)} %get-tuple-element.133.refs_0_, ...), custom_call_target="tpu_custom_call" | custom-call | flops 24000000000 | bytes 30000000 | tf_op jit(solution)/shard_map/feed_back/pallas_call | solution.py:708
  612.0 62.2 %spatial_stage.3 = (f32[4,208,768]{2,1,0:T(8,128)}, f32[8,768]{1,0:T(8,128)}, f32[8,1152]{1,0:T(8,128)}, bf16[768,1152]{1,0:T(8,128)(2,1)}, bf16[768,384]{1,0:T(...) custom-call(s32[1]{0:T(128)} %bitcast.33.count_ref.refs_0_, f32[4,208,768]{2,1,0:T(8,128)} %get-tuple-element.137.refs_1_, ...), custom_call_target="tpu_custom_call" | custom-call | flops 24000000000 | bytes 30000000 | tf_op jit(solution)/shard_map/spatial_stage/pallas_call | solution.py:835
  674.2 49.3 %temporal_stage.3 = (f32[4,208,768]{2,1,0:T(8,128)}, f32[8,768]{1,0:T(8,128)}, f32[8,1152]{1,0:T(8,128)}, bf16[768,1152]{1,0:T(8,128)(2,1)}, bf16[768,384]{1,0:T...) custom-call(f32[4,208,768]{2,1,0:T(8,128)} %get-tuple-element.140.refs_0_, ...), custom_call_target="tpu_custom_call" | custom-call | flops 24000000000 | bytes 30000000 | tf_op jit(solution)/shard_map/temporal_stage/pallas_call | solution.py:966
  730.4 5.1 concatenate.183
  738.1 2.2 fusion.26
  761.1 3.0 collective-permute-start.65
  770.0 4.7 collective-permute-done.72
  781.4 35.1 %sum_rows.1 = (f32[48,1152]{1,0:T(8,128)}, f32[48,384]{1,0:T(8,128)}, f32[48,384]{1,0:T(8,128)}) custom-call(bf16[4,2,2,48,1152]{4,3,2,1,0:T(8,128)(2,1)} %bitcast.375, bf16[4,2,2,48,384]{4,3,2,1,0:T(8,128)(2,1)} %bitcast.379, bf16[4,2,2,48,384]{4,3,2,1,0:T(8,128)(2,1)} %bitcast.331), custom_call_target="tpu_custom_call" | custom-call | flops 20000000000 | bytes 30000000 | tf_op jit(solution)/shard_map/sum_rows/pallas_call | solution.py:574
  828.8 4.1 collective-permute-done.60
  834.4 2.4 copy.89
  (619 shorter events, 188.7 us)
Async XLA Ops:
  1.7 25.8 %collective-permute-start.5 = (bf16[48,1152]{1,0:T(8,128)(2,1)S(1)}, bf16[48,1152]{1,0:T(8,128)(2,1)}, u32[]{:S(2)}, u32[]{:S(2)}) collective-permute-start(bf16[48,1152]{1,0:T(8,128)(2,1)S(1)} %pad_maximum_fusion.22), channel_id=1, source_target_pairs={{0,24},{1,25},{2,26},{3,27},{4,28},{5,29},{6,30},{7,31},{8,0},{9,1... | collective-permute-start | bytes 331784 | tf_op jit(solution)/shard_map/ppermute | solution.py:240
  6.8 20.8 %collective-permute-start.4 = (bf16[48,1152]{1,0:T(8,128)(2,1)S(1)}, bf16[48,1152]{1,0:T(8,128)(2,1)}, u32[]{:S(2)}, u32[]{:S(2)}) collective-permute-start(bf16[48,1152]{1,0:T(8,128)(2,1)S(1)} %pad_maximum_fusion.22), channel_id=1, source_target_pairs={{0,16},{1,17},{2,18},{3,19},{4,20},{5,21},{6,22},{7,23},{8,24},{9,... | collective-permute-start | bytes 331784 | tf_op jit(solution)/shard_map/ppermute | solution.py:240
  6.8 20.8 %collective-permute-start.3 = (bf16[48,1152]{1,0:T(8,128)(2,1)S(1)}, bf16[48,1152]{1,0:T(8,128)(2,1)}, u32[]{:S(2)}, u32[]{:S(2)}) collective-permute-start(bf16[48,1152]{1,0:T(8,128)(2,1)S(1)} %pad_maximum_fusion.22), channel_id=1, source_target_pairs={{0,8},{1,9},{2,10},{3,11},{4,12},{5,13},{6,14},{7,15},{8,16},{9,17... | collective-permute-start | bytes 331784 | tf_op jit(solution)/shard_map/ppermute | solution.py:240
  9.5 14.6 %collective-permute-start = (bf16[4,98,768]{2,0,1:T(4,128)(2,1)S(1)}, bf16[4,98,768]{2,0,1:T(4,128)(2,1)S(1)}, u32[]{:S(2)}, u32[]{:S(2)}) collective-permute-start(bf16[4,98,768]{2,0,1:T(4,128)(2,1)S(1)} %get-tuple-element.332), channel_id=1, source_target_pairs={{0,2},{1,3},{2,0},{3,1},{4,6},{5,7},{6,4},{7,5},{8,10},{9,11},{10,... | collective-permute-start | bytes 1806344 | tf_op jit(solution)/shard_map/ppermute | solution.py:240
  11.7 57.6 %collective-permute-start.21 = (f32[4608]{0:T(1024)}, f32[4608]{0:T(1024)}, u32[]{:S(2)}, u32[]{:S(2)}) collective-permute-start(f32[4608]{0:T(1024)} %pad_maximum_fusion.33), channel_id=1, source_target_pairs={{0,1},{1,0},{2,3},{3,2},{4,5},{5,4},{6,7},{7,6},{8,9},{9,8},{10,11... | collective-permute-start | bytes 55304 | tf_op jit(solution)/shard_map/ppermute | solution.py:240
  24.0 48.3 %collective-permute-start.35 = (bf16[48,1920]{1,0:T(8,128)(2,1)}, bf16[48,1920]{1,0:T(8,128)(2,1)S(1)}, u32[]{:S(2)}, u32[]{:S(2)}) collective-permute-start(bf16[48,1920]{1,0:T(8,128)(2,1)} %maximum_dynamic-update-slice_fusion.1), channel_id=1, source_target_pairs={{0,24},{1,25},{2,26},{3,27},{4,28},{5,29},{6,30},{7,31},{8,0},{9,1... | collective-permute-start | bytes 552968 | tf_op jit(solution)/shard_map/ppermute | solution.py:240
  27.5 15.9 %collective-permute-start.1 = (bf16[4,98,768]{2,0,1:T(4,128)(2,1)S(1)}, bf16[4,98,768]{2,0,1:T(4,128)(2,1)S(1)}, u32[]{:S(2)}, u32[]{:S(2)}) collective-permute-start(bf16[4,98,768]{2,0,1:T(4,128)(2,1)S(1)} %copy.59), channel_id=1, source_target_pairs={{0,1},{1,0},{2,3},{3,2},{4,5},{5,4},{6,7},{7,6},{8,9},{9,8},{10,11... | collective-permute-start | bytes 1806344 | tf_op jit(solution)/shard_map/ppermute | solution.py:240
  28.7 12.6 %collective-permute-start.6 = (bf16[4,48,1152]{2,1,0:T(8,128)(2,1)S(1)}, bf16[4,48,1152]{2,1,0:T(8,128)(2,1)S(1)}, u32[]{:S(2)}, u32[]{:S(2)}) collective-permute-start(bf16[4,48,1152]{2,1,0:T(8,128)(2,1)S(1)} %pad_maximum_fusion.18.own), channel_id=1, source_target_pairs={{0,4},{1,5},{2,6},{3,7},{4,0},{5,1},{6,2},{7,3},{8,12},{9,13},{10,... | collective-permute-start | bytes 1327112 | tf_op jit(solution)/shard_map/ppermute | solution.py:240
  30.3 12.3 %collective-permute-start.7 = (bf16[4,48,1152]{2,1,0:T(8,128)(2,1)S(1)}, bf16[4,48,1152]{2,1,0:T(8,128)(2,1)S(1)}, u32[]{:S(2)}, u32[]{:S(2)}) collective-permute-start(bf16[4,48,1152]{2,1,0:T(8,128)(2,1)S(1)} %pad_maximum_fusion.18.own), channel_id=1, source_target_pairs={{0,2},{1,3},{2,0},{3,1},{4,6},{5,7},{6,4},{7,5},{8,10},{9,11},{10,... | collective-permute-start | bytes 1327112 | tf_op jit(solution)/shard_map/ppermute | solution.py:240
  42.6 7.8 collective-permute-start.12
  43.1 19.4 %collective-permute-start.11 = (bf16[48,2304]{1,0:T(8,128)(2,1)S(1)}, bf16[48,2304]{1,0:T(8,128)(2,1)S(1)}, u32[]{:S(2)}, u32[]{:S(2)}) collective-permute-start(bf16[48,2304]{1,0:T(8,128)(2,1)S(1)} %get-tuple-element.94), channel_id=1, source_target_pairs={{0,16},{1,17},{2,18},{3,19},{4,20},{5,21},{6,22},{7,23},{8,24},{9,... | collective-permute-start | bytes 663560 | tf_op jit(solution)/shard_map/ppermute | solution.py:240
  43.5 19.7 %collective-permute-start.10 = (bf16[48,2304]{1,0:T(8,128)(2,1)S(1)}, bf16[48,2304]{1,0:T(8,128)(2,1)S(1)}, u32[]{:S(2)}, u32[]{:S(2)}) collective-permute-start(bf16[48,2304]{1,0:T(8,128)(2,1)S(1)} %get-tuple-element.94), channel_id=1, source_target_pairs={{0,8},{1,9},{2,10},{3,11},{4,12},{5,13},{6,14},{7,15},{8,16},{9,17... | collective-permute-start | bytes 663560 | tf_op jit(solution)/shard_map/ppermute | solution.py:240
  50.3 13.0 %collective-permute-start.8 = (bf16[2,48,1152]{2,1,0:T(8,128)(2,1)S(1)}, bf16[2,48,1152]{2,1,0:T(8,128)(2,1)S(1)}, u32[]{:S(2)}, u32[]{:S(2)}) collective-permute-start(bf16[2,48,1152]{2,1,0:T(8,128)(2,1)S(1)} %slice.908), channel_id=1, source_target_pairs={{0,2},{1,3},{2,0},{3,1},{4,6},{5,7},{6,4},{7,5},{8,10},{9,11},{10,... | collective-permute-start | bytes 663560 | tf_op jit(solution)/shard_map/ppermute | solution.py:240
  63.2 26.4 %collective-permute-start.2 = (bf16[4,208,768]{2,1,0:T(8,128)(2,1)S(1)}, bf16[4,208,768]{2,1,0:T(8,128)(2,1)S(1)}, u32[]{:S(2)}, u32[]{:S(2)}) collective-permute-start(bf16[4,208,768]{2,1,0:T(8,128)(2,1)S(1)} %get-tuple-element.324), channel_id=1, source_target_pairs={{0,1},{1,0},{2,3},{3,2},{4,5},{5,4},{6,7},{7,6},{8,9},{9,8},{10,11... | collective-permute-start | bytes 3833864 | tf_op jit(solution)/shard_map/ppermute | solution.py:240
  63.3 13.2 %collective-permute-start.34 = (bf16[48,1920]{1,0:T(8,128)(2,1)S(1)}, bf16[48,1920]{1,0:T(8,128)(2,1)S(1)}, u32[]{:S(2)}, u32[]{:S(2)}) collective-permute-start(bf16[48,1920]{1,0:T(8,128)(2,1)S(1)} %copy-done.62), channel_id=1, source_target_pairs={{0,16},{1,17},{2,18},{3,19},{4,20},{5,21},{6,22},{7,23},{8,24},{9,... | collective-permute-start | bytes 552968 | tf_op jit(solution)/shard_map/ppermute | solution.py:240
  68.6 19.4 %collective-permute-start.13 = (bf16[4,48,2304]{2,1,0:T(8,128)(2,1)S(1)}, bf16[4,48,2304]{2,1,0:T(8,128)(2,1)S(1)}, u32[]{:S(2)}, u32[]{:S(2)}) collective-permute-start(bf16[4,48,2304]{2,1,0:T(8,128)(2,1)S(1)} %pad_maximum_fusion.8.own), channel_id=1, source_target_pairs={{0,4},{1,5},{2,6},{3,7},{4,0},{5,1},{6,2},{7,3},{8,12},{9,13},{10,... | collective-permute-start | bytes 2654216 | tf_op jit(solution)/shard_map/ppermute | solution.py:240
  69.3 19.5 %collective-permute-start.14 = (bf16[4,48,2304]{2,1,0:T(8,128)(2,1)S(1)}, bf16[4,48,2304]{2,1,0:T(8,128)(2,1)S(1)}, u32[]{:S(2)}, u32[]{:S(2)}) collective-permute-start(bf16[4,48,2304]{2,1,0:T(8,128)(2,1)S(1)} %pad_maximum_fusion.8.own), channel_id=1, source_target_pairs={{0,2},{1,3},{2,0},{3,1},{4,6},{5,7},{6,4},{7,5},{8,10},{9,11},{10,... | collective-permute-start | bytes 2654216 | tf_op jit(solution)/shard_map/ppermute | solution.py:240
  72.4 7.3 collective-permute-start.33
  94.8 23.5 %collective-permute-start.25 = (bf16[48,3072]{1,0:T(8,128)(2,1)}, bf16[48,3072]{1,0:T(8,128)(2,1)}, u32[]{:S(2)}, u32[]{:S(2)}) collective-permute-start(bf16[48,3072]{1,0:T(8,128)(2,1)} %pad_maximum_fusion.19), channel_id=1, source_target_pairs={{0,24},{1,25},{2,26},{3,27},{4,28},{5,29},{6,30},{7,31},{8,0},{9,1... | collective-permute-start | bytes 884744 | tf_op jit(solution)/shard_map/ppermute | solution.py:240
  95.9 23.7 %collective-permute-start.24 = (bf16[48,3072]{1,0:T(8,128)(2,1)}, bf16[48,3072]{1,0:T(8,128)(2,1)}, u32[]{:S(2)}, u32[]{:S(2)}) collective-permute-start(bf16[48,3072]{1,0:T(8,128)(2,1)} %pad_maximum_fusion.19), channel_id=1, source_target_pairs={{0,16},{1,17},{2,18},{3,19},{4,20},{5,21},{6,22},{7,23},{8,24},{9,... | collective-permute-start | bytes 884744 | tf_op jit(solution)/shard_map/ppermute | solution.py:240
  95.9 23.7 %collective-permute-start.23 = (bf16[48,3072]{1,0:T(8,128)(2,1)}, bf16[48,3072]{1,0:T(8,128)(2,1)}, u32[]{:S(2)}, u32[]{:S(2)}) collective-permute-start(bf16[48,3072]{1,0:T(8,128)(2,1)} %pad_maximum_fusion.19), channel_id=1, source_target_pairs={{0,8},{1,9},{2,10},{3,11},{4,12},{5,13},{6,14},{7,15},{8,16},{9,17... | collective-permute-start | bytes 884744 | tf_op jit(solution)/shard_map/ppermute | solution.py:240
  97.4 15.9 %collective-permute-start.15 = (bf16[2,48,2304]{2,1,0:T(8,128)(2,1)}, bf16[2,48,2304]{2,1,0:T(8,128)(2,1)}, u32[]{:S(2)}, u32[]{:S(2)}) collective-permute-start(bf16[2,48,2304]{2,1,0:T(8,128)(2,1)} %slice.913), channel_id=1, source_target_pairs={{0,2},{1,3},{2,0},{3,1},{4,6},{5,7},{6,4},{7,5},{8,10},{9,11},{10,... | collective-permute-start | bytes 1327112 | tf_op jit(solution)/shard_map/ppermute | solution.py:240
  99.0 14.4 %collective-permute-start.16 = (bf16[2,48,2304]{2,1,0:T(8,128)(2,1)}, bf16[2,48,2304]{2,1,0:T(8,128)(2,1)}, u32[]{:S(2)}, u32[]{:S(2)}) collective-permute-start(bf16[2,48,2304]{2,1,0:T(8,128)(2,1)} %slice.915), channel_id=1, source_target_pairs={{0,4},{1,5},{2,6},{3,7},{4,0},{5,1},{6,2},{7,3},{8,12},{9,13},{10,... | collective-permute-start | bytes 1327112 | tf_op jit(solution)/shard_map/ppermute | solution.py:240
  113.3 11.6 %collective-permute-start.17 = (bf16[4,208,384]{2,1,0:T(8,128)(2,1)S(1)}, bf16[4,208,384]{2,1,0:T(8,128)(2,1)S(1)}, u32[]{:S(2)}, u32[]{:S(2)}) collective-permute-start(bf16[4,208,384]{2,1,0:T(8,128)(2,1)S(1)} %get-tuple-element.328), channel_id=1, source_target_pairs={{0,1},{1,0},{2,3},{3,2},{4,5},{5,4},{6,7},{7,6},{8,9},{9,8},{10,11... | collective-permute-start | bytes 1916936 | tf_op jit(solution)/shard_map/ppermute | solution.py:240
  117.7 6.2 collective-permute-start.19
  121.0 27.0 %collective-permute-start.26 = (bf16[4,48,3072]{2,1,0:T(8,128)(2,1)S(1)}, bf16[4,48,3072]{2,1,0:T(8,128)(2,1)S(1)}, u32[]{:S(2)}, u32[]{:S(2)}) collective-permute-start(bf16[4,48,3072]{2,1,0:T(8,128)(2,1)S(1)} %pad_maximum_fusion.5.own), channel_id=1, source_target_pairs={{0,4},{1,5},{2,6},{3,7},{4,0},{5,1},{6,2},{7,3},{8,12},{9,13},{10,... | collective-permute-start | bytes 3538952 | tf_op jit(solution)/shard_map/ppermute | solution.py:240
  122.4 27.0 %collective-permute-start.27 = (bf16[4,48,3072]{2,1,0:T(8,128)(2,1)S(1)}, bf16[4,48,3072]{2,1,0:T(8,128)(2,1)S(1)}, u32[]{:S(2)}, u32[]{:S(2)}) collective-permute-start(bf16[4,48,3072]{2,1,0:T(8,128)(2,1)S(1)} %pad_maximum_fusion.5.own), channel_id=1, source_target_pairs={{0,2},{1,3},{2,0},{3,1},{4,6},{5,7},{6,4},{7,5},{8,10},{9,11},{10,... | collective-permute-start | bytes 3538952 | tf_op jit(solution)/shard_map/ppermute | solution.py:240
  124.0 27.6 %collective-permute-start.20 = (bf16[768,1152]{1,0:T(8,128)(2,1)S(1)}, bf16[768,1152]{1,0:T(8,128)(2,1)S(1)}, u32[]{:S(2)}, u32[]{:S(2)}) collective-permute-start(bf16[768,1152]{1,0:T(8,128)(2,1)S(1)} %copy-done.117), channel_id=1, source_target_pairs={{0,1},{1,0},{2,3},{3,2},{4,5},{5,4},{6,7},{7,6},{8,9},{9,8},{10,11... | collective-permute-start | bytes 5308424 | tf_op jit(solution)/shard_map/ppermute | solution.py:240
  125.0 54.1 %collective-permute-start.22 = (bf16[768,384]{1,0:T(8,128)(2,1)}, bf16[768,384]{1,0:T(8,128)(2,1)}, u32[]{:S(2)}, u32[]{:S(2)}) collective-permute-start(bf16[768,384]{1,0:T(8,128)(2,1)} %get-tuple-element.102.refs_2_), channel_id=1, source_target_pairs={{0,1},{1,0},{2,3},{3,2},{4,5},{5,4},{6,7},{7,6},{8,9},{9,8},{10,11... | collective-permute-start | bytes 1769480 | tf_op jit(solution)/shard_map/ppermute | solution.py:240
  148.8 14.1 %collective-permute-start.28 = (bf16[2,48,3072]{2,1,0:T(8,128)(2,1)}, bf16[2,48,3072]{2,1,0:T(8,128)(2,1)S(1)}, u32[]{:S(2)}, u32[]{:S(2)}) collective-permute-start(bf16[2,48,3072]{2,1,0:T(8,128)(2,1)} %slice.923), channel_id=1, source_target_pairs={{0,2},{1,3},{2,0},{3,1},{4,6},{5,7},{6,4},{7,5},{8,10},{9,11},{10,... | collective-permute-start | bytes 1769480 | tf_op jit(solution)/shard_map/ppermute | solution.py:240
  150.3 13.1 %collective-permute-start.29 = (bf16[2,48,3072]{2,1,0:T(8,128)(2,1)}, bf16[2,48,3072]{2,1,0:T(8,128)(2,1)S(1)}, u32[]{:S(2)}, u32[]{:S(2)}) collective-permute-start(bf16[2,48,3072]{2,1,0:T(8,128)(2,1)} %slice.925), channel_id=1, source_target_pairs={{0,4},{1,5},{2,6},{3,7},{4,0},{5,1},{6,2},{7,3},{8,12},{9,13},{10,... | collective-permute-start | bytes 1769480 | tf_op jit(solution)/shard_map/ppermute | solution.py:240
  164.2 21.2 %collective-permute-start.36 = (bf16[4,48,1920]{2,1,0:T(8,128)(2,1)S(1)}, bf16[4,48,1920]{2,1,0:T(8,128)(2,1)S(1)}, u32[]{:S(2)}, u32[]{:S(2)}) collective-permute-start(bf16[4,48,1920]{2,1,0:T(8,128)(2,1)S(1)} %pad_maximum_fusion.9.own), channel_id=1, source_target_pairs={{0,4},{1,5},{2,6},{3,7},{4,0},{5,1},{6,2},{7,3},{8,12},{9,13},{10,... | collective-permute-start | bytes 2211848 | tf_op jit(solution)/shard_map/ppermute | solution.py:240
  164.7 23.9 %collective-permute-start.37 = (bf16[4,48,1920]{2,1,0:T(8,128)(2,1)S(1)}, bf16[4,48,1920]{2,1,0:T(8,128)(2,1)S(1)}, u32[]{:S(2)}, u32[]{:S(2)}) collective-permute-start(bf16[4,48,1920]{2,1,0:T(8,128)(2,1)S(1)} %pad_maximum_fusion.9.own), channel_id=1, source_target_pairs={{0,2},{1,3},{2,0},{3,1},{4,6},{5,7},{6,4},{7,5},{8,10},{9,11},{10,... | collective-permute-start | bytes 2211848 | tf_op jit(solution)/shard_map/ppermute | solution.py:240
  166.4 32.4 %collective-permute-start.45 = (bf16[48,4608]{1,0:T(8,128)(2,1)}, bf16[48,4608]{1,0:T(8,128)(2,1)}, u32[]{:S(2)}, u32[]{:S(2)}) collective-permute-start(bf16[48,4608]{1,0:T(8,128)(2,1)} %copy-done.53), channel_id=1, source_target_pairs={{0,24},{1,25},{2,26},{3,27},{4,28},{5,29},{6,30},{7,31},{8,0},{9,1... | collective-permute-start | bytes 1327112 | tf_op jit(solution)/shard_map/ppermute | solution.py:240
  170.5 38.2 %collective-permute-start.44 = (bf16[48,4608]{1,0:T(8,128)(2,1)}, bf16[48,4608]{1,0:T(8,128)(2,1)}, u32[]{:S(2)}, u32[]{:S(2)}) collective-permute-start(bf16[48,4608]{1,0:T(8,128)(2,1)} %copy-done.53), channel_id=1, source_target_pairs={{0,16},{1,17},{2,18},{3,19},{4,20},{5,21},{6,22},{7,23},{8,24},{9,... | collective-permute-start | bytes 1327112 | tf_op jit(solution)/shard_map/ppermute | solution.py:240
  179.1 47.3 %collective-permute-start.30 = (bf16[768,1536]{1,0:T(8,128)(2,1)}, bf16[768,1536]{1,0:T(8,128)(2,1)}, u32[]{:S(2)}, u32[]{:S(2)}) collective-permute-start(bf16[768,1536]{1,0:T(8,128)(2,1)} %get-tuple-element.108.refs_10_), channel_id=1, source_target_pairs={{0,1},{1,0},{2,3},{3,2},{4,5},{5,4},{6,7},{7,6},{8,9},{9,8},{10,11... | collective-permute-start | bytes 7077896 | tf_op jit(solution)/shard_map/ppermute | solution.py:240
  186.2 24.1 %collective-permute-start.43 = (bf16[48,4608]{1,0:T(8,128)(2,1)S(1)}, bf16[48,4608]{1,0:T(8,128)(2,1)S(1)}, u32[]{:S(2)}, u32[]{:S(2)}) collective-permute-start(bf16[48,4608]{1,0:T(8,128)(2,1)S(1)} %copy-done.54), channel_id=1, source_target_pairs={{0,8},{1,9},{2,10},{3,11},{4,12},{5,13},{6,14},{7,15},{8,16},{9,17... | collective-permute-start | bytes 1327112 | tf_op jit(solution)/shard_map/ppermute | solution.py:240
  189.4 43.8 %collective-permute-start.31 = (bf16[768,1536]{1,0:T(8,128)(2,1)}, bf16[768,1536]{1,0:T(8,128)(2,1)}, u32[]{:S(2)}, u32[]{:S(2)}) collective-permute-start(bf16[768,1536]{1,0:T(8,128)(2,1)} %get-tuple-element.109.refs_9_), channel_id=1, source_target_pairs={{0,1},{1,0},{2,3},{3,2},{4,5},{5,4},{6,7},{7,6},{8,9},{9,8},{10,11... | collective-permute-start | bytes 7077896 | tf_op jit(solution)/shard_map/ppermute | solution.py:240
  198.9 59.1 %collective-permute-start.56 = (bf16[4,98,768]{2,0,1:T(4,128)(2,1)}, bf16[4,98,768]{2,0,1:T(4,128)(2,1)}, u32[]{:S(2)}, u32[]{:S(2)}) collective-permute-start(bf16[4,98,768]{2,0,1:T(4,128)(2,1)} %get-tuple-element.330), channel_id=1, source_target_pairs={{0,2},{1,3},{2,0},{3,1},{4,6},{5,7},{6,4},{7,5},{8,10},{9,11},{10,... | collective-permute-start | bytes 1806344 | tf_op jit(solution)/shard_map/ppermute | solution.py:240
  208.7 14.3 %collective-permute-start.38 = (bf16[2,48,1920]{2,1,0:T(8,128)(2,1)S(1)}, bf16[2,48,1920]{2,1,0:T(8,128)(2,1)S(1)}, u32[]{:S(2)}, u32[]{:S(2)}) collective-permute-start(bf16[2,48,1920]{2,1,0:T(8,128)(2,1)S(1)} %slice.929), channel_id=1, source_target_pairs={{0,2},{1,3},{2,0},{3,1},{4,6},{5,7},{6,4},{7,5},{8,10},{9,11},{10,... | collective-permute-start | bytes 1105928 | tf_op jit(solution)/shard_map/ppermute | solution.py:240
  210.2 13.5 %collective-permute-start.39 = (bf16[2,48,1920]{2,1,0:T(8,128)(2,1)S(1)}, bf16[2,48,1920]{2,1,0:T(8,128)(2,1)S(1)}, u32[]{:S(2)}, u32[]{:S(2)}) collective-permute-start(bf16[2,48,1920]{2,1,0:T(8,128)(2,1)S(1)} %slice.931), channel_id=1, source_target_pairs={{0,4},{1,5},{2,6},{3,7},{4,0},{5,1},{6,2},{7,3},{8,12},{9,13},{10,... | collective-permute-start | bytes 1105928 | tf_op jit(solution)/shard_map/ppermute | solution.py:240
  224.5 51.8 %collective-permute-start.46 = (bf16[4,48,4608]{2,1,0:T(8,128)(2,1)S(1)}, bf16[4,48,4608]{2,1,0:T(8,128)(2,1)}, u32[]{:S(2)}, u32[]{:S(2)}) collective-permute-start(bf16[4,48,4608]{2,1,0:T(8,128)(2,1)S(1)} %pad_maximum_fusion.2.own), channel_id=1, source_target_pairs={{0,4},{1,5},{2,6},{3,7},{4,0},{5,1},{6,2},{7,3},{8,12},{9,13},{10,... | collective-permute-start | bytes 5308424 | tf_op jit(solution)/shard_map/ppermute | solution.py:240
  224.8 53.6 %collective-permute-start.47 = (bf16[4,48,4608]{2,1,0:T(8,128)(2,1)S(1)}, bf16[4,48,4608]{2,1,0:T(8,128)(2,1)}, u32[]{:S(2)}, u32[]{:S(2)}) collective-permute-start(bf16[4,48,4608]{2,1,0:T(8,128)(2,1)S(1)} %pad_maximum_fusion.2.own), channel_id=1, source_target_pairs={{0,2},{1,3},{2,0},{3,1},{4,6},{5,7},{6,4},{7,5},{8,10},{9,11},{10,... | collective-permute-start | bytes 5308424 | tf_op jit(solution)/shard_map/ppermute | solution.py:240
  257.9 22.7 %collective-permute-start.32 = (bf16[4,208,768]{2,1,0:T(8,128)(2,1)}, bf16[4,208,768]{2,1,0:T(8,128)(2,1)}, u32[]{:S(2)}, u32[]{:S(2)}) collective-permute-start(bf16[4,208,768]{2,1,0:T(8,128)(2,1)} %get-tuple-element.301), channel_id=1, source_target_pairs={{0,1},{1,0},{2,3},{3,2},{4,5},{5,4},{6,7},{7,6},{8,9},{9,8},{10,11... | collective-permute-start | bytes 3833864 | tf_op jit(solution)/shard_map/ppermute | solution.py:240
  260.3 13.3 %collective-permute-start.57 = (bf16[4,98,768]{2,0,1:T(4,128)(2,1)}, bf16[4,98,768]{2,0,1:T(4,128)(2,1)}, u32[]{:S(2)}, u32[]{:S(2)}) collective-permute-start(bf16[4,98,768]{2,0,1:T(4,128)(2,1)} %copy.71), channel_id=1, source_target_pairs={{0,1},{1,0},{2,3},{3,2},{4,5},{5,4},{6,7},{7,6},{8,9},{9,8},{10,11... | collective-permute-start | bytes 1806344 | tf_op jit(solution)/shard_map/ppermute | solution.py:240
  271.2 38.4 %collective-permute-start.42 = (bf16[768,384]{1,0:T(8,128)(2,1)}, bf16[768,384]{1,0:T(8,128)(2,1)}, u32[]{:S(2)}, u32[]{:S(2)}) collective-permute-start(bf16[768,384]{1,0:T(8,128)(2,1)} %get-tuple-element.115), channel_id=1, source_target_pairs={{0,1},{1,0},{2,3},{3,2},{4,5},{5,4},{6,7},{7,6},{8,9},{9,8},{10,11... | collective-permute-start | bytes 1769480 | tf_op jit(solution)/shard_map/ppermute | solution.py:240
  273.6 39.6 %collective-permute-start.41 = (bf16[768,384]{1,0:T(8,128)(2,1)}, bf16[768,384]{1,0:T(8,128)(2,1)}, u32[]{:S(2)}, u32[]{:S(2)}) collective-permute-start(bf16[768,384]{1,0:T(8,128)(2,1)} %get-tuple-element.114.refs_3_), channel_id=1, source_target_pairs={{0,1},{1,0},{2,3},{3,2},{4,5},{5,4},{6,7},{7,6},{8,9},{9,8},{10,11... | collective-permute-start | bytes 1769480 | tf_op jit(solution)/shard_map/ppermute | solution.py:240
  302.2 10.9 %collective-permute-start.40 = (bf16[4,208,384]{2,1,0:T(8,128)(2,1)}, bf16[4,208,384]{2,1,0:T(8,128)(2,1)}, u32[]{:S(2)}, u32[]{:S(2)}) collective-permute-start(bf16[4,208,384]{2,1,0:T(8,128)(2,1)} %get-tuple-element.326), channel_id=1, source_target_pairs={{0,1},{1,0},{2,3},{3,2},{4,5},{5,4},{6,7},{7,6},{8,9},{9,8},{10,11... | collective-permute-start | bytes 1916936 | tf_op jit(solution)/shard_map/ppermute | solution.py:240
  302.6 21.9 %collective-permute-start.48 = (bf16[2,48,4608]{2,1,0:T(8,128)(2,1)}, bf16[2,48,4608]{2,1,0:T(8,128)(2,1)S(1)}, u32[]{:S(2)}, u32[]{:S(2)}) collective-permute-start(bf16[2,48,4608]{2,1,0:T(8,128)(2,1)} %slice.938), channel_id=1, source_target_pairs={{0,2},{1,3},{2,0},{3,1},{4,6},{5,7},{6,4},{7,5},{8,10},{9,11},{10,... | collective-permute-start | bytes 2654216 | tf_op jit(solution)/shard_map/ppermute | solution.py:240
  303.1 21.6 %collective-permute-start.49 = (bf16[2,48,4608]{2,1,0:T(8,128)(2,1)}, bf16[2,48,4608]{2,1,0:T(8,128)(2,1)S(1)}, u32[]{:S(2)}, u32[]{:S(2)}) collective-permute-start(bf16[2,48,4608]{2,1,0:T(8,128)(2,1)} %slice.940), channel_id=1, source_target_pairs={{0,4},{1,5},{2,6},{3,7},{4,0},{5,1},{6,2},{7,3},{8,12},{9,13},{10,... | collective-permute-start | bytes 2654216 | tf_op jit(solution)/shard_map/ppermute | solution.py:240
  330.6 12.4 %collective-permute-start.50 = (bf16[768,1152]{1,0:T(8,128)(2,1)}, bf16[768,1152]{1,0:T(8,128)(2,1)}, u32[]{:S(2)}, u32[]{:S(2)}) collective-permute-start(bf16[768,1152]{1,0:T(8,128)(2,1)} %get-tuple-element.120.refs_8_), channel_id=1, source_target_pairs={{0,1},{1,0},{2,3},{3,2},{4,5},{5,4},{6,7},{7,6},{8,9},{9,8},{10,11... | collective-permute-start | bytes 5308424 | tf_op jit(solution)/shard_map/ppermute | solution.py:240
  337.5 18.6 %collective-permute-start.51 = (bf16[768,384]{1,0:T(8,128)(2,1)S(1)}, bf16[768,384]{1,0:T(8,128)(2,1)}, u32[]{:S(2)}, u32[]{:S(2)}) collective-permute-start(bf16[768,384]{1,0:T(8,128)(2,1)S(1)} %copy-done.9), channel_id=1, source_target_pairs={{0,1},{1,0},{2,3},{3,2},{4,5},{5,4},{6,7},{7,6},{8,9},{9,8},{10,11... | collective-permute-start | bytes 1769480 | tf_op jit(solution)/shard_map/ppermute | solution.py:240
  337.6 34.5 %collective-permute-start.52 = (bf16[768,1536]{1,0:T(8,128)(2,1)}, bf16[768,1536]{1,0:T(8,128)(2,1)}, u32[]{:S(2)}, u32[]{:S(2)}) collective-permute-start(bf16[768,1536]{1,0:T(8,128)(2,1)} %get-tuple-element.124.refs_10_), channel_id=1, source_target_pairs={{0,1},{1,0},{2,3},{3,2},{4,5},{5,4},{6,7},{7,6},{8,9},{9,8},{10,11... | collective-permute-start | bytes 7077896 | tf_op jit(solution)/shard_map/ppermute | solution.py:240
  338.0 41.9 %collective-permute-start.53 = (bf16[768,1536]{1,0:T(8,128)(2,1)}, bf16[768,1536]{1,0:T(8,128)(2,1)}, u32[]{:S(2)}, u32[]{:S(2)}) collective-permute-start(bf16[768,1536]{1,0:T(8,128)(2,1)} %get-tuple-element.125.refs_9_), channel_id=1, source_target_pairs={{0,1},{1,0},{2,3},{3,2},{4,5},{5,4},{6,7},{7,6},{8,9},{9,8},{10,11... | collective-permute-start | bytes 7077896 | tf_op jit(solution)/shard_map/ppermute | solution.py:240
  394.6 370.2 %collective-permute-start.54 = (bf16[4,98,768]{2,0,1:T(4,128)(2,1)}, bf16[4,98,768]{2,0,1:T(4,128)(2,1)}, u32[]{:S(2)}, u32[]{:S(2)}) collective-permute-start(bf16[4,98,768]{2,0,1:T(4,128)(2,1)} %copy.62), channel_id=1, source_target_pairs={{0,1},{1,0},{2,3},{3,2},{4,5},{5,4},{6,7},{7,6},{8,9},{9,8},{10,11... | collective-permute-start | bytes 1806344 | tf_op jit(solution)/shard_map/ppermute | solution.py:240
  726.7 94.0 %collective-permute-start.59 = (bf16[4,98,768]{2,0,1:T(4,128)(2,1)}, bf16[4,98,768]{2,0,1:T(4,128)(2,1)}, u32[]{:S(2)}, u32[]{:S(2)}) collective-permute-start(bf16[4,98,768]{2,0,1:T(4,128)(2,1)} %copy.81), channel_id=1, source_target_pairs={{0,1},{1,0},{2,3},{3,2},{4,5},{5,4},{6,7},{7,6},{8,9},{9,8},{10,11... | collective-permute-start | bytes 1806344 | tf_op jit(solution)/shard_map/ppermute | solution.py:240
  728.1 21.1 %collective-permute-start.68 = (f32[2304]{0:T(1024)}, f32[2304]{0:T(1024)}, u32[]{:S(2)}, u32[]{:S(2)}) collective-permute-start(f32[2304]{0:T(1024)} %pad_maximum_fusion.37), channel_id=1, source_target_pairs={{0,1},{1,0},{2,3},{3,2},{4,5},{5,4},{6,7},{7,6},{8,9},{9,8},{10,11... | collective-permute-start | bytes 27656 | tf_op jit(solution)/shard_map/ppermute | solution.py:240
  735.5 17.5 %collective-permute-start.66 = (f32[12544]{0:T(1024)S(1)}, f32[12544]{0:T(1024)}, u32[]{:S(2)}, u32[]{:S(2)}) collective-permute-start(f32[12544]{0:T(1024)S(1)} %concatenate.183), channel_id=1, source_target_pairs={{0,1},{1,0},{2,3},{3,2},{4,5},{5,4},{6,7},{7,6},{8,9},{9,8},{10,11... | collective-permute-start | bytes 150536 | tf_op jit(solution)/shard_map/ppermute | solution.py:240
  737.5 9.8 %collective-permute-start.61 = (f32[3072]{0:T(1024)}, f32[3072]{0:T(1024)}, u32[]{:S(2)}, u32[]{:S(2)}) collective-permute-start(f32[3072]{0:T(1024)} %pad_maximum_fusion.35), channel_id=1, source_target_pairs={{0,1},{1,0},{2,3},{3,2},{4,5},{5,4},{6,7},{7,6},{8,9},{9,8},{10,11... | collective-permute-start | bytes 36872 | tf_op jit(solution)/shard_map/ppermute | solution.py:240
  757.2 21.6 %collective-permute-start.73 = (bf16[16,24,768]{2,1,0:T(8,128)(2,1)}, bf16[16,24,768]{2,1,0:T(8,128)(2,1)}, u32[]{:S(2)}, u32[]{:S(2)}) collective-permute-start(bf16[16,24,768]{2,1,0:T(8,128)(2,1)} %fusion.26), channel_id=1, source_target_pairs={{0,1},{1,0},{2,3},{3,2},{4,5},{5,4},{6,7},{7,6},{8,9},{9,8},{10,11... | collective-permute-start | bytes 1769480 | tf_op jit(solution)/shard_map/ppermute | solution.py:240
  761.1 7.2 collective-permute-start.65
  767.2 58.5 %collective-permute-start.55 = (bf16[4,98,768]{2,0,1:T(4,128)(2,1)}, bf16[4,98,768]{2,0,1:T(4,128)(2,1)}, u32[]{:S(2)}, u32[]{:S(2)}) collective-permute-start(bf16[4,98,768]{2,0,1:T(4,128)(2,1)} %copy.65), channel_id=1, source_target_pairs={{0,2},{1,3},{2,0},{3,1},{4,6},{5,7},{6,4},{7,5},{8,10},{9,11},{10,... | collective-permute-start | bytes 1806344 | tf_op jit(solution)/shard_map/ppermute | solution.py:240
  768.6 6.1 collective-permute-start.72
  822.2 10.7 %collective-permute-start.60 = (bf16[4,98,768]{2,0,1:T(4,128)(2,1)S(1)}, bf16[4,98,768]{2,0,1:T(4,128)(2,1)S(1)}, u32[]{:S(2)}, u32[]{:S(2)}) collective-permute-start(bf16[4,98,768]{2,0,1:T(4,128)(2,1)S(1)} %copy.84), channel_id=1, source_target_pairs={{0,2},{1,3},{2,0},{3,1},{4,6},{5,7},{6,4},{7,5},{8,10},{9,11},{10,... | collective-permute-start | bytes 1806344 | tf_op jit(solution)/shard_map/ppermute | solution.py:240
  (134 other events, 1362.5 us)

commit v4 on v3

v4 whole, which is shorter than its diff:
```python
import functools
import math

import jax
import jax.numpy as jnp
from jax import lax
from jax.experimental import pallas as pl
from jax.experimental.pallas import tpu as pltpu
from jax.sharding import PartitionSpec as P

HEAD_DIM = 64
FRAMES = 8
LAYERS = 2
AXES = ("shard", "ctx", "tp")
BF = jnp.bfloat16
F32 = jnp.float32

far_below = -1000000000.0
epsilon = 1e-06
root_half = 0.7071067811865476
gauss_scale = 0.3989422804014327


def dot_nn(left, right):
    return lax.dot_general(left, right, (((1,), (0,)), ((), ())), preferred_element_type=F32)


def dot_nt(left, right):
    return lax.dot_general(left, right, (((1,), (1,)), ((), ())), preferred_element_type=F32)


def dot_tn(left, right):
    return lax.dot_general(left, right, (((0,), (0,)), ((), ())), preferred_element_type=F32)


def rows(value):
    return value.reshape(-1, value.shape[-1])


def row_total(value):
    return jnp.sum(rows(value).astype(F32), axis=0)


def lane_masks(shape):
    lane = lax.broadcasted_iota(jnp.int32, shape, 1)
    return lane < HEAD_DIM


def softmax_rows(scores):
    top = jnp.max(scores, axis=-1, keepdims=True)
    raised = jnp.exp(scores - top)
    total = jnp.sum(raised, axis=-1, keepdims=True)
    return raised * (1.0 / total)


def sides(value, first):
    zero = jnp.zeros_like(value)
    return [jnp.where(first, value, zero), jnp.where(first, zero, value)]


def heads_forward(qkv, fix, scale, put):
    first = lane_masks(qkv(0, 0).shape)
    scores = []
    for pair in range(3):
        k = qkv(1, pair)
        scores.append([dot_nt(q, k) for q in sides(qkv(0, pair), first)])
    shares = [[softmax_rows(fix(item * scale)).astype(BF) for item in both] for both in scores]
    for pair in range(3):
        v = qkv(2, pair)
        outs = [dot_nn(item, v) for item in shares[pair]]
        put(pair, jnp.where(first, outs[0], outs[1]).astype(BF))


def heads_backward(qkv, back, fix, scale, put):
    first = lane_masks(qkv(0, 0).shape)
    scores, backs = [], []
    for pair in range(3):
        k, v = qkv(1, pair), qkv(2, pair)
        scores.append([dot_nt(q, k) for q in sides(qkv(0, pair), first)])
        backs.append([dot_nt(b, v) for b in sides(back(pair), first)])
    low_shares, low_scores = [], []
    for pair in range(3):
        low_shares.append([])
        low_scores.append([])
        for side in range(2):
            shares = softmax_rows(fix(scores[pair][side] * scale))
            back_shares = backs[pair][side]
            inner = jnp.sum(back_shares * shares, axis=-1, keepdims=True)
            low_scores[pair].append((shares * (back_shares - inner)).astype(BF))
            low_shares[pair].append(shares.astype(BF))
    for pair in range(3):
        q, k, bm = qkv(0, pair), qkv(1, pair), back(pair)
        gq = [dot_nn(item, k) for item in low_scores[pair]]
        gk = [dot_tn(item, q) for item in low_scores[pair]]
        gv = [dot_tn(item, bm) for item in low_shares[pair]]
        put(0, pair, (jnp.where(first, gq[0], gq[1]) * scale).astype(BF))
        put(1, pair, (jnp.where(first, gk[0], gk[1]) * scale).astype(BF))
        put(2, pair, jnp.where(first, gv[0], gv[1]).astype(BF))


def column(part, pair):
    start = part * 384 + pair * 128
    return slice(start, start + 128)


def spatial_fix(count_ref, padded, places):
    col = lax.broadcasted_iota(jnp.int32, (padded, padded), 1)
    floor = jnp.where(col < places, far_below, 3.0 * far_below)
    allowed = col < jnp.minimum(count_ref[0], places)
    return lambda scores: jnp.where(allowed, scores, floor)


def temporal_fix(tile):
    size = FRAMES * tile
    row = lax.broadcasted_iota(jnp.int32, (size, size), 0)
    col = lax.broadcasted_iota(jnp.int32, (size, size), 1)
    same = (row & (tile - 1)) == (col & (tile - 1))
    return lambda scores: jnp.where(same, scores, 3.0 * far_below)


class Grid:
    def __init__(self):
        self.shards = lax.axis_size("shard")
        self.depth = self.shards // 2
        shard = lax.axis_index("shard")
        self.z = shard // 2
        self.x = shard % 2
        self.y = lax.axis_index("ctx")
        self.t = lax.axis_index("tp")
        self.direct = self.depth == 4

    def perm(self, move):
        pairs = []
        for z in range(self.depth):
            for x in range(2):
                for y in range(2):
                    for t in range(2):
                        tz, tx, ty, tt = move(z, x, y, t)
                        pairs.append(
                            (((z * 2 + x) * 2 + y) * 2 + t, ((tz * 2 + tx) * 2 + ty) * 2 + tt)
                        )
        return pairs

    def send(self, value, pairs):
        return lax.ppermute(value, AXES, pairs)

    def over_x(self, value):
        return self.send(value, self.perm(lambda z, x, y, t: (z, 1 - x, y, t)))

    def over_y(self, value):
        return self.send(value, self.perm(lambda z, x, y, t: (z, x, 1 - y, t)))

    def over_t(self, value):
        return self.send(value, self.perm(lambda z, x, y, t: (z, x, y, 1 - t)))

    def over_z(self, value, step):
        depth = self.depth
        return self.send(value, self.perm(lambda z, x, y, t: ((z + step) % depth, x, y, t)))

    def over_bit(self, value, bit):
        pairs = []
        for s in range(self.shards):
            for y in range(2):
                for t in range(2):
                    pairs.append(((s * 2 + y) * 2 + t, ((s ^ bit) * 2 + y) * 2 + t))
        return self.send(value, pairs)

    def total(self, value, across):
        if across:
            value = value + self.over_t(value)
        value = value + self.over_y(value)
        bit = 1
        while bit < self.shards:
            value = value + self.over_bit(value, bit)
            bit *= 2
        return value


class Sums:
    def __init__(self, place, source, part, own, ra, rb, sx, sy, rx, ry, low, gz, send, recv):
        self.place, self.source, self.part, self.own = place, source, part, own
        self.ra, self.rb, self.sx, self.sy = ra, rb, sx, sy
        self.rx, self.ry, self.low, self.gz = rx, ry, low, gz
        self.send, self.recv = send, recv
        self.depth = part.shape[0]
        self.half = part.shape[0] // 2

    def copy(self, number, src, dst, target):
        return remote(src, dst, self.send.at[number], self.recv.at[number], target)

    def far(self):
        x, y = self.place.x, self.place.y
        low, high = pl.ds(0, self.half), pl.ds(self.half, self.half)
        return [
            self.copy(0, self.source.at[low, 1 - x, 1 - y], self.ra, self.place.over_y()),
            self.copy(1, self.source.at[high, 1 - x, 1 - y], self.rb, self.place.over_x()),
        ]

    def near(self):
        return [
            self.copy(2, self.sx, self.rx, self.place.over_x()),
            self.copy(3, self.sy, self.ry, self.place.over_y()),
        ]

    def deep(self):
        return [
            self.copy(
                3 + k,
                self.low.at[lax.rem(self.place.z + k, self.depth)],
                self.gz.at[k - 1],
                self.place.over_z(k),
            )
            for k in range(1, self.depth)
        ]

    def first(self):
        for item in self.far():
            item.start()

    def second(self):
        x, y, half = self.place.x, self.place.y, self.half
        for item in self.far():
            item.wait()
        for k in range(2 * half):
            toward_x, toward_y = self.part[k, 1 - x, y], self.part[k, x, 1 - y]
            if k < half:
                toward_x = toward_x + self.ra[k]
            else:
                toward_y = toward_y + self.rb[k - half]
            self.sx[k] = toward_x
            self.sy[k] = toward_y
        for item in self.near():
            item.start()

    def kept(self, k):
        mine = self.part[k, self.place.x, self.place.y].astype(F32)
        return mine + self.rx[k].astype(F32) + self.ry[k].astype(F32)

    def third(self):
        for item in self.near():
            item.wait()
        for k in range(self.depth):
            mine = self.part[k, self.place.x, self.place.y]
            self.low[k] = mine + (self.rx[k] + self.ry[k])
        for item in self.deep():
            item.start()

    def last(self):
        for item in self.deep():
            item.wait()
        total = self.kept(self.place.z)
        for k in range(self.depth - 1):
            total = total + self.gz[k].astype(F32)
        self.own[...] = total


def remote(src, dst, send, recv, target):
    return pltpu.make_async_remote_copy(
        src_ref=src,
        dst_ref=dst,
        send_sem=send,
        recv_sem=recv,
        device_id=target,
        device_id_type=pl.DeviceIdType.MESH,
    )


class Place:
    def __init__(self, depth):
        self.depth = depth
        shard = lax.axis_index("shard")
        self.z = shard // 2
        self.x = lax.rem(shard, 2)
        self.y = lax.axis_index("ctx")
        self.t = lax.axis_index("tp")

    def over_x(self):
        return {"shard": self.z * 2 + 1 - self.x}

    def over_y(self):
        return {"ctx": 1 - self.y}

    def over_t(self):
        return {"tp": 1 - self.t}

    def over_z(self, step):
        return {"shard": lax.rem(self.z + step, self.depth) * 2 + self.x}

    def meet(self, chips, cores):
        barrier = pltpu.get_barrier_semaphore()
        targets = [self.over_t()] if cores else []
        if chips:
            targets += [self.over_x(), self.over_y()]
            targets += [self.over_z(k) for k in range(1, self.depth)]
        for target in targets:
            pl.semaphore_signal(
                barrier, inc=1, device_id=target, device_id_type=pl.DeviceIdType.MESH
            )
        pl.semaphore_wait(barrier, len(targets))


class Carrier:
    def __init__(self, place, cores, sources, parts, owns, scratch):
        self.place, self.cores = place, cores
        self.sums = [
            Sums(place, source, part, own, *scratch[10 * i : 10 * i + 10])
            for i, (source, part, own) in enumerate(zip(sources, parts, owns))
        ]

    def step(self, number):
        lead, rest = self.sums[:1], self.sums[1:]
        if number == 0:
            self.place.meet(bool(self.sums), self.cores)
            for item in lead + rest:
                item.first()
        elif number == 1:
            for item in lead:
                item.second()
        elif number == 2:
            for item in lead:
                item.third()
            for item in rest:
                item.second()
        elif number == 3:
            for item in rest:
                item.third()
        else:
            for item in lead + rest:
                item.last()


def carried(grid, parts):
    depth = grid.depth
    cubes, shapes, scratch = [], [], []
    for part in parts:
        step_rows, lanes = part.shape[0] // (depth * 4), part.shape[1]
        block = lambda count: pltpu.VMEM((count, step_rows, lanes), BF)
        cubes.append(part.reshape(depth, 2, 2, step_rows, lanes))
        shapes.append(jax.ShapeDtypeStruct((step_rows, lanes), F32))
        scratch += [block(depth // 2)] * 2 + [block(depth)] * 5 + [block(depth - 1)]
        scratch += [pltpu.SemaphoreType.DMA((3 + depth,))] * 2
    return cubes, shapes, scratch


def stage_params(number, vmem=58, sends=True):
    if not sends:
        return pltpu.CompilerParams(vmem_limit_bytes=vmem << 20)
    return pltpu.CompilerParams(
        collective_id=number, has_side_effects=True, vmem_limit_bytes=vmem << 20
    )


def stage_cost(flops):
    return pl.CostEstimate(flops=flops, bytes_accessed=30000000, transcendentals=0)


VMEM_SPEC = pl.BlockSpec(memory_space=pltpu.VMEM)
SMEM_SPEC = pl.BlockSpec(memory_space=pltpu.SMEM)


ANY_SPEC = pl.BlockSpec(memory_space=pl.ANY)


def is_big(item):
    return item.shape[-1] >= 128 and math.prod(item.shape) >= 65536


class Staging:
    def __init__(self, smem, ins, outs):
        self.smem = smem
        self.ins = [i >= smem and is_big(item) for i, item in enumerate(ins)]
        self.outs = [is_big(item) for item in outs]
        self.in_shapes = [item for item, big in zip(ins, self.ins) if big]
        self.out_shapes = [item for item, big in zip(outs, self.outs) if big]

    def in_specs(self):
        specs = [ANY_SPEC if big else VMEM_SPEC for big in self.ins]
        return [SMEM_SPEC] * self.smem + specs[self.smem :]

    def out_specs(self):
        return [ANY_SPEC if big else VMEM_SPEC for big in self.outs]

    def scratch(self):
        held = self.in_shapes + self.out_shapes
        blocks = [pltpu.VMEM(item.shape, item.dtype) for item in held]
        return blocks + [pltpu.SemaphoreType.DMA((len(held),))]

    def count(self):
        return len(self.in_shapes) + len(self.out_shapes) + 1

    def open(self, in_refs, out_refs, refs):
        refs = list(refs)
        sems = refs.pop()
        number = 0
        pairs = []
        for group, flags in ((in_refs, self.ins), (out_refs, self.outs)):
            view, moves = [], []
            for ref, big in zip(group, flags):
                if big:
                    moves.append((ref, refs[number], sems.at[number]))
                    ref = refs[number]
                    number += 1
                view.append(ref)
            pairs.append((view, moves))
        (self.in_view, self.in_moves), (self.out_view, self.out_moves) = pairs
        return self.in_view, self.out_view

    def fetch(self):
        copies = [pltpu.make_async_copy(src, dst, sem) for src, dst, sem in self.in_moves]
        for item in copies:
            item.start()
        for item in copies:
            item.wait()

    def flush(self):
        copies = [pltpu.make_async_copy(src, dst, sem) for dst, src, sem in self.out_moves]
        for item in copies:
            item.start()
        for item in copies:
            item.wait()


def row_of(ref, index):
    return ref.at[pl.ds(index, 1)]


def splitter(refs):
    refs = list(refs)
    return lambda count: [refs.pop(0) for _ in range(count)]


class Hops:
    def __init__(self, place, pieces, refs, total, held, came, send, recv):
        z = place.z
        targets = [place.over_t(), place.over_y(), place.over_x()]
        targets.append({"shard": (z + 1 - 2 * lax.rem(z, 2)) * 2 + place.x})
        targets.append({"shard": (z + 2 - 4 * (z // 2)) * 2 + place.x})
        self.pieces, self.refs = pieces, refs
        self.total, self.held, self.came = total, held, came
        self.copies = [
            remote(held.at[k], came.at[k], send.at[k], recv.at[k], target)
            for k, target in enumerate(targets)
        ]

    def begin(self):
        self.held[0] = jnp.zeros(self.held.shape[1:], F32)
        for ref, (start, count, row, lane) in zip(self.refs, self.pieces):
            lanes = ref.shape[1]
            self.held[0, row : row + count, lane : lane + lanes] = ref[start : start + count]
        self.copies[0].start()

    def hop(self, number):
        self.copies[number - 1].wait()
        value = self.held[number - 1] + self.came[number - 1]
        if number < len(self.copies):
            self.held[number] = value
            self.copies[number].start()
        else:
            self.total[...] = value


class Small:
    def __init__(self, width):
        self.arrays, self.pieces, self.rows, self.width = [], [], 0, width

    def add(self, array, start, count, lane=0, stay=False):
        self.arrays.append(array)
        self.pieces.append((start, count, self.rows, lane))
        if not stay:
            self.rows += count

    def shape(self):
        return jax.ShapeDtypeStruct((-(-self.rows // 8) * 8, self.width), F32)

    def plain(self):
        whole = jnp.zeros(self.shape().shape, F32)
        for array, (start, count, row, lane) in zip(self.arrays, self.pieces):
            whole = whole.at[row : row + count, lane : lane + array.shape[1]].set(
                array[start : start + count]
            )
        return lax.psum(whole, AXES)


def hop_scratch(small):
    block = pltpu.VMEM((5,) + small.shape().shape, F32)
    return [block, block] + [pltpu.SemaphoreType.DMA((5,))] * 2


def tail_body(depth, count, pieces, *refs):
    take = splitter(refs)
    parts, small, (away,) = take(count), take(len(pieces)), take(1)
    owns, (total, back) = take(count), take(2)
    hop_refs, (send, recv) = take(4), take(2)
    place = Place(depth)
    carrier = Carrier(place, True, parts, parts, owns, take(10 * count))
    hops = Hops(place, pieces, small, total, *hop_refs)
    across = remote(away, back, send.at[0], recv.at[0], place.over_y())
    carrier.step(0)
    hops.begin()
    for number in range(1, 5):
        hops.hop(number)
        if number < 4:
            carrier.step(number)
    across.start()
    hops.hop(5)
    carrier.step(4)
    across.wait()


def tail_sums(grid, number, parts, small, away):
    cubes, shapes, scratch = carried(grid, parts)
    count = len(small.arrays)
    result = pl.pallas_call(
        functools.partial(tail_body, grid.depth, len(parts), small.pieces),
        in_specs=[VMEM_SPEC] * (len(parts) + count + 1),
        out_specs=[VMEM_SPEC] * (len(parts) + 2),
        out_shape=shapes + [small.shape(), jax.ShapeDtypeStruct(away.shape, away.dtype)],
        scratch_shapes=hop_scratch(small) + [pltpu.SemaphoreType.DMA((1,))] * 2 + scratch,
        compiler_params=stage_params(number),
        cost_estimate=stage_cost(20000000000),
        name="sum_rows",
    )(*cubes, *small.arrays, away)
    return result[:-2], result[-2], result[-1]


def norm_back_rows(e, unit, scale, gain):
    along = e * gain
    lanes = e.shape[-1]
    mean_along = jnp.sum(along, axis=-1, keepdims=True) * (1.0 / lanes)
    mean_unit = jnp.sum(along * unit, axis=-1, keepdims=True) * (1.0 / lanes)
    return scale * (along - mean_along - unit * mean_unit)


def column_sum(value):
    return jnp.sum(value, axis=0, keepdims=True)


def tie(value, *others):
    return lax.optimization_barrier((value, *others))[0]


class Near:
    def __init__(self, place, line, whole, other, send, recv):
        self.place, self.line, self.whole, self.other = place, line, whole, other
        self.send, self.recv = send, recv
        self.depth = line.shape[0]

    def pair(self, number, src, dst, target):
        return remote(src, dst, self.send.at[number], self.recv.at[number], target)

    def at(self, ref, dx, dy, low=0, size=None):
        x = 1 - self.place.x if dx else self.place.x
        y = 1 - self.place.y if dy else self.place.y
        return ref.at[pl.ds(low, size or self.depth), x, y]

    def sides(self):
        dst = self.at(self.whole, 0, 0)
        return [
            self.pair(0, self.line, dst, self.place.over_x()),
            self.pair(1, self.line, dst, self.place.over_y()),
        ]

    def corners(self):
        half = self.depth // 2
        first = self.at(self.whole, 1, 0, 0, half)
        second = self.at(self.whole, 0, 1, half, half)
        return [
            self.pair(2, first, first, self.place.over_y()),
            self.pair(3, second, second, self.place.over_x()),
        ]

    def swap(self, number):
        if self.other is None:
            return []
        if number == 0:
            src, dst = self.line, self.at(self.other, 0, 0)
        else:
            dx, dy = number & 1, number >> 1
            src, dst = self.at(self.whole, dx, dy), self.at(self.other, dx, dy)
        return [self.pair(4 + number, src, dst, self.place.over_t())]

    def begin(self):
        for item in self.sides() + self.swap(0) + [self.keep()]:
            item.start()

    def keep(self):
        return pltpu.make_async_copy(self.line, self.at(self.whole, 0, 0), self.send.at[8])

    def middle(self):
        for item in self.sides():
            item.wait()
        for item in self.corners() + self.swap(1) + self.swap(2):
            item.start()

    def corner_in(self):
        for item in self.corners():
            item.wait()
        for item in self.swap(3):
            item.start()

    def end(self):
        for number in range(4):
            for item in self.swap(number):
                item.wait()
        self.keep().wait()


class Deep:
    def __init__(self, place, block, line, send, recv):
        self.place, self.block, self.line, self.send, self.recv = place, block, line, send, recv

    def copies(self):
        return [
            remote(
                self.block,
                self.line.at[self.place.z],
                self.send.at[k - 1],
                self.recv.at[k - 1],
                self.place.over_z(k),
            )
            for k in range(1, self.line.shape[0])
        ]

    def begin(self):
        for item in self.copies():
            item.start()
        self.line[self.place.z] = self.block[...]

    def end(self):
        for item in self.copies():
            item.wait()


class Load:
    def __init__(self, grid, near=(), swapped=(), deep=(), across=()):
        self.depth = grid.depth
        self.swapped = list(swapped)
        self.near_count, self.deep_count = len(near), len(deep)
        self.inputs = list(near) + list(deep) + list(across)
        self.across_count = len(across)
        self.shapes, self.scratch, self.specs = [], [], []
        for line, both in zip(near, swapped):
            depth, step_rows, lanes = line.shape
            shape = jax.ShapeDtypeStruct((depth, 2, 2, step_rows, lanes), BF)
            self.shapes += [shape] * (2 if both else 1)
            self.specs += [ANY_SPEC] * (2 if both else 1)
            self.scratch += [pltpu.SemaphoreType.DMA((9,)), pltpu.SemaphoreType.DMA((8,))]
        for block in deep:
            self.shapes.append(jax.ShapeDtypeStruct((self.depth,) + block.shape, BF))
            self.specs.append(VMEM_SPEC)
            self.scratch += [pltpu.SemaphoreType.DMA((self.depth - 1,))] * 2

        for item in across:
            self.shapes.append(jax.ShapeDtypeStruct(item.shape, item.dtype))
            self.specs.append(VMEM_SPEC)
            self.scratch += [pltpu.SemaphoreType.DMA((1,))] * 2

    def results(self, arrays):
        arrays = list(arrays)
        flat = lambda item: item.reshape(-1, item.shape[-1])
        near = []
        for both in self.swapped:
            own = flat(arrays.pop(0))
            near.append((own, flat(arrays.pop(0)) if both else None))
        return near, arrays


class Loader:
    def __init__(self, place, cores, load, ins, outs, sems):
        self.place, self.cores, self.load = place, cores, load
        ins, outs, sems = list(ins), list(outs), list(sems)
        self.near = []
        for both in load.swapped:
            whole = outs.pop(0)
            other = outs.pop(0) if both else None
            self.near.append(Near(place, ins.pop(0), whole, other, sems.pop(0), sems.pop(0)))
        self.deep = [
            Deep(place, ins.pop(0), outs.pop(0), sems.pop(0), sems.pop(0))
            for _ in range(load.deep_count)
        ]
        self.across = []
        for _ in range(load.across_count):
            send, recv = sems.pop(0), sems.pop(0)
            self.across.append(
                remote(ins.pop(0), outs.pop(0), send.at[0], recv.at[0], place.over_y())
            )

    def begin(self):
        chips = bool(self.near or self.deep or self.across)
        if chips or self.cores:
            self.place.meet(chips, self.cores or bool(self.near))
        for item in self.near + self.deep:
            item.begin()
        for item in self.across:
            item.start()

    def middle(self):
        for item in self.near:
            item.middle()

    def end(self):
        for item in self.near:
            item.corner_in()
        for item in self.near:
            item.end()
        for item in self.deep:
            item.end()
        for item in self.across:
            item.wait()


def open_kernel(load, staging, refs, scratch):
    take = splitter(refs)
    in_refs = take(len(staging.ins))
    load_ins = take(len(load.inputs))
    out_refs = take(len(staging.outs))
    load_outs = take(len(load.shapes))
    scratch_refs = take(scratch)
    in_refs, out_refs = staging.open(in_refs, out_refs, take(staging.count()))
    return in_refs, out_refs, scratch_refs, (load_ins, load_outs, take(len(load.scratch)))


def kernel_call(body, number, ins, shapes, scratch, load, name, smem=0, cores=False):
    staging = Staging(smem, ins, shapes)
    result = pl.pallas_call(
        functools.partial(body, staging),
        in_specs=staging.in_specs() + [VMEM_SPEC] * len(load.inputs),
        out_specs=staging.out_specs() + load.specs,
        out_shape=list(shapes) + load.shapes,
        scratch_shapes=list(scratch) + staging.scratch() + load.scratch,
        compiler_params=stage_params(number, sends=cores or bool(load.inputs)),
        cost_estimate=stage_cost(20000000000),
        name=name,
    )(*ins, *load.inputs)
    return result[: len(shapes)], load.results(result[len(shapes) :])


def first_body(count, depth, next_count, *refs):
    take = splitter(refs)
    blocks, next_blocks = take(count), take(next_count)
    swapped = [False] + [True] * (count - 1)
    wholes = [take(2) if both else take(1) + [None] for both in swapped]
    next_lines = take(next_count)
    lines = take(count)
    place = Place(depth)
    deep = [Deep(place, blocks[i], lines[i], *take(2)) for i in range(count)]
    near = [Near(place, lines[i], *wholes[i], *take(2)) for i in range(count)]
    after = [Deep(place, next_blocks[i], next_lines[i], *take(2)) for i in range(next_count)]
    place.meet(True, True)
    for item in deep:
        item.begin()
    for one, two in zip(deep, near):
        one.end()
        two.begin()
    for item in after:
        item.begin()
    for item in near:
        item.middle()
    for item in near:
        item.corner_in()
    for item in near:
        item.end()
    for item in after:
        item.end()


def first_gather(grid, number, blocks, next_blocks):
    depth = grid.depth
    whole = lambda item: jax.ShapeDtypeStruct((depth, 2, 2) + item.shape, BF)
    line = lambda item: (depth,) + item.shape
    shapes = [whole(blocks[0])]
    for item in blocks[1:]:
        shapes += [whole(item)] * 2
    shapes += [jax.ShapeDtypeStruct(line(item), BF) for item in next_blocks]
    sems = lambda size: [pltpu.SemaphoreType.DMA((size,))] * 2
    scratch = [pltpu.VMEM(line(item), BF) for item in blocks]
    for _ in blocks:
        scratch += sems(depth - 1)
    for _ in blocks:
        scratch += [pltpu.SemaphoreType.DMA((9,)), pltpu.SemaphoreType.DMA((8,))]
    for _ in next_blocks:
        scratch += sems(depth - 1)
    arrays = list(
        pl.pallas_call(
            functools.partial(first_body, len(blocks), depth, len(next_blocks)),
            in_specs=[VMEM_SPEC] * (len(blocks) + len(next_blocks)),
            out_specs=[ANY_SPEC] * (2 * len(blocks) - 1) + [VMEM_SPEC] * len(next_blocks),
            out_shape=shapes,
            scratch_shapes=scratch,
            compiler_params=stage_params(number),
            cost_estimate=stage_cost(20000000000),
            name="first_gather",
        )(*blocks, *next_blocks)
    )
    flat = lambda item: item.reshape(-1, item.shape[-1])
    near = [(flat(arrays.pop(0)), None)]
    for _ in blocks[1:]:
        near.append((flat(arrays.pop(0)), flat(arrays.pop(0))))
    return near, arrays


def norm_rows(state, gain, shift):
    lanes = state.shape[-1]
    center = state - jnp.sum(state, axis=-1, keepdims=True) * (1.0 / lanes)
    spread = jnp.sum(center * center, axis=-1, keepdims=True) * (1.0 / lanes)
    scale = lax.rsqrt(spread + epsilon)
    unit = center * scale
    return (unit * gain + shift).astype(BF), unit, scale


def square_sum(value, valid):
    return jnp.sum(jnp.sum(value * value, axis=-1, keepdims=True) * valid, axis=0, keepdims=True)


def temporal_body(load, att_scale, layer, staging, *refs):
    ins, outs, scratch, loads = open_kernel(load, staging, refs, 3)
    state, valid, gain, shift, tri, tri_bias, merge0, merge1, merge_bias, mixing, mix_bias = ins
    out, unit, scale, normed, qkv, mine, swap, joined, sq = outs
    away, send, recv = scratch
    gain, shift = row_of(gain, 3 * layer), row_of(shift, 3 * layer)
    tri_bias = row_of(tri_bias, layer)
    merge_bias, mix_bias = row_of(merge_bias, 4 * layer), row_of(mix_bias, 4 * layer + 1)
    place = Place(load.depth)
    loader = Loader(place, True, load, *loads)
    frames, padded, width = state.shape
    loader.begin()
    staging.fetch()

    def norm_one(f, carry):
        low, u, s = norm_rows(state[f], gain[...], shift[...])
        normed[f] = low
        unit[f] = u
        scale[f] = s
        return carry

    lax.fori_loop(0, frames, norm_one, 0)
    own = normed.at[pl.ds(0, frames)]
    swap_normed = remote(
        own, normed.at[pl.ds(frames, frames)], send.at[0], recv.at[0], place.over_t()
    )
    swap_normed.start()

    def project(f, carry):
        qkv[f] = (dot_nn(normed[f], tri[...]) + tri_bias[...]).astype(BF)
        return carry

    lax.fori_loop(0, frames, project, 0)
    swap_normed.wait()
    lax.fori_loop(frames, 2 * frames, project, 0)
    tile = 16
    fix = temporal_fix(tile)

    def one(i, carry):
        at = pl.ds(pl.multiple_of(i * tile, tile), tile)

        def put(pair, value):
            cols = slice(pair * 128, pair * 128 + 128)
            both = value.reshape(2 * frames, tile, 128)
            mine[:, at, cols] = both[:frames]
            away[:, at, cols] = both[frames:]

        heads_forward(
            lambda part, pair: qkv[:, at, column(part, pair)].reshape(2 * frames * tile, 128),
            fix,
            att_scale,
            put,
        )
        return carry

    lax.fori_loop(0, padded // tile, one, 0)
    swap_mixed = remote(away, swap, send.at[1], recv.at[1], place.over_t())
    swap_mixed.start()
    loader.middle()
    swap_mixed.wait()

    def finish(f, carry):
        low = (
            dot_nt(mine[f], merge0[...]) + dot_nt(swap[f], merge1[...]) + merge_bias[...]
        ).astype(BF)
        joined[f] = low
        branch = dot_nn(low, mixing[...]) + mix_bias[...]
        out[f] = state[f] + branch
        return carry + square_sum(branch, valid[...])

    total = lax.fori_loop(0, frames, finish, jnp.zeros((1, 1), F32))
    sq[...] = jnp.broadcast_to(total, sq.shape)
    staging.flush()
    loader.end()


def temporal_stage(number, layer, state, valid, gain, shift, w, biases, load, att_scale):
    frames, padded, width = state.shape
    split = w["merge_t"][0].shape[1]
    shape = lambda dims, kind=BF: jax.ShapeDtypeStruct(dims, kind)
    ins = [state, valid, gain, shift, w["triple_t"], biases[0], *w["merge_t"], biases[1]]
    ins += [w["mixing"], biases[2]]
    return kernel_call(
        functools.partial(temporal_body, load, att_scale, layer),
        number,
        ins,
        [
            shape((frames, padded, width), F32),
            shape((frames, padded, width), F32),
            shape((frames, padded, 1), F32),
            shape((2 * frames, padded, width)),
            shape((2 * frames, padded, 3 * split)),
            shape((frames, padded, split)),
            shape((frames, padded, split)),
            shape((frames, padded, width)),
            shape((8, 128), F32),
        ],
        [pltpu.VMEM((frames, padded, split), BF)] + [pltpu.SemaphoreType.DMA((2,))] * 2,
        load,
        "temporal_forward",
        cores=True,
    )


def spatial_body(load, places, att_scale, layer, staging, *refs):
    ins, outs, scratch, loads = open_kernel(load, staging, refs, 0)
    count_ref, state, valid, gain, shift, tri0, tri1, bias0, bias1, merge0, merge1, out_bias = ins
    out, unit, scale, normed, qkv0, qkv1, mixed0, mixed1, sq = outs
    gain, shift = row_of(gain, 3 * layer + 1), row_of(shift, 3 * layer + 1)
    bias0, bias1 = row_of(bias0, layer), row_of(bias1, layer)
    out_bias = row_of(out_bias, 4 * layer + 2)
    place = Place(load.depth)
    loader = Loader(place, False, load, *loads)
    frames, padded, width = state.shape
    fix = spatial_fix(count_ref, padded, places)
    loader.begin()
    staging.fetch()

    def one(f, carry):
        low, u, s = norm_rows(state[f], gain[...], shift[...])
        normed[f] = low
        unit[f] = u
        scale[f] = s
        for tri, bias, qkv, mixed in (
            (tri0, bias0, qkv0, mixed0),
            (tri1, bias1, qkv1, mixed1),
        ):
            qkv[f] = (dot_nn(low, tri[...]) + bias[...]).astype(BF)

            def put(pair, value, mixed=mixed):
                mixed[f, :, pair * 128 : pair * 128 + 128] = value

            heads_forward(
                lambda part, pair, qkv=qkv: qkv[f, :, column(part, pair)], fix, att_scale, put
            )
        branch = dot_nt(mixed0[f], merge0[...]) + dot_nt(mixed1[f], merge1[...]) + out_bias[...]
        out[f] = state[f] + branch
        return carry + square_sum(branch, valid[...])

    cut = frames - 1
    total = lax.fori_loop(0, cut, one, jnp.zeros((1, 1), F32))
    loader.middle()
    total = lax.fori_loop(cut, frames, one, total)
    sq[...] = jnp.broadcast_to(total, sq.shape)
    staging.flush()
    loader.end()


def spatial_stage(number, layer, count_ref, state, valid, gain, shift, w, biases, load, places, att_scale):
    frames, padded, width = state.shape
    split = w["merge_s"][0].shape[1]
    shape = lambda dims, kind=BF: jax.ShapeDtypeStruct(dims, kind)
    ins = [count_ref, state, valid, gain, shift, *w["triple_s"], biases[0], biases[1]]
    ins += [*w["merge_s"], biases[2]]
    return kernel_call(
        functools.partial(spatial_body, load, places, att_scale, layer),
        number,
        ins,
        [
            shape((frames, padded, width), F32),
            shape((frames, padded, width), F32),
            shape((frames, padded, 1), F32),
            shape((frames, padded, width)),
            shape((frames, padded, 3 * split)),
            shape((frames, padded, 3 * split)),
            shape((frames, padded, split)),
            shape((frames, padded, split)),
            shape((8, 128), F32),
        ],
        [],
        load,
        "spatial_forward",
        1,
    )


def feed_body(load, layer, staging, *refs):
    ins, outs, scratch, loads = open_kernel(load, staging, refs, 0)
    state, valid, gain, shift, up0, up1, bias0, bias1, down0, down1, out_bias = ins
    out, unit, scale, normed, act0, act1, slope0, slope1, sq = outs
    gain, shift = row_of(gain, 3 * layer + 2), row_of(shift, 3 * layer + 2)
    bias0, bias1 = row_of(bias0, layer), row_of(bias1, layer)
    out_bias = row_of(out_bias, 4 * layer + 3)
    place = Place(load.depth)
    loader = Loader(place, False, load, *loads)
    frames, padded, width = state.shape
    loader.begin()
    staging.fetch()

    def one(f, carry):
        low, u, s = norm_rows(state[f], gain[...], shift[...])
        normed[f] = low
        unit[f] = u
        scale[f] = s
        branch = jnp.broadcast_to(out_bias[...], (padded, width))
        for up, bias, down, act, slope in (
            (up0, bias0, down0, act0, slope0),
            (up1, bias1, down1, act1, slope1),
        ):
            lanes = up.shape[1]
            piece = lanes // 3
            for number in range(3):
                cols = slice(number * piece, (number + 1) * piece)
                hidden = dot_nn(low, up[:, cols]) + bias[:, cols]
                below = 0.5 * (1.0 + lax.erf(hidden * root_half))
                act[f, :, cols] = (hidden * below).astype(BF)
                slope[f, :, cols] = (
                    below + hidden * gauss_scale * jnp.exp(-0.5 * hidden * hidden)
                ).astype(BF)
            branch = branch + dot_nt(act[f], down[...])
        value = state[f] + branch
        out[f] = value
        return (
            carry[0] + square_sum(branch, valid[...]),
            carry[1] + square_sum(value, valid[...]),
        )

    zero = jnp.zeros((1, 1), F32)
    cut = frames - 1
    total = lax.fori_loop(0, cut, one, (zero, zero))
    loader.middle()
    total = lax.fori_loop(cut, frames, one, total)
    sq[...] = jnp.broadcast_to(total[0], sq.shape)
    sq[0:1] = jnp.broadcast_to(total[1], (1, sq.shape[1]))
    staging.flush()
    loader.end()


def feed_stage(number, layer, state, valid, gain, shift, w, biases, load):
    frames, padded, width = state.shape
    hid = w["up"][0].shape[1]
    shape = lambda dims, kind=BF: jax.ShapeDtypeStruct(dims, kind)
    ins = [state, valid, gain, shift, *w["up"], biases[0], biases[1], *w["down"], biases[2]]
    return kernel_call(
        functools.partial(feed_body, load, layer),
        number,
        ins,
        [
            shape((frames, padded, width), F32),
            shape((frames, padded, width), F32),
            shape((frames, padded, 1), F32),
            shape((frames, padded, width)),
        ]
        + [shape((frames, padded, hid))] * 4
        + [shape((8, 128), F32)],
        [],
        load,
        "feed_forward",
    )


def feed_back_body(depth, count, steps, layer, *refs):
    take = splitter(refs)
    state, normed, unit, scale, gain = take(5)
    gain = row_of(gain, 3 * layer + 2)
    oth, own = take(4), take(4)
    parts = take(count)
    out, sums, g_up, g_down, h_own, h_oth = take(6)
    owns = take(count)
    r, rt, nt, bh, s_up, s_down, r_up, r_down, send, recv = take(10)
    place = Place(depth)
    carrier = Carrier(place, True, parts, parts, owns, take(10 * count))
    frames, padded, width = state.shape
    rows_all = frames * padded
    i = pl.program_id(0)

    @pl.when(i == 0)
    def _():
        carrier.step(0)
        sums[...] = jnp.zeros_like(sums)

        def begin(f, carry):
            low = state[f].astype(BF)
            r[f] = low
            out[f] = jnp.zeros((padded, width), F32)
            return carry + column_sum(low.astype(F32))

        sums[2:3] = lax.fori_loop(0, frames, begin, jnp.zeros((1, width), F32))
        rt[...] = r[...].reshape(rows_all, width).T
        nt[...] = normed[...].reshape(rows_all, width).T

    def work(down, up, active, slope, h_sum):
        lanes = down.shape[1]

        def one(f, carry):
            value = (dot_nn(r[f], down[...]) * slope[f].astype(F32)).astype(BF)
            bh[f] = value
            out[f] += dot_nt(value, up[...])
            return carry + column_sum(value.astype(F32))

        h_sum[...] = lax.fori_loop(0, frames, one, jnp.zeros((1, lanes), F32))
        return (
            dot_nn(nt[...], bh[...].reshape(rows_all, lanes)),
            dot_nn(rt[...], active[...].reshape(rows_all, lanes)),
        )

    def swaps(j):
        return [
            remote(s_up.at[j], r_up.at[j], send.at[0, j], recv.at[0, j], place.over_t()),
            remote(s_down.at[j], r_down.at[j], send.at[1, j], recv.at[1, j], place.over_t()),
        ]

    @pl.when(i < steps)
    def _():
        up_part, down_part = work(*oth, h_oth)
        s_up[i] = up_part.astype(BF)
        s_down[i] = down_part.astype(BF)
        for item in swaps(i):
            item.start()

    for number, at in ((1, 1), (2, 3), (3, 4)):
        if count:

            @pl.when(i == at)
            def _(number=number):
                carrier.step(number)

    @pl.when(i >= steps)
    def _():
        j = i - steps
        up_part, down_part = work(*own, h_own)
        for item in swaps(j):
            item.wait()
        g_up[...] = (up_part + r_up[j].astype(F32)).astype(BF)
        g_down[...] = (down_part + r_down[j].astype(F32)).astype(BF)

    @pl.when(i == 2 * steps - 1)
    def _():
        def finish(f, carry):
            e, u = out[f], unit[f]
            out[f] = state[f] + norm_back_rows(e, u, scale[f], gain[...])
            return (carry[0] + column_sum(e * u), carry[1] + column_sum(e))

        zero = jnp.zeros((1, width), F32)
        sums[0:1], sums[1:2] = lax.fori_loop(0, frames, finish, (zero, zero))
        carrier.step(4)


def feed_back(grid, number, layer, state, kept, gain, w, parts):
    frames, padded, width = state.shape
    hid = w["up"][0].shape[1]
    steps = 3
    lanes = hid // steps
    cubes, shapes, scratch = carried(grid, parts)
    whole = lambda item: pl.BlockSpec(
        item.shape, lambda i: (0,) * item.ndim, pipeline_mode=pl.Buffered(1)
    )
    first = lambda i: jnp.minimum(i, steps - 1)
    later = lambda i: jnp.maximum(i - steps, 0)

    def side(at):
        weight = pl.BlockSpec((width, lanes), lambda i: (0, at(i)))
        token = pl.BlockSpec((frames, padded, lanes), lambda i: (0, 0, at(i)))
        return [weight, weight, token, token]

    tokens = lambda item: item.reshape(frames, padded, hid)
    sides = [
        [w["down"][k], w["up"][k], tokens(kept["active"][k]), tokens(kept["slope"][k])]
        for k in (1, 0)
    ]
    fixed = [state, kept["normed_m"], kept["unit_m"], kept["scale_m"], gain]
    vec = lambda at: pl.BlockSpec((1, lanes), lambda i: (0, at(i)))
    result = pl.pallas_call(
        functools.partial(feed_back_body, grid.depth, len(parts), steps, layer),
        grid=(2 * steps,),
        in_specs=[whole(item) for item in fixed]
        + side(first)
        + side(later)
        + [whole(item) for item in cubes],
        out_specs=[
            pl.BlockSpec((frames, padded, width), lambda i: (0, 0, 0)),
            pl.BlockSpec((8, width), lambda i: (0, 0)),
            pl.BlockSpec((width, lanes), lambda i: (0, later(i))),
            pl.BlockSpec((width, lanes), lambda i: (0, later(i))),
            vec(later),
            vec(first),
        ]
        + [pl.BlockSpec(item.shape, lambda i: (0, 0)) for item in shapes],
        out_shape=[
            jax.ShapeDtypeStruct((frames, padded, width), F32),
            jax.ShapeDtypeStruct((8, width), F32),
            jax.ShapeDtypeStruct((width, hid), BF),
            jax.ShapeDtypeStruct((width, hid), BF),
            jax.ShapeDtypeStruct((1, hid), F32),
            jax.ShapeDtypeStruct((1, hid), F32),
        ]
        + shapes,
        scratch_shapes=[
            pltpu.VMEM((frames, padded, width), BF),
            pltpu.VMEM((width, frames * padded), BF),
            pltpu.VMEM((width, frames * padded), BF),
            pltpu.VMEM((frames, padded, lanes), BF),
        ]
        + [pltpu.VMEM((steps, width, lanes), BF)] * 4
        + [pltpu.SemaphoreType.DMA((2, steps))] * 2
        + scratch,
        compiler_params=stage_params(number),
        cost_estimate=stage_cost(24000000000),
        name="feed_back",
    )(*fixed, *sides[0], *sides[1], *cubes)
    return result[0], result[1], result[2:4], (result[4], result[5]), result[6:]


def spatial_back_body(depth, count, places, att_scale, layer, staging, *refs):
    take = splitter(refs)
    in_refs, out_refs = take(14 + count), take(5 + count)
    own_scratch, sum_scratch = take(13), take(10 * count)
    sources = in_refs[14:]
    in_refs, out_refs = staging.open(in_refs, out_refs, take(staging.count()))
    take = splitter(in_refs + out_refs + own_scratch + sum_scratch)
    (count_ref, state, merge0, merge1, mixed0, mixed1, qkv0, qkv1) = take(8)
    tri0, tri1, normed, unit, scale, gain = take(6)
    gain = row_of(gain, 3 * layer + 1)
    parts = take(count)
    out, sums, q_sums, g_tri, g_merge = take(5)
    owns = take(count)
    r, bm0, bm1, b0, b1, rt, nt, s_tri, r_tri, s_merge, r_merge, send, recv = take(13)
    place = Place(depth)
    carrier = Carrier(place, True, sources, parts, owns, take(10 * count))
    frames, padded, width = state.shape
    rows_all = frames * padded
    split = merge0.shape[1]
    fix = spatial_fix(count_ref, padded, places)
    carrier.step(0)
    staging.fetch()

    def one(f, carry):
        low = state[f].astype(BF)
        r[f] = low
        for merge, bm, src, dst in ((merge0, bm0, qkv0, b0), (merge1, bm1, qkv1, b1)):
            bm[...] = dot_nn(low, merge[...]).astype(BF)

            def put(part, pair, value, dst=dst):
                dst[f, :, column(part, pair)] = value

            heads_backward(
                lambda part, pair, src=src: src[f, :, column(part, pair)],
                lambda pair, bm=bm: bm[:, pair * 128 : pair * 128 + 128],
                fix,
                att_scale,
                put,
            )
        return carry + column_sum(low.astype(F32))

    sums[...] = jnp.zeros_like(sums)
    q_sums[...] = jnp.zeros_like(q_sums)
    half = frames // 2
    total = lax.fori_loop(0, half, one, jnp.zeros((1, width), F32))
    carrier.step(1)
    sums[2:3] = lax.fori_loop(half, frames, one, total)
    carrier.step(2)
    rt[...] = r[...].reshape(rows_all, width).T
    nt[...] = normed[...].reshape(rows_all, width).T
    flat = lambda ref, part: ref[:, :, part * split : (part + 1) * split].reshape(rows_all, split)
    swap_tri = remote(s_tri, r_tri, send.at[0], recv.at[0], place.over_t())
    swap_merge = remote(s_merge, r_merge, send.at[1], recv.at[1], place.over_t())
    s_merge[...] = dot_nn(rt[...], mixed1[...]).astype(BF)
    swap_merge.start()
    for part in range(3):
        cols = slice(part * split, (part + 1) * split)
        s_tri[:, cols] = dot_nn(nt[...], flat(b1, part)).astype(BF)
    swap_tri.start()
    carrier.step(3)

    def finish(f, carry):
        e = dot_nt(b0[f], tri0[...]) + dot_nt(b1[f], tri1[...])
        u = unit[f]
        out[f] = state[f] + norm_back_rows(e, u, scale[f], gain[...])
        return (
            carry[0] + column_sum(e * u),
            carry[1] + column_sum(e),
            carry[2] + column_sum(b0[f].astype(F32)),
            carry[3] + column_sum(b1[f].astype(F32)),
        )

    zero, wide = jnp.zeros((1, width), F32), jnp.zeros((1, 3 * split), F32)
    sums[0:1], sums[1:2], mine, theirs = lax.fori_loop(
        0, frames, finish, (zero, zero, wide, wide)
    )
    for number, value in ((0, mine), (1, theirs)):
        q_sums[number : number + 1, :split] = value[:, :split]
        q_sums[number : number + 1, split:] = value[:, 2 * split :]
    swap_merge.wait()
    g_merge[...] = (dot_nn(rt[...], mixed0[...]) + r_merge[...].astype(F32)).astype(BF)
    swap_tri.wait()
    for part in range(3):
        cols = slice(part * split, (part + 1) * split)
        mine = dot_nn(nt[...], flat(b0, part))
        g_tri[:, cols] = (mine + r_tri[:, cols].astype(F32)).astype(BF)
    carrier.step(4)
    staging.flush()


def spatial_back(grid, number, layer, count_ref, state, kept, gain, w, parts, places, att_scale):
    frames, padded, width = state.shape
    split = w["merge_s"][0].shape[1]
    cubes, shapes, scratch = carried(grid, parts)
    flat = [item.reshape(frames * padded, split) for item in kept["mixed_s"]]
    fixed = [count_ref, state, *w["merge_s"], *flat, *kept["qkv_s"], *w["triple_s"]]
    fixed += [kept["normed_s"], kept["unit_s"], kept["scale_s"], gain]
    ins = fixed + cubes
    outs = [
        jax.ShapeDtypeStruct((frames, padded, width), F32),
        jax.ShapeDtypeStruct((8, width), F32),
        jax.ShapeDtypeStruct((8, 2 * split), F32),
        jax.ShapeDtypeStruct((width, 3 * split), BF),
        jax.ShapeDtypeStruct((width, split), BF),
    ] + shapes
    staging = Staging(1, ins, outs)
    result = pl.pallas_call(
        functools.partial(
            spatial_back_body, grid.depth, len(parts), places, att_scale, layer, staging
        ),
        in_specs=staging.in_specs(),
        out_specs=staging.out_specs(),
        out_shape=outs,
        scratch_shapes=[pltpu.VMEM((frames, padded, width), BF)]
        + [pltpu.VMEM((padded, split), BF)] * 2
        + [pltpu.VMEM((frames, padded, 3 * split), BF)] * 2
        + [pltpu.VMEM((width, frames * padded), BF)] * 2
        + [pltpu.VMEM((width, 3 * split), BF)] * 2
        + [pltpu.VMEM((width, split), BF)] * 2
        + [pltpu.SemaphoreType.DMA((2,))] * 2
        + scratch
        + staging.scratch(),
        compiler_params=stage_params(number),
        cost_estimate=stage_cost(24000000000),
        name="spatial_stage",
    )(*ins)
    return result[0], result[1], result[2], result[3:5], result[5:]


def temporal_back_body(depth, count, att_scale, layer, staging, pieces, *refs):
    take = splitter(refs)
    chained = 1 if pieces else 0
    in_refs, small = take(13 + count), take(len(pieces))
    out_refs, total = take(6 + count), take(chained)
    own_scratch, sum_scratch, hop_refs = take(13), take(10 * count), take(4 * chained)
    sources = in_refs[13:]
    in_refs, out_refs = staging.open(in_refs, out_refs, take(staging.count()))
    take = splitter(in_refs + out_refs + own_scratch + sum_scratch)
    state, mixing, joined, merge0, merge1, mine, swap, qkv, tri = take(9)
    normed, unit, scale, gain = take(4)
    gain = row_of(gain, 3 * layer)
    parts = take(count)
    out, sums, q_sums, g_tri, g_merge, g_mix = take(6)
    owns = take(count)
    r, bj, away, bm, b, nt, rt, s_merge, r_merge, s_back, r_back, send, recv = take(13)
    place = Place(depth)
    carrier = Carrier(place, True, sources, parts, owns, take(10 * count))
    frames, padded, width = state.shape
    rows_all = frames * padded
    split = merge0.shape[1]
    carrier.step(0)
    hops = Hops(place, pieces, small, *total, *hop_refs) if chained else None
    if chained:
        hops.begin()
    staging.fetch()

    def begin(f, carry):
        low = state[f].astype(BF)
        r[f] = low
        value = dot_nt(low, mixing[...]).astype(BF)
        bj[f] = value
        bm[f] = dot_nn(value, merge0[...]).astype(BF)
        away[f] = dot_nn(value, merge1[...]).astype(BF)
        return (carry[0] + column_sum(low.astype(F32)), carry[1] + column_sum(value.astype(F32)))

    sums[...] = jnp.zeros_like(sums)
    q_sums[...] = jnp.zeros_like(q_sums)
    zero = jnp.zeros((1, width), F32)
    sums[3:4], sums[2:3] = lax.fori_loop(0, frames, begin, (zero, zero))
    swap_bm = remote(
        away, bm.at[pl.ds(frames, frames)], send.at[0], recv.at[0], place.over_t()
    )
    swap_bm.start()
    rt[...] = bj[...].reshape(rows_all, width).T
    s_merge[...] = dot_nn(rt[...], swap[...].reshape(rows_all, split)).astype(BF)
    swap_merge = remote(s_merge, r_merge, send.at[1], recv.at[1], place.over_t())
    swap_merge.start()
    carrier.step(1)
    if chained:
        hops.hop(1)
    rt[...] = joined[...].reshape(rows_all, width).T
    for half in range(2):
        cols = slice(half * split, (half + 1) * split)
        g_mix[:, cols] = dot_nn(rt[...], r[:, :, cols].reshape(rows_all, split))
    rt[...] = bj[...].reshape(rows_all, width).T
    swap_merge.wait()
    g_merge[...] = (dot_nn(rt[...], mine[...].reshape(rows_all, split)) + r_merge[...].astype(F32)).astype(BF)
    swap_bm.wait()
    tile = 16
    fix = temporal_fix(tile)

    def one(i, carry):
        at = pl.ds(pl.multiple_of(i * tile, tile), tile)

        def put(part, pair, value):
            b[:, at, column(part, pair)] = value.reshape(FRAMES, tile, 128)

        heads_backward(
            lambda part, pair: qkv[:, at, column(part, pair)].reshape(FRAMES * tile, 128),
            lambda pair: bm[:, at, pair * 128 : pair * 128 + 128].reshape(FRAMES * tile, 128),
            fix,
            att_scale,
            put,
        )
        return carry

    tiles = padded // tile
    lax.fori_loop(0, tiles // 3, one, 0)
    if chained:
        hops.hop(2)
    lax.fori_loop(tiles // 3, 2 * tiles // 3, one, 0)
    carrier.step(2)
    if chained:
        hops.hop(3)
    lax.fori_loop(2 * tiles // 3, tiles, one, 0)
    if chained:
        hops.hop(4)
    carrier.step(3)

    def toward(f, carry):
        s_back[f] = dot_nt(b[f + frames], tri[...]).astype(BF)
        return carry

    lax.fori_loop(0, frames, toward, 0)
    swap_back = remote(s_back, r_back, send.at[2], recv.at[2], place.over_t())
    swap_back.start()
    nt[...] = normed[...].reshape(2 * rows_all, width).T
    for part in range(3):
        cols = slice(part * split, (part + 1) * split)
        g_tri[:, cols] = dot_nn(
            nt[...], b[:, :, cols].reshape(2 * rows_all, split)
        ).astype(BF)
    swap_back.wait()

    def finish(f, carry):
        e = dot_nt(b[f], tri[...]) + r_back[f].astype(F32)
        u = unit[f]
        out[f] = state[f] + norm_back_rows(e, u, scale[f], gain[...])
        both = column_sum(b[f].astype(F32)) + column_sum(b[f + frames].astype(F32))
        return (carry[0] + column_sum(e * u), carry[1] + column_sum(e), carry[2] + both)

    sums[0:1], sums[1:2], wide = lax.fori_loop(
        0, frames, finish, (zero, zero, jnp.zeros((1, 3 * split), F32))
    )
    q_sums[0:1, :split] = wide[:, :split]
    q_sums[0:1, split:] = wide[:, 2 * split :]
    if chained:
        hops.hop(5)
    carrier.step(4)
    staging.flush()


def temporal_back(grid, number, layer, state, kept, gain, w, parts, att_scale, small=None):
    frames, padded, width = state.shape
    split = w["merge_t"][0].shape[1]
    cubes, shapes, scratch = carried(grid, parts)
    fixed = [state, w["mixing"], kept["joined"], *w["merge_t"], *kept["mixed_t"], kept["qkv_t"]]
    fixed += [w["triple_t"], kept["normed_t"], kept["unit_t"], kept["scale_t"], gain]
    ins = fixed + cubes
    outs = [
        jax.ShapeDtypeStruct((frames, padded, width), F32),
        jax.ShapeDtypeStruct((8, width), F32),
        jax.ShapeDtypeStruct((8, 2 * split), F32),
        jax.ShapeDtypeStruct((width, 3 * split), BF),
        jax.ShapeDtypeStruct((width, split), BF),
        jax.ShapeDtypeStruct((width, width), F32),
    ] + shapes
    staging = Staging(0, ins, outs)
    pieces = small.pieces if small else []
    chained = 1 if small else 0
    result = pl.pallas_call(
        functools.partial(
            temporal_back_body, grid.depth, len(parts), att_scale, layer, staging, pieces
        ),
        in_specs=staging.in_specs() + [VMEM_SPEC] * len(pieces),
        out_specs=staging.out_specs() + [VMEM_SPEC] * chained,
        out_shape=outs + ([small.shape()] if small else []),
        scratch_shapes=[pltpu.VMEM((frames, padded, width), BF)] * 2
        + [pltpu.VMEM((frames, padded, split), BF)]
        + [pltpu.VMEM((2 * frames, padded, split), BF)]
        + [pltpu.VMEM((2 * frames, padded, 3 * split), BF)]
        + [pltpu.VMEM((width, 2 * frames * padded), BF)]
        + [pltpu.VMEM((width, frames * padded), BF)]
        + [pltpu.VMEM((width, split), BF)] * 2
        + [pltpu.VMEM((frames, padded, width), BF)] * 2
        + [pltpu.SemaphoreType.DMA((3,))] * 2
        + scratch
        + (hop_scratch(small) if chained else [])
        + staging.scratch(),
        compiler_params=stage_params(number, 60),
        cost_estimate=stage_cost(24000000000),
        name="temporal_stage",
    )(*ins, *(small.arrays if small else []))
    end = 6 + len(parts)
    return result[0], result[1], result[2], result[3:6], result[6:end], result[end:]


def plain_sums(parts):
    return [
        lax.psum_scatter(part.astype(F32), ("shard", "ctx"), scatter_dimension=0, tiled=True)
        for part in parts
    ]


def split_columns(value, widths):
    outs, start = [], 0
    for width in widths:
        outs.append(value[..., start : start + width])
        start += width
    return outs


def per_device(
    video_clips,
    cotangent,
    slot_clip,
    valid_places,
    norm_gain,
    norm_bias,
    triple_weight,
    entry_bias,
    merge_weight,
    branch_bias,
    mixing_weight,
    up_weight,
    up_bias,
    down_weight,
):
    grid = Grid()
    slots, frames_here, places_here, width = video_clips.shape
    places = places_here * 2
    padded = -(-places // 16) * 16
    scale = HEAD_DIM ** (-0.5)
    step_rows = triple_weight.shape[2]
    half_rows = step_rows // 2
    own_first = grid.t == 0
    straight = grid.t == grid.y

    clip_ids = jnp.arange(valid_places.shape[0], dtype=jnp.int32)
    my_clip = lax.dynamic_index_in_dim(slot_clip, grid.y, 0, keepdims=False)
    count = jnp.sum(jnp.where(my_clip == clip_ids, valid_places, 0)).astype(jnp.int32)
    valid_here = (jnp.arange(padded, dtype=jnp.int32) < count).astype(F32)[None, :, None]
    count_ref = count.reshape(1)

    def spread_in(value):
        mine = lax.dynamic_index_in_dim(value, grid.y, 0, keepdims=False)
        theirs = lax.dynamic_index_in_dim(value, 1 - grid.y, 0, keepdims=False)
        return spread_in_last(mine, grid.over_y(theirs))

    def spread_in_last(mine, got):
        keep = jnp.where(straight, mine, got)
        send = jnp.where(straight, got, mine)
        swap = grid.over_t(send)
        low = jnp.where(own_first, keep, swap)
        high = jnp.where(own_first, swap, keep)
        gap = jnp.zeros((frames_here, padded - places, width), mine.dtype)
        return jnp.concatenate([low, high, gap], axis=1)

    def spread_first(value):
        low = value[:, :places_here]
        high = value[:, places_here:places]
        keep = jnp.where(own_first, low, high)
        send = jnp.where(own_first, high, low)
        swap = grid.over_t(send)
        return jnp.where(straight, swap, keep), jnp.where(straight, keep, swap)

    def spread_last(got, mine):
        first = jnp.where(grid.y == 0, mine, got)
        second = jnp.where(grid.y == 0, got, mine)
        return jnp.stack([first, second])

    def spread_out(value):
        away, mine = spread_first(value)
        return spread_last(grid.over_y(away), mine)

    def pack_mix(item):
        return jnp.concatenate([item[..., : width // 2], item[..., width // 2 :]], axis=-2)

    def block_triple(layer, part):
        return [triple_weight[layer, part, :, i] for i in range(3)]

    def block_out(layer):
        return [merge_weight[layer, 0].T, pack_mix(mixing_weight[layer])]

    def block_s(layer):
        return block_triple(layer, 1) + [merge_weight[layer, 1].T]

    def block_m(layer):
        return [up_weight[layer], down_weight[layer].T]

    split = triple_weight.shape[-1]
    hid = up_weight.shape[-1]
    wide_t = (3 * split, split, width // 2)
    wide_s = (3 * split, split)
    wide_m = (hid, hid)

    def unpack_mix(item):
        cube = item.reshape(-1, 2, half_rows, width // 2)
        return jnp.concatenate([cube[:, 0], cube[:, 1]], axis=-1)

    def with_other(item):
        return (item, grid.over_t(item))

    def mixing_of(both):
        mix_own, mix_oth = [unpack_mix(item) for item in both]
        return jnp.stack(
            [jnp.where(own_first, mix_own, mix_oth), jnp.where(own_first, mix_oth, mix_own)],
            axis=1,
        ).reshape(width, width)

    def blocks_of(layer, stage):
        if stage == "t":
            triple = jnp.concatenate(block_triple(layer, 0), axis=1)
            return [triple] + block_out(layer)
        if stage == "s":
            return [jnp.concatenate(block_triple(layer, 1), axis=1), merge_weight[layer, 1].T]
        return block_m(layer)

    order = [(layer, stage) for layer in range(LAYERS) for stage in "tsm"]
    gathered = [dict() for _ in range(LAYERS)]

    def settle(key, near):
        w = gathered[key[0]]
        if key[1] == "t":
            w.update(triple_t=near[0][0], merge_t=near[1], mixing=mixing_of(near[2]))
        elif key[1] == "s":
            w.update(triple_s=near[0], merge_s=near[1])
        else:
            w.update(up=near[0], down=near[1])

    def direct_gather(block):
        return lax.all_gather(block, ("shard", "ctx"), axis=0, tiled=True)

    lines = {}
    if grid.direct:
        near, lines[order[1]] = first_gather(
            grid, 7, blocks_of(*order[0]), blocks_of(*order[1])
        )
        settle(order[0], near)
    else:
        for key in order:
            settle(key, [with_other(direct_gather(item)) for item in blocks_of(*key)])

    def load_at(index):
        if not grid.direct:
            return Load(grid)
        near, swapped, deep, across = (), (), (), ()
        if index + 1 < len(order):
            near = lines[order[index + 1]]
            swapped = [not (order[index + 1][1] == "t" and i == 0) for i in range(len(near))]
        if index + 2 < len(order):
            deep = blocks_of(*order[index + 2])
        if index + 1 == len(order):
            across = [far_cotangent]
        return Load(grid, near, swapped, deep, across)

    def loaded(index, got):
        near, new_lines = got
        if index + 1 == len(order):
            lines["across"] = new_lines[0] if grid.direct else grid.over_y(far_cotangent)
            new_lines = ()
        if grid.direct and index + 1 < len(order):
            settle(order[index + 1], near)
        if grid.direct and index + 2 < len(order):
            lines[order[index + 2]] = new_lines

    small = jnp.concatenate([entry_bias[:, 1].reshape(LAYERS, -1), up_bias], axis=1)
    small_oth = grid.over_t(small)
    middle = jnp.zeros((LAYERS, split), F32)

    def query_value(both):
        return jnp.concatenate([both[:, :split], middle, both[:, split : 2 * split]], axis=1)

    gains, shifts = [item.reshape(3 * LAYERS, width) for item in (norm_gain, norm_bias)]
    biases = branch_bias.reshape(4 * LAYERS, width)
    bias_t = query_value(entry_bias[:, 0].reshape(LAYERS, -1))
    bias_s = [query_value(item) for item in (small, small_oth)]
    bias_m = [up_bias, small_oth[:, 2 * split :]]

    state = spread_in(video_clips).astype(F32)
    valid_rows = valid_here[0]
    low_cotangent = cotangent.astype(BF)
    near_cotangent = lax.dynamic_index_in_dim(low_cotangent, grid.y, 0, keepdims=False)
    far_cotangent = lax.dynamic_index_in_dim(low_cotangent, 1 - grid.y, 0, keepdims=False)
    stored = []
    squares = []
    for layer in range(LAYERS):
        w = gathered[layer]
        first = 3 * layer
        (state, unit_t, scale_t, normed_t, qkv_t, mine, swap, joined, sq_t), got = temporal_stage(
            8 + first,
            layer,
            state,
            valid_rows,
            gains,
            shifts,
            w,
            [bias_t, biases, biases],
            load_at(first),
            scale,
        )
        loaded(first, got)
        (state, unit_s, scale_s, normed_s, qkv0, qkv1, mixed0, mixed1, sq_s), got = spatial_stage(
            9 + first,
            layer,
            count_ref,
            state,
            valid_rows,
            gains,
            shifts,
            w,
            bias_s + [biases],
            load_at(first + 1),
            places,
            scale,
        )
        loaded(first + 1, got)
        (state, unit_m, scale_m, normed_m, act0, act1, slope0, slope1, sq_m), got = feed_stage(
            10 + first,
            layer,
            state,
            valid_rows,
            gains,
            shifts,
            w,
            bias_m + [biases],
            load_at(first + 2),
        )
        loaded(first + 2, got)
        squares.append((sq_t, sq_s, sq_m))
        stored.append(
            dict(
                unit_t=unit_t,
                scale_t=scale_t,
                normed_t=normed_t,
                qkv_t=qkv_t,
                mixed_t=(mine, swap),
                joined=joined,
                unit_s=unit_s,
                scale_s=scale_s,
                normed_s=normed_s,
                qkv_s=[qkv0, qkv1],
                mixed_s=[mixed0, mixed1],
                unit_m=unit_m,
                scale_m=scale_m,
                normed_m=normed_m,
                active=[act0, act1],
                slope=[slope0, slope1],
            )
        )
    upstream = spread_in_last(near_cotangent, lines["across"]).astype(F32) * valid_here
    block_output = spread_out(state.astype(BF))

    shards = [None] * LAYERS
    sums = {}
    vectors, half_rows_of = [None] * LAYERS, [None] * LAYERS
    waiting = None

    def both_cores(mine, theirs):
        return [jnp.where(own_first, mine, theirs), jnp.where(own_first, theirs, mine)]

    def carry_sums(names, parts):
        nonlocal waiting
        if not grid.direct:
            sums.update(zip(names, plain_sums(parts)))
            return
        waiting = (names, parts)

    def carried_parts():
        return waiting[1] if waiting else []

    def arrived_sums(result):
        nonlocal waiting
        if waiting:
            sums.update(zip(waiting[0], result))
        waiting = None

    for layer in range(LAYERS - 1, -1, -1):
        w, kept = gathered[layer], stored[layer]
        upstream, vec_m, parts_m, hidden_part, got = feed_back(
            grid, layer, layer, upstream, kept, gains, w, carried_parts()
        )
        arrived_sums(got)
        carry_sums([("up", layer)], parts_m[:1])
        upstream, vec_s, entry_s, parts_s, got = spatial_back(
            grid,
            2 + layer,
            layer,
            count_ref,
            upstream,
            kept,
            gains,
            w,
            carried_parts(),
            places,
            scale,
        )
        arrived_sums(got)
        carry_sums(
            [("down", layer), ("triple_s", layer), ("merge_s", layer)], [parts_m[1]] + list(parts_s)
        )
        per_row = hid // width
        hidden_rows = [item.reshape(per_row, width) for item in hidden_part]
        half_rows_of[layer] = both_cores(
            jnp.concatenate([entry_s[:1], hidden_rows[0]]),
            jnp.concatenate([entry_s[1:2], hidden_rows[1]]),
        )
        vectors[layer] = [vec_s, vec_m]
        early = None
        if layer == 0:
            early = Small(width)
            for vec_pair in vectors:
                early.add(vec_pair[0], 0, 3)
                early.add(vec_pair[1], 0, 3)
            early.add(last_vec, 0, 4)
            for item in half_rows_of:
                early.add(item[0], 0, 3)
                early.add(item[1], 0, 3)
            for item in last_half:
                early.add(item, 0, 1)
            for sq_t, sq_s, sq_m in squares:
                for place_at, (item, start) in enumerate(
                    ((sq_t, 0), (sq_s, 0), (sq_m, 1), (sq_m, 0))
                ):
                    early.add(item, start, 1, 128 * place_at, place_at < 3)
        early_rows = early
        upstream, vec_t, entry_t, parts_t, got, early = temporal_back(
            grid,
            4 + layer,
            layer,
            upstream,
            kept,
            gains,
            w,
            carried_parts(),
            scale,
            early if grid.direct else None,
        )
        arrived_sums(got)
        mix_part = parts_t[2].reshape(-1, 2, half_rows, width)
        mix_mine = lax.dynamic_index_in_dim(mix_part, grid.t, 1, keepdims=False)
        mix_theirs = lax.dynamic_index_in_dim(mix_part, 1 - grid.t, 1, keepdims=False)
        mix_got = grid.over_t(mix_theirs.astype(BF)).astype(F32)
        mix_sum = pack_mix((mix_mine + mix_got).astype(BF)).reshape(width, width // 2)
        carry_sums(
            [("triple_t", layer), ("merge_t", layer), ("mix", layer)],
            [parts_t[0], parts_t[1], mix_sum],
        )
        last_vec = vec_t
        last_half = both_cores(entry_t[:1], jnp.zeros_like(entry_t[:1]))

    small = Small(width)
    small.add(last_vec, 0, 4)
    for item in last_half:
        small.add(item, 0, 1)
    out_low, out_ready = spread_first(upstream.astype(BF))
    if waiting:
        got, small, out_got = tail_sums(grid, 6, carried_parts(), small, out_low)
        arrived_sums(got)
        (early,) = early
    else:
        small, early = small.plain(), early_rows.plain()
        out_got = grid.over_y(out_low)
    input_grad = spread_last(out_got, out_ready).astype(F32)
    names = ("triple_t", "merge_t", "mix", "triple_s", "merge_s", "up", "down")
    for layer in range(LAYERS):
        shards[layer] = [sums[name, layer] for name in names]
    block = 6 * LAYERS
    pairs = early[:block].reshape(LAYERS, 2, 3, width)
    ends = jnp.stack([small[:4], early[block : block + 4]])
    gain_sum, shift_sum = [
        jnp.concatenate([ends[:, k : k + 1], pairs[:, :, k]], axis=1) for k in range(2)
    ]
    bias_sum = jnp.concatenate([ends[:, 2:4], pairs[:, :, 2]], axis=1)
    start = block + 4
    half_sums = early[start : start + 6 * LAYERS].reshape(LAYERS, 2, 3, width)
    end_sums = jnp.stack([small[4:6], early[start + 6 * LAYERS : start + 6 * LAYERS + 2]])
    half_sums = lax.dynamic_index_in_dim(half_sums, grid.t, 1, keepdims=False)
    end_sums = lax.dynamic_index_in_dim(end_sums, grid.t, 1, keepdims=False)
    entry_sum = jnp.stack([end_sums, half_sums[:, 0]], axis=1).reshape(LAYERS, 2, 2, split)
    hidden_sum = half_sums[:, 1:].reshape(LAYERS, hid)
    start = start + 6 * LAYERS + 2
    square_sums = early[start : start + LAYERS, : 4 * 128].reshape(LAYERS, 4, 128)[:, :, 0]
    tokens = FRAMES * width * jnp.sum(valid_places).astype(F32)
    root_squares = jnp.sqrt(square_sums / tokens)

    def unpack_rows(item):
        return jnp.concatenate([item[:half_rows], item[half_rows:]], axis=-1)

    def triple_shape(item):
        return item.reshape(step_rows, 3, split)

    return (
        block_output,
        input_grad,
        gain_sum,
        shift_sum,
        jnp.stack([jnp.stack([triple_shape(s[0]), triple_shape(s[3])]) for s in shards]),
        entry_sum,
        jnp.stack([jnp.stack([s[1].T, s[4].T]) for s in shards]),
        bias_sum,
        jnp.stack([unpack_rows(s[2]) for s in shards]),
        jnp.stack([s[5] for s in shards]),
        hidden_sum,
        jnp.stack([s[6].T for s in shards]),
        root_squares,
    )


def solution(mesh):
    return jax.shard_map(
        per_device,
        mesh=mesh,
        in_specs=(
            P("shard", "ctx", "tp", None),
            P("shard", "ctx", "tp", None),
            P("shard"),
            P(),
            P(),
            P(),
            P(None, None, ("shard", "ctx"), None, "tp"),
            P(None, None, None, "tp"),
            P(None, None, "tp", ("shard", "ctx")),
            P(),
            P(None, ("shard", "ctx", "tp"), None),
            P(None, ("shard", "ctx"), "tp"),
            P(None, "tp"),
            P(None, "tp", ("shard", "ctx")),
        ),
        out_specs=(
            P("shard", "ctx", "tp", None),
            P("shard", "ctx", "tp", None),
            P(),
            P(),
            P(None, None, ("shard", "ctx"), None, "tp"),
            P(None, None, None, "tp"),
            P(None, None, "tp", ("shard", "ctx")),
            P(),
            P(None, ("shard", "ctx", "tp"), None),
            P(None, ("shard", "ctx"), "tp"),
            P(None, "tp"),
            P(None, "tp", ("shard", "ctx")),
            P(),
        ),
        check_vma=False,
    )
```

time: 847 us -> 742 us (0.88)
  Pallas kernels: 410 us -> 636 us
  matrix products: 94 us -> 0 us
  waiting for transfers between devices: 92 us -> 1.06 us
  starting transfers between devices: 68.3 us -> 6 us
  local copies, waits for them, and re-layouts: 85.8 us -> 45.4 us
  other arithmetic: 82.7 us -> 44.4 us
    pallas_call x10 -> x8, Pallas kernels: 91.6 us -> 320 us  [the longest x6 230 us: kernel_call(): pl.pallas_call(functools.partial(body, staging), in_specs=staging.in_spec...]
    dot_general x24 -> x0, matrix products: 94 us -> none  [the longest x12 57.3 us: dot_nn(): lax.dot_general(left, right, (((1,), (0,)), ((), ())), preferred_element_...]
    ppermute x74 -> x9, waiting for transfers between devices: 92 us -> 1.06 us  [send(): return lax.ppermute(value, AXES, pairs)]
    ppermute x74 -> x9, starting transfers between devices: 68.3 us -> 6 us  [send(): return lax.ppermute(value, AXES, pairs)]
    pallas_call x2, Pallas kernels: 130 us -> 94.3 us  [spatial_back(): pl.pallas_call(functools.partial(spatial_back_body, grid.depth, len(parts...]
    pallas_call x2, Pallas kernels: 96.9 us -> 130 us  [temporal_back(): pl.pallas_call(functools.partial(temporal_back_body, grid.depth, len(part...]
    slice x54 -> x10, local copies, waits for them, and re-layouts: 25.8 us -> 5.05 us  [the longest x2 1.64 us: per_device(): entry_s[:1]]
    convert_element_type x6 -> x4, other arithmetic: 19.7 us -> 4.28 us  [the longest x1 1.85 us: per_device(): block_output = spread_out(state.astype(BF))]
  transfers between devices with their start and end apart: 74 -> 9, of which waited for: 22 -> 1; matrix products, arithmetic and copies ran while one was open for 27% -> 9% of each run, Pallas kernels for 48% -> 49%
where the time goes in v4:
time: 742 us; the launch traced here: 736 us
  Pallas kernels  636 us (86%)
  local copies, waits for them, and re-layouts  45.4 us (6%)
  other arithmetic  44.4 us (6%)
    pallas_call x6, Pallas kernels, kernel_call(): pl.pallas_call(functools.partial(body, staging), in_specs=staging.in_spec...  230 us
    pallas_call x2, Pallas kernels, temporal_back(): pl.pallas_call(functools.partial(temporal_back_body, grid.depth, len(part...  130 us
    pallas_call x2, Pallas kernels, spatial_back(): pl.pallas_call(functools.partial(spatial_back_body, grid.depth, len(parts...  94.3 us
    pallas_call x2, Pallas kernels, feed_back(): pl.pallas_call(functools.partial(feed_back_body, grid.depth, len(parts),...  92.2 us
    pallas_call x1, Pallas kernels, tail_sums(): pl.pallas_call(functools.partial(tail_body, grid.depth, len(parts), small...  47.1 us
    pallas_call x1, Pallas kernels, first_gather(): pl.pallas_call(functools.partial(first_body, len(blocks), depth, len(next...  42.9 us
  transfers between devices with their start and end apart: 9, of which 1 were waited for; matrix products, arithmetic and copies ran while one was open for 9% of the time, Pallas kernels for 49%

profile of v4, /device:TPU:0, one launch (start us, length us, event | category | flops | bytes accessed | tf_op | source)
XLA Modules:
  0.0 735.5 jit_solution(14848830128906199705)
XLA Ops:
  0.7 1.7 constant_dynamic-slice_fusion.2
  2.5 3.0 collective-permute-start
  8.3 42.9 %first_gather.1 = (bf16[4,2,2,48,1152]{4,3,2,1,0:T(8,128)(2,1)}, bf16[4,2,2,48,384]{4,3,2,1,0:T(8,128)(2,1)}, bf16[4,2,2,48,384]{4,3,2,1,0:T(8,128)(2,1)}, bf16[...) custom-call(bf16[48,1152]{1,0:T(8,128)(2,1)} %get-tuple-element.432., ...), custom_call_target="tpu_custom_call" | custom-call | flops 20000000000 | bytes 30000000 | tf_op jit(solution)/shard_map/first_gather/pallas_call | solution.py:784
  51.2 1.3 fusion.20
  52.5 1.1 fusion.19
  55.5 1.4 fusion.14
  57.1 1.1 pad_maximum_fusion.1
  59.5 1.3 fusion.4.refs_1_.refs_2_
  64.1 0.9 copy.141
  67.1 1.0 collective-permute-done.1
  68.4 1.8 maximum_convert_fusion.refs_0_
  70.2 39.3 %temporal_forward.2 = (f32[4,208,768]{2,1,0:T(8,128)}, f32[4,208,768]{2,1,0:T(8,128)}, f32[4,208,1]{2,1,0:T(8,128)}, bf16[8,208,768]{2,1,0:T(8,128)(2,1)}, bf16[...) custom-call(f32[4,208,768]{2,1,0:T(8,128)} %maximum_convert_fusion.r, ...), custom_call_target="tpu_custom_call" | custom-call | flops 20000000000 | bytes 30000000 | tf_op jit(solution)/shard_map/temporal_forward/pallas_call | solution.py:725
  109.5 47.1 %spatial_forward.2 = (f32[4,208,768]{2,1,0:T(8,128)}, f32[4,208,768]{2,1,0:T(8,128)}, f32[4,208,1]{2,1,0:T(8,128)}, bf16[4,208,768]{2,1,0:T(8,128)(2,1)}, bf16[4...) custom-call(s32[1]{0:T(128)} %bitcast.1.refs_0_, ...), custom_call_target="tpu_custom_call" | custom-call | flops 20000000000 | bytes 30000000 | tf_op jit(solution)/shard_map/spatial_forward/pallas_call | solution.py:725
  156.6 34.5 %feed_forward.2 = (f32[4,208,768]{2,1,0:T(8,128)}, f32[4,208,768]{2,1,0:T(8,128)}, f32[4,208,1]{2,1,0:T(8,128)}, bf16[4,208,768]{2,1,0:T(8,128)(2,1)}, bf16[4,20...) custom-call(f32[4,208,768]{2,1,0:T(8,128)} %get-tuple-element.170.re, ...), custom_call_target="tpu_custom_call" | custom-call | flops 20000000000 | bytes 30000000 | tf_op jit(solution)/shard_map/feed_forward/pallas_call | solution.py:725
  191.1 1.1 fusion.18
  192.2 1.1 fusion.17
  193.6 1.1 pad_maximum_fusion.2
  194.7 35.8 %temporal_forward.3 = (f32[4,208,768]{2,1,0:T(8,128)}, f32[4,208,768]{2,1,0:T(8,128)}, f32[4,208,1]{2,1,0:T(8,128)}, bf16[8,208,768]{2,1,0:T(8,128)(2,1)}, bf16[...) custom-call(f32[4,208,768]{2,1,0:T(8,128)} %get-tuple-element.178.re, ...), custom_call_target="tpu_custom_call" | custom-call | flops 20000000000 | bytes 30000000 | tf_op jit(solution)/shard_map/temporal_forward/pallas_call | solution.py:725
  230.5 46.3 %spatial_forward.3 = (f32[4,208,768]{2,1,0:T(8,128)}, f32[4,208,768]{2,1,0:T(8,128)}, f32[4,208,1]{2,1,0:T(8,128)}, bf16[4,208,768]{2,1,0:T(8,128)(2,1)}, bf16[4...) custom-call(s32[1]{0:T(128)} %bitcast.1.refs_0_, ...), custom_call_target="tpu_custom_call" | custom-call | flops 20000000000 | bytes 30000000 | tf_op jit(solution)/shard_map/spatial_forward/pallas_call | solution.py:725
  276.8 27.4 %feed_forward.3 = (f32[4,208,768]{2,1,0:T(8,128)}, f32[4,208,768]{2,1,0:T(8,128)}, f32[4,208,1]{2,1,0:T(8,128)}, bf16[4,208,768]{2,1,0:T(8,128)(2,1)}, bf16[4,20...) custom-call(f32[4,208,768]{2,1,0:T(8,128)} %get-tuple-element.193.re, ...), custom_call_target="tpu_custom_call" | custom-call | flops 20000000000 | bytes 30000000 | tf_op jit(solution)/shard_map/feed_forward/pallas_call | solution.py:725
  304.3 1.2 bitcast_select_fusion
  305.4 1.1 copy.76
  307.8 1.8 convert_element_type.64
  310.7 1.3 broadcast_select_fusion.3
  312.0 2.1 convert_multiply_fusion.refs_0_
  314.1 39.2 %feed_back.2 = (f32[4,208,768]{2,1,0:T(8,128)}, f32[8,768]{1,0:T(8,128)}, bf16[768,1536]{1,0:T(8,128)(2,1)}, bf16[768,1536]{1,0:T(8,128)(2,1)}, f32[1,1536]{1,0:T(1,128)}, /*index=5*/f32[1,1536]{1,0:T(1,128)}) custom-call(f32[4,208,768]{2,1,0:T(8,128)} %convert_multiply_fusion.refs_0_, bf16[4,208,768]{2,1,0:T(8,128)(2,1)} %get-tuple-element.200.refs_1_, ...), custom_call_target="tpu_custom_call" | custom-call | flops 24000000000 | bytes 30000000 | tf_op jit(solution)/shard_map/feed_back/pallas_call | solution.py:1177
  353.2 48.3 %spatial_stage.2 = (f32[4,208,768]{2,1,0:T(8,128)}, f32[8,768]{1,0:T(8,128)}, f32[8,768]{1,0:T(8,128)}, bf16[768,1152]{1,0:T(8,128)(2,1)}, bf16[768,384]{1,0:T(8,128)(2,1)}, /*index=5*/f32[48,1536]{1,0:T(8,128)}) custom-call(s32[1]{0:T(128)} %bitcast.1.refs_0_, f32[4,208,768]{2,1,0:T(8,128)} %get-tuple-element.207.refs_1_, bf16[768,384]{1,0:T(8,128)(2,1)} %bitcast.301, ...), custom_call_target="tpu_custom_call" | custom-call | flops 24000000000 | bytes 30000000 | tf_op jit(solution)/shard_map/spatial_stage/pallas_call | solution.py:1324
  401.6 59.6 %temporal_stage.2 = (f32[4,208,768]{2,1,0:T(8,128)}, f32[8,768]{1,0:T(8,128)}, f32[8,768]{1,0:T(8,128)}, bf16[768,1152]{1,0:T(8,128)(2,1)}, bf16[768,384]{1,0:T(...) custom-call(f32[4,208,768]{2,1,0:T(8,128)} %get-tuple-element.216.refs_0_, ...), custom_call_target="tpu_custom_call" | custom-call | flops 24000000000 | bytes 30000000 | tf_op jit(solution)/shard_map/temporal_stage/pallas_call | solution.py:1488
  461.2 2.2 fusion.2
  463.6 1.1 copy.72
  464.7 1.4 collective-permute-start.4
  466.3 0.8 fusion.27
  467.7 1.3 broadcast_select_fusion.18
  469.0 1.6 fusion.1
  470.7 0.9 pad_maximum_fusion.8
  471.6 53.1 %feed_back.3 = (f32[4,208,768]{2,1,0:T(8,128)}, f32[8,768]{1,0:T(8,128)}, bf16[768,1536]{1,0:T(8,128)(2,1)}, bf16[768,1536]{1,0:T(8,128)(2,1)}, f32[1,1536]{1,0:...) custom-call(f32[4,208,768]{2,1,0:T(8,128)} %get-tuple-element.227.refs_0_, ...), custom_call_target="tpu_custom_call" | custom-call | flops 24000000000 | bytes 30000000 | tf_op jit(solution)/shard_map/feed_back/pallas_call | solution.py:1177
  525.4 46.0 %spatial_stage.3 = (f32[4,208,768]{2,1,0:T(8,128)}, f32[8,768]{1,0:T(8,128)}, f32[8,768]{1,0:T(8,128)}, bf16[768,1152]{1,0:T(8,128)(2,1)}, bf16[768,384]{1,0:T(8,128)(2,1)}, /*index=5*/f32[48,1536]{1,0:T(8,128)}) custom-call(s32[1]{0:T(128)} %bitcast.1.refs_0_, f32[4,208,768]{2,1,0:T(8,128)} %get-tuple-element.238.refs_1_, bf16[768,384]{1,0:T(8,128)(2,1)} %bitcast.292, ...), custom_call_target="tpu_custom_call" | custom-call | flops 24000000000 | bytes 30000000 | tf_op jit(solution)/shard_map/spatial_stage/pallas_call | solution.py:1324
  571.4 0.8 fusion.28
  572.8 69.9 %temporal_stage.3 = (f32[4,208,768]{2,1,0:T(8,128)}, f32[8,768]{1,0:T(8,128)}, f32[8,768]{1,0:T(8,128)}, bf16[768,1152]{1,0:T(8,128)(2,1)}, bf16[768,384]{1,0:T(...) custom-call(f32[4,208,768]{2,1,0:T(8,128)} %get-tuple-element.247.re, ...), custom_call_target="tpu_custom_call" | custom-call | flops 24000000000 | bytes 30000000 | tf_op jit(solution)/shard_map/temporal_stage/pallas_call | solution.py:1488
  642.8 0.7 slice_bitcast_fusion.23
  643.5 1.4 fusion.21
  644.9 1.3 slice_bitcast_fusion.25
  647.0 2.2 fusion.3
  649.2 1.3 broadcast_select_fusion.16
  650.5 1.8 convert_element_type.71
  652.5 1.1 copy.80
  654.1 0.8 reshape.449
  655.6 1.4 fusion.23
  657.7 1.9 pad_maximum_fusion.10
  659.6 1.6 maximum_bitcast_fusion.3
  661.2 1.9 pad_maximum_fusion.11
  663.2 1.7 stack_reshape.14
  664.9 1.8 stack_reshape.13
  666.7 1.3 copy.99
  668.6 1.9 maximum_bitcast_fusion.1
  670.6 1.3 select_bitcast_fusion.3
  672.0 1.5 copy.86
  674.1 1.2 fusion
  675.4 0.9 pad_maximum_fusion.9
  676.3 1.1 broadcast_select_fusion.8
  677.4 47.1 %sum_rows.1 = (f32[48,1152]{1,0:T(8,128)}, f32[48,384]{1,0:T(8,128)}, f32[48,384]{1,0:T(8,128)}, f32[8,768]{1,0:T(8,128)}, bf16[4,98,768]{2,1,0:T(8,128)(2,1)}) custom-call(bf16[4,2,2,48,1152]{4,3,2,1,0:T(8,128)(2,1)} %bitcast.275, bf16[4,2,2,48,384]{4,3,2,1,0:T(8,128)(2,1)} %bitcast.299, bf16[4,2,2,48,384]{4,3,2,1,0:T(8,128)(2,1)} %bitcast.228, ...), custom_call_target="tpu_custom_call" | custom-call | flops 20000000000 | bytes 30000000 | tf_op jit(solution)/shard_map/sum_rows/pallas_call | solution.py:513
  725.9 1.2 select_bitcast_fusion.1
  727.4 2.4 copy.87
  731.6 1.0 copy.90
  (166 shorter events, 26.5 us)
Async XLA Ops:
  0.6 4.8 copy-start.25
  0.7 4.8 copy-start.26
  0.7 4.9 copy-start.31
  0.7 5.5 copy-start.6
  0.7 5.6 copy-start.11
  0.7 6.2 copy-start.14
  2.5 63.2 %collective-permute-start = (bf16[4,98,768]{2,0,1:T(4,128)(2,1)S(1)}, bf16[4,98,768]{2,0,1:T(4,128)(2,1)S(1)}, u32[]{:S(2)}, u32[]{:S(2)}) collective-permute-start(bf16[4,98,768]{2,0,1:T(4,128)(2,1)S(1)} %get-tuple-element.355), channel_id=1, source_target_pairs={{0,2},{1,3},{2,0},{3,1},{4,6},{5,7},{6,4},{7,5},{8,10},{9,11},{10,... | collective-permute-start | bytes 1806344 | tf_op jit(solution)/shard_map/ppermute | solution.py:145
  5.5 59.6 %collective-permute-start.2 = (f32[2,2304]{1,0:T(2,128)S(1)}, f32[2,2304]{1,0:T(2,128)S(1)}, u32[]{:S(2)}, u32[]{:S(2)}) collective-permute-start(f32[2,2304]{1,0:T(2,128)S(1)} %pad_maximum_fusion.21), channel_id=1, source_target_pairs={{0,1},{1,0},{2,3},{3,2},{4,5},{5,4},{6,7},{7,6},{8,9},{9,8},{10,11... | collective-permute-start | bytes 55304 | tf_op jit(solution)/shard_map/ppermute | solution.py:145
  8.3 45.3 %copy-start.7 = (bf16[2,48,1536]{2,1,0:T(8,128)(2,1)S(1)}, bf16[2,48,1536]{2,1,0:T(8,128)(2,1)}, u32[]{:S(2)}) copy-start(bf16[2,48,1536]{2,1,0:T(8,128)(2,1)} %param.25) | copy-start | bytes 884740
  51.2 3.2 copy-start.1
  54.8 0.7 copy-start.30
  57.0 3.8 copy-start.8
  57.0 5.2 copy-start.23
  57.1 5.8 copy-start.24
  57.1 6.4 copy-start.21
  66.1 2.1 collective-permute-start.1
  306.5 4.1 collective-permute-start.5
  309.6 1.1 copy-start
  310.1 153.3 %collective-permute-start.3 = (bf16[4,98,768]{2,0,1:T(4,128)(2,1)S(1)}, bf16[4,98,768]{2,0,1:T(4,128)(2,1)S(1)}, u32[]{:S(2)}, u32[]{:S(2)}) collective-permute-start(bf16[4,98,768]{2,0,1:T(4,128)(2,1)S(1)} %copy.69), channel_id=1, source_target_pairs={{0,1},{1,0},{2,3},{3,2},{4,5},{5,4},{6,7},{7,6},{8,9},{9,8},{10,11... | collective-permute-start | bytes 1806344 | tf_op jit(solution)/shard_map/ppermute | solution.py:145
  463.4 2.7 copy-start.28
  463.4 2.8 copy-start.27
  463.4 2.8 copy-start.9
  463.4 5.7 collective-permute-start.6
  464.7 205.9 %collective-permute-start.4 = (bf16[4,98,768]{2,0,1:T(4,128)(2,1)}, bf16[4,98,768]{2,0,1:T(4,128)(2,1)}, u32[]{:S(2)}, u32[]{:S(2)}) collective-permute-start(bf16[4,98,768]{2,0,1:T(4,128)(2,1)} %copy.72), channel_id=1, source_target_pairs={{0,2},{1,3},{2,0},{3,1},{4,6},{5,7},{6,4},{7,5},{8,10},{9,11},{10,... | collective-permute-start | bytes 1806344 | tf_op jit(solution)/shard_map/ppermute | solution.py:145
  525.4 46.8 %copy-start.29 = (f32[1,1536]{1,0:T(1,128)S(1)}, f32[1,1536]{1,0:T(1,128)}, u32[]{:S(2)}) copy-start(f32[1,1536]{1,0:T(1,128)} %get-tuple-element.264) | copy-start | bytes 18436
  649.2 24.3 %collective-permute-start.8 = (bf16[16,24,768]{2,1,0:T(8,128)(2,1)}, bf16[16,24,768]{2,1,0:T(8,128)(2,1)}, u32[]{:S(2)}, u32[]{:S(2)}) collective-permute-start(bf16[16,24,768]{2,1,0:T(8,128)(2,1)} %fusion.3), channel_id=1, source_target_pairs={{0,1},{1,0},{2,3},{3,2},{4,5},{5,4},{6,7},{7,6},{8,9},{9,8},{10,11... | collective-permute-start | bytes 1769480 | tf_op jit(solution)/shard_map/ppermute | solution.py:145
  653.6 22.7 %collective-permute-start.7 = (bf16[4,98,768]{2,0,1:T(4,128)(2,1)}, bf16[4,98,768]{2,0,1:T(4,128)(2,1)S(1)}, u32[]{:S(2)}, u32[]{:S(2)}) collective-permute-start(bf16[4,98,768]{2,0,1:T(4,128)(2,1)} %copy.80), channel_id=1, source_target_pairs={{0,1},{1,0},{2,3},{3,2},{4,5},{5,4},{6,7},{7,6},{8,9},{9,8},{10,11... | collective-permute-start | bytes 1806344 | tf_op jit(solution)/shard_map/ppermute | solution.py:145
  655.6 7.5 %copy-start.13 = (f32[2,3,768]{2,1,0:T(4,128)}, f32[2,3,768]{2,1,0:T(4,128)S(1)}, u32[]{:S(2)}) copy-start(f32[2,3,768]{2,1,0:T(4,128)S(1)} %dynamic-slice_bitcast_fusion.1) | copy-start | bytes 55300
  657.6 5.5 copy-start.12
  657.6 5.5 copy-start.20
  657.6 5.5 copy-start.19
  657.6 9.0 %copy-start.18 = (f32[2,2,1,768]{3,2,1,0:T(1,128)S(1)}, f32[2,2,1,768]{3,2,1,0:T(1,128)}, u32[]{:S(2)}) copy-start(f32[2,2,1,768]{3,2,1,0:T(1,128)} %get-tuple-element.400) | copy-start | bytes 36868
  672.0 2.1 copy-start.3
  727.4 3.6 copy-start.10
  727.4 3.7 copy-start.4
  729.7 1.5 copy-start.2
  731.2 1.3 copy-start.22
  731.3 1.3 slice-start
  731.3 2.6 copy-start.15
  731.3 2.6 copy-start.16
  731.3 2.6 copy-start.17
  731.6 2.3 copy-start.5

commit v5 on v4

--- a/solution.py
+++ b/solution.py
@@ -300,8 +300,11 @@
 
 
 class Carrier:
-    def __init__(self, place, cores, sources, parts, owns, scratch):
+    def __init__(self, place, cores, starts, sources, parts, owns, scratch):
         self.place, self.cores = place, cores
+        lanes = [pl.ds(start, own.shape[1]) for start, own in zip(starts, owns)]
+        sources = [ref.at[:, :, :, :, cols] for ref, cols in zip(sources, lanes)]
+        parts = [ref.at[:, :, :, :, cols] for ref, cols in zip(parts, lanes)]
         self.sums = [
             Sums(place, source, part, own, *scratch[10 * i : 10 * i + 10])
             for i, (source, part, own) in enumerate(zip(sources, parts, owns))
@@ -332,10 +335,10 @@
 def carried(grid, parts):
     depth = grid.depth
     cubes, shapes, scratch = [], [], []
-    for part in parts:
-        step_rows, lanes = part.shape[0] // (depth * 4), part.shape[1]
+    for part, start, lanes in parts:
+        step_rows = part.shape[0] // (depth * 4)
         block = lambda count: pltpu.VMEM((count, step_rows, lanes), BF)
-        cubes.append(part.reshape(depth, 2, 2, step_rows, lanes))
+        cubes.append(part.reshape(depth, 2, 2, step_rows, part.shape[1]))
         shapes.append(jax.ShapeDtypeStruct((step_rows, lanes), F32))
         scratch += [block(depth // 2)] * 2 + [block(depth)] * 5 + [block(depth - 1)]
         scratch += [pltpu.SemaphoreType.DMA((3 + depth,))] * 2
@@ -486,13 +489,14 @@
     return [block, block] + [pltpu.SemaphoreType.DMA((5,))] * 2
 
 
-def tail_body(depth, count, pieces, *refs):
+def tail_body(depth, starts, pieces, *refs):
     take = splitter(refs)
+    count = len(starts)
     parts, small, (away,) = take(count), take(len(pieces)), take(1)
     owns, (total, back) = take(count), take(2)
     hop_refs, (send, recv) = take(4), take(2)
     place = Place(depth)
-    carrier = Carrier(place, True, parts, parts, owns, take(10 * count))
+    carrier = Carrier(place, True, starts, parts, parts, owns, take(10 * count))
     hops = Hops(place, pieces, small, total, *hop_refs)
     across = remote(away, back, send.at[0], recv.at[0], place.over_y())
     carrier.step(0)
@@ -507,11 +511,15 @@
     across.wait()
 
 
+def starts_of(parts):
+    return [start for _, start, _ in parts]
+
+
 def tail_sums(grid, number, parts, small, away):
     cubes, shapes, scratch = carried(grid, parts)
     count = len(small.arrays)
     result = pl.pallas_call(
-        functools.partial(tail_body, grid.depth, len(parts), small.pieces),
+        functools.partial(tail_body, grid.depth, starts_of(parts), small.pieces),
         in_specs=[VMEM_SPEC] * (len(parts) + count + 1),
         out_specs=[VMEM_SPEC] * (len(parts) + 2),
         out_shape=shapes + [small.shape(), jax.ShapeDtypeStruct(away.shape, away.dtype)],
@@ -551,7 +559,8 @@
     def at(self, ref, dx, dy, low=0, size=None):
         x = 1 - self.place.x if dx else self.place.x
         y = 1 - self.place.y if dy else self.place.y
-        return ref.at[pl.ds(low, size or self.depth), x, y]
+        view = ref.at[pl.ds(low, size or self.depth), x, y]
+        return view.at[:, self.place.t] if len(ref.shape) == 6 else view
 
     def sides(self):
         dst = self.at(self.whole, 0, 0)
@@ -631,6 +640,20 @@
             item.wait()
 
 
+def landing(line, both):
+    depth, step_rows, lanes = line
+    if both == "one":
+        return [jax.ShapeDtypeStruct((depth, 2, 2, 2, step_rows, lanes), BF)]
+    return [jax.ShapeDtypeStruct((depth, 2, 2, step_rows, lanes), BF)] * (2 if both else 1)
+
+
+def landed(outs, both):
+    whole = outs.pop(0)
+    if both == "one":
+        return whole, whole
+    return whole, outs.pop(0) if both else None
+
+
 class Load:
     def __init__(self, grid, near=(), swapped=(), deep=(), across=()):
         self.depth = grid.depth
@@ -640,10 +663,9 @@
         self.across_count = len(across)
         self.shapes, self.scratch, self.specs = [], [], []
         for line, both in zip(near, swapped):
-            depth, step_rows, lanes = line.shape
-            shape = jax.ShapeDtypeStruct((depth, 2, 2, step_rows, lanes), BF)
-            self.shapes += [shape] * (2 if both else 1)
-            self.specs += [ANY_SPEC] * (2 if both else 1)
+            shapes = landing(line.shape, both)
+            self.shapes += shapes
+            self.specs += [ANY_SPEC] * len(shapes)
             self.scratch += [pltpu.SemaphoreType.DMA((9,)), pltpu.SemaphoreType.DMA((8,))]
         for block in deep:
             self.shapes.append(jax.ShapeDtypeStruct((self.depth,) + block.shape, BF))
@@ -660,8 +682,7 @@
         flat = lambda item: item.reshape(-1, item.shape[-1])
         near = []
         for both in self.swapped:
-            own = flat(arrays.pop(0))
-            near.append((own, flat(arrays.pop(0)) if both else None))
+            near.append([None if item is None else flat(item) for item in landed(arrays, both)])
         return near, arrays
 
 
@@ -671,8 +692,7 @@
         ins, outs, sems = list(ins), list(outs), list(sems)
         self.near = []
         for both in load.swapped:
-            whole = outs.pop(0)
-            other = outs.pop(0) if both else None
+            whole, other = landed(outs, both)
             self.near.append(Near(place, ins.pop(0), whole, other, sems.pop(0), sems.pop(0)))
         self.deep = [
             Deep(place, ins.pop(0), outs.pop(0), sems.pop(0), sems.pop(0))
@@ -735,11 +755,11 @@
     return result[: len(shapes)], load.results(result[len(shapes) :])
 
 
-def first_body(count, depth, next_count, *refs):
+def first_body(swapped, depth, next_count, *refs):
     take = splitter(refs)
+    count = len(swapped)
     blocks, next_blocks = take(count), take(next_count)
-    swapped = [False] + [True] * (count - 1)
-    wholes = [take(2) if both else take(1) + [None] for both in swapped]
+    wholes = [landed(take(2 if both is True else 1), both) for both in swapped]
     next_lines = take(next_count)
     lines = take(count)
     place = Place(depth)
@@ -764,13 +784,13 @@
         item.end()
 
 
-def first_gather(grid, number, blocks, next_blocks):
+def first_gather(grid, number, blocks, swapped, next_blocks):
     depth = grid.depth
-    whole = lambda item: jax.ShapeDtypeStruct((depth, 2, 2) + item.shape, BF)
     line = lambda item: (depth,) + item.shape
-    shapes = [whole(blocks[0])]
-    for item in blocks[1:]:
-        shapes += [whole(item)] * 2
+    shapes = []
+    for item, both in zip(blocks, swapped):
+        shapes += landing(line(item), both)
+    specs = [ANY_SPEC] * len(shapes) + [VMEM_SPEC] * len(next_blocks)
     shapes += [jax.ShapeDtypeStruct(line(item), BF) for item in next_blocks]
     sems = lambda size: [pltpu.SemaphoreType.DMA((size,))] * 2
     scratch = [pltpu.VMEM(line(item), BF) for item in blocks]
@@ -782,9 +802,9 @@
         scratch += sems(depth - 1)
     arrays = list(
         pl.pallas_call(
-            functools.partial(first_body, len(blocks), depth, len(next_blocks)),
+            functools.partial(first_body, tuple(swapped), depth, len(next_blocks)),
             in_specs=[VMEM_SPEC] * (len(blocks) + len(next_blocks)),
-            out_specs=[ANY_SPEC] * (2 * len(blocks) - 1) + [VMEM_SPEC] * len(next_blocks),
+            out_specs=specs,
             out_shape=shapes,
             scratch_shapes=scratch,
             compiler_params=stage_params(number),
@@ -792,10 +812,8 @@
             name="first_gather",
         )(*blocks, *next_blocks)
     )
-    flat = lambda item: item.reshape(-1, item.shape[-1])
-    near = [(flat(arrays.pop(0)), None)]
-    for _ in blocks[1:]:
-        near.append((flat(arrays.pop(0)), flat(arrays.pop(0))))
+    flat = lambda item: None if item is None else item.reshape(-1, item.shape[-1])
+    near = [[flat(item) for item in landed(arrays, both)] for both in swapped]
     return near, arrays
 
 
@@ -1063,8 +1081,9 @@
     )
 
 
-def feed_back_body(depth, count, steps, layer, *refs):
+def feed_back_body(depth, starts, steps, layer, *refs):
     take = splitter(refs)
+    count = len(starts)
     state, normed, unit, scale, gain = take(5)
     gain = row_of(gain, 3 * layer + 2)
     oth, own = take(4), take(4)
@@ -1073,7 +1092,7 @@
     owns = take(count)
     r, rt, nt, bh, s_up, s_down, r_up, r_down, send, recv = take(10)
     place = Place(depth)
-    carrier = Carrier(place, True, parts, parts, owns, take(10 * count))
+    carrier = Carrier(place, True, starts, parts, parts, owns, take(10 * count))
     frames, padded, width = state.shape
     rows_all = frames * padded
     i = pl.program_id(0)
@@ -1175,7 +1194,7 @@
     fixed = [state, kept["normed_m"], kept["unit_m"], kept["scale_m"], gain]
     vec = lambda at: pl.BlockSpec((1, lanes), lambda i: (0, at(i)))
     result = pl.pallas_call(
-        functools.partial(feed_back_body, grid.depth, len(parts), steps, layer),
+        functools.partial(feed_back_body, grid.depth, starts_of(parts), steps, layer),
         grid=(2 * steps,),
         in_specs=[whole(item) for item in fixed]
         + side(first)
@@ -1215,8 +1234,9 @@
     return result[0], result[1], result[2:4], (result[4], result[5]), result[6:]
 
 
-def spatial_back_body(depth, count, places, att_scale, layer, staging, *refs):
+def spatial_back_body(depth, starts, places, att_scale, layer, staging, *refs):
     take = splitter(refs)
+    count = len(starts)
     in_refs, out_refs = take(14 + count), take(5 + count)
     own_scratch, sum_scratch = take(13), take(10 * count)
     sources = in_refs[14:]
@@ -1230,7 +1250,7 @@
     owns = take(count)
     r, bm0, bm1, b0, b1, rt, nt, s_tri, r_tri, s_merge, r_merge, send, recv = take(13)
     place = Place(depth)
-    carrier = Carrier(place, True, sources, parts, owns, take(10 * count))
+    carrier = Carrier(place, True, starts, sources, parts, owns, take(10 * count))
     frames, padded, width = state.shape
     rows_all = frames * padded
     split = merge0.shape[1]
@@ -1323,7 +1343,7 @@
     staging = Staging(1, ins, outs)
     result = pl.pallas_call(
         functools.partial(
-            spatial_back_body, grid.depth, len(parts), places, att_scale, layer, staging
+            spatial_back_body, grid.depth, starts_of(parts), places, att_scale, layer, staging
         ),
         in_specs=staging.in_specs(),
         out_specs=staging.out_specs(),
@@ -1344,12 +1364,14 @@
     return result[0], result[1], result[2], result[3:5], result[5:]
 
 
-def temporal_back_body(depth, count, att_scale, layer, staging, pieces, *refs):
+def temporal_back_body(depth, starts, att_scale, layer, staging, pieces, joined_mix, *refs):
     take = splitter(refs)
+    count = len(starts)
     chained = 1 if pieces else 0
     in_refs, small = take(13 + count), take(len(pieces))
     out_refs, total = take(6 + count), take(chained)
     own_scratch, sum_scratch, hop_refs = take(13), take(10 * count), take(4 * chained)
+    mix_refs = take(3) if joined_mix else None
     sources = in_refs[13:]
     in_refs, out_refs = staging.open(in_refs, out_refs, take(staging.count()))
     take = splitter(in_refs + out_refs + own_scratch + sum_scratch)
@@ -1360,8 +1382,11 @@
     out, sums, q_sums, g_tri, g_merge, g_mix = take(6)
     owns = take(count)
     r, bj, away, bm, b, nt, rt, s_merge, r_merge, s_back, r_back, send, recv = take(13)
+    joins = len(g_mix.shape) == 3
+    if joins:
+        (whole_mix, s_mix, r_mix), shard_mix = mix_refs, g_mix
     place = Place(depth)
-    carrier = Carrier(place, True, sources, parts, owns, take(10 * count))
+    carrier = Carrier(place, True, starts, sources, parts, owns, take(10 * count))
     frames, padded, width = state.shape
     rows_all = frames * padded
     split = merge0.shape[1]
@@ -1398,7 +1423,19 @@
     rt[...] = joined[...].reshape(rows_all, width).T
     for half in range(2):
         cols = slice(half * split, (half + 1) * split)
-        g_mix[:, cols] = dot_nn(rt[...], r[:, :, cols].reshape(rows_all, split))
+        mix_part = dot_nn(rt[...], r[:, :, cols].reshape(rows_all, split))
+        (whole_mix if joins else g_mix)[:, cols] = mix_part
+    if joins:
+        blocks, step = shard_mix.shape[0], shard_mix.shape[1]
+
+        def mix_rows(k, core):
+            at = pl.multiple_of((2 * k + core) * step, 8)
+            return whole_mix[pl.ds(at, step), :]
+
+        for k in range(blocks):
+            s_mix[k] = mix_rows(k, 1 - place.t).astype(BF)
+        swap_mix = remote(s_mix, r_mix, send.at[3], recv.at[3], place.over_t())
+        swap_mix.start()
     rt[...] = bj[...].reshape(rows_all, width).T
     swap_merge.wait()
     g_merge[...] = (dot_nn(rt[...], mine[...].reshape(rows_all, split)) + r_merge[...].astype(F32)).astype(BF)
@@ -1423,6 +1460,10 @@
 
     tiles = padded // tile
     lax.fori_loop(0, tiles // 3, one, 0)
+    if joins:
+        swap_mix.wait()
+        for k in range(blocks):
+            shard_mix[k] = (mix_rows(k, place.t) + r_mix[k].astype(F32)).astype(BF)
     if chained:
         hops.hop(2)
     lax.fori_loop(tiles // 3, 2 * tiles // 3, one, 0)
@@ -1482,12 +1523,18 @@
         jax.ShapeDtypeStruct((width, split), BF),
         jax.ShapeDtypeStruct((width, width), F32),
     ] + shapes
+    mix_scratch = []
+    if grid.direct:
+        step = width // (4 * grid.depth) // 2
+        outs[5] = jax.ShapeDtypeStruct((4 * grid.depth, step, width), BF)
+        mix_scratch = [pltpu.VMEM((width, width), F32)]
+        mix_scratch += [pltpu.VMEM((4 * grid.depth, step, width), BF)] * 2
     staging = Staging(0, ins, outs)
     pieces = small.pieces if small else []
     chained = 1 if small else 0
     result = pl.pallas_call(
         functools.partial(
-            temporal_back_body, grid.depth, len(parts), att_scale, layer, staging, pieces
+            temporal_back_body, grid.depth, starts_of(parts), att_scale, layer, staging, pieces, grid.direct
         ),
         in_specs=staging.in_specs() + [VMEM_SPEC] * len(pieces),
         out_specs=staging.out_specs() + [VMEM_SPEC] * chained,
@@ -1500,9 +1547,10 @@
         + [pltpu.VMEM((width, frames * padded), BF)]
         + [pltpu.VMEM((width, split), BF)] * 2
         + [pltpu.VMEM((frames, padded, width), BF)] * 2
-        + [pltpu.SemaphoreType.DMA((3,))] * 2
+        + [pltpu.SemaphoreType.DMA((4,))] * 2
         + scratch
         + (hop_scratch(small) if chained else [])
+        + mix_scratch
         + staging.scratch(),
         compiler_params=stage_params(number, 60),
         cost_estimate=stage_cost(24000000000),
@@ -1625,61 +1673,76 @@
             axis=1,
         ).reshape(width, width)
 
-    def blocks_of(layer, stage):
-        if stage == "t":
-            triple = jnp.concatenate(block_triple(layer, 0), axis=1)
-            return [triple] + block_out(layer)
-        if stage == "s":
-            return [jnp.concatenate(block_triple(layer, 1), axis=1), merge_weight[layer, 1].T]
-        return block_m(layer)
-
-    order = [(layer, stage) for layer in range(LAYERS) for stage in "tsm"]
+    def block_named(layer, name):
+        if name == "triple_t":
+            return jnp.concatenate(block_triple(layer, 0), axis=1)
+        if name == "triple_s":
+            return jnp.concatenate(block_triple(layer, 1), axis=1)
+        if name == "merge_t":
+            return merge_weight[layer, 0].T
+        if name == "mix":
+            return mixing_weight[layer] if grid.direct else pack_mix(mixing_weight[layer])
+        if name == "merge_s":
+            return merge_weight[layer, 1].T
+        return block_m(layer)[0 if name == "up" else 1]
+
     gathered = [dict() for _ in range(LAYERS)]
 
-    def settle(key, near):
-        w = gathered[key[0]]
-        if key[1] == "t":
-            w.update(triple_t=near[0][0], merge_t=near[1], mixing=mixing_of(near[2]))
-        elif key[1] == "s":
-            w.update(triple_s=near[0], merge_s=near[1])
-        else:
-            w.update(up=near[0], down=near[1])
-
-    def direct_gather(block):
-        return lax.all_gather(block, ("shard", "ctx"), axis=0, tiled=True)
-
+    def settle(keys, near):
+        for (layer, name), both in zip(keys, near):
+            w = gathered[layer]
+            if name == "triple_t":
+                w[name] = both[0]
+            elif name == "mix":
+                w["mixing"] = both[0] if grid.direct else mixing_of(both)
+            else:
+                w[name] = both
+
+    ahead = [
+        [(0, "triple_t"), (0, "merge_t"), (0, "mix")],
+        [(0, "triple_s"), (0, "merge_s"), (0, "up")],
+        [(0, "down")],
+        [(1, "triple_t"), (1, "merge_t"), (1, "mix")],
+        [(1, "triple_s"), (1, "merge_s"), (1, "up")],
+        [(1, "down")],
+        [],
+        [],
+    ]
+    named = lambda keys: [block_named(*key) for key in keys]
+    modes = {"triple_t": False, "mix": "one"}
+    modes_of = lambda keys: [modes.get(name, True) for _, name in keys]
     lines = {}
     if grid.direct:
-        near, lines[order[1]] = first_gather(
-            grid, 7, blocks_of(*order[0]), blocks_of(*order[1])
+        near, lines[1] = first_gather(
+            grid, 7, named(ahead[0]), modes_of(ahead[0]), named(ahead[1])
         )
-        settle(order[0], near)
+        settle(ahead[0], near)
     else:
-        for key in order:
-            settle(key, [with_other(direct_gather(item)) for item in blocks_of(*key)])
+        for keys in ahead:
+            settle(
+                keys,
+                [
+                    with_other(lax.all_gather(item, ("shard", "ctx"), axis=0, tiled=True))
+                    for item in named(keys)
+                ],
+            )
 
     def load_at(index):
+        across = [far_cotangent] if index == 3 * LAYERS - 1 and grid.direct else []
         if not grid.direct:
             return Load(grid)
-        near, swapped, deep, across = (), (), (), ()
-        if index + 1 < len(order):
-            near = lines[order[index + 1]]
-            swapped = [not (order[index + 1][1] == "t" and i == 0) for i in range(len(near))]
-        if index + 2 < len(order):
-            deep = blocks_of(*order[index + 2])
-        if index + 1 == len(order):
-            across = [far_cotangent]
-        return Load(grid, near, swapped, deep, across)
+        keys = ahead[index + 1]
+        swapped = modes_of(keys)
+        near = lines[index + 1] if keys else []
+        return Load(grid, near, swapped, named(ahead[index + 2]), across)
 
     def loaded(index, got):
         near, new_lines = got
-        if index + 1 == len(order):
+        if index == 3 * LAYERS - 1:
             lines["across"] = new_lines[0] if grid.direct else grid.over_y(far_cotangent)
-            new_lines = ()
-        if grid.direct and index + 1 < len(order):
-            settle(order[index + 1], near)
-        if grid.direct and index + 2 < len(order):
-            lines[order[index + 2]] = new_lines
+        elif grid.direct:
+            settle(ahead[index + 1], near)
+            lines[index + 2] = new_lines
 
     small = jnp.concatenate([entry_bias[:, 1].reshape(LAYERS, -1), up_bias], axis=1)
     small_oth = grid.over_t(small)
@@ -1779,7 +1842,9 @@
     def carry_sums(names, parts):
         nonlocal waiting
         if not grid.direct:
-            sums.update(zip(names, plain_sums(parts)))
+            sums.update(
+                zip(names, plain_sums([item[:, start : start + size] for item, start, size in parts]))
+            )
             return
         waiting = (names, parts)
 
@@ -1798,7 +1863,10 @@
             grid, layer, layer, upstream, kept, gains, w, carried_parts()
         )
         arrived_sums(got)
-        carry_sums([("up", layer)], parts_m[:1])
+        cut = hid // 2
+        carry_sums(
+            [("up", layer), ("down_a", layer)], [(parts_m[0], 0, hid), (parts_m[1], 0, cut)]
+        )
         upstream, vec_s, entry_s, parts_s, got = spatial_back(
             grid,
             2 + layer,
@@ -1814,7 +1882,8 @@
         )
         arrived_sums(got)
         carry_sums(
-            [("down", layer), ("triple_s", layer), ("merge_s", layer)], [parts_m[1]] + list(parts_s)
+            [("triple_s", layer), ("down_b", layer), ("merge_s", layer)],
+            [(parts_s[0], 0, 3 * split), (parts_m[1], cut, cut), (parts_s[1], 0, split)],
         )
         per_row = hid // width
         hidden_rows = [item.reshape(per_row, width) for item in hidden_part]
@@ -1854,14 +1923,17 @@
             early if grid.direct else None,
         )
         arrived_sums(got)
-        mix_part = parts_t[2].reshape(-1, 2, half_rows, width)
-        mix_mine = lax.dynamic_index_in_dim(mix_part, grid.t, 1, keepdims=False)
-        mix_theirs = lax.dynamic_index_in_dim(mix_part, 1 - grid.t, 1, keepdims=False)
-        mix_got = grid.over_t(mix_theirs.astype(BF)).astype(F32)
-        mix_sum = pack_mix((mix_mine + mix_got).astype(BF)).reshape(width, width // 2)
+        if grid.direct:
+            mix_sum = parts_t[2].reshape(width // 2, width)
+        else:
+            mix_part = parts_t[2].reshape(-1, 2, half_rows, width)
+            mix_mine = lax.dynamic_index_in_dim(mix_part, grid.t, 1, keepdims=False)
+            mix_theirs = lax.dynamic_index_in_dim(mix_part, 1 - grid.t, 1, keepdims=False)
+            mix_got = grid.over_t(mix_theirs.astype(BF)).astype(F32)
+            mix_sum = (mix_mine + mix_got).astype(BF).reshape(width // 2, width)
         carry_sums(
             [("triple_t", layer), ("merge_t", layer), ("mix", layer)],
-            [parts_t[0], parts_t[1], mix_sum],
+            [(parts_t[0], 0, 3 * split), (parts_t[1], 0, split), (mix_sum, 0, width)],
         )
         last_vec = vec_t
         last_half = both_cores(entry_t[:1], jnp.zeros_like(entry_t[:1]))
@@ -1879,9 +1951,10 @@
         small, early = small.plain(), early_rows.plain()
         out_got = grid.over_y(out_low)
     input_grad = spread_last(out_got, out_ready).astype(F32)
-    names = ("triple_t", "merge_t", "mix", "triple_s", "merge_s", "up", "down")
+    names = ("triple_t", "merge_t", "mix", "triple_s", "merge_s", "up")
     for layer in range(LAYERS):
-        shards[layer] = [sums[name, layer] for name in names]
+        down = jnp.concatenate([sums["down_a", layer], sums["down_b", layer]], axis=1)
+        shards[layer] = [sums[name, layer] for name in names] + [down]
     block = 6 * LAYERS
     pairs = early[:block].reshape(LAYERS, 2, 3, width)
     ends = jnp.stack([small[:4], early[block : block + 4]])
@@ -1901,9 +1974,6 @@
     tokens = FRAMES * width * jnp.sum(valid_places).astype(F32)
     root_squares = jnp.sqrt(square_sums / tokens)
 
-    def unpack_rows(item):
-        return jnp.concatenate([item[:half_rows], item[half_rows:]], axis=-1)
-
     def triple_shape(item):
         return item.reshape(step_rows, 3, split)
 
@@ -1916,7 +1986,7 @@
         entry_sum,
         jnp.stack([jnp.stack([s[1].T, s[4].T]) for s in shards]),
         bias_sum,
-        jnp.stack([unpack_rows(s[2]) for s in shards]),
+        jnp.stack([s[2] for s in shards]),
         jnp.stack([s[5] for s in shards]),
         hidden_sum,
         jnp.stack([s[6].T for s in shards]),

time: 742 us -> 700 us (0.943)
  local copies, waits for them, and re-layouts: 45.4 us -> 29.8 us
  other arithmetic: 44.4 us -> 29.7 us
    pallas_call x6, Pallas kernels: 230 us -> 217 us  [kernel_call(): pl.pallas_call(functools.partial(body, staging), in_specs=staging.in_spec...]
  transfers between devices with their start and end apart: 9 -> 7, of which waited for: 1 -> 1; matrix products, arithmetic and copies ran while one was open for 9% -> 6% of each run, Pallas kernels for 49% -> 59%
where the time goes in v5:
time: 700 us; the launch traced here: 696 us
  Pallas kernels  629 us (90%)
  local copies, waits for them, and re-layouts  29.8 us (4%)
  other arithmetic  29.7 us (4%)
    pallas_call x6, Pallas kernels, kernel_call(): pl.pallas_call(functools.partial(body, staging), in_specs=staging.in_spec...  217 us
    pallas_call x2, Pallas kernels, temporal_back(): pl.pallas_call(functools.partial(temporal_back_body, grid.depth, starts_o...  115 us
    pallas_call x2, Pallas kernels, spatial_back(): pl.pallas_call(functools.partial(spatial_back_body, grid.depth, starts_of...  107 us
    pallas_call x2, Pallas kernels, feed_back(): pl.pallas_call(functools.partial(feed_back_body, grid.depth, starts_of(pa...  89.1 us
    pallas_call x1, Pallas kernels, tail_sums(): pl.pallas_call(functools.partial(tail_body, grid.depth, starts_of(parts),...  51.4 us
    pallas_call x1, Pallas kernels, first_gather(): pl.pallas_call(functools.partial(first_body, tuple(swapped), depth, len(n...  48.4 us
  transfers between devices with their start and end apart: 7, of which 1 were waited for; matrix products, arithmetic and copies ran while one was open for 6% of the time, Pallas kernels for 59%

profile of v5, /device:TPU:0, one launch (start us, length us, event | category | flops | bytes accessed | tf_op | source)
XLA Modules:
  0.0 696.3 jit_solution(14052790782514236562)
XLA Ops:
  0.7 0.8 slice_bitcast_fusion.27
  1.5 0.7 pad_maximum_fusion.11
  2.7 1.8 constant_dynamic-slice_fusion.2
  4.6 2.6 collective-permute-start
  8.4 0.6 slice_bitcast_fusion.4
  9.1 0.7 slice_bitcast_fusion.1
  10.7 0.7 pad_maximum_fusion.9.refs_14_
  11.4 0.7 pad_maximum_fusion.8.refs_13_
  12.0 0.7 pad_maximum_fusion.7.refs_3_
  12.7 0.7 pad_maximum_fusion.6.refs_0_
  13.3 48.4 %first_gather.1 = (bf16[4,2,2,48,1152]{4,3,2,1,0:T(8,128)(2,1)}, bf16[4,2,2,48,384]{4,3,2,1,0:T(8,128)(2,1)}, bf16[4,2,2,48,384]{4,3,2,1,0:T(8,128)(2,1)}, bf16[...) custom-call(bf16[48,1152]{1,0:T(8,128)(2,1)} %pad_maximum_fusion.6.r, ...), custom_call_target="tpu_custom_call" | custom-call | flops 20000000000 | bytes 30000000 | tf_op jit(solution)/shard_map/first_gather/pallas_call | solution.py:804
  61.8 1.4 fusion.10
  63.1 0.7 slice_bitcast_fusion
  63.9 1.3 fusion.refs_1_.refs_2_
  67.1 0.9 copy.133
  69.8 1.4 collective-permute-done.1
  71.4 1.8 maximum_convert_fusion.refs_0_
  73.2 49.8 %temporal_forward.2 = (f32[4,208,768]{2,1,0:T(8,128)}, f32[4,208,768]{2,1,0:T(8,128)}, f32[4,208,1]{2,1,0:T(8,128)}, bf16[8,208,768]{2,1,0:T(8,128)(2,1)}, bf16[...) custom-call(f32[4,208,768]{2,1,0:T(8,128)} %maximum_convert_fusion.r, ...), custom_call_target="tpu_custom_call" | custom-call | flops 20000000000 | bytes 30000000 | tf_op jit(solution)/shard_map/temporal_forward/pallas_call | solution.py:745
  123.0 28.8 %spatial_forward.2 = (f32[4,208,768]{2,1,0:T(8,128)}, f32[4,208,768]{2,1,0:T(8,128)}, f32[4,208,1]{2,1,0:T(8,128)}, bf16[4,208,768]{2,1,0:T(8,128)(2,1)}, bf16[4...) custom-call(s32[1]{0:T(128)} %bitcast.1.refs_0_, ...), custom_call_target="tpu_custom_call" | custom-call | flops 20000000000 | bytes 30000000 | tf_op jit(solution)/shard_map/spatial_forward/pallas_call | solution.py:745
  151.8 35.0 %feed_forward.2 = (f32[4,208,768]{2,1,0:T(8,128)}, f32[4,208,768]{2,1,0:T(8,128)}, f32[4,208,1]{2,1,0:T(8,128)}, bf16[4,208,768]{2,1,0:T(8,128)(2,1)}, bf16[4,20...) custom-call(f32[4,208,768]{2,1,0:T(8,128)} %get-tuple-element.169.re, ...), custom_call_target="tpu_custom_call" | custom-call | flops 20000000000 | bytes 30000000 | tf_op jit(solution)/shard_map/feed_forward/pallas_call | solution.py:745
  186.8 46.3 %temporal_forward.3 = (f32[4,208,768]{2,1,0:T(8,128)}, f32[4,208,768]{2,1,0:T(8,128)}, f32[4,208,1]{2,1,0:T(8,128)}, bf16[8,208,768]{2,1,0:T(8,128)(2,1)}, bf16[...) custom-call(f32[4,208,768]{2,1,0:T(8,128)} %get-tuple-element.177.re, ...), custom_call_target="tpu_custom_call" | custom-call | flops 20000000000 | bytes 30000000 | tf_op jit(solution)/shard_map/temporal_forward/pallas_call | solution.py:745
  233.1 30.8 %spatial_forward.3 = (f32[4,208,768]{2,1,0:T(8,128)}, f32[4,208,768]{2,1,0:T(8,128)}, f32[4,208,1]{2,1,0:T(8,128)}, bf16[4,208,768]{2,1,0:T(8,128)(2,1)}, bf16[4...) custom-call(s32[1]{0:T(128)} %bitcast.1.refs_0_, ...), custom_call_target="tpu_custom_call" | custom-call | flops 20000000000 | bytes 30000000 | tf_op jit(solution)/shard_map/spatial_forward/pallas_call | solution.py:745
  263.9 26.8 %feed_forward.3 = (f32[4,208,768]{2,1,0:T(8,128)}, f32[4,208,768]{2,1,0:T(8,128)}, f32[4,208,1]{2,1,0:T(8,128)}, bf16[4,208,768]{2,1,0:T(8,128)(2,1)}, bf16[4,20...) custom-call(f32[4,208,768]{2,1,0:T(8,128)} %get-tuple-element.191.re, ...), custom_call_target="tpu_custom_call" | custom-call | flops 20000000000 | bytes 30000000 | tf_op jit(solution)/shard_map/feed_forward/pallas_call | solution.py:745
  290.7 1.3 bitcast_select_fusion
  292.0 1.1 copy.72
  293.7 0.7 compare_convert_fusion
  294.8 1.1 copy.65
  296.3 1.3 broadcast_select_fusion.3
  297.6 2.1 convert_multiply_fusion.refs_0_
  299.7 38.9 %feed_back.2 = (f32[4,208,768]{2,1,0:T(8,128)}, f32[8,768]{1,0:T(8,128)}, bf16[768,1536]{1,0:T(8,128)(2,1)}, bf16[768,1536]{1,0:T(8,128)(2,1)}, f32[1,1536]{1,0:T(1,128)}, /*index=5*/f32[1,1536]{1,0:T(1,128)}) custom-call(f32[4,208,768]{2,1,0:T(8,128)} %convert_multiply_fusion.refs_0_, bf16[4,208,768]{2,1,0:T(8,128)(2,1)} %get-tuple-element.198.refs_1_, ...), custom_call_target="tpu_custom_call" | custom-call | flops 24000000000 | bytes 30000000 | tf_op jit(solution)/shard_map/feed_back/pallas_call | solution.py:1196
  338.6 55.5 %spatial_stage.2 = (f32[4,208,768]{2,1,0:T(8,128)}, f32[8,768]{1,0:T(8,128)}, f32[8,768]{1,0:T(8,128)}, bf16[768,1152]{1,0:T(8,128)(2,1)}, bf16[768,384]{1,0:T(8...) custom-call(s32[1]{0:T(128)} %bitcast.1.refs_0_, f32[4,208,768]{2,1,0:T(8,128)} %get-tuple-element.205.refs_1_, ...), custom_call_target="tpu_custom_call" | custom-call | flops 24000000000 | bytes 30000000 | tf_op jit(solution)/shard_map/spatial_stage/pallas_call | solution.py:1344
  394.1 55.3 %temporal_stage.2 = (f32[4,208,768]{2,1,0:T(8,128)}, f32[8,768]{1,0:T(8,128)}, f32[8,768]{1,0:T(8,128)}, bf16[768,1152]{1,0:T(8,128)(2,1)}, bf16[768,384]{1,0:T(...) custom-call(f32[4,208,768]{2,1,0:T(8,128)} %get-tuple-element.215.refs_0, ...), custom_call_target="tpu_custom_call" | custom-call | flops 24000000000 | bytes 30000000 | tf_op jit(solution)/shard_map/temporal_stage/pallas_call | solution.py:1535
  449.4 50.2 %feed_back.3 = (f32[4,208,768]{2,1,0:T(8,128)}, f32[8,768]{1,0:T(8,128)}, bf16[768,1536]{1,0:T(8,128)(2,1)}, bf16[768,1536]{1,0:T(8,128)(2,1)}, f32[1,1536]{1,0:...) custom-call(f32[4,208,768]{2,1,0:T(8,128)} %get-tuple-element.225.refs_0_, ...), custom_call_target="tpu_custom_call" | custom-call | flops 24000000000 | bytes 30000000 | tf_op jit(solution)/shard_map/feed_back/pallas_call | solution.py:1196
  499.6 51.8 %spatial_stage.3 = (f32[4,208,768]{2,1,0:T(8,128)}, f32[8,768]{1,0:T(8,128)}, f32[8,768]{1,0:T(8,128)}, bf16[768,1152]{1,0:T(8,128)(2,1)}, bf16[768,384]{1,0:T(8...) custom-call(s32[1]{0:T(128)} %bitcast.1.refs_0_, f32[4,208,768]{2,1,0:T(8,128)} %get-tuple-element.236.refs_1_, ...), custom_call_target="tpu_custom_call" | custom-call | flops 24000000000 | bytes 30000000 | tf_op jit(solution)/shard_map/spatial_stage/pallas_call | solution.py:1344
  551.4 0.8 fusion.14
  552.2 1.3 broadcast_select_fusion.14
  553.6 0.8 fusion.13
  554.6 0.6 fusion.4
  555.2 60.0 %temporal_stage.3 = (f32[4,208,768]{2,1,0:T(8,128)}, f32[8,768]{1,0:T(8,128)}, f32[8,768]{1,0:T(8,128)}, bf16[768,1152]{1,0:T(8,128)(2,1)}, bf16[768,384]{1,0:T(...) custom-call(f32[4,208,768]{2,1,0:T(8,128)} %get-tuple-element.246.re, ...), custom_call_target="tpu_custom_call" | custom-call | flops 24000000000 | bytes 30000000 | tf_op jit(solution)/shard_map/temporal_stage/pallas_call | solution.py:1535
  615.3 0.7 slice.226
  616.0 0.8 fusion.11
  616.9 0.9 slice_bitcast_fusion.25
  617.8 0.7 slice_bitcast_fusion.23
  618.6 1.3 broadcast_select_fusion.10
  619.9 1.1 copy.68
  621.1 0.7 copy.92
  621.8 1.3 broadcast_select_fusion.12
  624.0 0.8 stack_reshape.14
  624.8 0.8 stack_reshape.15
  626.2 1.0 maximum_bitcast_fusion.3
  627.2 1.0 maximum_bitcast_fusion.1
  628.1 0.7 maximum_bitcast_fusion.5
  628.8 0.9 pad_maximum_fusion.3
  629.7 0.9 pad_maximum_fusion.2
  630.5 1.1 broadcast_select_fusion.8
  631.6 51.4 %sum_rows.1 = (f32[48,1152]{1,0:T(8,128)}, f32[48,384]{1,0:T(8,128)}, f32[24,768]{1,0:T(8,128)}, f32[8,768]{1,0:T(8,128)}, bf16[4,98,768]{2,1,0:T(8,128)(2,1)}) custom-call(bf16[4,2,2,48,1152]{4,3,2,1,0:T(8,128)(2,1)} %bitcast.237, bf16[4,2,2,48,384]{4,3,2,1,0:T(8,128)(2,1)} %bitcast.265, bf16[4,2,2,24,768]{4,3,2,1,0:T(8,128)(2,1)} %bitcast.266, ...), custom_call_target="tpu_custom_call" | custom-call | flops 20000000000 | bytes 30000000 | tf_op jit(solution)/shard_map/sum_rows/pallas_call | solution.py:521
  683.0 0.7 slice_bitcast_fusion.26
  683.7 0.7 slice_bitcast_fusion.24
  684.5 1.4 select_bitcast_fusion.3
  686.1 1.5 copy.80
  690.7 1.0 copy.84
  692.0 2.4 copy.81
  694.4 0.7 pad_maximum_fusion.4
  695.2 0.7 pad_maximum_fusion.5
  (158 shorter events, 12.6 us)
Async XLA Ops:
  0.6 6.5 copy-start.39
  0.7 7.1 %copy-start.24 = (bf16[2,24,768]{2,1,0:T(8,128)(2,1)S(1)}, bf16[2,24,768]{2,1,0:T(8,128)(2,1)}, u32[]{:S(2)}) copy-start(bf16[2,24,768]{2,1,0:T(8,128)(2,1)} %param.24) | copy-start | bytes 221188
  0.7 7.7 %copy-start.20 = (bf16[2,2,384,48]{2,3,1,0:T(8,128)(2,1)S(1)}, bf16[2,2,384,48]{2,3,1,0:T(8,128)(2,1)}, u32[]{:S(2)}) copy-start(bf16[2,2,384,48]{2,3,1,0:T(8,128)(2,1)} %param.22) | copy-start | bytes 442372
  0.7 8.4 %copy-start.12 = (bf16[2,48,1536]{2,1,0:T(8,128)(2,1)S(1)}, bf16[2,48,1536]{2,1,0:T(8,128)(2,1)}, u32[]{:S(2)}) copy-start(bf16[2,48,1536]{2,1,0:T(8,128)(2,1)} %param.25) | copy-start | bytes 884740
  0.7 9.1 %copy-start.11 = (bf16[2,2,48,3,384]{4,2,3,1,0:T(8,128)(2,1)S(1)}, bf16[2,2,48,3,384]{4,2,3,1,0:T(8,128)(2,1)}, u32[]{:S(2)}) copy-start(bf16[2,2,48,3,384]{4,2,3,1,0:T(8,128)(2,1)} %param.20) | copy-start | bytes 1327108
  2.2 65.8 %collective-permute-start.2 = (f32[2,2304]{1,0:T(2,128)S(1)}, f32[2,2304]{1,0:T(2,128)S(1)}, u32[]{:S(2)}, u32[]{:S(2)}) collective-permute-start(f32[2,2304]{1,0:T(2,128)S(1)} %pad_maximum_fusion.11), channel_id=1, source_target_pairs={{0,1},{1,0},{2,3},{3,2},{4,5},{5,4},{6,7},{7,6},{8,9},{9,8},{10,11... | collective-permute-start | bytes 55304 | tf_op jit(solution)/shard_map/ppermute | solution.py:145
  2.7 7.1 %copy-start.5 = (f32[2,4,98,768]{3,1,2,0:T(4,128)S(1)}, f32[2,4,98,768]{3,1,2,0:T(4,128)}, u32[]{:S(2)}) copy-start(f32[2,4,98,768]{3,1,2,0:T(4,128)} %param.15) | copy-start | bytes 7225348
  4.6 64.1 %collective-permute-start = (bf16[4,98,768]{2,0,1:T(4,128)(2,1)S(1)}, bf16[4,98,768]{2,0,1:T(4,128)(2,1)S(1)}, u32[]{:S(2)}, u32[]{:S(2)}) collective-permute-start(bf16[4,98,768]{2,0,1:T(4,128)(2,1)S(1)} %get-tuple-element.355), channel_id=1, source_target_pairs={{0,2},{1,3},{2,0},{3,1},{4,6},{5,7},{6,4},{7,5},{8,10},{9,11},{10,... | collective-permute-start | bytes 1806344 | tf_op jit(solution)/shard_map/ppermute | solution.py:145
  13.3 48.4 %copy-start.38 = (s32[10]{0:T(128)S(1)}, s32[10]{0:T(128)}, u32[]{:S(2)}) copy-start(s32[10]{0:T(128)} %param.17) | copy-start | bytes 124
  13.3 49.8 %copy-start.13 = (bf16[2,1536,48]{1,2,0:T(8,128)(2,1)S(1)}, bf16[2,1536,48]{1,2,0:T(8,128)(2,1)}, u32[]{:S(2)}) copy-start(bf16[2,1536,48]{1,2,0:T(8,128)(2,1)} %param.27) | copy-start | bytes 884740
  13.3 51.9 %copy-start.31 = (f32[2,4,768]{2,1,0:T(4,128)S(1)}, f32[2,4,768]{2,1,0:T(4,128)}, u32[]{:S(2)}) copy-start(f32[2,4,768]{2,1,0:T(4,128)} %param.23) | copy-start | bytes 73732
  13.3 52.5 %copy-start.32 = (f32[2,3,768]{2,0,1:T(2,128)S(1)}, f32[2,3,768]{2,0,1:T(2,128)}, u32[]{:S(2)}) copy-start(f32[2,3,768]{2,0,1:T(2,128)} %param.18) | copy-start | bytes 55300
  13.3 53.1 %copy-start.33 = (f32[2,3,768]{2,0,1:T(2,128)S(1)}, f32[2,3,768]{2,0,1:T(2,128)}, u32[]{:S(2)}) copy-start(f32[2,3,768]{2,0,1:T(2,128)} %param.19) | copy-start | bytes 55300
  69.1 2.1 collective-permute-start.1
  290.7 3.8 copy-start.3
  293.0 3.3 collective-permute-start.5
  294.6 3.0 copy-start
  294.6 1.8 copy-start.4
  295.8 322.7 %collective-permute-start.3 = (bf16[4,98,768]{2,0,1:T(4,128)(2,1)}, bf16[4,98,768]{2,0,1:T(4,128)(2,1)}, u32[]{:S(2)}, u32[]{:S(2)}) collective-permute-start(bf16[4,98,768]{2,0,1:T(4,128)(2,1)} %copy.65), channel_id=1, source_target_pairs={{0,1},{1,0},{2,3},{3,2},{4,5},{5,4},{6,7},{7,6},{8,9},{9,8},{10,11... | collective-permute-start | bytes 1806344 | tf_op jit(solution)/shard_map/ppermute | solution.py:145
  499.6 54.8 %copy-start.37 = (f32[1,1536]{1,0:T(1,128)S(1)}, f32[1,1536]{1,0:T(1,128)}, u32[]{:S(2)}) copy-start(f32[1,1536]{1,0:T(1,128)} %get-tuple-element.262) | copy-start | bytes 18436
  499.6 54.8 %copy-start.36 = (f32[1,1536]{1,0:T(1,128)S(1)}, f32[1,1536]{1,0:T(1,128)}, u32[]{:S(2)}) copy-start(f32[1,1536]{1,0:T(1,128)} %get-tuple-element.263) | copy-start | bytes 18436
  499.6 54.9 %copy-start.35 = (f32[1,1536]{1,0:T(1,128)S(1)}, f32[1,1536]{1,0:T(1,128)}, u32[]{:S(2)}) copy-start(f32[1,1536]{1,0:T(1,128)} %get-tuple-element.265) | copy-start | bytes 18436
  499.6 54.9 %copy-start.34 = (f32[1,1536]{1,0:T(1,128)S(1)}, f32[1,1536]{1,0:T(1,128)}, u32[]{:S(2)}) copy-start(f32[1,1536]{1,0:T(1,128)} %get-tuple-element.266) | copy-start | bytes 18436
  555.2 63.3 %copy-start.1 = (bf16[4,208,768]{2,1,0:T(8,128)(2,1)S(1)}, bf16[4,208,768]{2,1,0:T(8,128)(2,1)}, u32[]{:S(2)}) copy-start(bf16[4,208,768]{2,1,0:T(8,128)(2,1)} %copy-done) | copy-start | bytes 3833860
  616.8 4.1 copy-start.2
  616.9 4.2 copy-start.23
  620.9 2.9 copy-start.18
  620.9 3.0 copy-start.17
  620.9 63.5 %collective-permute-start.4 = (bf16[4,98,768]{2,0,1:T(4,128)(2,1)}, bf16[4,98,768]{2,0,1:T(4,128)(2,1)}, u32[]{:S(2)}, u32[]{:S(2)}) collective-permute-start(bf16[4,98,768]{2,0,1:T(4,128)(2,1)} %copy.68), channel_id=1, source_target_pairs={{0,2},{1,3},{2,0},{3,1},{4,6},{5,7},{6,4},{7,5},{8,10},{9,11},{10,... | collective-permute-start | bytes 1806344 | tf_op jit(solution)/shard_map/ppermute | solution.py:145
  620.9 3.8 copy-start.16
  623.8 2.3 copy-start.21
  623.8 2.3 copy-start.22
  625.6 1.6 copy-start.7
  625.6 1.6 copy-start.8
  625.6 2.6 copy-start.26
  625.6 2.6 copy-start.27
  625.8 3.9 copy-start.14
  625.8 3.9 copy-start.15
  626.0 4.5 collective-permute-start.6
  685.9 1.7 slice-start
  685.9 4.2 copy-start.19
  686.1 4.3 copy-start.6
  690.4 1.3 copy-start.9
  692.0 2.4 copy-start.28
  692.0 2.4 copy-start.30
  692.0 2.4 copy-start.10
  692.0 3.1 copy-start.25
  692.0 3.1 copy-start.29

commit v6 on v5

--- a/solution.py
+++ b/solution.py
@@ -300,7 +300,7 @@
 
 
 class Carrier:
-    def __init__(self, place, cores, starts, sources, parts, owns, scratch):
+    def __init__(self, place, cores, starts, sources, parts, owns, scratch, most=2):
         self.place, self.cores = place, cores
         lanes = [pl.ds(start, own.shape[1]) for start, own in zip(starts, owns)]
         sources = [ref.at[:, :, :, :, cols] for ref, cols in zip(sources, lanes)]
@@ -309,27 +309,30 @@
             Sums(place, source, part, own, *scratch[10 * i : 10 * i + 10])
             for i, (source, part, own) in enumerate(zip(sources, parts, owns))
         ]
+        self.groups = [[item] for item in self.sums[: most - 1]]
+        if self.sums[most - 1 :]:
+            self.groups.append(self.sums[most - 1 :])
+
+    def begin(self):
+        self.place.meet(bool(self.sums), self.cores)
+        for item in self.sums:
+            item.first()
 
     def step(self, number):
-        lead, rest = self.sums[:1], self.sums[1:]
         if number == 0:
-            self.place.meet(bool(self.sums), self.cores)
-            for item in lead + rest:
-                item.first()
-        elif number == 1:
-            for item in lead:
+            self.begin()
+            return
+        last = len(self.groups)
+        if 2 <= number <= last + 1:
+            for item in self.groups[number - 2]:
+                item.third()
+        if number <= last:
+            for item in self.groups[number - 1]:
                 item.second()
-        elif number == 2:
-            for item in lead:
-                item.third()
-            for item in rest:
-                item.second()
-        elif number == 3:
-            for item in rest:
-                item.third()
-        else:
-            for item in lead + rest:
-                item.last()
+
+    def end(self):
+        for item in self.sums:
+            item.last()
 
 
 def carried(grid, parts):
@@ -415,13 +418,20 @@
         for item in copies:
             item.wait()
 
-    def flush(self):
-        copies = [pltpu.make_async_copy(src, dst, sem) for dst, src, sem in self.out_moves]
+    def move_out(self, moves):
+        copies = [pltpu.make_async_copy(src, dst, sem) for dst, src, sem in moves]
         for item in copies:
             item.start()
         for item in copies:
             item.wait()
 
+    def flush(self, count=None):
+        self.moved = len(self.out_moves) if count is None else sum(self.outs[:count])
+        self.move_out(self.out_moves[: self.moved])
+
+    def flush_rest(self):
+        self.move_out(self.out_moves[self.moved :])
+
 
 def row_of(ref, index):
     return ref.at[pl.ds(index, 1)]
@@ -435,9 +445,10 @@
 class Hops:
     def __init__(self, place, pieces, refs, total, held, came, send, recv):
         z = place.z
-        targets = [place.over_t(), place.over_y(), place.over_x()]
+        targets = [place.over_t()]
         targets.append({"shard": (z + 1 - 2 * lax.rem(z, 2)) * 2 + place.x})
         targets.append({"shard": (z + 2 - 4 * (z // 2)) * 2 + place.x})
+        targets += [place.over_x(), place.over_y()]
         self.pieces, self.refs = pieces, refs
         self.total, self.held, self.came = total, held, came
         self.copies = [
@@ -501,13 +512,13 @@
     across = remote(away, back, send.at[0], recv.at[0], place.over_y())
     carrier.step(0)
     hops.begin()
-    for number in range(1, 5):
+    for number in range(1, 4):
         hops.hop(number)
-        if number < 4:
-            carrier.step(number)
+        carrier.step(number)
+    hops.hop(4)
     across.start()
     hops.hop(5)
-    carrier.step(4)
+    carrier.end()
     across.wait()
 
 
@@ -1115,13 +1126,11 @@
     def work(down, up, active, slope, h_sum):
         lanes = down.shape[1]
 
-        def one(f, carry):
-            value = (dot_nn(r[f], down[...]) * slope[f].astype(F32)).astype(BF)
-            bh[f] = value
-            out[f] += dot_nt(value, up[...])
-            return carry + column_sum(value.astype(F32))
-
-        h_sum[...] = lax.fori_loop(0, frames, one, jnp.zeros((1, lanes), F32))
+        value = dot_nn(r[...].reshape(rows_all, width), down[...])
+        value = (value * slope[...].reshape(rows_all, lanes).astype(F32)).astype(BF)
+        bh[...] = value.reshape(frames, padded, lanes)
+        h_sum[...] = column_sum(value.astype(F32))
+        out[...] += dot_nt(value, up[...]).reshape(frames, padded, width)
         return (
             dot_nn(nt[...], bh[...].reshape(rows_all, lanes)),
             dot_nn(rt[...], active[...].reshape(rows_all, lanes)),
@@ -1166,7 +1175,7 @@
 
         zero = jnp.zeros((1, width), F32)
         sums[0:1], sums[1:2] = lax.fori_loop(0, frames, finish, (zero, zero))
-        carrier.step(4)
+        carrier.end()
 
 
 def feed_back(grid, number, layer, state, kept, gain, w, parts):
@@ -1250,7 +1259,7 @@
     owns = take(count)
     r, bm0, bm1, b0, b1, rt, nt, s_tri, r_tri, s_merge, r_merge, send, recv = take(13)
     place = Place(depth)
-    carrier = Carrier(place, True, starts, sources, parts, owns, take(10 * count))
+    carrier = Carrier(place, True, starts, sources, parts, owns, take(10 * count), 3)
     frames, padded, width = state.shape
     rows_all = frames * padded
     split = merge0.shape[1]
@@ -1278,11 +1287,12 @@
 
     sums[...] = jnp.zeros_like(sums)
     q_sums[...] = jnp.zeros_like(q_sums)
-    half = frames // 2
-    total = lax.fori_loop(0, half, one, jnp.zeros((1, width), F32))
-    carrier.step(1)
-    sums[2:3] = lax.fori_loop(half, frames, one, total)
-    carrier.step(2)
+    total = jnp.zeros((1, width), F32)
+    for number in range(3):
+        total = lax.fori_loop(number, number + 1, one, total)
+        carrier.step(number + 1)
+    sums[2:3] = lax.fori_loop(3, frames, one, total)
+    carrier.step(4)
     rt[...] = r[...].reshape(rows_all, width).T
     nt[...] = normed[...].reshape(rows_all, width).T
     flat = lambda ref, part: ref[:, :, part * split : (part + 1) * split].reshape(rows_all, split)
@@ -1294,7 +1304,6 @@
         cols = slice(part * split, (part + 1) * split)
         s_tri[:, cols] = dot_nn(nt[...], flat(b1, part)).astype(BF)
     swap_tri.start()
-    carrier.step(3)
 
     def finish(f, carry):
         e = dot_nt(b0[f], tri0[...]) + dot_nt(b1[f], tri1[...])
@@ -1321,8 +1330,9 @@
         cols = slice(part * split, (part + 1) * split)
         mine = dot_nn(nt[...], flat(b0, part))
         g_tri[:, cols] = (mine + r_tri[:, cols].astype(F32)).astype(BF)
-    carrier.step(4)
-    staging.flush()
+    staging.flush(5)
+    carrier.end()
+    staging.flush_rest()
 
 
 def spatial_back(grid, number, layer, count_ref, state, kept, gain, w, parts, places, att_scale):
@@ -1504,8 +1514,9 @@
     q_sums[0:1, split:] = wide[:, 2 * split :]
     if chained:
         hops.hop(5)
-    carrier.step(4)
-    staging.flush()
+    staging.flush(6)
+    carrier.end()
+    staging.flush_rest()
 
 
 def temporal_back(grid, number, layer, state, kept, gain, w, parts, att_scale, small=None):
@@ -1865,7 +1876,8 @@
         arrived_sums(got)
         cut = hid // 2
         carry_sums(
-            [("up", layer), ("down_a", layer)], [(parts_m[0], 0, hid), (parts_m[1], 0, cut)]
+            [("up_a", layer), ("up_b", layer), ("down_a", layer)],
+            [(parts_m[0], 0, cut), (parts_m[0], cut, cut), (parts_m[1], 0, cut)],
         )
         upstream, vec_s, entry_s, parts_s, got = spatial_back(
             grid,
@@ -1951,10 +1963,13 @@
         small, early = small.plain(), early_rows.plain()
         out_got = grid.over_y(out_low)
     input_grad = spread_last(out_got, out_ready).astype(F32)
-    names = ("triple_t", "merge_t", "mix", "triple_s", "merge_s", "up")
+    names = ("triple_t", "merge_t", "mix", "triple_s", "merge_s")
     for layer in range(LAYERS):
-        down = jnp.concatenate([sums["down_a", layer], sums["down_b", layer]], axis=1)
-        shards[layer] = [sums[name, layer] for name in names] + [down]
+        up, down = [
+            jnp.concatenate([sums[name + "_a", layer], sums[name + "_b", layer]], axis=1)
+            for name in ("up", "down")
+        ]
+        shards[layer] = [sums[name, layer] for name in names] + [up, down]
     block = 6 * LAYERS
     pairs = early[:block].reshape(LAYERS, 2, 3, width)
     ends = jnp.stack([small[:4], early[block : block + 4]])

time: 700 us -> 679 us (0.970)
  Pallas kernels: 629 us -> 606 us
    pallas_call x2, Pallas kernels: 89.1 us -> 78.2 us  [feed_back(): pl.pallas_call(functools.partial(feed_back_body, grid.depth, starts_of(pa...]
  transfers between devices with their start and end apart: 7 -> 7, of which waited for: 1 -> 1; matrix products, arithmetic and copies ran while one was open for 6% -> 6% of each run, Pallas kernels for 59% -> 58%
where the time goes in v6:
time: 679 us; the launch traced here: 674 us
  Pallas kernels  606 us (89%)
  local copies, waits for them, and re-layouts  29.9 us (4%)
  other arithmetic  29.5 us (4%)
    pallas_call x6, Pallas kernels, kernel_call(): pl.pallas_call(functools.partial(body, staging), in_specs=staging.in_spec...  217 us
    pallas_call x2, Pallas kernels, temporal_back(): pl.pallas_call(functools.partial(temporal_back_body, grid.depth, starts_o...  110 us
    pallas_call x2, Pallas kernels, spatial_back(): pl.pallas_call(functools.partial(spatial_back_body, grid.depth, starts_of...  105 us
    pallas_call x2, Pallas kernels, feed_back(): pl.pallas_call(functools.partial(feed_back_body, grid.depth, starts_of(pa...  78.2 us
    pallas_call x1, Pallas kernels, first_gather(): pl.pallas_call(functools.partial(first_body, tuple(swapped), depth, len(n...  48.4 us
    pallas_call x1, Pallas kernels, tail_sums(): pl.pallas_call(functools.partial(tail_body, grid.depth, starts_of(parts),...  47.7 us
  transfers between devices with their start and end apart: 7, of which 1 were waited for; matrix products, arithmetic and copies ran while one was open for 6% of the time, Pallas kernels for 58%

profile of v6, /device:TPU:0, one launch (start us, length us, event | category | flops | bytes accessed | tf_op | source)
XLA Modules:
  0.0 674.3 jit_solution(10388948304129616008)
XLA Ops:
  0.7 0.8 slice_bitcast_fusion.27
  1.5 0.7 pad_maximum_fusion.11
  2.7 1.8 constant_dynamic-slice_fusion.2
  4.6 2.6 collective-permute-start
  7.8 0.6 slice_bitcast_fusion.8
  8.4 0.7 slice_bitcast_fusion.4
  9.1 0.7 slice_bitcast_fusion.1
  10.7 0.7 pad_maximum_fusion.9.refs_14_
  11.4 0.7 pad_maximum_fusion.8.refs_13_
  12.0 0.7 pad_maximum_fusion.7.refs_3_
  12.7 0.7 pad_maximum_fusion.6.refs_0_
  13.4 48.4 %first_gather.1 = (bf16[4,2,2,48,1152]{4,3,2,1,0:T(8,128)(2,1)}, bf16[4,2,2,48,384]{4,3,2,1,0:T(8,128)(2,1)}, bf16[4,2,2,48,384]{4,3,2,1,0:T(8,128)(2,1)}, bf16[...) custom-call(bf16[48,1152]{1,0:T(8,128)(2,1)} %pad_maximum_fusion.6.r, ...), custom_call_target="tpu_custom_call" | custom-call | flops 20000000000 | bytes 30000000 | tf_op jit(solution)/shard_map/first_gather/pallas_call | solution.py:815
  61.8 1.3 fusion.10
  63.1 0.7 slice_bitcast_fusion
  63.8 1.2 fusion.refs_1_.refs_2_
  66.9 0.9 copy.133
  69.6 1.4 collective-permute-done.1
  71.2 1.8 maximum_convert_fusion.refs_0_
  73.0 49.8 %temporal_forward.2 = (f32[4,208,768]{2,1,0:T(8,128)}, f32[4,208,768]{2,1,0:T(8,128)}, f32[4,208,1]{2,1,0:T(8,128)}, bf16[8,208,768]{2,1,0:T(8,128)(2,1)}, bf16[...) custom-call(f32[4,208,768]{2,1,0:T(8,128)} %maximum_convert_fusion.r, ...), custom_call_target="tpu_custom_call" | custom-call | flops 20000000000 | bytes 30000000 | tf_op jit(solution)/shard_map/temporal_forward/pallas_call | solution.py:756
  122.8 28.7 %spatial_forward.2 = (f32[4,208,768]{2,1,0:T(8,128)}, f32[4,208,768]{2,1,0:T(8,128)}, f32[4,208,1]{2,1,0:T(8,128)}, bf16[4,208,768]{2,1,0:T(8,128)(2,1)}, bf16[4...) custom-call(s32[1]{0:T(128)} %bitcast.1.refs_0_, ...), custom_call_target="tpu_custom_call" | custom-call | flops 20000000000 | bytes 30000000 | tf_op jit(solution)/shard_map/spatial_forward/pallas_call | solution.py:756
  151.5 34.8 %feed_forward.2 = (f32[4,208,768]{2,1,0:T(8,128)}, f32[4,208,768]{2,1,0:T(8,128)}, f32[4,208,1]{2,1,0:T(8,128)}, bf16[4,208,768]{2,1,0:T(8,128)(2,1)}, bf16[4,20...) custom-call(f32[4,208,768]{2,1,0:T(8,128)} %get-tuple-element.171.re, ...), custom_call_target="tpu_custom_call" | custom-call | flops 20000000000 | bytes 30000000 | tf_op jit(solution)/shard_map/feed_forward/pallas_call | solution.py:756
  186.4 46.3 %temporal_forward.3 = (f32[4,208,768]{2,1,0:T(8,128)}, f32[4,208,768]{2,1,0:T(8,128)}, f32[4,208,1]{2,1,0:T(8,128)}, bf16[8,208,768]{2,1,0:T(8,128)(2,1)}, bf16[...) custom-call(f32[4,208,768]{2,1,0:T(8,128)} %get-tuple-element.179.re, ...), custom_call_target="tpu_custom_call" | custom-call | flops 20000000000 | bytes 30000000 | tf_op jit(solution)/shard_map/temporal_forward/pallas_call | solution.py:756
  232.7 30.7 %spatial_forward.3 = (f32[4,208,768]{2,1,0:T(8,128)}, f32[4,208,768]{2,1,0:T(8,128)}, f32[4,208,1]{2,1,0:T(8,128)}, bf16[4,208,768]{2,1,0:T(8,128)(2,1)}, bf16[4...) custom-call(s32[1]{0:T(128)} %bitcast.1.refs_0_, ...), custom_call_target="tpu_custom_call" | custom-call | flops 20000000000 | bytes 30000000 | tf_op jit(solution)/shard_map/spatial_forward/pallas_call | solution.py:756
  263.4 26.6 %feed_forward.3 = (f32[4,208,768]{2,1,0:T(8,128)}, f32[4,208,768]{2,1,0:T(8,128)}, f32[4,208,1]{2,1,0:T(8,128)}, bf16[4,208,768]{2,1,0:T(8,128)(2,1)}, bf16[4,20...) custom-call(f32[4,208,768]{2,1,0:T(8,128)} %get-tuple-element.193.re, ...), custom_call_target="tpu_custom_call" | custom-call | flops 20000000000 | bytes 30000000 | tf_op jit(solution)/shard_map/feed_forward/pallas_call | solution.py:756
  289.9 1.3 bitcast_select_fusion
  291.3 1.1 copy.72
  293.9 1.1 copy.65
  295.4 1.3 broadcast_select_fusion.3
  296.7 2.1 convert_multiply_fusion.refs_0_
  298.8 32.1 %feed_back.2 = (f32[4,208,768]{2,1,0:T(8,128)}, f32[8,768]{1,0:T(8,128)}, bf16[768,1536]{1,0:T(8,128)(2,1)}, bf16[768,1536]{1,0:T(8,128)(2,1)}, f32[1,1536]{1,0:T(1,128)}, /*index=5*/f32[1,1536]{1,0:T(1,128)}) custom-call(f32[4,208,768]{2,1,0:T(8,128)} %convert_multiply_fusion.refs_0_, bf16[4,208,768]{2,1,0:T(8,128)(2,1)} %get-tuple-element.200.refs_1_, ...), custom_call_target="tpu_custom_call" | custom-call | flops 24000000000 | bytes 30000000 | tf_op jit(solution)/shard_map/feed_back/pallas_call | solution.py:1205
  330.8 54.1 %spatial_stage.2 = (f32[4,208,768]{2,1,0:T(8,128)}, f32[8,768]{1,0:T(8,128)}, f32[8,768]{1,0:T(8,128)}, bf16[768,1152]{1,0:T(8,128)(2,1)}, bf16[768,384]{1,0:T(8...) custom-call(s32[1]{0:T(128)} %bitcast.1.refs_0_, f32[4,208,768]{2,1,0:T(8,128)} %get-tuple-element.207.refs_1_, ...), custom_call_target="tpu_custom_call" | custom-call | flops 24000000000 | bytes 30000000 | tf_op jit(solution)/shard_map/spatial_stage/pallas_call | solution.py:1354
  384.9 52.8 %temporal_stage.2 = (f32[4,208,768]{2,1,0:T(8,128)}, f32[8,768]{1,0:T(8,128)}, f32[8,768]{1,0:T(8,128)}, bf16[768,1152]{1,0:T(8,128)(2,1)}, bf16[768,384]{1,0:T(...) custom-call(f32[4,208,768]{2,1,0:T(8,128)} %get-tuple-element.217.refs_0, ...), custom_call_target="tpu_custom_call" | custom-call | flops 24000000000 | bytes 30000000 | tf_op jit(solution)/shard_map/temporal_stage/pallas_call | solution.py:1546
  437.7 46.2 %feed_back.3 = (f32[4,208,768]{2,1,0:T(8,128)}, f32[8,768]{1,0:T(8,128)}, bf16[768,1536]{1,0:T(8,128)(2,1)}, bf16[768,1536]{1,0:T(8,128)(2,1)}, f32[1,1536]{1,0:...) custom-call(f32[4,208,768]{2,1,0:T(8,128)} %get-tuple-element.227.refs_0_, ...), custom_call_target="tpu_custom_call" | custom-call | flops 24000000000 | bytes 30000000 | tf_op jit(solution)/shard_map/feed_back/pallas_call | solution.py:1205
  484.0 51.0 %spatial_stage.3 = (f32[4,208,768]{2,1,0:T(8,128)}, f32[8,768]{1,0:T(8,128)}, f32[8,768]{1,0:T(8,128)}, bf16[768,1152]{1,0:T(8,128)(2,1)}, bf16[768,384]{1,0:T(8...) custom-call(s32[1]{0:T(128)} %bitcast.1.refs_0_, f32[4,208,768]{2,1,0:T(8,128)} %get-tuple-element.238.refs_1_, ...), custom_call_target="tpu_custom_call" | custom-call | flops 24000000000 | bytes 30000000 | tf_op jit(solution)/shard_map/spatial_stage/pallas_call | solution.py:1354
  535.0 0.8 fusion.14
  535.8 1.3 broadcast_select_fusion.14
  537.1 0.8 fusion.13
  538.8 57.4 %temporal_stage.3 = (f32[4,208,768]{2,1,0:T(8,128)}, f32[8,768]{1,0:T(8,128)}, f32[8,768]{1,0:T(8,128)}, bf16[768,1152]{1,0:T(8,128)(2,1)}, bf16[768,384]{1,0:T(...) custom-call(f32[4,208,768]{2,1,0:T(8,128)} %get-tuple-element.248.re, ...), custom_call_target="tpu_custom_call" | custom-call | flops 24000000000 | bytes 30000000 | tf_op jit(solution)/shard_map/temporal_stage/pallas_call | solution.py:1546
  596.1 0.7 slice.226
  596.9 0.8 fusion.11
  597.8 0.9 slice_bitcast_fusion.25
  598.7 0.7 slice_bitcast_fusion.23
  599.4 1.3 broadcast_select_fusion.10
  600.8 1.1 copy.68
  601.8 0.8 collective-permute-start.4
  602.8 0.7 copy.92
  603.5 1.3 broadcast_select_fusion.12
  605.7 0.8 stack_reshape.14
  606.5 0.8 stack_reshape.15
  607.9 1.0 maximum_bitcast_fusion.2
  608.9 1.0 maximum_bitcast_fusion.1
  609.9 0.7 maximum_bitcast_fusion.7
  610.6 0.9 pad_maximum_fusion.3
  611.5 0.9 pad_maximum_fusion.2
  612.4 1.1 broadcast_select_fusion.8
  613.4 47.7 %sum_rows.1 = (f32[48,1152]{1,0:T(8,128)}, f32[48,384]{1,0:T(8,128)}, f32[24,768]{1,0:T(8,128)}, f32[8,768]{1,0:T(8,128)}, bf16[4,98,768]{2,1,0:T(8,128)(2,1)}) custom-call(bf16[4,2,2,48,1152]{4,3,2,1,0:T(8,128)(2,1)} %bitcast.239, bf16[4,2,2,48,384]{4,3,2,1,0:T(8,128)(2,1)} %bitcast.267, bf16[4,2,2,24,768]{4,3,2,1,0:T(8,128)(2,1)} %bitcast.268, ...), custom_call_target="tpu_custom_call" | custom-call | flops 20000000000 | bytes 30000000 | tf_op jit(solution)/shard_map/sum_rows/pallas_call | solution.py:532
  661.2 0.7 slice_bitcast_fusion.26
  661.9 0.7 slice_bitcast_fusion.24
  662.7 1.4 select_bitcast_fusion.3
  664.3 1.5 copy.80
  668.9 1.0 copy.84
  670.2 2.4 copy.81
  672.6 0.7 pad_maximum_fusion.4
  673.4 0.7 pad_maximum_fusion.5
  (163 shorter events, 13.2 us)
Async XLA Ops:
  0.6 6.5 copy-start.41
  0.7 7.1 %copy-start.26 = (bf16[2,24,768]{2,1,0:T(8,128)(2,1)S(1)}, bf16[2,24,768]{2,1,0:T(8,128)(2,1)}, u32[]{:S(2)}) copy-start(bf16[2,24,768]{2,1,0:T(8,128)(2,1)} %param.24) | copy-start | bytes 221188
  0.7 7.8 %copy-start.22 = (bf16[2,2,384,48]{2,3,1,0:T(8,128)(2,1)S(1)}, bf16[2,2,384,48]{2,3,1,0:T(8,128)(2,1)}, u32[]{:S(2)}) copy-start(bf16[2,2,384,48]{2,3,1,0:T(8,128)(2,1)} %param.22) | copy-start | bytes 442372
  0.7 8.4 %copy-start.12 = (bf16[2,48,1536]{2,1,0:T(8,128)(2,1)S(1)}, bf16[2,48,1536]{2,1,0:T(8,128)(2,1)}, u32[]{:S(2)}) copy-start(bf16[2,48,1536]{2,1,0:T(8,128)(2,1)} %param.25) | copy-start | bytes 884740
  0.7 9.1 %copy-start.11 = (bf16[2,2,48,3,384]{4,2,3,1,0:T(8,128)(2,1)S(1)}, bf16[2,2,48,3,384]{4,2,3,1,0:T(8,128)(2,1)}, u32[]{:S(2)}) copy-start(bf16[2,2,48,3,384]{4,2,3,1,0:T(8,128)(2,1)} %param.20) | copy-start | bytes 1327108
  2.2 65.7 %collective-permute-start.2 = (f32[2,2304]{1,0:T(2,128)S(1)}, f32[2,2304]{1,0:T(2,128)S(1)}, u32[]{:S(2)}, u32[]{:S(2)}) collective-permute-start(f32[2,2304]{1,0:T(2,128)S(1)} %pad_maximum_fusion.11), channel_id=1, source_target_pairs={{0,1},{1,0},{2,3},{3,2},{4,5},{5,4},{6,7},{7,6},{8,9},{9,8},{10,11... | collective-permute-start | bytes 55304 | tf_op jit(solution)/shard_map/ppermute | solution.py:145
  2.7 7.1 %copy-start.5 = (f32[2,4,98,768]{3,1,2,0:T(4,128)S(1)}, f32[2,4,98,768]{3,1,2,0:T(4,128)}, u32[]{:S(2)}) copy-start(f32[2,4,98,768]{3,1,2,0:T(4,128)} %param.15) | copy-start | bytes 7225348
  4.6 63.9 %collective-permute-start = (bf16[4,98,768]{2,0,1:T(4,128)(2,1)S(1)}, bf16[4,98,768]{2,0,1:T(4,128)(2,1)S(1)}, u32[]{:S(2)}, u32[]{:S(2)}) collective-permute-start(bf16[4,98,768]{2,0,1:T(4,128)(2,1)S(1)} %get-tuple-element.359), channel_id=1, source_target_pairs={{0,2},{1,3},{2,0},{3,1},{4,6},{5,7},{6,4},{7,5},{8,10},{9,11},{10,... | collective-permute-start | bytes 1806344 | tf_op jit(solution)/shard_map/ppermute | solution.py:145
  13.3 48.4 %copy-start.40 = (s32[10]{0:T(128)S(1)}, s32[10]{0:T(128)}, u32[]{:S(2)}) copy-start(s32[10]{0:T(128)} %param.17) | copy-start | bytes 124
  13.3 49.7 %copy-start.13 = (bf16[2,1536,48]{1,2,0:T(8,128)(2,1)S(1)}, bf16[2,1536,48]{1,2,0:T(8,128)(2,1)}, u32[]{:S(2)}) copy-start(bf16[2,1536,48]{1,2,0:T(8,128)(2,1)} %param.27) | copy-start | bytes 884740
  13.3 51.7 %copy-start.33 = (f32[2,4,768]{2,1,0:T(4,128)S(1)}, f32[2,4,768]{2,1,0:T(4,128)}, u32[]{:S(2)}) copy-start(f32[2,4,768]{2,1,0:T(4,128)} %param.23) | copy-start | bytes 73732
  13.4 52.3 %copy-start.34 = (f32[2,3,768]{2,0,1:T(2,128)S(1)}, f32[2,3,768]{2,0,1:T(2,128)}, u32[]{:S(2)}) copy-start(f32[2,3,768]{2,0,1:T(2,128)} %param.18) | copy-start | bytes 55300
  13.4 52.9 %copy-start.35 = (f32[2,3,768]{2,0,1:T(2,128)S(1)}, f32[2,3,768]{2,0,1:T(2,128)}, u32[]{:S(2)}) copy-start(f32[2,3,768]{2,0,1:T(2,128)} %param.19) | copy-start | bytes 55300
  68.9 2.1 collective-permute-start.1
  289.9 3.6 copy-start.3
  292.3 3.1 collective-permute-start.5
  293.7 3.0 copy-start
  293.7 1.8 copy-start.4
  294.9 304.5 %collective-permute-start.3 = (bf16[4,98,768]{2,0,1:T(4,128)(2,1)}, bf16[4,98,768]{2,0,1:T(4,128)(2,1)}, u32[]{:S(2)}, u32[]{:S(2)}) collective-permute-start(bf16[4,98,768]{2,0,1:T(4,128)(2,1)} %copy.65), channel_id=1, source_target_pairs={{0,1},{1,0},{2,3},{3,2},{4,5},{5,4},{6,7},{7,6},{8,9},{9,8},{10,11... | collective-permute-start | bytes 1806344 | tf_op jit(solution)/shard_map/ppermute | solution.py:145
  483.9 54.0 %copy-start.39 = (f32[1,1536]{1,0:T(1,128)S(1)}, f32[1,1536]{1,0:T(1,128)}, u32[]{:S(2)}) copy-start(f32[1,1536]{1,0:T(1,128)} %get-tuple-element.264) | copy-start | bytes 18436
  483.9 54.0 %copy-start.38 = (f32[1,1536]{1,0:T(1,128)S(1)}, f32[1,1536]{1,0:T(1,128)}, u32[]{:S(2)}) copy-start(f32[1,1536]{1,0:T(1,128)} %get-tuple-element.265) | copy-start | bytes 18436
  483.9 54.1 %copy-start.37 = (f32[1,1536]{1,0:T(1,128)S(1)}, f32[1,1536]{1,0:T(1,128)}, u32[]{:S(2)}) copy-start(f32[1,1536]{1,0:T(1,128)} %get-tuple-element.267) | copy-start | bytes 18436
  483.9 54.1 %copy-start.36 = (f32[1,1536]{1,0:T(1,128)S(1)}, f32[1,1536]{1,0:T(1,128)}, u32[]{:S(2)}) copy-start(f32[1,1536]{1,0:T(1,128)} %get-tuple-element.268) | copy-start | bytes 18436
  538.8 60.7 %copy-start.1 = (bf16[4,208,768]{2,1,0:T(8,128)(2,1)S(1)}, bf16[4,208,768]{2,1,0:T(8,128)(2,1)}, u32[]{:S(2)}) copy-start(bf16[4,208,768]{2,1,0:T(8,128)(2,1)} %copy-done) | copy-start | bytes 3833860
  597.7 4.9 copy-start.2
  597.7 5.0 copy-start.25
  601.8 3.7 copy-start.16
  601.8 3.8 copy-start.15
  601.8 60.9 %collective-permute-start.4 = (bf16[4,98,768]{2,0,1:T(4,128)(2,1)}, bf16[4,98,768]{2,0,1:T(4,128)(2,1)}, u32[]{:S(2)}, u32[]{:S(2)}) collective-permute-start(bf16[4,98,768]{2,0,1:T(4,128)(2,1)} %copy.68), channel_id=1, source_target_pairs={{0,2},{1,3},{2,0},{3,1},{4,6},{5,7},{6,4},{7,5},{8,10},{9,11},{10,... | collective-permute-start | bytes 1806344 | tf_op jit(solution)/shard_map/ppermute | solution.py:145
  602.7 3.8 copy-start.14
  605.5 2.3 copy-start.23
  605.5 2.3 copy-start.24
  607.3 1.6 copy-start.7
  607.3 1.6 copy-start.8
  607.3 2.6 copy-start.18
  607.3 2.6 copy-start.19
  607.3 2.6 copy-start.20
  607.3 2.6 copy-start.21
  607.5 2.4 copy-start.28
  607.5 2.4 copy-start.29
  607.7 4.6 collective-permute-start.6
  664.1 1.7 slice-start
  664.1 4.2 copy-start.17
  664.3 4.3 copy-start.6
  668.6 1.3 copy-start.9
  670.2 2.4 copy-start.30
  670.2 2.4 copy-start.32
  670.2 2.4 copy-start.10
  670.2 3.1 copy-start.27
  670.2 3.1 copy-start.31

commit v7 on v6

--- a/solution.py
+++ b/solution.py
@@ -1142,6 +1142,13 @@
             remote(s_down.at[j], r_down.at[j], send.at[1, j], recv.at[1, j], place.over_t()),
         ]
 
+    for number, at in ((1, 1), (2, 3), (3, 4)):
+        if count:
+
+            @pl.when(i == at)
+            def _(number=number):
+                carrier.step(number)
+
     @pl.when(i < steps)
     def _():
         up_part, down_part = work(*oth, h_oth)
@@ -1149,13 +1156,6 @@
         s_down[i] = down_part.astype(BF)
         for item in swaps(i):
             item.start()
-
-    for number, at in ((1, 1), (2, 3), (3, 4)):
-        if count:
-
-            @pl.when(i == at)
-            def _(number=number):
-                carrier.step(number)
 
     @pl.when(i >= steps)
     def _():
@@ -1288,11 +1288,11 @@
     sums[...] = jnp.zeros_like(sums)
     q_sums[...] = jnp.zeros_like(q_sums)
     total = jnp.zeros((1, width), F32)
-    for number in range(3):
-        total = lax.fori_loop(number, number + 1, one, total)
-        carrier.step(number + 1)
+    total = lax.fori_loop(0, 2, one, total)
+    carrier.step(1)
+    total = lax.fori_loop(2, 3, one, total)
+    carrier.step(2)
     sums[2:3] = lax.fori_loop(3, frames, one, total)
-    carrier.step(4)
     rt[...] = r[...].reshape(rows_all, width).T
     nt[...] = normed[...].reshape(rows_all, width).T
     flat = lambda ref, part: ref[:, :, part * split : (part + 1) * split].reshape(rows_all, split)
@@ -1304,6 +1304,7 @@
         cols = slice(part * split, (part + 1) * split)
         s_tri[:, cols] = dot_nn(nt[...], flat(b1, part)).astype(BF)
     swap_tri.start()
+    carrier.step(3)
 
     def finish(f, carry):
         e = dot_nt(b0[f], tri0[...]) + dot_nt(b1[f], tri1[...])
@@ -1320,6 +1321,7 @@
     sums[0:1], sums[1:2], mine, theirs = lax.fori_loop(
         0, frames, finish, (zero, zero, wide, wide)
     )
+    carrier.step(4)
     for number, value in ((0, mine), (1, theirs)):
         q_sums[number : number + 1, :split] = value[:, :split]
         q_sums[number : number + 1, split:] = value[:, 2 * split :]
@@ -1423,11 +1425,11 @@
         away, bm.at[pl.ds(frames, frames)], send.at[0], recv.at[0], place.over_t()
     )
     swap_bm.start()
+    carrier.step(1)
     rt[...] = bj[...].reshape(rows_all, width).T
     s_merge[...] = dot_nn(rt[...], swap[...].reshape(rows_all, split)).astype(BF)
     swap_merge = remote(s_merge, r_merge, send.at[1], recv.at[1], place.over_t())
     swap_merge.start()
-    carrier.step(1)
     if chained:
         hops.hop(1)
     rt[...] = joined[...].reshape(rows_all, width).T
@@ -1474,10 +1476,10 @@
         swap_mix.wait()
         for k in range(blocks):
             shard_mix[k] = (mix_rows(k, place.t) + r_mix[k].astype(F32)).astype(BF)
+    carrier.step(2)
     if chained:
         hops.hop(2)
     lax.fori_loop(tiles // 3, 2 * tiles // 3, one, 0)
-    carrier.step(2)
     if chained:
         hops.hop(3)
     lax.fori_loop(2 * tiles // 3, tiles, one, 0)

time: 679 us -> 673 us (level)
    pallas_call x2, Pallas kernels: 105 us -> 96.3 us  [spatial_back(): pl.pallas_call(functools.partial(spatial_back_body, grid.depth, starts_of...]
  transfers between devices with their start and end apart: 7 -> 7, of which waited for: 1 -> 1; matrix products, arithmetic and copies ran while one was open for 6% -> 6% of each run, Pallas kernels for 58% -> 57%
where the time goes in v7:
time: 673 us; the launch traced here: 669 us
  Pallas kernels  600 us (89%)
  local copies, waits for them, and re-layouts  29.9 us (4%)
  other arithmetic  29.5 us (4%)
    pallas_call x6, Pallas kernels, kernel_call(): pl.pallas_call(functools.partial(body, staging), in_specs=staging.in_spec...  217 us
    pallas_call x2, Pallas kernels, temporal_back(): pl.pallas_call(functools.partial(temporal_back_body, grid.depth, starts_o...  110 us
    pallas_call x2, Pallas kernels, spatial_back(): pl.pallas_call(functools.partial(spatial_back_body, grid.depth, starts_of...  96.3 us
    pallas_call x2, Pallas kernels, feed_back(): pl.pallas_call(functools.partial(feed_back_body, grid.depth, starts_of(pa...  79.5 us
    pallas_call x1, Pallas kernels, tail_sums(): pl.pallas_call(functools.partial(tail_body, grid.depth, starts_of(parts),...  48.5 us
    pallas_call x1, Pallas kernels, first_gather(): pl.pallas_call(functools.partial(first_body, tuple(swapped), depth, len(n...  48.4 us
  transfers between devices with their start and end apart: 7, of which 1 were waited for; matrix products, arithmetic and copies ran while one was open for 6% of the time, Pallas kernels for 57%

profile of v7, /device:TPU:0, one launch (start us, length us, event | category | flops | bytes accessed | tf_op | source)
XLA Modules:
  0.0 668.5 jit_solution(15659432021341825189)
XLA Ops:
  0.7 0.8 slice_bitcast_fusion.27
  1.5 0.7 pad_maximum_fusion.11
  2.7 1.8 constant_dynamic-slice_fusion.2
  4.6 2.6 collective-permute-start
  7.8 0.6 slice_bitcast_fusion.8
  8.4 0.7 slice_bitcast_fusion.4
  9.1 0.7 slice_bitcast_fusion.1
  10.7 0.7 pad_maximum_fusion.9.refs_14_
  11.4 0.7 pad_maximum_fusion.8.refs_13_
  12.0 0.7 pad_maximum_fusion.7.refs_3_
  12.7 0.7 pad_maximum_fusion.6.refs_0_
  13.4 48.4 %first_gather.1 = (bf16[4,2,2,48,1152]{4,3,2,1,0:T(8,128)(2,1)}, bf16[4,2,2,48,384]{4,3,2,1,0:T(8,128)(2,1)}, bf16[4,2,2,48,384]{4,3,2,1,0:T(8,128)(2,1)}, bf16[...) custom-call(bf16[48,1152]{1,0:T(8,128)(2,1)} %pad_maximum_fusion.6.r, ...), custom_call_target="tpu_custom_call" | custom-call | flops 20000000000 | bytes 30000000 | tf_op jit(solution)/shard_map/first_gather/pallas_call | solution.py:815
  61.8 1.3 fusion.10
  63.1 0.7 slice_bitcast_fusion
  63.8 1.2 fusion.refs_1_.refs_2_
  66.9 0.9 copy.133
  69.6 1.4 collective-permute-done.1
  71.2 1.8 maximum_convert_fusion.refs_0_
  73.0 49.8 %temporal_forward.2 = (f32[4,208,768]{2,1,0:T(8,128)}, f32[4,208,768]{2,1,0:T(8,128)}, f32[4,208,1]{2,1,0:T(8,128)}, bf16[8,208,768]{2,1,0:T(8,128)(2,1)}, bf16[...) custom-call(f32[4,208,768]{2,1,0:T(8,128)} %maximum_convert_fusion.r, ...), custom_call_target="tpu_custom_call" | custom-call | flops 20000000000 | bytes 30000000 | tf_op jit(solution)/shard_map/temporal_forward/pallas_call | solution.py:756
  122.8 28.7 %spatial_forward.2 = (f32[4,208,768]{2,1,0:T(8,128)}, f32[4,208,768]{2,1,0:T(8,128)}, f32[4,208,1]{2,1,0:T(8,128)}, bf16[4,208,768]{2,1,0:T(8,128)(2,1)}, bf16[4...) custom-call(s32[1]{0:T(128)} %bitcast.1.refs_0_, ...), custom_call_target="tpu_custom_call" | custom-call | flops 20000000000 | bytes 30000000 | tf_op jit(solution)/shard_map/spatial_forward/pallas_call | solution.py:756
  151.5 35.0 %feed_forward.2 = (f32[4,208,768]{2,1,0:T(8,128)}, f32[4,208,768]{2,1,0:T(8,128)}, f32[4,208,1]{2,1,0:T(8,128)}, bf16[4,208,768]{2,1,0:T(8,128)(2,1)}, bf16[4,20...) custom-call(f32[4,208,768]{2,1,0:T(8,128)} %get-tuple-element.171.re, ...), custom_call_target="tpu_custom_call" | custom-call | flops 20000000000 | bytes 30000000 | tf_op jit(solution)/shard_map/feed_forward/pallas_call | solution.py:756
  186.5 46.3 %temporal_forward.3 = (f32[4,208,768]{2,1,0:T(8,128)}, f32[4,208,768]{2,1,0:T(8,128)}, f32[4,208,1]{2,1,0:T(8,128)}, bf16[8,208,768]{2,1,0:T(8,128)(2,1)}, bf16[...) custom-call(f32[4,208,768]{2,1,0:T(8,128)} %get-tuple-element.179.re, ...), custom_call_target="tpu_custom_call" | custom-call | flops 20000000000 | bytes 30000000 | tf_op jit(solution)/shard_map/temporal_forward/pallas_call | solution.py:756
  232.8 30.7 %spatial_forward.3 = (f32[4,208,768]{2,1,0:T(8,128)}, f32[4,208,768]{2,1,0:T(8,128)}, f32[4,208,1]{2,1,0:T(8,128)}, bf16[4,208,768]{2,1,0:T(8,128)(2,1)}, bf16[4...) custom-call(s32[1]{0:T(128)} %bitcast.1.refs_0_, ...), custom_call_target="tpu_custom_call" | custom-call | flops 20000000000 | bytes 30000000 | tf_op jit(solution)/shard_map/spatial_forward/pallas_call | solution.py:756
  263.5 26.8 %feed_forward.3 = (f32[4,208,768]{2,1,0:T(8,128)}, f32[4,208,768]{2,1,0:T(8,128)}, f32[4,208,1]{2,1,0:T(8,128)}, bf16[4,208,768]{2,1,0:T(8,128)(2,1)}, bf16[4,20...) custom-call(f32[4,208,768]{2,1,0:T(8,128)} %get-tuple-element.193.re, ...), custom_call_target="tpu_custom_call" | custom-call | flops 20000000000 | bytes 30000000 | tf_op jit(solution)/shard_map/feed_forward/pallas_call | solution.py:756
  290.3 1.3 bitcast_select_fusion
  291.6 1.1 copy.72
  294.2 1.1 copy.65
  295.8 1.3 broadcast_select_fusion.3
  297.1 2.1 convert_multiply_fusion.refs_0_
  299.1 32.0 %feed_back.2 = (f32[4,208,768]{2,1,0:T(8,128)}, f32[8,768]{1,0:T(8,128)}, bf16[768,1536]{1,0:T(8,128)(2,1)}, bf16[768,1536]{1,0:T(8,128)(2,1)}, f32[1,1536]{1,0:T(1,128)}, /*index=5*/f32[1,1536]{1,0:T(1,128)}) custom-call(f32[4,208,768]{2,1,0:T(8,128)} %convert_multiply_fusion.refs_0_, bf16[4,208,768]{2,1,0:T(8,128)(2,1)} %get-tuple-element.200.refs_1_, ...), custom_call_target="tpu_custom_call" | custom-call | flops 24000000000 | bytes 30000000 | tf_op jit(solution)/shard_map/feed_back/pallas_call | solution.py:1205
  331.2 49.4 %spatial_stage.2 = (f32[4,208,768]{2,1,0:T(8,128)}, f32[8,768]{1,0:T(8,128)}, f32[8,768]{1,0:T(8,128)}, bf16[768,1152]{1,0:T(8,128)(2,1)}, bf16[768,384]{1,0:T(8...) custom-call(s32[1]{0:T(128)} %bitcast.1.refs_0_, f32[4,208,768]{2,1,0:T(8,128)} %get-tuple-element.207.refs_1_, ...), custom_call_target="tpu_custom_call" | custom-call | flops 24000000000 | bytes 30000000 | tf_op jit(solution)/shard_map/spatial_stage/pallas_call | solution.py:1356
  380.6 50.6 %temporal_stage.2 = (f32[4,208,768]{2,1,0:T(8,128)}, f32[8,768]{1,0:T(8,128)}, f32[8,768]{1,0:T(8,128)}, bf16[768,1152]{1,0:T(8,128)(2,1)}, bf16[768,384]{1,0:T(...) custom-call(f32[4,208,768]{2,1,0:T(8,128)} %get-tuple-element.217.refs_0, ...), custom_call_target="tpu_custom_call" | custom-call | flops 24000000000 | bytes 30000000 | tf_op jit(solution)/shard_map/temporal_stage/pallas_call | solution.py:1548
  431.2 47.4 %feed_back.3 = (f32[4,208,768]{2,1,0:T(8,128)}, f32[8,768]{1,0:T(8,128)}, bf16[768,1536]{1,0:T(8,128)(2,1)}, bf16[768,1536]{1,0:T(8,128)(2,1)}, f32[1,1536]{1,0:...) custom-call(f32[4,208,768]{2,1,0:T(8,128)} %get-tuple-element.227.refs_0_, ...), custom_call_target="tpu_custom_call" | custom-call | flops 24000000000 | bytes 30000000 | tf_op jit(solution)/shard_map/feed_back/pallas_call | solution.py:1205
  478.7 46.8 %spatial_stage.3 = (f32[4,208,768]{2,1,0:T(8,128)}, f32[8,768]{1,0:T(8,128)}, f32[8,768]{1,0:T(8,128)}, bf16[768,1152]{1,0:T(8,128)(2,1)}, bf16[768,384]{1,0:T(8...) custom-call(s32[1]{0:T(128)} %bitcast.1.refs_0_, f32[4,208,768]{2,1,0:T(8,128)} %get-tuple-element.238.refs_1_, ...), custom_call_target="tpu_custom_call" | custom-call | flops 24000000000 | bytes 30000000 | tf_op jit(solution)/shard_map/spatial_stage/pallas_call | solution.py:1356
  525.6 0.8 fusion.14
  526.4 1.3 broadcast_select_fusion.14
  527.7 0.8 fusion.13
  529.4 59.7 %temporal_stage.3 = (f32[4,208,768]{2,1,0:T(8,128)}, f32[8,768]{1,0:T(8,128)}, f32[8,768]{1,0:T(8,128)}, bf16[768,1152]{1,0:T(8,128)(2,1)}, bf16[768,384]{1,0:T(...) custom-call(f32[4,208,768]{2,1,0:T(8,128)} %get-tuple-element.248.re, ...), custom_call_target="tpu_custom_call" | custom-call | flops 24000000000 | bytes 30000000 | tf_op jit(solution)/shard_map/temporal_stage/pallas_call | solution.py:1548
  589.0 0.7 slice.226
  589.7 0.8 fusion.11
  590.6 0.9 slice_bitcast_fusion.25
  591.5 0.7 slice_bitcast_fusion.23
  592.3 1.3 broadcast_select_fusion.10
  593.6 1.1 copy.68
  594.7 1.5 collective-permute-start.4
  596.4 0.7 copy.92
  597.0 1.3 broadcast_select_fusion.12
  599.2 0.8 stack_reshape.14
  600.0 0.8 stack_reshape.15
  601.4 1.0 maximum_bitcast_fusion.2
  602.4 1.0 maximum_bitcast_fusion.1
  603.5 0.7 maximum_bitcast_fusion.7
  604.1 0.9 pad_maximum_fusion.3
  605.0 0.9 pad_maximum_fusion.2
  605.9 1.1 broadcast_select_fusion.8
  607.0 48.5 %sum_rows.1 = (f32[48,1152]{1,0:T(8,128)}, f32[48,384]{1,0:T(8,128)}, f32[24,768]{1,0:T(8,128)}, f32[8,768]{1,0:T(8,128)}, bf16[4,98,768]{2,1,0:T(8,128)(2,1)}) custom-call(bf16[4,2,2,48,1152]{4,3,2,1,0:T(8,128)(2,1)} %bitcast.239, bf16[4,2,2,48,384]{4,3,2,1,0:T(8,128)(2,1)} %bitcast.267, bf16[4,2,2,24,768]{4,3,2,1,0:T(8,128)(2,1)} %bitcast.268, ...), custom_call_target="tpu_custom_call" | custom-call | flops 20000000000 | bytes 30000000 | tf_op jit(solution)/shard_map/sum_rows/pallas_call | solution.py:532
  655.5 0.7 slice_bitcast_fusion.26
  656.2 0.7 slice_bitcast_fusion.24
  657.0 1.4 select_bitcast_fusion.3
  658.6 1.5 copy.80
  663.1 1.0 copy.84
  664.5 2.4 copy.81
  666.9 0.7 pad_maximum_fusion.4
  667.6 0.7 pad_maximum_fusion.5
  (163 shorter events, 13.2 us)
Async XLA Ops:
  0.6 6.5 copy-start.41
  0.7 7.1 %copy-start.26 = (bf16[2,24,768]{2,1,0:T(8,128)(2,1)S(1)}, bf16[2,24,768]{2,1,0:T(8,128)(2,1)}, u32[]{:S(2)}) copy-start(bf16[2,24,768]{2,1,0:T(8,128)(2,1)} %param.24) | copy-start | bytes 221188
  0.7 7.8 %copy-start.22 = (bf16[2,2,384,48]{2,3,1,0:T(8,128)(2,1)S(1)}, bf16[2,2,384,48]{2,3,1,0:T(8,128)(2,1)}, u32[]{:S(2)}) copy-start(bf16[2,2,384,48]{2,3,1,0:T(8,128)(2,1)} %param.22) | copy-start | bytes 442372
  0.7 8.4 %copy-start.12 = (bf16[2,48,1536]{2,1,0:T(8,128)(2,1)S(1)}, bf16[2,48,1536]{2,1,0:T(8,128)(2,1)}, u32[]{:S(2)}) copy-start(bf16[2,48,1536]{2,1,0:T(8,128)(2,1)} %param.25) | copy-start | bytes 884740
  0.7 9.1 %copy-start.11 = (bf16[2,2,48,3,384]{4,2,3,1,0:T(8,128)(2,1)S(1)}, bf16[2,2,48,3,384]{4,2,3,1,0:T(8,128)(2,1)}, u32[]{:S(2)}) copy-start(bf16[2,2,48,3,384]{4,2,3,1,0:T(8,128)(2,1)} %param.20) | copy-start | bytes 1327108
  2.2 65.7 %collective-permute-start.2 = (f32[2,2304]{1,0:T(2,128)S(1)}, f32[2,2304]{1,0:T(2,128)S(1)}, u32[]{:S(2)}, u32[]{:S(2)}) collective-permute-start(f32[2,2304]{1,0:T(2,128)S(1)} %pad_maximum_fusion.11), channel_id=1, source_target_pairs={{0,1},{1,0},{2,3},{3,2},{4,5},{5,4},{6,7},{7,6},{8,9},{9,8},{10,11... | collective-permute-start | bytes 55304 | tf_op jit(solution)/shard_map/ppermute | solution.py:145
  2.7 7.1 %copy-start.5 = (f32[2,4,98,768]{3,1,2,0:T(4,128)S(1)}, f32[2,4,98,768]{3,1,2,0:T(4,128)}, u32[]{:S(2)}) copy-start(f32[2,4,98,768]{3,1,2,0:T(4,128)} %param.15) | copy-start | bytes 7225348
  4.6 63.9 %collective-permute-start = (bf16[4,98,768]{2,0,1:T(4,128)(2,1)S(1)}, bf16[4,98,768]{2,0,1:T(4,128)(2,1)S(1)}, u32[]{:S(2)}, u32[]{:S(2)}) collective-permute-start(bf16[4,98,768]{2,0,1:T(4,128)(2,1)S(1)} %get-tuple-element.359), channel_id=1, source_target_pairs={{0,2},{1,3},{2,0},{3,1},{4,6},{5,7},{6,4},{7,5},{8,10},{9,11},{10,... | collective-permute-start | bytes 1806344 | tf_op jit(solution)/shard_map/ppermute | solution.py:145
  13.3 48.4 %copy-start.40 = (s32[10]{0:T(128)S(1)}, s32[10]{0:T(128)}, u32[]{:S(2)}) copy-start(s32[10]{0:T(128)} %param.17) | copy-start | bytes 124
  13.3 49.7 %copy-start.13 = (bf16[2,1536,48]{1,2,0:T(8,128)(2,1)S(1)}, bf16[2,1536,48]{1,2,0:T(8,128)(2,1)}, u32[]{:S(2)}) copy-start(bf16[2,1536,48]{1,2,0:T(8,128)(2,1)} %param.27) | copy-start | bytes 884740
  13.3 51.7 %copy-start.33 = (f32[2,4,768]{2,1,0:T(4,128)S(1)}, f32[2,4,768]{2,1,0:T(4,128)}, u32[]{:S(2)}) copy-start(f32[2,4,768]{2,1,0:T(4,128)} %param.23) | copy-start | bytes 73732
  13.4 52.3 %copy-start.34 = (f32[2,3,768]{2,0,1:T(2,128)S(1)}, f32[2,3,768]{2,0,1:T(2,128)}, u32[]{:S(2)}) copy-start(f32[2,3,768]{2,0,1:T(2,128)} %param.18) | copy-start | bytes 55300
  13.4 52.9 %copy-start.35 = (f32[2,3,768]{2,0,1:T(2,128)S(1)}, f32[2,3,768]{2,0,1:T(2,128)}, u32[]{:S(2)}) copy-start(f32[2,3,768]{2,0,1:T(2,128)} %param.19) | copy-start | bytes 55300
  68.9 2.1 collective-permute-start.1
  290.3 3.6 copy-start.3
  292.7 3.1 collective-permute-start.5
  294.0 3.0 copy-start
  294.0 1.8 copy-start.4
  295.3 297.0 %collective-permute-start.3 = (bf16[4,98,768]{2,0,1:T(4,128)(2,1)}, bf16[4,98,768]{2,0,1:T(4,128)(2,1)}, u32[]{:S(2)}, u32[]{:S(2)}) collective-permute-start(bf16[4,98,768]{2,0,1:T(4,128)(2,1)} %copy.65), channel_id=1, source_target_pairs={{0,1},{1,0},{2,3},{3,2},{4,5},{5,4},{6,7},{7,6},{8,9},{9,8},{10,11... | collective-permute-start | bytes 1806344 | tf_op jit(solution)/shard_map/ppermute | solution.py:145
  478.7 49.8 %copy-start.39 = (f32[1,1536]{1,0:T(1,128)S(1)}, f32[1,1536]{1,0:T(1,128)}, u32[]{:S(2)}) copy-start(f32[1,1536]{1,0:T(1,128)} %get-tuple-element.264) | copy-start | bytes 18436
  478.7 49.9 %copy-start.38 = (f32[1,1536]{1,0:T(1,128)S(1)}, f32[1,1536]{1,0:T(1,128)}, u32[]{:S(2)}) copy-start(f32[1,1536]{1,0:T(1,128)} %get-tuple-element.265) | copy-start | bytes 18436
  478.7 49.9 %copy-start.37 = (f32[1,1536]{1,0:T(1,128)S(1)}, f32[1,1536]{1,0:T(1,128)}, u32[]{:S(2)}) copy-start(f32[1,1536]{1,0:T(1,128)} %get-tuple-element.267) | copy-start | bytes 18436
  478.7 50.0 %copy-start.36 = (f32[1,1536]{1,0:T(1,128)S(1)}, f32[1,1536]{1,0:T(1,128)}, u32[]{:S(2)}) copy-start(f32[1,1536]{1,0:T(1,128)} %get-tuple-element.268) | copy-start | bytes 18436
  529.3 63.0 %copy-start.1 = (bf16[4,208,768]{2,1,0:T(8,128)(2,1)S(1)}, bf16[4,208,768]{2,1,0:T(8,128)(2,1)}, u32[]{:S(2)}) copy-start(bf16[4,208,768]{2,1,0:T(8,128)(2,1)} %copy-done) | copy-start | bytes 3833860
  590.6 5.6 copy-start.2
  590.6 5.7 copy-start.25
  594.7 4.4 copy-start.16
  594.7 4.5 copy-start.15
  594.7 62.3 %collective-permute-start.4 = (bf16[4,98,768]{2,0,1:T(4,128)(2,1)}, bf16[4,98,768]{2,0,1:T(4,128)(2,1)}, u32[]{:S(2)}, u32[]{:S(2)}) collective-permute-start(bf16[4,98,768]{2,0,1:T(4,128)(2,1)} %copy.68), channel_id=1, source_target_pairs={{0,2},{1,3},{2,0},{3,1},{4,6},{5,7},{6,4},{7,5},{8,10},{9,11},{10,... | collective-permute-start | bytes 1806344 | tf_op jit(solution)/shard_map/ppermute | solution.py:145
  596.2 3.8 copy-start.14
  599.0 2.3 copy-start.23
  599.1 2.3 copy-start.24
  600.8 1.6 copy-start.7
  600.8 1.6 copy-start.8
  600.8 2.6 copy-start.18
  600.8 2.6 copy-start.19
  600.8 2.6 copy-start.20
  600.8 2.6 copy-start.21
  601.0 2.4 copy-start.28
  601.0 2.4 copy-start.29
  601.3 4.6 collective-permute-start.6
  658.4 1.7 slice-start
  658.4 4.2 copy-start.17
  658.6 4.3 copy-start.6
  662.9 1.3 copy-start.9
  664.5 2.4 copy-start.30
  664.5 2.4 copy-start.32
  664.5 2.4 copy-start.10
  664.5 3.1 copy-start.27
  664.5 3.1 copy-start.31

commit v8 on v7

--- a/solution.py
+++ b/solution.py
@@ -1483,8 +1483,6 @@
     if chained:
         hops.hop(3)
     lax.fori_loop(2 * tiles // 3, tiles, one, 0)
-    if chained:
-        hops.hop(4)
     carrier.step(3)
 
     def toward(f, carry):
@@ -1494,6 +1492,8 @@
     lax.fori_loop(0, frames, toward, 0)
     swap_back = remote(s_back, r_back, send.at[2], recv.at[2], place.over_t())
     swap_back.start()
+    if chained:
+        hops.hop(4)
     nt[...] = normed[...].reshape(2 * rows_all, width).T
     for part in range(3):
         cols = slice(part * split, (part + 1) * split)

time: 673 us -> 673 us (level)
  no operation moved by 1% of the time
where the time goes in v8:
time: 673 us; the launch traced here: 669 us
  Pallas kernels  600 us (89%)
  local copies, waits for them, and re-layouts  29.9 us (4%)
  other arithmetic  29.5 us (4%)
    pallas_call x6, Pallas kernels, kernel_call(): pl.pallas_call(functools.partial(body, staging), in_specs=staging.in_spec...  217 us
    pallas_call x2, Pallas kernels, temporal_back(): pl.pallas_call(functools.partial(temporal_back_body, grid.depth, starts_o...  110 us
    pallas_call x2, Pallas kernels, spatial_back(): pl.pallas_call(functools.partial(spatial_back_body, grid.depth, starts_of...  96.3 us
    pallas_call x2, Pallas kernels, feed_back(): pl.pallas_call(functools.partial(feed_back_body, grid.depth, starts_of(pa...  79.5 us
    pallas_call x1, Pallas kernels, tail_sums(): pl.pallas_call(functools.partial(tail_body, grid.depth, starts_of(parts),...  48.5 us
    pallas_call x1, Pallas kernels, first_gather(): pl.pallas_call(functools.partial(first_body, tuple(swapped), depth, len(n...  48.4 us
  transfers between devices with their start and end apart: 7, of which 1 were waited for; matrix products, arithmetic and copies ran while one was open for 6% of the time, Pallas kernels for 57%

profile of v8, /device:TPU:0, one launch (start us, length us, event | category | flops | bytes accessed | tf_op | source)
XLA Modules:
  0.0 668.6 jit_solution(12011937220290814522)
XLA Ops:
  0.7 0.8 slice_bitcast_fusion.27
  1.5 0.7 pad_maximum_fusion.11
  2.7 1.8 constant_dynamic-slice_fusion.2
  4.6 2.6 collective-permute-start
  7.8 0.6 slice_bitcast_fusion.8
  8.4 0.7 slice_bitcast_fusion.4
  9.1 0.7 slice_bitcast_fusion.1
  10.7 0.7 pad_maximum_fusion.9.refs_14_
  11.4 0.7 pad_maximum_fusion.8.refs_13_
  12.0 0.7 pad_maximum_fusion.7.refs_3_
  12.7 0.7 pad_maximum_fusion.6.refs_0_
  13.4 48.4 %first_gather.1 = (bf16[4,2,2,48,1152]{4,3,2,1,0:T(8,128)(2,1)}, bf16[4,2,2,48,384]{4,3,2,1,0:T(8,128)(2,1)}, bf16[4,2,2,48,384]{4,3,2,1,0:T(8,128)(2,1)}, bf16[...) custom-call(bf16[48,1152]{1,0:T(8,128)(2,1)} %pad_maximum_fusion.6.r, ...), custom_call_target="tpu_custom_call" | custom-call | flops 20000000000 | bytes 30000000 | tf_op jit(solution)/shard_map/first_gather/pallas_call | solution.py:815
  61.8 1.3 fusion.10
  63.1 0.7 slice_bitcast_fusion
  63.8 1.2 fusion.refs_1_.refs_2_
  66.9 0.9 copy.133
  69.6 1.4 collective-permute-done.1
  71.2 1.8 maximum_convert_fusion.refs_0_
  73.0 49.8 %temporal_forward.2 = (f32[4,208,768]{2,1,0:T(8,128)}, f32[4,208,768]{2,1,0:T(8,128)}, f32[4,208,1]{2,1,0:T(8,128)}, bf16[8,208,768]{2,1,0:T(8,128)(2,1)}, bf16[...) custom-call(f32[4,208,768]{2,1,0:T(8,128)} %maximum_convert_fusion.r, ...), custom_call_target="tpu_custom_call" | custom-call | flops 20000000000 | bytes 30000000 | tf_op jit(solution)/shard_map/temporal_forward/pallas_call | solution.py:756
  122.8 28.7 %spatial_forward.2 = (f32[4,208,768]{2,1,0:T(8,128)}, f32[4,208,768]{2,1,0:T(8,128)}, f32[4,208,1]{2,1,0:T(8,128)}, bf16[4,208,768]{2,1,0:T(8,128)(2,1)}, bf16[4...) custom-call(s32[1]{0:T(128)} %bitcast.1.refs_0_, ...), custom_call_target="tpu_custom_call" | custom-call | flops 20000000000 | bytes 30000000 | tf_op jit(solution)/shard_map/spatial_forward/pallas_call | solution.py:756
  151.5 35.0 %feed_forward.2 = (f32[4,208,768]{2,1,0:T(8,128)}, f32[4,208,768]{2,1,0:T(8,128)}, f32[4,208,1]{2,1,0:T(8,128)}, bf16[4,208,768]{2,1,0:T(8,128)(2,1)}, bf16[4,20...) custom-call(f32[4,208,768]{2,1,0:T(8,128)} %get-tuple-element.171.re, ...), custom_call_target="tpu_custom_call" | custom-call | flops 20000000000 | bytes 30000000 | tf_op jit(solution)/shard_map/feed_forward/pallas_call | solution.py:756
  186.5 46.3 %temporal_forward.3 = (f32[4,208,768]{2,1,0:T(8,128)}, f32[4,208,768]{2,1,0:T(8,128)}, f32[4,208,1]{2,1,0:T(8,128)}, bf16[8,208,768]{2,1,0:T(8,128)(2,1)}, bf16[...) custom-call(f32[4,208,768]{2,1,0:T(8,128)} %get-tuple-element.179.re, ...), custom_call_target="tpu_custom_call" | custom-call | flops 20000000000 | bytes 30000000 | tf_op jit(solution)/shard_map/temporal_forward/pallas_call | solution.py:756
  232.8 30.7 %spatial_forward.3 = (f32[4,208,768]{2,1,0:T(8,128)}, f32[4,208,768]{2,1,0:T(8,128)}, f32[4,208,1]{2,1,0:T(8,128)}, bf16[4,208,768]{2,1,0:T(8,128)(2,1)}, bf16[4...) custom-call(s32[1]{0:T(128)} %bitcast.1.refs_0_, ...), custom_call_target="tpu_custom_call" | custom-call | flops 20000000000 | bytes 30000000 | tf_op jit(solution)/shard_map/spatial_forward/pallas_call | solution.py:756
  263.5 26.8 %feed_forward.3 = (f32[4,208,768]{2,1,0:T(8,128)}, f32[4,208,768]{2,1,0:T(8,128)}, f32[4,208,1]{2,1,0:T(8,128)}, bf16[4,208,768]{2,1,0:T(8,128)(2,1)}, bf16[4,20...) custom-call(f32[4,208,768]{2,1,0:T(8,128)} %get-tuple-element.193.re, ...), custom_call_target="tpu_custom_call" | custom-call | flops 20000000000 | bytes 30000000 | tf_op jit(solution)/shard_map/feed_forward/pallas_call | solution.py:756
  290.3 1.3 bitcast_select_fusion
  291.6 1.1 copy.72
  294.2 1.1 copy.65
  295.8 1.3 broadcast_select_fusion.3
  297.1 2.1 convert_multiply_fusion.refs_0_
  299.1 32.0 %feed_back.2 = (f32[4,208,768]{2,1,0:T(8,128)}, f32[8,768]{1,0:T(8,128)}, bf16[768,1536]{1,0:T(8,128)(2,1)}, bf16[768,1536]{1,0:T(8,128)(2,1)}, f32[1,1536]{1,0:T(1,128)}, /*index=5*/f32[1,1536]{1,0:T(1,128)}) custom-call(f32[4,208,768]{2,1,0:T(8,128)} %convert_multiply_fusion.refs_0_, bf16[4,208,768]{2,1,0:T(8,128)(2,1)} %get-tuple-element.200.refs_1_, ...), custom_call_target="tpu_custom_call" | custom-call | flops 24000000000 | bytes 30000000 | tf_op jit(solution)/shard_map/feed_back/pallas_call | solution.py:1205
  331.2 49.4 %spatial_stage.2 = (f32[4,208,768]{2,1,0:T(8,128)}, f32[8,768]{1,0:T(8,128)}, f32[8,768]{1,0:T(8,128)}, bf16[768,1152]{1,0:T(8,128)(2,1)}, bf16[768,384]{1,0:T(8...) custom-call(s32[1]{0:T(128)} %bitcast.1.refs_0_, f32[4,208,768]{2,1,0:T(8,128)} %get-tuple-element.207.refs_1_, ...), custom_call_target="tpu_custom_call" | custom-call | flops 24000000000 | bytes 30000000 | tf_op jit(solution)/shard_map/spatial_stage/pallas_call | solution.py:1356
  380.6 50.6 %temporal_stage.2 = (f32[4,208,768]{2,1,0:T(8,128)}, f32[8,768]{1,0:T(8,128)}, f32[8,768]{1,0:T(8,128)}, bf16[768,1152]{1,0:T(8,128)(2,1)}, bf16[768,384]{1,0:T(...) custom-call(f32[4,208,768]{2,1,0:T(8,128)} %get-tuple-element.217.refs_0, ...), custom_call_target="tpu_custom_call" | custom-call | flops 24000000000 | bytes 30000000 | tf_op jit(solution)/shard_map/temporal_stage/pallas_call | solution.py:1548
  431.2 47.4 %feed_back.3 = (f32[4,208,768]{2,1,0:T(8,128)}, f32[8,768]{1,0:T(8,128)}, bf16[768,1536]{1,0:T(8,128)(2,1)}, bf16[768,1536]{1,0:T(8,128)(2,1)}, f32[1,1536]{1,0:...) custom-call(f32[4,208,768]{2,1,0:T(8,128)} %get-tuple-element.227.refs_0_, ...), custom_call_target="tpu_custom_call" | custom-call | flops 24000000000 | bytes 30000000 | tf_op jit(solution)/shard_map/feed_back/pallas_call | solution.py:1205
  478.7 46.8 %spatial_stage.3 = (f32[4,208,768]{2,1,0:T(8,128)}, f32[8,768]{1,0:T(8,128)}, f32[8,768]{1,0:T(8,128)}, bf16[768,1152]{1,0:T(8,128)(2,1)}, bf16[768,384]{1,0:T(8...) custom-call(s32[1]{0:T(128)} %bitcast.1.refs_0_, f32[4,208,768]{2,1,0:T(8,128)} %get-tuple-element.238.refs_1_, ...), custom_call_target="tpu_custom_call" | custom-call | flops 24000000000 | bytes 30000000 | tf_op jit(solution)/shard_map/spatial_stage/pallas_call | solution.py:1356
  525.6 0.8 fusion.14
  526.4 1.3 broadcast_select_fusion.14
  527.7 0.8 fusion.13
  529.4 59.7 %temporal_stage.3 = (f32[4,208,768]{2,1,0:T(8,128)}, f32[8,768]{1,0:T(8,128)}, f32[8,768]{1,0:T(8,128)}, bf16[768,1152]{1,0:T(8,128)(2,1)}, bf16[768,384]{1,0:T(...) custom-call(f32[4,208,768]{2,1,0:T(8,128)} %get-tuple-element.248.re, ...), custom_call_target="tpu_custom_call" | custom-call | flops 24000000000 | bytes 30000000 | tf_op jit(solution)/shard_map/temporal_stage/pallas_call | solution.py:1548
  589.0 0.7 slice.226
  589.7 0.8 fusion.11
  590.6 0.9 slice_bitcast_fusion.25
  591.5 0.7 slice_bitcast_fusion.23
  592.3 1.3 broadcast_select_fusion.10
  593.6 1.1 copy.68
  594.7 1.5 collective-permute-start.4
  596.4 0.7 copy.92
  597.0 1.3 broadcast_select_fusion.12
  599.2 0.8 stack_reshape.14
  600.0 0.8 stack_reshape.15
  601.4 1.0 maximum_bitcast_fusion.2
  602.4 1.0 maximum_bitcast_fusion.1
  603.5 0.7 maximum_bitcast_fusion.7
  604.1 0.9 pad_maximum_fusion.3
  605.0 0.9 pad_maximum_fusion.2
  605.9 1.1 broadcast_select_fusion.8
  607.0 48.5 %sum_rows.1 = (f32[48,1152]{1,0:T(8,128)}, f32[48,384]{1,0:T(8,128)}, f32[24,768]{1,0:T(8,128)}, f32[8,768]{1,0:T(8,128)}, bf16[4,98,768]{2,1,0:T(8,128)(2,1)}) custom-call(bf16[4,2,2,48,1152]{4,3,2,1,0:T(8,128)(2,1)} %bitcast.239, bf16[4,2,2,48,384]{4,3,2,1,0:T(8,128)(2,1)} %bitcast.267, bf16[4,2,2,24,768]{4,3,2,1,0:T(8,128)(2,1)} %bitcast.268, ...), custom_call_target="tpu_custom_call" | custom-call | flops 20000000000 | bytes 30000000 | tf_op jit(solution)/shard_map/sum_rows/pallas_call | solution.py:532
  655.5 0.7 slice_bitcast_fusion.26
  656.2 0.7 slice_bitcast_fusion.24
  657.0 1.4 select_bitcast_fusion.3
  658.6 1.5 copy.80
  663.2 1.0 copy.84
  664.5 2.4 copy.81
  666.9 0.7 pad_maximum_fusion.4
  667.7 0.7 pad_maximum_fusion.5
  (163 shorter events, 13.2 us)
Async XLA Ops:
  0.6 6.5 copy-start.41
  0.7 7.1 %copy-start.26 = (bf16[2,24,768]{2,1,0:T(8,128)(2,1)S(1)}, bf16[2,24,768]{2,1,0:T(8,128)(2,1)}, u32[]{:S(2)}) copy-start(bf16[2,24,768]{2,1,0:T(8,128)(2,1)} %param.24) | copy-start | bytes 221188
  0.7 7.8 %copy-start.22 = (bf16[2,2,384,48]{2,3,1,0:T(8,128)(2,1)S(1)}, bf16[2,2,384,48]{2,3,1,0:T(8,128)(2,1)}, u32[]{:S(2)}) copy-start(bf16[2,2,384,48]{2,3,1,0:T(8,128)(2,1)} %param.22) | copy-start | bytes 442372
  0.7 8.4 %copy-start.12 = (bf16[2,48,1536]{2,1,0:T(8,128)(2,1)S(1)}, bf16[2,48,1536]{2,1,0:T(8,128)(2,1)}, u32[]{:S(2)}) copy-start(bf16[2,48,1536]{2,1,0:T(8,128)(2,1)} %param.25) | copy-start | bytes 884740
  0.7 9.1 %copy-start.11 = (bf16[2,2,48,3,384]{4,2,3,1,0:T(8,128)(2,1)S(1)}, bf16[2,2,48,3,384]{4,2,3,1,0:T(8,128)(2,1)}, u32[]{:S(2)}) copy-start(bf16[2,2,48,3,384]{4,2,3,1,0:T(8,128)(2,1)} %param.20) | copy-start | bytes 1327108
  2.2 65.7 %collective-permute-start.2 = (f32[2,2304]{1,0:T(2,128)S(1)}, f32[2,2304]{1,0:T(2,128)S(1)}, u32[]{:S(2)}, u32[]{:S(2)}) collective-permute-start(f32[2,2304]{1,0:T(2,128)S(1)} %pad_maximum_fusion.11), channel_id=1, source_target_pairs={{0,1},{1,0},{2,3},{3,2},{4,5},{5,4},{6,7},{7,6},{8,9},{9,8},{10,11... | collective-permute-start | bytes 55304 | tf_op jit(solution)/shard_map/ppermute | solution.py:145
  2.7 7.1 %copy-start.5 = (f32[2,4,98,768]{3,1,2,0:T(4,128)S(1)}, f32[2,4,98,768]{3,1,2,0:T(4,128)}, u32[]{:S(2)}) copy-start(f32[2,4,98,768]{3,1,2,0:T(4,128)} %param.15) | copy-start | bytes 7225348
  4.6 63.9 %collective-permute-start = (bf16[4,98,768]{2,0,1:T(4,128)(2,1)S(1)}, bf16[4,98,768]{2,0,1:T(4,128)(2,1)S(1)}, u32[]{:S(2)}, u32[]{:S(2)}) collective-permute-start(bf16[4,98,768]{2,0,1:T(4,128)(2,1)S(1)} %get-tuple-element.359), channel_id=1, source_target_pairs={{0,2},{1,3},{2,0},{3,1},{4,6},{5,7},{6,4},{7,5},{8,10},{9,11},{10,... | collective-permute-start | bytes 1806344 | tf_op jit(solution)/shard_map/ppermute | solution.py:145
  13.3 48.4 %copy-start.40 = (s32[10]{0:T(128)S(1)}, s32[10]{0:T(128)}, u32[]{:S(2)}) copy-start(s32[10]{0:T(128)} %param.17) | copy-start | bytes 124
  13.3 49.7 %copy-start.13 = (bf16[2,1536,48]{1,2,0:T(8,128)(2,1)S(1)}, bf16[2,1536,48]{1,2,0:T(8,128)(2,1)}, u32[]{:S(2)}) copy-start(bf16[2,1536,48]{1,2,0:T(8,128)(2,1)} %param.27) | copy-start | bytes 884740
  13.3 51.7 %copy-start.33 = (f32[2,4,768]{2,1,0:T(4,128)S(1)}, f32[2,4,768]{2,1,0:T(4,128)}, u32[]{:S(2)}) copy-start(f32[2,4,768]{2,1,0:T(4,128)} %param.23) | copy-start | bytes 73732
  13.4 52.3 %copy-start.34 = (f32[2,3,768]{2,0,1:T(2,128)S(1)}, f32[2,3,768]{2,0,1:T(2,128)}, u32[]{:S(2)}) copy-start(f32[2,3,768]{2,0,1:T(2,128)} %param.18) | copy-start | bytes 55300
  13.4 52.9 %copy-start.35 = (f32[2,3,768]{2,0,1:T(2,128)S(1)}, f32[2,3,768]{2,0,1:T(2,128)}, u32[]{:S(2)}) copy-start(f32[2,3,768]{2,0,1:T(2,128)} %param.19) | copy-start | bytes 55300
  68.9 2.1 collective-permute-start.1
  290.3 3.6 copy-start.3
  292.7 3.1 collective-permute-start.5
  294.0 3.0 copy-start
  294.0 1.8 copy-start.4
  295.3 297.0 %collective-permute-start.3 = (bf16[4,98,768]{2,0,1:T(4,128)(2,1)}, bf16[4,98,768]{2,0,1:T(4,128)(2,1)}, u32[]{:S(2)}, u32[]{:S(2)}) collective-permute-start(bf16[4,98,768]{2,0,1:T(4,128)(2,1)} %copy.65), channel_id=1, source_target_pairs={{0,1},{1,0},{2,3},{3,2},{4,5},{5,4},{6,7},{7,6},{8,9},{9,8},{10,11... | collective-permute-start | bytes 1806344 | tf_op jit(solution)/shard_map/ppermute | solution.py:145
  478.7 49.8 %copy-start.39 = (f32[1,1536]{1,0:T(1,128)S(1)}, f32[1,1536]{1,0:T(1,128)}, u32[]{:S(2)}) copy-start(f32[1,1536]{1,0:T(1,128)} %get-tuple-element.264) | copy-start | bytes 18436
  478.7 49.9 %copy-start.38 = (f32[1,1536]{1,0:T(1,128)S(1)}, f32[1,1536]{1,0:T(1,128)}, u32[]{:S(2)}) copy-start(f32[1,1536]{1,0:T(1,128)} %get-tuple-element.265) | copy-start | bytes 18436
  478.7 49.9 %copy-start.37 = (f32[1,1536]{1,0:T(1,128)S(1)}, f32[1,1536]{1,0:T(1,128)}, u32[]{:S(2)}) copy-start(f32[1,1536]{1,0:T(1,128)} %get-tuple-element.267) | copy-start | bytes 18436
  478.7 50.0 %copy-start.36 = (f32[1,1536]{1,0:T(1,128)S(1)}, f32[1,1536]{1,0:T(1,128)}, u32[]{:S(2)}) copy-start(f32[1,1536]{1,0:T(1,128)} %get-tuple-element.268) | copy-start | bytes 18436
  529.3 62.9 %copy-start.1 = (bf16[4,208,768]{2,1,0:T(8,128)(2,1)S(1)}, bf16[4,208,768]{2,1,0:T(8,128)(2,1)}, u32[]{:S(2)}) copy-start(bf16[4,208,768]{2,1,0:T(8,128)(2,1)} %copy-done) | copy-start | bytes 3833860
  590.6 5.6 copy-start.2
  590.6 5.7 copy-start.25
  594.7 4.4 copy-start.16
  594.7 4.5 copy-start.15
  594.7 62.3 %collective-permute-start.4 = (bf16[4,98,768]{2,0,1:T(4,128)(2,1)}, bf16[4,98,768]{2,0,1:T(4,128)(2,1)}, u32[]{:S(2)}, u32[]{:S(2)}) collective-permute-start(bf16[4,98,768]{2,0,1:T(4,128)(2,1)} %copy.68), channel_id=1, source_target_pairs={{0,2},{1,3},{2,0},{3,1},{4,6},{5,7},{6,4},{7,5},{8,10},{9,11},{10,... | collective-permute-start | bytes 1806344 | tf_op jit(solution)/shard_map/ppermute | solution.py:145
  596.2 3.8 copy-start.14
  599.1 2.3 copy-start.23
  599.1 2.3 copy-start.24
  600.8 1.6 copy-start.7
  600.8 1.6 copy-start.8
  600.8 2.6 copy-start.18
  600.8 2.6 copy-start.19
  600.8 2.6 copy-start.20
  600.8 2.6 copy-start.21
  601.0 2.4 copy-start.28
  601.0 2.4 copy-start.29
  601.3 4.6 collective-permute-start.6
  658.4 1.7 slice-start
  658.4 4.2 copy-start.17
  658.6 4.3 copy-start.6
  662.9 1.3 copy-start.9
  664.5 2.4 copy-start.30
  664.5 2.4 copy-start.32
  664.5 2.4 copy-start.10
  664.5 3.1 copy-start.27
  664.5 3.1 copy-start.31
